TPU v7x, 32 devices: a whole 2x2x4 slice. The times are simulated.
32 devices in a mesh: lev: 4 (over x, core), gy: 8 (over z, y).
Axes of the slice: x: 2, y: 2, z: 4, core: 2. Of those that a mesh axis runs over, the one named last changes fastest.
Arguments:
- forcing: bfloat16 [4, 32, 768, 1024], P('lev', None, 'gy'), may hold values from -6 to 6
- spectral_weight: bfloat16 [2, 128, 32, 32, 128], P(None, 'gy'), may hold values from -4.1875 to 4.1875
- point_weight: bfloat16 [32, 32], replicated, may hold values from -1 to 1
- point_bias: float32 [32], replicated, may hold values from -3 to 3
- decoder: bfloat16 [4, 32], replicated, may hold values from -1 to 1
- coriolis: float32 [768], P('gy'), may hold values from -1.5 to 1.5
- layer_depth: float32 [4], replicated, may hold values from 0.5 to 2
Outputs:
- equilibrium: float32 [4, 32, 768, 1024], P('lev', None, 'gy')
- residual: float32 [3, 4, 768, 1024], P(None, 'lev', 'gy')
All inputs are finite; a program needn't handle non-finite values.
Results may differ from a plain program's by a relative error of at most 0.015.
Values may be sent and summed in bfloat16 or wider, within the bound.
No kernel may reach another device: no remote copies, remote signals or barrier semaphores. Data moves between devices by JAX's collectives and lax.ppermute only.
A program may use at most 128 MiB of HBM per device.

v0:
```python
import math

import jax
import jax.numpy as jnp
from jax import lax
from jax.sharding import PartitionSpec as P

ITERS = 3


def prefix(value, axis, combine, identity):
    peers, place = (lax.axis_size(axis), lax.axis_index(axis))
    everything = lax.all_gather(value, axis)
    start = jnp.broadcast_to(jnp.asarray(identity, value.dtype), value.shape)

    def hop(k, before):
        reached = k < place
        new = combine(before, everything[k])
        return jnp.where(reached, new, before)

    return lax.fori_loop(0, peers, hop, start)


def from_behind(value, axis, steps):
    count = lax.axis_size(axis)
    initial, last = (max(0, -steps), min(count, count - steps))
    return lax.ppermute(value, axis, [(source, source + steps) for source in range(initial, last)])


def extended(value, sides, width):
    for axis, dim in sides:
        peers, length = (lax.axis_size(axis), value.shape[dim])
        up = [(i, (i + 1) % peers) for i in range(peers)]
        down = [(j, i) for i, j in up]
        last = lax.slice_in_dim(value, length - width, length, axis=dim)
        initial = lax.slice_in_dim(value, 0, width, axis=dim)
        before = lax.ppermute(last, axis, up)
        after = lax.ppermute(initial, axis, down)
        value = jnp.concatenate([before, value, after], axis=dim)
    return value


def angles(row_index, col_index, length):
    phase = row_index[:, None] * col_index[None, :] % length
    return phase.astype(jnp.float32) * (2.0 * math.pi / length)


def signed_modes(length, count):
    index = jnp.arange(count, dtype=jnp.int32)
    return jnp.where(index < count // 2, index, index + (length - count))


def forward_x(length, count):
    turned = angles(jnp.arange(length, dtype=jnp.int32), jnp.arange(count, dtype=jnp.int32), length)
    return jnp.stack([jnp.cos(turned), -jnp.sin(turned)], 0).astype(jnp.bfloat16)


def forward_y(row_index, length, count):
    turned = angles(row_index, signed_modes(length, count), length)
    cosine = jnp.cos(turned)
    sine = jnp.sin(turned)
    return jnp.stack([jnp.stack([cosine, -sine], 1), jnp.stack([sine, cosine], 1)], 0).astype(
        jnp.bfloat16
    )


def inverse_y(row_index, length, count):
    turned = angles(signed_modes(length, count), row_index, length)
    cosine = jnp.cos(turned)
    sine = jnp.sin(turned)
    return jnp.stack([jnp.stack([cosine, sine], 1), jnp.stack([-sine, cosine], 1)], 0).astype(
        jnp.bfloat16
    )


def inverse_x(length, count, total):
    index = jnp.arange(count, dtype=jnp.int32)
    turned = angles(index, jnp.arange(length, dtype=jnp.int32), length)
    factor = jnp.where(index == 0, 1.0, 2.0).astype(jnp.float32)[:, None] / total
    return jnp.stack([factor * jnp.cos(turned), -factor * jnp.sin(turned)], 0).astype(jnp.bfloat16)


def mix_modes(spectrum, weights):
    real_part = spectrum[:, :, 0]
    imag_part = spectrum[:, :, 1]
    weight_real = weights[0].astype(jnp.float32)
    weight_imag = weights[1].astype(jnp.float32)
    highest = lax.Precision.HIGHEST
    out_real = jnp.einsum(
        "klim,kiom->klom", real_part, weight_real, precision=highest
    ) - jnp.einsum("klim,kiom->klom", imag_part, weight_imag, precision=highest)
    out_imag = jnp.einsum(
        "klim,kiom->klom", real_part, weight_imag, precision=highest
    ) + jnp.einsum("klim,kiom->klom", imag_part, weight_real, precision=highest)
    return jnp.stack([out_real, out_imag], 2).astype(jnp.bfloat16)


def add_terms(earlier, later):
    return earlier + later


def roll_diff(field, axis):
    return (jnp.roll(field, -1, axis) - jnp.roll(field, 1, axis)) * 0.5


def on_device(forcing, spectral_weight, point_weight, point_bias, decoder, coriolis, layer_depth):
    level_count, channels, row_count, cell_count = forcing.shape
    group_size = lax.axis_size("gy")
    total_rows = row_count * group_size
    own_mode_count = spectral_weight.shape[1]
    mode_count = own_mode_count * group_size
    ymode_count = spectral_weight.shape[4]
    every_row = jnp.arange(total_rows, dtype=jnp.int32)
    table_fx = forward_x(cell_count, mode_count)
    table_ix = inverse_x(cell_count, mode_count, cell_count * total_rows)
    source = forcing.astype(jnp.float32) + point_bias[None, :, None, None]
    current = forcing
    updated = source
    for iteration in range(ITERS):
        near_modes = jnp.einsum(
            "lcyx,rxk->lrcky", current, table_fx, preferred_element_type=jnp.float32
        ).astype(jnp.bfloat16)
        all_rows = lax.all_to_all(near_modes, "gy", split_axis=3, concat_axis=4, tiled=True)
        table_fy = forward_y(every_row, total_rows, ymode_count)
        spectrum = jnp.einsum(
            "lrcky,ryqm->klqcm", all_rows, table_fy, preferred_element_type=jnp.float32
        )
        mixed = mix_modes(spectrum, spectral_weight)
        table_iy = inverse_y(every_row, total_rows, ymode_count)
        back_rows = jnp.einsum(
            "klqcm,qmry->lrcky", mixed, table_iy, preferred_element_type=jnp.float32
        ).astype(jnp.bfloat16)
        own_modes = lax.all_to_all(back_rows, "gy", split_axis=4, concat_axis=3, tiled=True)
        spread = jnp.einsum(
            "lrcky,rkx->lcyx", own_modes, table_ix, preferred_element_type=jnp.float32
        )
        pointwise = jnp.einsum(
            "lcyx,co->loyx", current, point_weight, preferred_element_type=jnp.float32
        )
        updated = jax.nn.gelu(spread + pointwise + source, approximate=True)
        current = updated.astype(jnp.bfloat16)
    fields = jnp.einsum(
        "lcyx,fc->flyx", updated, decoder.astype(jnp.float32), precision=lax.Precision.HIGHEST
    )
    turning = coriolis[:, None]
    east_wind = fields[0]
    north_wind = fields[1]
    upward = fields[2]
    heat = fields[3]
    level_start = lax.axis_index("lev") * level_count
    own_depth = lax.dynamic_slice_in_dim(layer_depth, level_start, level_count, 0)
    inside = jnp.cumsum(own_depth[:, None, None] * heat, axis=0)
    lower_sum = prefix(inside[-1], "lev", add_terms, jnp.zeros_like(inside[-1]))
    geopotential = inside + lower_sum[None]
    lower_wind = from_behind(upward[-1], "lev", 1)
    below_level = jnp.concatenate([lower_wind[None], upward[:-1]], 0)
    rimmed = extended(jnp.stack([north_wind, geopotential], 0), (("gy", 2),), 1)
    along_y = (rimmed[:, :, 2:, :] - rimmed[:, :, :-2, :]) * 0.5
    continuity = roll_diff(east_wind, 2) + along_y[0] + upward - below_level
    balance_x = turning * north_wind - roll_diff(geopotential, 2)
    balance_y = turning * east_wind + along_y[1]
    residual = jnp.stack([continuity, balance_x, balance_y], 0)
    return (updated, residual)


def solution(mesh):
    return jax.shard_map(
        on_device,
        mesh=mesh,
        in_specs=(
            P("lev", None, "gy", None),
            P(None, "gy", None, None, None),
            P(),
            P(),
            P(),
            P("gy"),
            P(),
        ),
        out_specs=(P("lev", None, "gy", None), P(None, "lev", "gy", None)),
        check_vma=False,
    )
```

profile of v0, /device:TPU:1, one launch (start us, length us, event | category | flops | bytes accessed | tf_op | source)
XLA Modules:
  0.0 566.2 jit_solution(12187804742954895769)
XLA Ops:
  7.2 2.2 negate_convert_fusion
  9.4 4.7 fusion.67
  14.1 2.9 copy.119
  17.0 6.9 %all-to-all-start = ((bf16[1,2,32,128,96]{4,2,1,0,3:T(8,128)(2,1)}), bf16[1,2,32,128,96]{4,2,1,0,3:T(8,128)(2,1)S(1)}, u32[]{:S(2)}, u32[]{:S(2)}) async-start(bf16[1,2,32,128,96]{4,2,1,0,3:T(8,128)(2,1)} %copy.119), calls=%async_computation | async-start | bytes 4194304 | tf_op jit(solution)/shard_map/all_to_all | solution.py:123
  23.9 1.7 negate_convert_fusion.1
  26.5 1.8 fusion.105
  28.3 42.9 %all-to-all-done = bf16[1,2,32,128,96]{4,2,1,0,3:T(8,128)(2,1)S(1)} async-done(((bf16[1,2,32,128,96]{4,2,1,0,3:T(8,128)(2,1)}), bf16[1,2,32,128,96]{4,2,1,0,3:T(8,128)(2,1)S(1)}, u32[]{:S(2)}, u32[]{:S(2)}) %all-to-all-start) | async-done | bytes 1572896 | tf_op jit(solution)/shard_map/all_to_all | solution.py:123
  71.3 1.4 copy.120
  73.2 2.7 reshape.706
  75.8 2.1 convolution_bitcast_fusion.2
  78.0 5.1 fusion.31
  83.8 9.2 %copy.122 = bf16[1,2,32,16,768]{2,3,1,0,4:T(8,128)(2,1)} copy(bf16[1,2,32,16,768]{4,2,3,1,0:T(8,128)(2,1)S(1)} %fusion.58) | data formatting | bytes 3145728 | tf_op jit(solution)/shard_map/convert_element_type | solution.py:132
  93.0 9.5 %reshape.756 = bf16[8,2,49152]{2,1,0:T(2,128)(2,1)} reshape(bf16[768,1,2,16,32]{4,3,2,1,0:T(8,128)(2,1)} %bitcast.368) | data formatting | bytes 3145728
  102.5 4.8 all-to-all-start.1
  107.4 3.0 multiply_convert_fusion
  110.3 16.3 %fusion.47 = f32[32,96,1024]{2,0,1:T(8,128)} fusion(bf16[32,96,1024]{2,1,0:T(8,128)(2,1)} %bitcast.383, bf16[32,32]{1,0:T(8,128)(2,1)S(1)} %copy-done), kind=kOutput, calls=%fused_computation.70 | convolution fusion | flops 201326592 | bytes 18876416 | tf_op jit(solution)/shard_map/lcyx,co->loyx/dot_general | solution.py:137
  126.6 17.0 %all-to-all-done.1 = bf16[8,2,49152]{2,1,0:T(2,128)(2,1)S(1)} async-done(((bf16[8,2,49152]{2,1,0:T(2,128)(2,1)}), bf16[8,2,49152]{2,1,0:T(2,128)(2,1)S(1)}, u32[]{:S(2)}, u32[]{:S(2)}) %all-to-all-start.1) | async-done | bytes 1572896 | tf_op jit(solution)/shard_map/all_to_all | solution.py:133
  143.7 5.3 reshape.757
  149.0 8.5 %copy.123 = bf16[1,2,32,16,8,96]{5,3,4,2,1,0:T(8,128)(2,1)S(1)} copy(bf16[1,2,32,16,8,96]{2,3,1,5,4,0:T(8,128)(2,1)} %bitcast.369) | data formatting | bytes 3145728 | tf_op jit(solution)/shard_map/all_to_all | solution.py:133
  157.5 16.4 %fusion.7 = bf16[1,32,96,1024]{3,2,1,0:T(8,128)(2,1)S(1)} fusion(f32[32,96,1024]{2,0,1:T(8,128)} %fusion.47, bf16[1,32,96,1024]{3,2,1,0:T(8,128)(2,1)} %param.9, f32[32]{0:T(128)S(1)} %copy-done.13, bf16[2,32,128,96]{3,2,1,0:T(8,128)(2,1)S(1)} %bitcast.387, bf16[1,128,1024]{2,1,0:T(8,128)(2,1)} %get-tuple-element.164, ...), kind=kOutput, calls=%fused_computation.23 | convolution fusion | flops 1651769344 | bytes 27263104 | tf_op jit(solution)/shard_map/lrcky,rkx->lcyx/dot_general | solution.py:134
  174.0 2.6 copy-done.3
  176.6 2.9 fusion.64
  179.5 3.4 copy.128
  182.9 51.9 %all_to_all.90 = bf16[1,2,32,128,96]{4,2,1,0,3:T(8,128)(2,1)S(1)} all-to-all(bf16[1,2,32,128,96]{4,2,1,0,3:T(8,128)(2,1)S(1)} %copy.128), channel_id=1, replica_groups=mesh['lev'=4,'gy'=8] {'gy'}, dimensions={3} | all-to-all | bytes 3145728 | tf_op jit(solution)/shard_map/all_to_all | solution.py:123
  234.8 1.4 copy.129
  236.7 2.7 reshape.723
  239.4 2.1 convolution_bitcast_fusion.1
  241.6 5.1 fusion.33
  247.4 9.2 %copy.131 = bf16[1,2,32,16,768]{2,3,1,0,4:T(8,128)(2,1)} copy(bf16[1,2,32,16,768]{4,2,3,1,0:T(8,128)(2,1)S(1)} %fusion.59) | data formatting | bytes 3145728 | tf_op jit(solution)/shard_map/convert_element_type | solution.py:132
  256.5 9.5 %reshape.758 = bf16[8,2,49152]{2,1,0:T(2,128)(2,1)} reshape(bf16[768,1,2,16,32]{4,3,2,1,0:T(8,128)(2,1)} %bitcast.370) | data formatting | bytes 3145728
  266.0 4.5 all-to-all-start.3
  270.5 11.6 %fusion.45 = f32[96,1024,32]{1,2,0:T(8,128)} fusion(bf16[32,96,1024]{2,1,0:T(8,128)(2,1)} %bitcast.385, bf16[32,32]{1,0:T(8,128)(2,1)S(1)} %copy-done), kind=kOutput, calls=%fused_computation.68 | convolution fusion | flops 201326592 | bytes 18876416 | tf_op jit(solution)/shard_map/lcyx,co->loyx/dot_general | solution.py:137
  282.1 24.2 %all-to-all-done.3 = bf16[8,2,49152]{2,1,0:T(2,128)(2,1)S(1)} async-done(((bf16[8,2,49152]{2,1,0:T(2,128)(2,1)}), bf16[8,2,49152]{2,1,0:T(2,128)(2,1)S(1)}, u32[]{:S(2)}, u32[]{:S(2)}) %all-to-all-start.3) | async-done | bytes 1572896 | tf_op jit(solution)/shard_map/all_to_all | solution.py:133
  306.3 5.3 reshape.759
  311.6 8.5 %copy.132 = bf16[1,2,32,16,8,96]{5,3,4,2,1,0:T(8,128)(2,1)S(1)} copy(bf16[1,2,32,16,8,96]{2,3,1,5,4,0:T(8,128)(2,1)} %bitcast.371) | data formatting | bytes 3145728 | tf_op jit(solution)/shard_map/all_to_all | solution.py:133
  320.1 16.4 %fusion.15 = bf16[1,32,96,1024]{3,2,1,0:T(8,128)(2,1)S(1)} fusion(f32[96,1024,32]{1,2,0:T(8,128)} %fusion.45, bf16[1,32,96,1024]{3,2,1,0:T(8,128)(2,1)} %param.9, f32[32]{0:T(128)S(1)} %copy-done.13, bf16[2,32,128,96]{3,2,1,0:T(8,128)(2,1)S(1)} %bitcast.388, bf16[1,128,1024]{2,1,0:T(8,128)(2,1)} %get-tuple-element.164, ...), kind=kOutput, calls=%fused_computation.31 | convolution fusion | flops 1651769344 | bytes 27263104 | tf_op jit(solution)/shard_map/lrcky,rkx->lcyx/dot_general | solution.py:134
  336.6 2.6 copy-done.2
  339.2 2.9 fusion.61
  342.1 3.4 copy.137
  345.5 52.0 %all_to_all.91 = bf16[1,2,32,128,96]{4,2,1,0,3:T(8,128)(2,1)S(1)} all-to-all(bf16[1,2,32,128,96]{4,2,1,0,3:T(8,128)(2,1)S(1)} %copy.137), channel_id=1, replica_groups=mesh['lev'=4,'gy'=8] {'gy'}, dimensions={3} | all-to-all | bytes 3145728 | tf_op jit(solution)/shard_map/all_to_all | solution.py:123
  397.6 1.4 copy.138
  399.5 2.7 reshape.738
  402.1 2.1 convolution_bitcast_fusion
  404.3 5.1 fusion.35
  410.1 9.2 %copy.140 = bf16[1,2,32,16,768]{2,3,1,0,4:T(8,128)(2,1)} copy(bf16[1,2,32,16,768]{4,2,3,1,0:T(8,128)(2,1)S(1)} %fusion.60) | data formatting | bytes 3145728 | tf_op jit(solution)/shard_map/convert_element_type | solution.py:132
  419.3 9.5 %reshape.760 = bf16[8,2,49152]{2,1,0:T(2,128)(2,1)} reshape(bf16[768,1,2,16,32]{4,3,2,1,0:T(8,128)(2,1)} %bitcast.372) | data formatting | bytes 3145728
  428.8 4.2 all-to-all-start.5
  434.1 11.6 %fusion.43 = f32[96,1024,32]{1,2,0:T(8,128)} fusion(bf16[32,96,1024]{2,1,0:T(8,128)(2,1)} %bitcast.384, bf16[32,32]{1,0:T(8,128)(2,1)S(1)} %copy-done), kind=kOutput, calls=%fused_computation.66 | convolution fusion | flops 201326592 | bytes 18876416 | tf_op jit(solution)/shard_map/lcyx,co->loyx/dot_general | solution.py:137
  445.7 23.2 %all-to-all-done.5 = bf16[8,2,49152]{2,1,0:T(2,128)(2,1)S(1)} async-done(((bf16[8,2,49152]{2,1,0:T(2,128)(2,1)}), bf16[8,2,49152]{2,1,0:T(2,128)(2,1)S(1)}, u32[]{:S(2)}, u32[]{:S(2)}) %all-to-all-start.5) | async-done | bytes 1572896 | tf_op jit(solution)/shard_map/all_to_all | solution.py:133
  468.9 5.3 reshape.761
  474.2 8.5 %copy.141 = bf16[1,2,32,16,8,96]{5,3,4,2,1,0:T(8,128)(2,1)S(1)} copy(bf16[1,2,32,16,8,96]{2,3,1,5,4,0:T(8,128)(2,1)} %bitcast.373) | data formatting | bytes 3145728 | tf_op jit(solution)/shard_map/all_to_all | solution.py:133
  482.8 17.6 %fusion.22 = f32[1,32,96,1024]{3,2,1,0:T(8,128)S(1)} fusion(f32[96,1024,32]{1,2,0:T(8,128)} %fusion.43, bf16[1,32,96,1024]{3,2,1,0:T(8,128)(2,1)} %param.9, f32[32]{0:T(128)S(1)} %copy-done.13, bf16[2,32,128,96]{3,2,1,0:T(8,128)(2,1)S(1)} %bitcast.386, bf16[1,128,1024]{2,1,0:T(8,128)(2,1)S(1)} %copy-done.8, bf16[1,128,1024]{2,1,0:T(8,128)(2,1)S(1)} %copy-done.9), kind=kOutput, calls=%fused_computation.38 | convolution fusion | flops 1648623616 | bytes 33554560 | tf_op jit(solution)/shard_map/lrcky,rkx->lcyx/dot_general | solution.py:134
  500.4 11.3 %fusion.23 = f32[96,1024,4]{1,2,0:T(4,128)S(1)} fusion(f32[32,96,1024]{2,1,0:T(8,128)S(1)} %bitcast.379, bf16[4,32]{1,0:T(4,128)(2,1)S(1)} %copy-done.10), kind=kOutput, calls=%fused_computation.45 | convolution fusion | flops 150994944 | bytes 14156032 | tf_op jit(solution)/shard_map/lcyx,fc->flyx/dot_general | solution.py:142
  512.8 1.4 slice_bitcast_fusion.5
  514.3 20.7 %all-gather.2.cloned.1.call-done = f32[4,96,1024]{2,1,0:T(8,128)} async-done(((f32[1,96,1024]{2,1,0:T(8,128)}), f32[4,96,1024]{2,1,0:T(8,128)}) %all-gather.2.cloned.1.call-update) | async-done | bytes 1572880 | tf_op jit(solution)/shard_map/all_gather | solution.py:13
  534.9 4.6 while.14
  534.9 1.1 add_select_fusion.6
  536.1 1.1 add_select_fusion.6
  537.2 1.1 add_select_fusion.6
  538.4 1.1 add_select_fusion.6
  539.7 4.0 collective-permute-start
  544.5 4.4 collective-permute-done.1
  549.3 3.8 collective-permute-start.2
  553.4 4.4 collective-permute-done.2
  (63 shorter events, 9.7 us)
Async XLA Ops:
  7.2 103.2 %copy-start = (bf16[32,32]{1,0:T(8,128)(2,1)S(1)}, bf16[32,32]{1,0:T(8,128)(2,1)}, u32[]{:S(2)}) copy-start(bf16[32,32]{1,0:T(8,128)(2,1)} %param.11) | copy-start | bytes 6148
  9.4 4.7 copy-start.5
  17.0 54.3 %all-to-all-start = ((bf16[1,2,32,128,96]{4,2,1,0,3:T(8,128)(2,1)}), bf16[1,2,32,128,96]{4,2,1,0,3:T(8,128)(2,1)S(1)}, u32[]{:S(2)}, u32[]{:S(2)}) async-start(bf16[1,2,32,128,96]{4,2,1,0,3:T(8,128)(2,1)} %copy.119), calls=%async_computation | async-start | bytes 4194304 | tf_op jit(solution)/shard_map/all_to_all | solution.py:123
  102.5 41.2 %all-to-all-start.1 = ((bf16[8,2,49152]{2,1,0:T(2,128)(2,1)}), bf16[8,2,49152]{2,1,0:T(2,128)(2,1)S(1)}, u32[]{:S(2)}, u32[]{:S(2)}) async-start(bf16[8,2,49152]{2,1,0:T(2,128)(2,1)} %reshape.756), calls=%async_computation.1 | async-start | bytes 3145728 | tf_op jit(solution)/shard_map/all_to_all | solution.py:133
  126.6 30.9 %copy-start.13 = (f32[32]{0:T(128)S(1)}, f32[32]{0:T(128)}, u32[]{:S(2)}) copy-start(f32[32]{0:T(128)} %param.12) | copy-start | bytes 388
  157.5 19.1 %copy-start.6 = (bf16[1,1024,128]{2,1,0:T(8,128)(2,1)S(1)}, bf16[1,1024,128]{2,1,0:T(8,128)(2,1)}, u32[]{:S(2)}) copy-start(bf16[1,1024,128]{2,1,0:T(8,128)(2,1)} %copy-done.5) | copy-start | bytes 786436
  174.0 2.6 copy-start.3
  266.0 40.2 %all-to-all-start.3 = ((bf16[8,2,49152]{2,1,0:T(2,128)(2,1)}), bf16[8,2,49152]{2,1,0:T(2,128)(2,1)S(1)}, u32[]{:S(2)}, u32[]{:S(2)}) async-start(bf16[8,2,49152]{2,1,0:T(2,128)(2,1)} %reshape.758), calls=%async_computation.3 | async-start | bytes 3145728 | tf_op jit(solution)/shard_map/all_to_all | solution.py:133
  320.1 19.1 %copy-start.7 = (bf16[1,1024,128]{2,1,0:T(8,128)(2,1)S(1)}, bf16[1,1024,128]{2,1,0:T(8,128)(2,1)}, u32[]{:S(2)}) copy-start(bf16[1,1024,128]{2,1,0:T(8,128)(2,1)} %copy-done.5) | copy-start | bytes 786436
  336.6 2.6 copy-start.2
  419.3 14.2 %copy-start.12 = (f32[4]{0:T(128)S(1)}, f32[4]{0:T(128)}, u32[]{:S(2)}) copy-start(f32[4]{0:T(128)} %param.15) | copy-start | bytes 52
  428.8 40.1 %all-to-all-start.5 = ((bf16[8,2,49152]{2,1,0:T(2,128)(2,1)}), bf16[8,2,49152]{2,1,0:T(2,128)(2,1)S(1)}, u32[]{:S(2)}, u32[]{:S(2)}) async-start(bf16[8,2,49152]{2,1,0:T(2,128)(2,1)} %reshape.760), calls=%async_computation.5 | async-start | bytes 3145728 | tf_op jit(solution)/shard_map/all_to_all | solution.py:133
  433.1 101.9 %all-gather.2.cloned.1.call-start = ((), (), s32[]{:S(2)}) async-start(), calls=%async_computation.6 | async-start | bytes 1966080 | tf_op jit(solution)/shard_map/all_gather | solution.py:13
  445.7 37.0 %copy-start.8 = (bf16[1,128,1024]{2,1,0:T(8,128)(2,1)S(1)}, bf16[1,128,1024]{2,1,0:T(8,128)(2,1)}, u32[]{:S(2)}) copy-start(bf16[1,128,1024]{2,1,0:T(8,128)(2,1)} %get-tuple-element.164) | copy-start | bytes 786436
  445.7 37.0 %copy-start.9 = (bf16[1,128,1024]{2,1,0:T(8,128)(2,1)S(1)}, bf16[1,128,1024]{2,1,0:T(8,128)(2,1)}, u32[]{:S(2)}) copy-start(bf16[1,128,1024]{2,1,0:T(8,128)(2,1)} %get-tuple-element.165) | copy-start | bytes 786436
  482.8 17.6 %copy-start.10 = (bf16[4,32]{1,0:T(4,128)(2,1)S(1)}, bf16[4,32]{1,0:T(4,128)(2,1)}, u32[]{:S(2)}) copy-start(bf16[4,32]{1,0:T(4,128)(2,1)} %param.13) | copy-start | bytes 772
  500.4 11.3 %copy-start.1 = (f32[1,32,96,1024]{3,2,1,0:T(8,128)}, f32[1,32,96,1024]{3,2,1,0:T(8,128)S(1)}, u32[]{:S(2)}) copy-start(f32[1,32,96,1024]{3,2,1,0:T(8,128)S(1)} %fusion.22) | copy-start | bytes 37748740
  514.2 25.3 %copy-start.4 = (f32[1,96,1024]{2,1,0:T(8,128)S(1)}, f32[1,96,1024]{2,1,0:T(8,128)}, u32[]{:S(2)}) copy-start(f32[1,96,1024]{2,1,0:T(8,128)} %get-tuple-element.137) | copy-start | bytes 1179652
  514.2 34.8 %copy-start.11 = (f32[96]{0:T(128)S(1)}, f32[96]{0:T(128)}, u32[]{:S(2)}) copy-start(f32[96]{0:T(128)} %param.14) | copy-start | bytes 1156
  539.7 4.8 collective-permute-start
  543.7 5.2 collective-permute-start.1
  549.3 8.5 %collective-permute-start.2 = (f32[96,1024]{1,0:T(8,128)S(1)}, f32[96,1024]{1,0:T(8,128)S(1)}, u32[]{:S(2)}, u32[]{:S(2)}) collective-permute-start(f32[96,1024]{1,0:T(8,128)S(1)} %get-tuple-element.135), channel_id=1, source_target_pairs={{0,8},{8,16},{16,24},{1,9},{9,17},{17,25},{2,10},{10,18},{18,26},{... | collective-permute-start | bytes 1179656 | tf_op jit(solution)/shard_map/ppermute | solution.py:27
Sparse Core Ops, SparseCore 0:
  514.4 20.5 all-gather.1
where the time goes:
time: 571 us; the launch traced here: 566 us
  waiting for transfers between devices  137 us (24%)
  local copies, waits for them, and re-layouts  129 us (23%)
  matrix products  120 us (21%)
  blocking collectives  104 us (18%)
  other arithmetic  32.9 us (6%)
  starting transfers between devices  28.7 us (5%)
  between operations  14.8 us (3%)
    all_to_all x2, blocking collectives, on_device(): lax.all_to_all(near_modes, 'gy', split_axis=3, concat_axis=4, tiled=True)  104 us
    all_to_all x3, waiting for transfers between devices, on_device(): lax.all_to_all(back_rows, 'gy', split_axis=4, concat_axis=3, tiled=True)  64.4 us
    dot_general x3, matrix products, on_device(): jnp.einsum('lrcky,rkx->lcyx', own_modes, table_ix, preferred_element_type...  50.4 us
    unnamed x37, local copies, waits for them, and re-layouts  50 us
    all_to_all x1, waiting for transfers between devices, on_device(): lax.all_to_all(near_modes, 'gy', split_axis=3, concat_axis=4, tiled=True)  42.9 us
    dot_general x3, matrix products, on_device(): jnp.einsum('lcyx,co->loyx', current, point_weight, preferred_element_type...  39.5 us
    convert_element_type x3, local copies, waits for them, and re-layouts, on_device(): back_rows = jnp.einsum('klqcm,qmry->lrcky', mixed, table_iy, preferred_el...  27.5 us
    all_to_all x3, local copies, waits for them, and re-layouts, on_device(): lax.all_to_all(back_rows, 'gy', split_axis=4, concat_axis=3, tiled=True)  25.5 us
  transfers between devices with their start and end apart: 8, of which 8 were waited for; matrix products, arithmetic and copies ran while one was open for 8% of the time, Pallas kernels for 0%

commit v1 on v0

v1 whole, which is shorter than its diff:
```python
import functools
import math

import jax
import jax.numpy as jnp
import numpy as np
from jax import lax
from jax.experimental import pallas as pl
from jax.experimental.pallas import tpu as pltpu
from jax.sharding import PartitionSpec as P

ITERS = 3
CHUNKS = 2
BF = jnp.bfloat16
F32 = jnp.float32
LANES = 128
PARAMS = dict(vmem_limit_bytes=48 << 20)


def cost(flops, bytes_accessed, transcendentals=0):
    return pl.CostEstimate(
        flops=int(flops), bytes_accessed=int(bytes_accessed), transcendentals=int(transcendentals)
    )


def turned(rows, cols, length):
    phase = (rows[:, None] * cols[None, :]) % length
    return phase.astype(np.float32) * np.float32(2.0 * math.pi / length)


def x_tables(cells, modes, slices, total):
    angle = turned(np.arange(modes, dtype=np.int64), np.arange(cells, dtype=np.int64), cells)
    pair = np.stack([np.cos(angle), -np.sin(angle)], 0).astype(np.float32)
    factor = (np.where(np.arange(modes) == 0, 1.0, 2.0).astype(np.float32) / np.float32(total))
    inverse = pair * factor[None, :, None]
    own = modes // slices

    def by_slice(table):
        table = table.reshape(2, slices, own, cells).transpose(1, 0, 2, 3)
        return table.reshape(slices, 2 * own, cells).astype(BF)

    return by_slice(pair), by_slice(inverse)


def y_table(rows, modes, slices):
    index = np.arange(modes, dtype=np.int64)
    signed = np.where(index < modes // 2, index, index + (rows - modes))
    angle = turned(np.arange(rows, dtype=np.int64), signed, rows)
    both = np.concatenate([np.cos(angle), np.sin(angle)], 1).astype(np.float32)
    return both.reshape(slices, rows // slices, 2 * modes).astype(BF)


def dot(a, b, dims):
    return lax.dot_general(a, b, (dims, ((), ())), preferred_element_type=F32)


def store_near(state, table, near_refs, pack, rows):
    peers = len(near_refs)
    width = LANES // pack
    near = dot(state, table, ((1,), (0,)))
    for d in range(peers):
        parts = [
            near[j * rows : (j + 1) * rows, d * width : (d + 1) * width] for j in range(pack)
        ]
        near_refs[d][0] = jnp.concatenate(parts, 1).astype(BF)


def near_kernel(pack, state_ref, table_ref, *near_refs):
    rows, cells = state_ref.shape[1:]
    state = state_ref[...].reshape(pack * rows, cells)
    store_near(state, table_ref[...], near_refs, pack, rows)


def forward_y_kernel(pack, own, peers, *refs):
    near_refs, table_ref, keep_ref, send_ref = refs[:peers], refs[peers], refs[-2], refs[-1]
    modes = table_ref.shape[1] // 2
    near = jnp.concatenate([ref[0] for ref in near_refs], 0)
    both = dot(near, table_ref[...], ((0,), (0,)))
    for j in range(pack):
        for h, out_ref in ((0, keep_ref), (1, send_ref)):
            at = (j * 2 + h) * 2 * own
            real = both[at : at + own]
            imag = both[at + own : at + 2 * own]
            out_ref[j, :, :modes] = (real[:, :modes] + imag[:, modes:]).astype(out_ref.dtype)
            out_ref[j, :, modes:] = (imag[:, :modes] - real[:, modes:]).astype(out_ref.dtype)


def mix_kernel(chunks, *refs):
    keep_refs, got_refs = refs[:chunks], refs[chunks : 2 * chunks]
    weight_ref, out_ref, spectrum, mixed = refs[2 * chunks :]
    k = pl.program_id(0)
    size = keep_refs[0].shape[0]
    modes = weight_ref.shape[-1]
    outs = weight_ref.shape[3]

    @pl.when(k == 0)
    def _():
        for n in range(chunks):
            spectrum[n * size : (n + 1) * size] = keep_refs[n][...] + got_refs[n][...].astype(F32)

    def step(i, sums):
        real, imag = sums
        value = spectrum[i, pl.ds(k, 1), :]
        s0, s1 = value[:, :modes], value[:, modes:]
        w0 = weight_ref[0, 0, i].astype(F32)
        w1 = weight_ref[1, 0, i].astype(F32)
        return real + (s0 * w0 - s1 * w1), imag + (s0 * w1 + s1 * w0)

    zero = jnp.zeros((outs, modes), F32)
    real, imag = lax.fori_loop(0, size * chunks, step, (zero, zero), unroll=8)
    mixed[k, :, :modes] = real
    mixed[k, :, modes:] = imag

    @pl.when(k == pl.num_programs(0) - 1)
    def _():
        out_ref[...] = jnp.swapaxes(mixed[...], 0, 1).astype(BF)


def inverse_y_kernel(pack, own, peers, mine_ref, theirs_ref, table_ref, *back_refs):
    modes = table_ref.shape[1] // 2
    rows = table_ref.shape[0] // peers
    parts = []
    for j in range(pack):
        for ref in (mine_ref, theirs_ref):
            value = ref[j].astype(F32)
            real, imag = value[:, :modes], value[:, modes:]
            parts.append(jnp.concatenate([real, -imag], 1))
            parts.append(jnp.concatenate([imag, real], 1))
    turned_modes = jnp.concatenate(parts, 0).astype(BF)
    back = dot(table_ref[...], turned_modes, ((1,), (1,)))
    for d in range(peers):
        back_refs[d][0] = back[d * rows : (d + 1) * rows].astype(BF)


def spread_of(pack, back_refs, table_ref):
    width = LANES // pack
    values = [ref[0].astype(F32) for ref in back_refs]
    blocks = [
        jnp.concatenate([v[:, j * width : (j + 1) * width] for v in values], 1).astype(BF)
        for j in range(pack)
    ]
    return dot(jnp.concatenate(blocks, 0), table_ref[...], ((1,), (0,)))


def update_kernel(pack, peers, *refs):
    back_refs, (point_ref, inverse_ref, forward_ref) = refs[:peers], refs[peers : peers + 3]
    state_ref, near_refs = refs[peers + 3], refs[peers + 4 :]
    rows, cells = state_ref.shape[1:]
    point = point_ref[...].reshape(pack * rows, cells)
    updated = jax.nn.gelu(spread_of(pack, back_refs, inverse_ref) + point, approximate=True)
    state = updated.astype(BF)
    state_ref[...] = state.reshape(pack, rows, cells)
    store_near(state, forward_ref[...], near_refs, pack, rows)


def last_kernel(pack, peers, first_group, *refs):
    back_refs = refs[:peers]
    point_ref, inverse_ref, decoder_ref, updated_ref, fields_ref = refs[peers:]
    rows, cells = updated_ref.shape[1:]
    group = pl.program_id(0)
    point = point_ref[...].reshape(pack * rows, cells)
    updated = jax.nn.gelu(spread_of(pack, back_refs, inverse_ref) + point, approximate=True)
    updated_ref[...] = updated.reshape(pack, rows, cells)

    @pl.when(group == 0)
    def _():
        fields_ref[...] = jnp.zeros_like(fields_ref)

    for f in range(fields_ref.shape[0]):
        total = fields_ref[f]
        for j in range(pack):
            weight = decoder_ref[f, (first_group + group) * pack + j]
            total = total + weight * updated[j * rows : (j + 1) * rows]
        fields_ref[f] = total


def pointwise_kernel(chunks, *refs):
    state_refs, (forcing_ref, weight_ref, bias_ref, out_ref) = refs[:chunks], refs[chunks:]
    channels, rows, cells = out_ref.shape
    state = jnp.concatenate([ref[...] for ref in state_refs], 0).reshape(channels * rows, cells)
    source = forcing_ref[...].reshape(channels * rows, cells).astype(F32) + bias_ref[...]
    out = dot(weight_ref[...], state, ((1,), (0,))) + source
    out_ref[...] = out.reshape(channels, rows, cells)


def on_device(forcing, spectral_weight, point_weight, point_bias, decoder, coriolis, layer_depth):
    level_count, channels, rows, cells = forcing.shape
    assert level_count == 1
    forcing = forcing[0]
    slices = lax.axis_size("gy")
    peers = slices // 2
    own = spectral_weight.shape[1]
    modes = own * slices
    ymodes = spectral_weight.shape[4]
    total_rows = rows * slices
    pack = LANES // (4 * own)
    groups = channels // pack
    part = groups // CHUNKS
    size = channels // CHUNKS
    wide = peers * 4 * own
    me = lax.axis_index("gy")

    forward_x, inverse_x = x_tables(cells, modes, slices, cells * total_rows)
    order = jnp.stack([me ^ d ^ (h * peers) for d in range(peers) for h in range(2)])
    near_table = jnp.take(jnp.asarray(forward_x), order, axis=0).reshape(wide, cells).T
    spread_table = jnp.take(jnp.asarray(inverse_x), order, axis=0).reshape(wide, cells)
    row_table = jnp.take(jnp.asarray(y_table(total_rows, ymodes, slices)), order[::2], axis=0)
    row_table = row_table.reshape(peers * rows, 2 * ymodes)

    block = next(b for b in (16, 8, rows) if rows % b == 0)
    square = jnp.kron(point_weight.T.astype(F32), jnp.eye(block, dtype=F32)).astype(BF)
    bias = jnp.repeat(point_bias, block)[:, None]

    def swap(value, distance):
        return lax.ppermute(value, "gy", [(g, g ^ distance) for g in range(slices)])

    def whole(shape):
        return pl.BlockSpec(shape, lambda i: (0,) * len(shape))

    cells_spec = pl.BlockSpec((pack, rows, cells), lambda i: (i, 0, 0))
    lane_spec = pl.BlockSpec((1, rows, LANES), lambda i: (i, 0, 0))
    lane_shape = jax.ShapeDtypeStruct((part, rows, LANES), BF)
    mode_spec = pl.BlockSpec((pack, own, 2 * ymodes), lambda i: (i, 0, 0))
    params = pltpu.CompilerParams(dimension_semantics=("arbitrary",), **PARAMS)
    tile = size * rows * cells

    def offset_spec(n):
        return pl.BlockSpec((pack, rows, cells), lambda i: (i + n * part, 0, 0))

    def near_of(n):
        return pl.pallas_call(
            functools.partial(near_kernel, pack),
            grid=(part,),
            in_specs=[offset_spec(n), whole((cells, wide))],
            out_specs=[lane_spec] * peers,
            out_shape=[lane_shape] * peers,
            compiler_params=params,
            cost_estimate=cost(2 * tile * wide, tile * 2),
            name="near",
        )(forcing, near_table)

    def exchange(parts):
        return [parts[0]] + [swap(parts[d], d) for d in range(1, peers)]

    def forward_y(parts):
        return pl.pallas_call(
            functools.partial(forward_y_kernel, pack, own, peers),
            grid=(part,),
            in_specs=[lane_spec] * peers + [whole(row_table.shape)],
            out_specs=[mode_spec] * 2,
            out_shape=[
                jax.ShapeDtypeStruct((size, own, 2 * ymodes), F32),
                jax.ShapeDtypeStruct((size, own, 2 * ymodes), BF),
            ],
            compiler_params=params,
            cost_estimate=cost(4 * part * LANES * peers * rows * ymodes, 2 * size * rows * wide),
            name="forward_y",
        )(*parts, row_table)

    def mix(kept, got, n):
        mode_whole = whole((size, own, 2 * ymodes))
        return pl.pallas_call(
            functools.partial(mix_kernel, CHUNKS),
            grid=(own,),
            in_specs=[mode_whole] * (2 * CHUNKS)
            + [pl.BlockSpec((2, 1, channels, size, ymodes), lambda k: (0, k, 0, n, 0))],
            out_specs=mode_whole,
            out_shape=jax.ShapeDtypeStruct((size, own, 2 * ymodes), BF),
            scratch_shapes=[
                pltpu.VMEM((channels, own, 2 * ymodes), F32),
                pltpu.VMEM((own, size, 2 * ymodes), F32),
            ],
            compiler_params=params,
            cost_estimate=cost(
                8 * own * channels * size * ymodes, 4 * own * channels * size * ymodes
            ),
            name="mix",
        )(*kept, *got, spectral_weight)

    def inverse_y(mine, theirs):
        return pl.pallas_call(
            functools.partial(inverse_y_kernel, pack, own, peers),
            grid=(part,),
            in_specs=[mode_spec] * 2 + [whole(row_table.shape)],
            out_specs=[lane_spec] * peers,
            out_shape=[lane_shape] * peers,
            compiler_params=params,
            cost_estimate=cost(4 * part * LANES * peers * rows * ymodes, 2 * size * rows * wide),
            name="inverse_y",
        )(mine, theirs, row_table)

    def pointwise(states):
        if len(states) == 1:
            specs = [pl.BlockSpec((channels, block, cells), lambda i: (0, i, 0))]
        else:
            specs = [pl.BlockSpec((size, block, cells), lambda i: (0, i, 0))] * CHUNKS
        return pl.pallas_call(
            functools.partial(pointwise_kernel, len(states)),
            grid=(rows // block,),
            in_specs=specs
            + [
                pl.BlockSpec((channels, block, cells), lambda i: (0, i, 0)),
                whole(square.shape),
                whole(bias.shape),
            ],
            out_specs=pl.BlockSpec((channels, block, cells), lambda i: (0, i, 0)),
            out_shape=jax.ShapeDtypeStruct((channels, rows, cells), F32),
            compiler_params=params,
            cost_estimate=cost(
                2 * channels * block * channels * rows * cells, 8 * channels * rows * cells
            ),
            name="pointwise",
        )(*states, forcing, square, bias)

    def update(backs, point, n):
        out = pl.pallas_call(
            functools.partial(update_kernel, pack, peers),
            grid=(part,),
            in_specs=[lane_spec] * peers
            + [offset_spec(n), whole(spread_table.shape), whole(near_table.shape)],
            out_specs=[cells_spec] + [lane_spec] * peers,
            out_shape=[jax.ShapeDtypeStruct((size, rows, cells), BF)] + [lane_shape] * peers,
            compiler_params=params,
            cost_estimate=cost(4 * tile * wide, 6 * tile, tile),
            name="update",
        )(*backs, point, spread_table, near_table)
        return out[0], out[1:]

    decoder_full = decoder.astype(F32)

    def last(backs, point, n):
        count = decoder.shape[0]
        return pl.pallas_call(
            functools.partial(last_kernel, pack, peers, n * part),
            grid=(part,),
            in_specs=[lane_spec] * peers
            + [
                offset_spec(n),
                whole(spread_table.shape),
                pl.BlockSpec(memory_space=pltpu.SMEM),
            ],
            out_specs=[cells_spec, whole((count, rows, cells))],
            out_shape=[
                jax.ShapeDtypeStruct((size, rows, cells), F32),
                jax.ShapeDtypeStruct((count, rows, cells), F32),
            ],
            compiler_params=params,
            cost_estimate=cost(2 * tile * wide, 8 * tile, tile),
            name="last",
        )(*backs, point, spread_table, decoder_full)

    every = range(CHUNKS)
    nears = [near_of(n) for n in every]
    states = [forcing]
    for iteration in range(ITERS):
        arrived = [exchange(parts) for parts in nears]
        point = pointwise(states)
        halves = [forward_y(parts) for parts in arrived]
        kept = [half[0] for half in halves]
        got = [swap(half[1], peers) for half in halves]
        mixed = [mix(kept, got, n) for n in every]
        theirs = [swap(value, peers) for value in mixed]
        backs = [exchange(inverse_y(mixed[n], theirs[n])) for n in every]
        if iteration < ITERS - 1:
            done = [update(backs[n], point, n) for n in every]
            states = [pair[0] for pair in done]
            nears = [pair[1] for pair in done]
    done = [last(backs[n], point, n) for n in every]
    updated = jnp.concatenate([pair[0] for pair in done], 0)
    east, north, upward, heat = [sum(pair[1][f] for pair in done) for f in range(4)]

    levels = lax.axis_size("lev")
    level = lax.axis_index("lev")

    def from_below(value, step):
        return lax.ppermute(value, "lev", [(s, s + step) for s in range(levels - step)])

    below = from_below(upward, 1)
    geopotential = lax.dynamic_index_in_dim(layer_depth, level, 0, keepdims=False) * heat
    step = 1
    while step < levels:
        geopotential = geopotential + from_below(geopotential, step)
        step *= 2

    up = [(i, (i + 1) % slices) for i in range(slices)]
    down = [(j, i) for i, j in up]
    pair = jnp.stack([north, geopotential], 0)
    before = lax.ppermute(pair[:, -1:], "gy", up)
    after = lax.ppermute(pair[:, :1], "gy", down)
    rimmed = jnp.concatenate([before, pair, after], 1)
    along_y = (rimmed[:, 2:] - rimmed[:, :-2]) * 0.5

    def along_x(field):
        return (jnp.roll(field, -1, 1) - jnp.roll(field, 1, 1)) * 0.5

    turning = coriolis[:, None]
    continuity = along_x(east) + along_y[0] + upward - below
    balance_x = turning * north - along_x(geopotential)
    balance_y = turning * east + along_y[1]
    return updated[None], jnp.stack([continuity, balance_x, balance_y], 0)[:, None]


def solution(mesh):
    return jax.shard_map(
        on_device,
        mesh=mesh,
        in_specs=(
            P("lev", None, "gy", None),
            P(None, "gy", None, None, None),
            P(),
            P(),
            P(),
            P("gy"),
            P(),
        ),
        out_specs=(P("lev", None, "gy", None), P(None, "lev", "gy", None)),
        check_vma=False,
    )
```

time: 571 us -> 355 us (0.62)
  Pallas kernels: 0 us -> 176 us
  matrix products: 120 us -> 0 us
  local copies, waits for them, and re-layouts: 129 us -> 20.4 us
  blocking collectives: 104 us -> 0 us
  waiting for transfers between devices: 137 us -> 65 us
  starting transfers between devices: 28.7 us -> 69.2 us
  between operations: 14.8 us -> 1.2 us
  other arithmetic: 32.9 us -> 19.9 us
    pallas_call x0 -> x29, Pallas kernels: none -> 176 us  [the longest x6 53.8 us: mix(): pl.pallas_call(functools.partial(mix_kernel, CHUNKS), grid=(own,), in_spe...]
    dot_general x16 -> x0, matrix products: 120 us -> none  [the longest x3 50.4 us: on_device(): jnp.einsum('lrcky,rkx->lcyx', own_modes, table_ix, preferred_element_type...]
    all_to_all x4 -> x0, waiting for transfers between devices: 107 us -> none  [the longest x3 64.4 us: on_device(): lax.all_to_all(back_rows, 'gy', split_axis=4, concat_axis=3, tiled=True)]
    all_to_all x2 -> x0, blocking collectives: 104 us -> none  [on_device(): lax.all_to_all(near_modes, 'gy', split_axis=3, concat_axis=4, tiled=True)]
    ppermute x3 -> x53, starting transfers between devices: 7.8 us -> 69.2 us  [the longest x48 43.5 us: swap(): return lax.ppermute(value, 'gy', [(g, g ^ distance) for g in range(slices)])]
    ppermute x3 -> x53, waiting for transfers between devices: 9.39 us -> 65 us  [the longest x48 50.6 us: swap(): return lax.ppermute(value, 'gy', [(g, g ^ distance) for g in range(slices)])]
    unnamed x37 -> x20, local copies, waits for them, and re-layouts: 50 us -> 5.16 us
    all_to_all x9 -> x0, local copies, waits for them, and re-layouts: 31.2 us -> none  [the longest x3 25.5 us: on_device(): lax.all_to_all(back_rows, 'gy', split_axis=4, concat_axis=3, tiled=True)]
  transfers between devices with their start and end apart: 8 -> 53, of which waited for: 8 -> 14; matrix products, arithmetic and copies ran while one was open for 8% -> 8% of each run, Pallas kernels for 0% -> 37%
where the time goes in v1:
time: 355 us; the launch traced here: 352 us
  Pallas kernels  176 us (50%)
  starting transfers between devices  69.2 us (19%)
  waiting for transfers between devices  65 us (18%)
  local copies, waits for them, and re-layouts  20.4 us (6%)
  other arithmetic  19.9 us (6%)
    pallas_call x6, Pallas kernels, mix(): pl.pallas_call(functools.partial(mix_kernel, CHUNKS), grid=(own,), in_spe...  53.8 us
    ppermute x48, waiting for transfers between devices, swap(): return lax.ppermute(value, 'gy', [(g, g ^ distance) for g in range(slices)])  50.6 us
    ppermute x48, starting transfers between devices, swap(): return lax.ppermute(value, 'gy', [(g, g ^ distance) for g in range(slices)])  43.5 us
    pallas_call x3, Pallas kernels, pointwise(): pl.pallas_call(functools.partial(pointwise_kernel, len(states)), grid=(ro...  33.8 us
    pallas_call x4, Pallas kernels, update(): pl.pallas_call(functools.partial(update_kernel, pack, peers), grid=(part,...  32.8 us
    ppermute x3, starting transfers between devices, from_below(): lax.ppermute(value, 'lev', [(s, s + step) for s in range(levels - step)])  22.7 us
    pallas_call x2, Pallas kernels, last(): pl.pallas_call(functools.partial(last_kernel, pack, peers, n * part), gri...  19.5 us
    ppermute x3, waiting for transfers between devices, from_below(): lax.ppermute(value, 'lev', [(s, s + step) for s in range(levels - step)])  14.4 us
  transfers between devices with their start and end apart: 53, of which 14 were waited for; matrix products, arithmetic and copies ran while one was open for 8% of the time, Pallas kernels for 37%

profile of v1, /device:TPU:1, one launch (start us, length us, event | category | flops | bytes accessed | tf_op | source)
XLA Modules:
  0.0 351.7 jit_solution(12451173063972160067)
XLA Ops:
  0.8 1.6 gather_fusion.2
  2.4 1.6 gather_fusion.1
  4.4 5.9 %near.3 = (bf16[8,96,128]{2,1,0:T(8,128)(2,1)S(1)}, bf16[8,96,128]{2,1,0:T(8,128)(2,1)S(1)}, bf16[8,96,128]{2,1,0:T(8,128)(2,1)S(1)}, bf16[8,96,128]{2,1,0:T(8,128)(2,1)S(1)}) custom-call(bf16[32,96,1024]{2,1,0:T(8,128)(2,1)} %bitcast.64, bf16[1024,256]{1,0:T(8,128)(2,1)S(1)} %bitcast.58), custom_call_target="tpu_custom_call" | custom-call | flops 805306368 | bytes 3145728 | tf_op jit(solution)/shard_map/near/pallas_call | solution.py:231
  10.3 2.1 collective-permute-start.3
  13.7 6.6 %near.2 = (bf16[8,96,128]{2,1,0:T(8,128)(2,1)S(1)}, bf16[8,96,128]{2,1,0:T(8,128)(2,1)}, bf16[8,96,128]{2,1,0:T(8,128)(2,1)S(1)}, bf16[8,96,128]{2,1,0:T(8,128)(2,1)S(1)}) custom-call(bf16[32,96,1024]{2,1,0:T(8,128)(2,1)} %bitcast.65, bf16[1024,256]{1,0:T(8,128)(2,1)S(1)} %bitcast.59), custom_call_target="tpu_custom_call" | custom-call | flops 805306368 | bytes 3145728 | tf_op jit(solution)/shard_map/near/pallas_call | solution.py:231
  23.2 2.2 gather_fusion
  26.5 3.6 %forward_y.7 = (f32[16,16,256]{2,1,0:T(8,128)S(1)}, bf16[16,16,256]{2,1,0:T(8,128)(2,1)}) custom-call(bf16[8,96,128]{2,1,0:T(8,128)(2,1)S(1)} %get-tuple-element.76.refs_0_, bf16[8,96,128]{2,1,0:T(8,128)(2,1)S(1)} %collective-permute-done.3.refs_1_, bf16[8,96,128]{2,1,0:T(8,128)(2,1)S(1)} %collective-permute-done.4.refs_2_, ...), custom_call_target="tpu_custom_call" | custom-call | flops 201326592 | bytes 786432 | tf_op jit(solution)/shard_map/forward_y/pallas_call | solution.py:246
  30.2 2.4 collective-permute-start.7
  32.6 1.9 forward_y.6
  35.3 1.8 collective-permute-done.7.refs_3_
  37.1 8.0 %collective-permute-done.6.refs_2_ = bf16[16,16,256]{2,1,0:T(8,128)(2,1)S(1)} collective-permute-done((bf16[16,16,256]{2,1,0:T(8,128)(2,1)S(1)}, bf16[16,16,256]{2,1,0:T(8,128)(2,1)S(1)}, u32[]{:S(2)}, u32[]{:S(2)}) %collective-permute-start.6) | collective-permute-done | bytes 131104 | tf_op jit(solution)/shard_map/ppermute | solution.py:215
  45.0 9.0 %mix.7.mine_ref = bf16[16,16,256]{2,1,0:T(8,128)(2,1)S(1)} custom-call(f32[16,16,256]{2,1,0:T(8,128)S(1)} %get-tuple-element.75.refs_0_, f32[16,16,256]{2,1,0:T(8,128)S(1)} %get-tuple-element.80.refs_1_, bf16[16,16,256]{2,1,0:T(8,128)(2,1)S(1)} %collective-permute-done.6.refs_2_, bf16[16,16,256]{2,1,0:T(8,128)(2,1)S(1)} %collective-permute-done.7.refs_3_, ...), custom_call_target="tpu_custom_call" | custom-call | flops 8388608 | bytes 4194304 | tf_op jit(solution)/shard_map/mix/pallas_call | solution.py:262
  54.1 2.8 multiply_convert_fusion
  57.1 7.8 %convert_element_type.25.refs_2_.refs_3_ = bf16[512,512]{1,0:T(8,128)(2,1)S(1)} reshape(bf16[32,16,32,16]{3,2,1,0:T(8,128)(2,1)} %multiply_convert_fusion) | data formatting | bytes 1048576 | tf_op jit(solution)/shard_map/convert_element_type | solution.py:211
  64.9 9.0 %mix.6.mine_ref = bf16[16,16,256]{2,1,0:T(8,128)(2,1)S(1)} custom-call(f32[16,16,256]{2,1,0:T(8,128)S(1)} %get-tuple-element.75.refs_0_, f32[16,16,256]{2,1,0:T(8,128)S(1)} %get-tuple-element.80.refs_1_, bf16[16,16,256]{2,1,0:T(8,128)(2,1)S(1)} %collective-permute-done.6.refs_2_, bf16[16,16,256]{2,1,0:T(8,128)(2,1)S(1)} %collective-permute-done.7.refs_3_, ...), custom_call_target="tpu_custom_call" | custom-call | flops 8388608 | bytes 4194304 | tf_op jit(solution)/shard_map/mix/pallas_call | solution.py:262
  73.9 2.4 collective-permute-start.8
  76.3 1.8 inverse_y.7
  80.8 11.9 %pointwise.3.refs_4_ = f32[32,96,1024]{2,1,0:T(8,128)} custom-call(bf16[32,96,1024]{2,1,0:T(8,128)(2,1)} %bitcast.66, bf16[32,96,1024]{2,1,0:T(8,128)(2,1)} %bitcast.67, bf16[512,512]{1,0:T(8,128)(2,1)S(1)} %convert_element_type.25.refs_2_.refs_3_, f32[512,1]{1,0:T(8,128)S(1)} %broadcast_in_dim_reshape.4.refs_3_.refs_4_), custom_call_target="tpu_custom_call" | custom-call | flops 3221225472 | bytes 25165824 | tf_op jit(solution)/shard_map/pointwise/pallas_call | solution.py:297
  92.7 1.8 inverse_y.6
  97.2 8.2 %update.5 = (bf16[16,96,1024]{2,1,0:T(8,128)(2,1)S(1)}, bf16[8,96,128]{2,1,0:T(8,128)(2,1)S(1)}, bf16[8,96,128]{2,1,0:T(8,128)(2,1)S(1)}, bf16[8,96,128]{2,1,0:T(8,128)(2,1)S(1)}, bf16[8,96,128]{2,1,0:T(8,128)(2,1)S(1)}) custom-call(bf16[8,96,128]{2,1,0:T(8,128)(2,1)S(1)} %get-tuple-element.92.refs_0_, ...), custom_call_target="tpu_custom_call" | custom-call | flops 1610612736 | bytes 9437184 | tf_op jit(solution)/shard_map/update/pallas_call | solution.py:316
  105.4 1.6 copy-done.1
  109.7 8.2 %update.4 = (bf16[16,96,1024]{2,1,0:T(8,128)(2,1)S(1)}, bf16[8,96,128]{2,1,0:T(8,128)(2,1)S(1)}, bf16[8,96,128]{2,1,0:T(8,128)(2,1)S(1)}, bf16[8,96,128]{2,1,0:T(8,128)(2,1)S(1)}, bf16[8,96,128]{2,1,0:T(8,128)(2,1)S(1)}) custom-call(bf16[8,96,128]{2,1,0:T(8,128)(2,1)S(1)} %get-tuple-element.83.refs_0_, ...), custom_call_target="tpu_custom_call" | custom-call | flops 1610612736 | bytes 9437184 | tf_op jit(solution)/shard_map/update/pallas_call | solution.py:316
  120.6 1.9 forward_y.9
  123.8 2.0 collective-permute-done.14.refs_3_
  125.8 1.9 forward_y.8
  127.7 1.6 collective-permute-start.22
  129.3 7.2 %collective-permute-done.22.refs_2_ = bf16[16,16,256]{2,1,0:T(8,128)(2,1)S(1)} collective-permute-done((bf16[16,16,256]{2,1,0:T(8,128)(2,1)S(1)}, bf16[16,16,256]{2,1,0:T(8,128)(2,1)S(1)}, u32[]{:S(2)}, u32[]{:S(2)}) %collective-permute-start.22) | collective-permute-done | bytes 131104 | tf_op jit(solution)/shard_map/ppermute | solution.py:215
  136.6 9.0 %mix.9.mine_ref = bf16[16,16,256]{2,1,0:T(8,128)(2,1)S(1)} custom-call(f32[16,16,256]{2,1,0:T(8,128)S(1)} %get-tuple-element.91.refs_0_, f32[16,16,256]{2,1,0:T(8,128)S(1)} %get-tuple-element.100.refs_1_, bf16[16,16,256]{2,1,0:T(8,128)(2,1)S(1)} %collective-permute-done.22.refs_2_, bf16[16,16,256]{2,1,0:T(8,128)(2,1)S(1)} %collective-permute-done.23.refs_3_, ...), custom_call_target="tpu_custom_call" | custom-call | flops 8388608 | bytes 4194304 | tf_op jit(solution)/shard_map/mix/pallas_call | solution.py:262
  145.6 6.1 %collective-permute-done.31.theirs_ref = bf16[16,16,256]{2,1,0:T(8,128)(2,1)S(1)} collective-permute-done((bf16[16,16,256]{2,1,0:T(8,128)(2,1)S(1)}, bf16[16,16,256]{2,1,0:T(8,128)(2,1)S(1)}, u32[]{:S(2)}, u32[]{:S(2)}) %collective-permute-start.31) | collective-permute-done | bytes 131104 | tf_op jit(solution)/shard_map/ppermute | solution.py:215
  151.7 1.8 inverse_y.9
  154.9 8.9 %mix.8.mine_ref = bf16[16,16,256]{2,1,0:T(8,128)(2,1)S(1)} custom-call(f32[16,16,256]{2,1,0:T(8,128)S(1)} %get-tuple-element.91.refs_0_, f32[16,16,256]{2,1,0:T(8,128)S(1)} %get-tuple-element.100.refs_1_, bf16[16,16,256]{2,1,0:T(8,128)(2,1)S(1)} %collective-permute-done.22.refs_2_, bf16[16,16,256]{2,1,0:T(8,128)(2,1)S(1)} %collective-permute-done.23.refs_3_, ...), custom_call_target="tpu_custom_call" | custom-call | flops 8388608 | bytes 4194304 | tf_op jit(solution)/shard_map/mix/pallas_call | solution.py:262
  165.3 3.5 %collective-permute-done.24.theirs_ref = bf16[16,16,256]{2,1,0:T(8,128)(2,1)S(1)} collective-permute-done((bf16[16,16,256]{2,1,0:T(8,128)(2,1)S(1)}, bf16[16,16,256]{2,1,0:T(8,128)(2,1)S(1)}, u32[]{:S(2)}, u32[]{:S(2)}) %collective-permute-start.24) | collective-permute-done | bytes 131104 | tf_op jit(solution)/shard_map/ppermute | solution.py:215
  168.8 1.8 inverse_y.8
  171.0 2.3 collective-permute-start.27
  173.3 11.0 %pointwise.4.refs_4_ = f32[32,96,1024]{2,1,0:T(8,128)} custom-call(bf16[16,96,1024]{2,1,0:T(8,128)(2,1)S(1)} %get-tuple-element.107.refs_0_, bf16[16,96,1024]{2,1,0:T(8,128)(2,1)} %copy-done.1, bf16[32,96,1024]{2,1,0:T(8,128)(2,1)} %bitcast.68, bf16[512,512]{1,0:T(8,128)(2,1)S(1)} %convert_element_type.25.refs_2_.refs_3_, ...), custom_call_target="tpu_custom_call" | custom-call | flops 3221225472 | bytes 25165824 | tf_op jit(solution)/shard_map/pointwise/pallas_call | solution.py:297
  184.3 8.2 %update.7 = (bf16[16,96,1024]{2,1,0:T(8,128)(2,1)S(1)}, bf16[8,96,128]{2,1,0:T(8,128)(2,1)S(1)}, bf16[8,96,128]{2,1,0:T(8,128)(2,1)S(1)}, bf16[8,96,128]{2,1,0:T(8,128)(2,1)S(1)}, bf16[8,96,128]{2,1,0:T(8,128)(2,1)S(1)}) custom-call(bf16[8,96,128]{2,1,0:T(8,128)(2,1)S(1)} %get-tuple-element.114.refs_0_, ...), custom_call_target="tpu_custom_call" | custom-call | flops 1610612736 | bytes 9437184 | tf_op jit(solution)/shard_map/update/pallas_call | solution.py:316
  192.5 1.6 copy-done
  194.5 2.3 collective-permute-start.37
  196.8 8.2 %update.6 = (bf16[16,96,1024]{2,1,0:T(8,128)(2,1)S(1)}, bf16[8,96,128]{2,1,0:T(8,128)(2,1)S(1)}, bf16[8,96,128]{2,1,0:T(8,128)(2,1)S(1)}, bf16[8,96,128]{2,1,0:T(8,128)(2,1)S(1)}, bf16[8,96,128]{2,1,0:T(8,128)(2,1)S(1)}) custom-call(bf16[8,96,128]{2,1,0:T(8,128)(2,1)S(1)} %get-tuple-element.103.refs_0_, ...), custom_call_target="tpu_custom_call" | custom-call | flops 1610612736 | bytes 9437184 | tf_op jit(solution)/shard_map/update/pallas_call | solution.py:316
  205.4 2.3 collective-permute-start.30
  207.7 1.9 forward_y.11
  210.7 1.6 collective-permute-done.29.refs_2_
  212.3 4.8 %collective-permute-done.30.refs_3_ = bf16[8,96,128]{2,1,0:T(8,128)(2,1)S(1)} collective-permute-done((bf16[8,96,128]{2,1,0:T(8,128)(2,1)S(1)}, bf16[8,96,128]{2,1,0:T(8,128)(2,1)S(1)}, u32[]{:S(2)}, u32[]{:S(2)}) %collective-permute-start.30) | collective-permute-done | bytes 196640 | tf_op jit(solution)/shard_map/ppermute | solution.py:215
  217.1 1.9 forward_y.10
  219.1 8.2 %collective-permute-done.38.refs_2_ = bf16[16,16,256]{2,1,0:T(8,128)(2,1)S(1)} collective-permute-done((bf16[16,16,256]{2,1,0:T(8,128)(2,1)S(1)}, bf16[16,16,256]{2,1,0:T(8,128)(2,1)S(1)}, u32[]{:S(2)}, u32[]{:S(2)}) %collective-permute-start.38) | collective-permute-done | bytes 131104 | tf_op jit(solution)/shard_map/ppermute | solution.py:215
  227.3 9.0 %mix.11.mine_ref = bf16[16,16,256]{2,1,0:T(8,128)(2,1)S(1)} custom-call(f32[16,16,256]{2,1,0:T(8,128)S(1)} %get-tuple-element.113.refs_0_, f32[16,16,256]{2,1,0:T(8,128)S(1)} %get-tuple-element.122.refs_1_, bf16[16,16,256]{2,1,0:T(8,128)(2,1)S(1)} %collective-permute-done.38.refs_2_, bf16[16,16,256]{2,1,0:T(8,128)(2,1)S(1)} %collective-permute-done.39.refs_3_, ...), custom_call_target="tpu_custom_call" | custom-call | flops 8388608 | bytes 4194304 | tf_op jit(solution)/shard_map/mix/pallas_call | solution.py:262
  236.4 5.4 %collective-permute-done.44.theirs_ref = bf16[16,16,256]{2,1,0:T(8,128)(2,1)S(1)} collective-permute-done((bf16[16,16,256]{2,1,0:T(8,128)(2,1)S(1)}, bf16[16,16,256]{2,1,0:T(8,128)(2,1)S(1)}, u32[]{:S(2)}, u32[]{:S(2)}) %collective-permute-start.44) | collective-permute-done | bytes 131104 | tf_op jit(solution)/shard_map/ppermute | solution.py:215
  241.8 1.8 inverse_y.11
  243.6 9.0 %mix.10.mine_ref = bf16[16,16,256]{2,1,0:T(8,128)(2,1)S(1)} custom-call(f32[16,16,256]{2,1,0:T(8,128)S(1)} %get-tuple-element.113.refs_0_, f32[16,16,256]{2,1,0:T(8,128)S(1)} %get-tuple-element.122.refs_1_, bf16[16,16,256]{2,1,0:T(8,128)(2,1)S(1)} %collective-permute-done.38.refs_2_, bf16[16,16,256]{2,1,0:T(8,128)(2,1)S(1)} %collective-permute-done.39.refs_3_, ...), custom_call_target="tpu_custom_call" | custom-call | flops 8388608 | bytes 4194304 | tf_op jit(solution)/shard_map/mix/pallas_call | solution.py:262
  253.3 1.9 collective-permute-start.46
  256.3 1.8 collective-permute-done.40.theirs_ref
  258.2 1.8 inverse_y.10
  259.9 1.5 collective-permute-start.41
  262.7 1.9 copy-done.3
  264.6 11.0 %pointwise.5.refs_4_ = f32[32,96,1024]{2,1,0:T(8,128)} custom-call(bf16[16,96,1024]{2,1,0:T(8,128)(2,1)S(1)} %copy-done.3, bf16[16,96,1024]{2,1,0:T(8,128)(2,1)} %copy-done, bf16[32,96,1024]{2,1,0:T(8,128)(2,1)} %bitcast.69, bf16[512,512]{1,0:T(8,128)(2,1)S(1)} %convert_element_type.25.refs_2_.refs_3_, f32[512,1]{1,0:T(8,128)S(1)} %broadcast_in_dim_reshape.4.refs_3_.refs_4_), custom_call_target="tpu_custom_call" | custom-call | flops 3221225472 | bytes 25165824 | tf_op jit(solution)/shard_map/pointwise/pallas_call | solution.py:297
  275.6 9.7 %last.3 = (f32[16,96,1024]{2,1,0:T(8,128)}, f32[4,96,1024]{2,1,0:T(8,128)S(1)}) custom-call(bf16[8,96,128]{2,1,0:T(8,128)(2,1)S(1)} %get-tuple-element.132.refs_0_, bf16[8,96,128]{2,1,0:T(8,128)(2,1)S(1)} %collective-permute-done.45.refs_1_, bf16[8,96,128]{2,1,0:T(8,128)(2,1)S(1)} %collective-permute-done.46.refs_2_, ...), custom_call_target="tpu_custom_call" | custom-call | flops 805306368 | bytes 12582912 | tf_op jit(solution)/shard_map/last/pallas_call | solution.py:333
  285.3 9.8 %last.2 = (f32[16,96,1024]{2,1,0:T(8,128)}, f32[4,96,1024]{2,1,0:T(8,128)S(1)}) custom-call(bf16[8,96,128]{2,1,0:T(8,128)(2,1)S(1)} %get-tuple-element.125.refs_0_, bf16[8,96,128]{2,1,0:T(8,128)(2,1)S(1)} %collective-permute-done.41.refs_1_, bf16[8,96,128]{2,1,0:T(8,128)(2,1)S(1)} %collective-permute-done.42.refs_2_, ...), custom_call_target="tpu_custom_call" | custom-call | flops 805306368 | bytes 12582912 | tf_op jit(solution)/shard_map/last/pallas_call | solution.py:333
  295.8 13.0 %collective-permute-start.48 = (f32[96,1024]{1,0:T(8,128)S(1)}, f32[96,1024]{1,0:T(8,128)S(1)}, u32[]{:S(2)}, u32[]{:S(2)}) collective-permute-start(f32[96,1024]{1,0:T(8,128)S(1)} %multiply_bitcast_fusion), channel_id=1, source_target_pairs={{0,8},{8,16},{16,24},{1,9},{9,17},{17,25},{2,10},{10,18},{18,26},{... | collective-permute-start | bytes 1179656 | tf_op jit(solution)/shard_map/ppermute | solution.py:376
  308.8 4.7 %collective-permute-done.48 = f32[96,1024]{1,0:T(8,128)S(1)} collective-permute-done((f32[96,1024]{1,0:T(8,128)S(1)}, f32[96,1024]{1,0:T(8,128)S(1)}, u32[]{:S(2)}, u32[]{:S(2)}) %collective-permute-start.48) | collective-permute-done | bytes 393248 | tf_op jit(solution)/shard_map/ppermute | solution.py:376
  314.9 5.2 %collective-permute-done.49 = f32[96,1024]{1,0:T(8,128)S(1)} collective-permute-done((f32[96,1024]{1,0:T(8,128)S(1)}, f32[96,1024]{1,0:T(8,128)S(1)}, u32[]{:S(2)}, u32[]{:S(2)}) %collective-permute-start.49) | collective-permute-done | bytes 393248 | tf_op jit(solution)/shard_map/ppermute | solution.py:376
  320.7 3.1 collective-permute-start.50
  323.8 12.1 %maximum_bitcast_fusion = f32[1,32,96,1024]{3,2,1,0:T(8,128)} fusion(f32[16,96,1024]{2,1,0:T(8,128)} %get-tuple-element.136, f32[16,96,1024]{2,1,0:T(8,128)} %get-tuple-element.131), kind=kLoop, calls=%fused_computation.3 | loop fusion | flops 3145728 | bytes 25165824 | tf_op jit(solution)/shard_map/broadcast_in_dim | solution.py:400
  337.3 8.3 %collective-permute-start.52 = (f32[96,1024]{1,0:T(8,128)S(1)}, f32[96,1024]{1,0:T(8,128)S(1)}, u32[]{:S(2)}, u32[]{:S(2)}) collective-permute-start(f32[96,1024]{1,0:T(8,128)S(1)} %get-tuple-element.147), channel_id=1, source_target_pairs={{0,8},{8,16},{16,24},{1,9},{9,17},{17,25},{2,10},{10,18},{18,26},{... | collective-permute-start | bytes 1179656 | tf_op jit(solution)/shard_map/ppermute | solution.py:376
  345.9 4.4 %collective-permute-done.52 = f32[96,1024]{1,0:T(8,128)S(1)} collective-permute-done((f32[96,1024]{1,0:T(8,128)S(1)}, f32[96,1024]{1,0:T(8,128)S(1)}, u32[]{:S(2)}, u32[]{:S(2)}) %collective-permute-start.52) | collective-permute-done | bytes 393248 | tf_op jit(solution)/shard_map/ppermute | solution.py:376
  (130 shorter events, 33.0 us)
Async XLA Ops:
  10.3 15.2 %collective-permute-start.3 = (bf16[8,96,128]{2,1,0:T(8,128)(2,1)S(1)}, bf16[8,96,128]{2,1,0:T(8,128)(2,1)S(1)}, u32[]{:S(2)}, u32[]{:S(2)}) collective-permute-start(bf16[8,96,128]{2,1,0:T(8,128)(2,1)S(1)} %get-tuple-element.77), channel_id=1, source_target_pairs={{0,1},{1,0},{2,3},{3,2},{4,5},{5,4},{6,7},{7,6},{8,9},{9,8},{10,11... | collective-permute-start | bytes 589832 | tf_op jit(solution)/shard_map/ppermute | solution.py:215
  12.4 14.1 %collective-permute-start.4 = (bf16[8,96,128]{2,1,0:T(8,128)(2,1)S(1)}, bf16[8,96,128]{2,1,0:T(8,128)(2,1)S(1)}, u32[]{:S(2)}, u32[]{:S(2)}) collective-permute-start(bf16[8,96,128]{2,1,0:T(8,128)(2,1)S(1)} %get-tuple-element.78), channel_id=1, source_target_pairs={{0,2},{1,3},{2,0},{3,1},{4,6},{5,7},{6,4},{7,5},{8,10},{9,11},{10,... | collective-permute-start | bytes 589832 | tf_op jit(solution)/shard_map/ppermute | solution.py:215
  13.7 21.5 %copy-start.5 = (bf16[32,32]{1,0:T(8,128)(2,1)S(1)}, bf16[32,32]{1,0:T(8,128)(2,1)}, u32[]{:S(2)}) copy-start(bf16[32,32]{1,0:T(8,128)(2,1)} %param.14) | copy-start | bytes 6148
  13.7 12.9 %collective-permute-start.5 = (bf16[8,96,128]{2,1,0:T(8,128)(2,1)S(1)}, bf16[8,96,128]{2,1,0:T(8,128)(2,1)S(1)}, u32[]{:S(2)}, u32[]{:S(2)}) collective-permute-start(bf16[8,96,128]{2,1,0:T(8,128)(2,1)S(1)} %get-tuple-element.79), channel_id=1, source_target_pairs={{0,3},{1,2},{2,1},{3,0},{4,7},{5,6},{6,5},{7,4},{8,11},{9,10},{10,... | collective-permute-start | bytes 589832 | tf_op jit(solution)/shard_map/ppermute | solution.py:215
  20.3 12.3 %collective-permute-start = (bf16[8,96,128]{2,1,0:T(8,128)(2,1)}, bf16[8,96,128]{2,1,0:T(8,128)(2,1)S(1)}, u32[]{:S(2)}, u32[]{:S(2)}) collective-permute-start(bf16[8,96,128]{2,1,0:T(8,128)(2,1)} %get-tuple-element.72), channel_id=1, source_target_pairs={{0,1},{1,0},{2,3},{3,2},{4,5},{5,4},{6,7},{7,6},{8,9},{9,8},{10,11... | collective-permute-start | bytes 589832 | tf_op jit(solution)/shard_map/ppermute | solution.py:215
  21.7 10.9 %collective-permute-start.1 = (bf16[8,96,128]{2,1,0:T(8,128)(2,1)S(1)}, bf16[8,96,128]{2,1,0:T(8,128)(2,1)S(1)}, u32[]{:S(2)}, u32[]{:S(2)}) collective-permute-start(bf16[8,96,128]{2,1,0:T(8,128)(2,1)S(1)} %get-tuple-element.73), channel_id=1, source_target_pairs={{0,2},{1,3},{2,0},{3,1},{4,6},{5,7},{6,4},{7,5},{8,10},{9,11},{10,... | collective-permute-start | bytes 589832 | tf_op jit(solution)/shard_map/ppermute | solution.py:215
  25.5 7.1 %collective-permute-start.2 = (bf16[8,96,128]{2,1,0:T(8,128)(2,1)S(1)}, bf16[8,96,128]{2,1,0:T(8,128)(2,1)S(1)}, u32[]{:S(2)}, u32[]{:S(2)}) collective-permute-start(bf16[8,96,128]{2,1,0:T(8,128)(2,1)S(1)} %get-tuple-element.74), channel_id=1, source_target_pairs={{0,3},{1,2},{2,1},{3,0},{4,7},{5,6},{6,5},{7,4},{8,11},{9,10},{10,... | collective-permute-start | bytes 589832 | tf_op jit(solution)/shard_map/ppermute | solution.py:215
  30.2 6.9 %collective-permute-start.7 = (bf16[16,16,256]{2,1,0:T(8,128)(2,1)}, bf16[16,16,256]{2,1,0:T(8,128)(2,1)S(1)}, u32[]{:S(2)}, u32[]{:S(2)}) collective-permute-start(bf16[16,16,256]{2,1,0:T(8,128)(2,1)} %get-tuple-element.82), channel_id=1, source_target_pairs={{0,4},{1,5},{2,6},{3,7},{4,0},{5,1},{6,2},{7,3},{8,12},{9,13},{10,... | collective-permute-start | bytes 393224 | tf_op jit(solution)/shard_map/ppermute | solution.py:215
  34.5 10.5 %collective-permute-start.6 = (bf16[16,16,256]{2,1,0:T(8,128)(2,1)S(1)}, bf16[16,16,256]{2,1,0:T(8,128)(2,1)S(1)}, u32[]{:S(2)}, u32[]{:S(2)}) collective-permute-start(bf16[16,16,256]{2,1,0:T(8,128)(2,1)S(1)} %get-tuple-element.81), channel_id=1, source_target_pairs={{0,4},{1,5},{2,6},{3,7},{4,0},{5,1},{6,2},{7,3},{8,12},{9,13},{10,... | collective-permute-start | bytes 393224 | tf_op jit(solution)/shard_map/ppermute | solution.py:215
  54.0 2.9 copy-start.8
  54.0 22.2 %collective-permute-start.15 = (bf16[16,16,256]{2,1,0:T(8,128)(2,1)S(1)}, bf16[16,16,256]{2,1,0:T(8,128)(2,1)S(1)}, u32[]{:S(2)}, u32[]{:S(2)}) collective-permute-start(bf16[16,16,256]{2,1,0:T(8,128)(2,1)S(1)} %mix.7.mine_ref), channel_id=1, source_target_pairs={{0,4},{1,5},{2,6},{3,7},{4,0},{5,1},{6,2},{7,3},{8,12},{9,13},{10,... | collective-permute-start | bytes 393224 | tf_op jit(solution)/shard_map/ppermute | solution.py:215
  73.9 18.8 %collective-permute-start.8 = (bf16[16,16,256]{2,1,0:T(8,128)(2,1)S(1)}, bf16[16,16,256]{2,1,0:T(8,128)(2,1)S(1)}, u32[]{:S(2)}, u32[]{:S(2)}) collective-permute-start(bf16[16,16,256]{2,1,0:T(8,128)(2,1)S(1)} %mix.6.mine_ref), channel_id=1, source_target_pairs={{0,4},{1,5},{2,6},{3,7},{4,0},{5,1},{6,2},{7,3},{8,12},{9,13},{10,... | collective-permute-start | bytes 393224 | tf_op jit(solution)/shard_map/ppermute | solution.py:215
  78.1 18.0 %collective-permute-start.16 = (bf16[8,96,128]{2,1,0:T(8,128)(2,1)S(1)}, bf16[8,96,128]{2,1,0:T(8,128)(2,1)S(1)}, u32[]{:S(2)}, u32[]{:S(2)}) collective-permute-start(bf16[8,96,128]{2,1,0:T(8,128)(2,1)S(1)} %get-tuple-element.93), channel_id=1, source_target_pairs={{0,1},{1,0},{2,3},{3,2},{4,5},{5,4},{6,7},{7,6},{8,9},{9,8},{10,11... | collective-permute-start | bytes 589832 | tf_op jit(solution)/shard_map/ppermute | solution.py:215
  79.4 17.8 %collective-permute-start.17 = (bf16[8,96,128]{2,1,0:T(8,128)(2,1)S(1)}, bf16[8,96,128]{2,1,0:T(8,128)(2,1)S(1)}, u32[]{:S(2)}, u32[]{:S(2)}) collective-permute-start(bf16[8,96,128]{2,1,0:T(8,128)(2,1)S(1)} %get-tuple-element.94), channel_id=1, source_target_pairs={{0,2},{1,3},{2,0},{3,1},{4,6},{5,7},{6,4},{7,5},{8,10},{9,11},{10,... | collective-permute-start | bytes 589832 | tf_op jit(solution)/shard_map/ppermute | solution.py:215
  79.7 17.5 %collective-permute-start.18 = (bf16[8,96,128]{2,1,0:T(8,128)(2,1)S(1)}, bf16[8,96,128]{2,1,0:T(8,128)(2,1)S(1)}, u32[]{:S(2)}, u32[]{:S(2)}) collective-permute-start(bf16[8,96,128]{2,1,0:T(8,128)(2,1)S(1)} %get-tuple-element.95), channel_id=1, source_target_pairs={{0,3},{1,2},{2,1},{3,0},{4,7},{5,6},{6,5},{7,4},{8,11},{9,10},{10,... | collective-permute-start | bytes 589832 | tf_op jit(solution)/shard_map/ppermute | solution.py:215
  94.5 14.1 %collective-permute-start.9 = (bf16[8,96,128]{2,1,0:T(8,128)(2,1)S(1)}, bf16[8,96,128]{2,1,0:T(8,128)(2,1)S(1)}, u32[]{:S(2)}, u32[]{:S(2)}) collective-permute-start(bf16[8,96,128]{2,1,0:T(8,128)(2,1)S(1)} %get-tuple-element.84), channel_id=1, source_target_pairs={{0,1},{1,0},{2,3},{3,2},{4,5},{5,4},{6,7},{7,6},{8,9},{9,8},{10,11... | collective-permute-start | bytes 589832 | tf_op jit(solution)/shard_map/ppermute | solution.py:215
  95.8 13.9 %collective-permute-start.10 = (bf16[8,96,128]{2,1,0:T(8,128)(2,1)S(1)}, bf16[8,96,128]{2,1,0:T(8,128)(2,1)S(1)}, u32[]{:S(2)}, u32[]{:S(2)}) collective-permute-start(bf16[8,96,128]{2,1,0:T(8,128)(2,1)S(1)} %get-tuple-element.85), channel_id=1, source_target_pairs={{0,2},{1,3},{2,0},{3,1},{4,6},{5,7},{6,4},{7,5},{8,10},{9,11},{10,... | collective-permute-start | bytes 589832 | tf_op jit(solution)/shard_map/ppermute | solution.py:215
  96.1 13.6 %collective-permute-start.11 = (bf16[8,96,128]{2,1,0:T(8,128)(2,1)S(1)}, bf16[8,96,128]{2,1,0:T(8,128)(2,1)S(1)}, u32[]{:S(2)}, u32[]{:S(2)}) collective-permute-start(bf16[8,96,128]{2,1,0:T(8,128)(2,1)S(1)} %get-tuple-element.86), channel_id=1, source_target_pairs={{0,3},{1,2},{2,1},{3,0},{4,7},{5,6},{6,5},{7,4},{8,11},{9,10},{10,... | collective-permute-start | bytes 589832 | tf_op jit(solution)/shard_map/ppermute | solution.py:215
  105.4 1.6 copy-start.1
  107.0 12.5 %collective-permute-start.19 = (bf16[8,96,128]{2,1,0:T(8,128)(2,1)S(1)}, bf16[8,96,128]{2,1,0:T(8,128)(2,1)S(1)}, u32[]{:S(2)}, u32[]{:S(2)}) collective-permute-start(bf16[8,96,128]{2,1,0:T(8,128)(2,1)S(1)} %get-tuple-element.97), channel_id=1, source_target_pairs={{0,1},{1,0},{2,3},{3,2},{4,5},{5,4},{6,7},{7,6},{8,9},{9,8},{10,11... | collective-permute-start | bytes 589832 | tf_op jit(solution)/shard_map/ppermute | solution.py:215
  108.2 12.3 %collective-permute-start.20 = (bf16[8,96,128]{2,1,0:T(8,128)(2,1)S(1)}, bf16[8,96,128]{2,1,0:T(8,128)(2,1)S(1)}, u32[]{:S(2)}, u32[]{:S(2)}) collective-permute-start(bf16[8,96,128]{2,1,0:T(8,128)(2,1)S(1)} %get-tuple-element.98), channel_id=1, source_target_pairs={{0,2},{1,3},{2,0},{3,1},{4,6},{5,7},{6,4},{7,5},{8,10},{9,11},{10,... | collective-permute-start | bytes 589832 | tf_op jit(solution)/shard_map/ppermute | solution.py:215
  108.6 12.0 %collective-permute-start.21 = (bf16[8,96,128]{2,1,0:T(8,128)(2,1)S(1)}, bf16[8,96,128]{2,1,0:T(8,128)(2,1)S(1)}, u32[]{:S(2)}, u32[]{:S(2)}) collective-permute-start(bf16[8,96,128]{2,1,0:T(8,128)(2,1)S(1)} %get-tuple-element.99), channel_id=1, source_target_pairs={{0,3},{1,2},{2,1},{3,0},{4,7},{5,6},{6,5},{7,4},{8,11},{9,10},{10,... | collective-permute-start | bytes 589832 | tf_op jit(solution)/shard_map/ppermute | solution.py:215
  117.9 6.0 %collective-permute-start.12 = (bf16[8,96,128]{2,1,0:T(8,128)(2,1)S(1)}, bf16[8,96,128]{2,1,0:T(8,128)(2,1)S(1)}, u32[]{:S(2)}, u32[]{:S(2)}) collective-permute-start(bf16[8,96,128]{2,1,0:T(8,128)(2,1)S(1)} %get-tuple-element.88), channel_id=1, source_target_pairs={{0,1},{1,0},{2,3},{3,2},{4,5},{5,4},{6,7},{7,6},{8,9},{9,8},{10,11... | collective-permute-start | bytes 589832 | tf_op jit(solution)/shard_map/ppermute | solution.py:215
  119.2 4.7 %collective-permute-start.13 = (bf16[8,96,128]{2,1,0:T(8,128)(2,1)S(1)}, bf16[8,96,128]{2,1,0:T(8,128)(2,1)S(1)}, u32[]{:S(2)}, u32[]{:S(2)}) collective-permute-start(bf16[8,96,128]{2,1,0:T(8,128)(2,1)S(1)} %get-tuple-element.89), channel_id=1, source_target_pairs={{0,2},{1,3},{2,0},{3,1},{4,6},{5,7},{6,4},{7,5},{8,10},{9,11},{10,... | collective-permute-start | bytes 589832 | tf_op jit(solution)/shard_map/ppermute | solution.py:215
  119.5 6.3 %collective-permute-start.14 = (bf16[8,96,128]{2,1,0:T(8,128)(2,1)S(1)}, bf16[8,96,128]{2,1,0:T(8,128)(2,1)S(1)}, u32[]{:S(2)}, u32[]{:S(2)}) collective-permute-start(bf16[8,96,128]{2,1,0:T(8,128)(2,1)S(1)} %get-tuple-element.90), channel_id=1, source_target_pairs={{0,3},{1,2},{2,1},{3,0},{4,7},{5,6},{6,5},{7,4},{8,11},{9,10},{10,... | collective-permute-start | bytes 589832 | tf_op jit(solution)/shard_map/ppermute | solution.py:215
  122.5 6.8 %collective-permute-start.23 = (bf16[16,16,256]{2,1,0:T(8,128)(2,1)S(1)}, bf16[16,16,256]{2,1,0:T(8,128)(2,1)S(1)}, u32[]{:S(2)}, u32[]{:S(2)}) collective-permute-start(bf16[16,16,256]{2,1,0:T(8,128)(2,1)S(1)} %get-tuple-element.102), channel_id=1, source_target_pairs={{0,4},{1,5},{2,6},{3,7},{4,0},{5,1},{6,2},{7,3},{8,12},{9,13},{10,... | collective-permute-start | bytes 393224 | tf_op jit(solution)/shard_map/ppermute | solution.py:215
  127.7 8.8 %collective-permute-start.22 = (bf16[16,16,256]{2,1,0:T(8,128)(2,1)S(1)}, bf16[16,16,256]{2,1,0:T(8,128)(2,1)S(1)}, u32[]{:S(2)}, u32[]{:S(2)}) collective-permute-start(bf16[16,16,256]{2,1,0:T(8,128)(2,1)S(1)} %get-tuple-element.101), channel_id=1, source_target_pairs={{0,4},{1,5},{2,6},{3,7},{4,0},{5,1},{6,2},{7,3},{8,12},{9,13},{10,... | collective-permute-start | bytes 393224 | tf_op jit(solution)/shard_map/ppermute | solution.py:215
  145.5 6.2 %collective-permute-start.31 = (bf16[16,16,256]{2,1,0:T(8,128)(2,1)S(1)}, bf16[16,16,256]{2,1,0:T(8,128)(2,1)S(1)}, u32[]{:S(2)}, u32[]{:S(2)}) collective-permute-start(bf16[16,16,256]{2,1,0:T(8,128)(2,1)S(1)} %mix.9.mine_ref), channel_id=1, source_target_pairs={{0,4},{1,5},{2,6},{3,7},{4,0},{5,1},{6,2},{7,3},{8,12},{9,13},{10,... | collective-permute-start | bytes 393224 | tf_op jit(solution)/shard_map/ppermute | solution.py:215
  153.5 17.5 %collective-permute-start.32 = (bf16[8,96,128]{2,1,0:T(8,128)(2,1)S(1)}, bf16[8,96,128]{2,1,0:T(8,128)(2,1)S(1)}, u32[]{:S(2)}, u32[]{:S(2)}) collective-permute-start(bf16[8,96,128]{2,1,0:T(8,128)(2,1)S(1)} %get-tuple-element.115), channel_id=1, source_target_pairs={{0,1},{1,0},{2,3},{3,2},{4,5},{5,4},{6,7},{7,6},{8,9},{9,8},{10,11... | collective-permute-start | bytes 589832 | tf_op jit(solution)/shard_map/ppermute | solution.py:215
  163.9 5.0 %collective-permute-start.24 = (bf16[16,16,256]{2,1,0:T(8,128)(2,1)S(1)}, bf16[16,16,256]{2,1,0:T(8,128)(2,1)S(1)}, u32[]{:S(2)}, u32[]{:S(2)}) collective-permute-start(bf16[16,16,256]{2,1,0:T(8,128)(2,1)S(1)} %mix.8.mine_ref), channel_id=1, source_target_pairs={{0,4},{1,5},{2,6},{3,7},{4,0},{5,1},{6,2},{7,3},{8,12},{9,13},{10,... | collective-permute-start | bytes 393224 | tf_op jit(solution)/shard_map/ppermute | solution.py:215
  163.9 20.3 %collective-permute-start.33 = (bf16[8,96,128]{2,1,0:T(8,128)(2,1)S(1)}, bf16[8,96,128]{2,1,0:T(8,128)(2,1)S(1)}, u32[]{:S(2)}, u32[]{:S(2)}) collective-permute-start(bf16[8,96,128]{2,1,0:T(8,128)(2,1)S(1)} %get-tuple-element.116), channel_id=1, source_target_pairs={{0,2},{1,3},{2,0},{3,1},{4,6},{5,7},{6,4},{7,5},{8,10},{9,11},{10,... | collective-permute-start | bytes 589832 | tf_op jit(solution)/shard_map/ppermute | solution.py:215
  165.2 19.1 %collective-permute-start.34 = (bf16[8,96,128]{2,1,0:T(8,128)(2,1)S(1)}, bf16[8,96,128]{2,1,0:T(8,128)(2,1)S(1)}, u32[]{:S(2)}, u32[]{:S(2)}) collective-permute-start(bf16[8,96,128]{2,1,0:T(8,128)(2,1)S(1)} %get-tuple-element.117), channel_id=1, source_target_pairs={{0,3},{1,2},{2,1},{3,0},{4,7},{5,6},{6,5},{7,4},{8,11},{9,10},{10,... | collective-permute-start | bytes 589832 | tf_op jit(solution)/shard_map/ppermute | solution.py:215
  170.6 23.8 %collective-permute-start.25 = (bf16[8,96,128]{2,1,0:T(8,128)(2,1)S(1)}, bf16[8,96,128]{2,1,0:T(8,128)(2,1)S(1)}, u32[]{:S(2)}, u32[]{:S(2)}) collective-permute-start(bf16[8,96,128]{2,1,0:T(8,128)(2,1)S(1)} %get-tuple-element.104), channel_id=1, source_target_pairs={{0,1},{1,0},{2,3},{3,2},{4,5},{5,4},{6,7},{7,6},{8,9},{9,8},{10,11... | collective-permute-start | bytes 589832 | tf_op jit(solution)/shard_map/ppermute | solution.py:215
  171.0 25.8 %collective-permute-start.26 = (bf16[8,96,128]{2,1,0:T(8,128)(2,1)S(1)}, bf16[8,96,128]{2,1,0:T(8,128)(2,1)S(1)}, u32[]{:S(2)}, u32[]{:S(2)}) collective-permute-start(bf16[8,96,128]{2,1,0:T(8,128)(2,1)S(1)} %get-tuple-element.105), channel_id=1, source_target_pairs={{0,2},{1,3},{2,0},{3,1},{4,6},{5,7},{6,4},{7,5},{8,10},{9,11},{10,... | collective-permute-start | bytes 589832 | tf_op jit(solution)/shard_map/ppermute | solution.py:215
  171.0 25.8 %collective-permute-start.27 = (bf16[8,96,128]{2,1,0:T(8,128)(2,1)S(1)}, bf16[8,96,128]{2,1,0:T(8,128)(2,1)S(1)}, u32[]{:S(2)}, u32[]{:S(2)}) collective-permute-start(bf16[8,96,128]{2,1,0:T(8,128)(2,1)S(1)} %get-tuple-element.106), channel_id=1, source_target_pairs={{0,3},{1,2},{2,1},{3,0},{4,7},{5,6},{6,5},{7,4},{8,11},{9,10},{10,... | collective-permute-start | bytes 589832 | tf_op jit(solution)/shard_map/ppermute | solution.py:215
  192.5 1.6 copy-start
  194.1 11.3 %collective-permute-start.35 = (bf16[8,96,128]{2,1,0:T(8,128)(2,1)S(1)}, bf16[8,96,128]{2,1,0:T(8,128)(2,1)S(1)}, u32[]{:S(2)}, u32[]{:S(2)}) collective-permute-start(bf16[8,96,128]{2,1,0:T(8,128)(2,1)S(1)} %get-tuple-element.119), channel_id=1, source_target_pairs={{0,1},{1,0},{2,3},{3,2},{4,5},{5,4},{6,7},{7,6},{8,9},{9,8},{10,11... | collective-permute-start | bytes 589832 | tf_op jit(solution)/shard_map/ppermute | solution.py:215
  194.5 13.3 %collective-permute-start.36 = (bf16[8,96,128]{2,1,0:T(8,128)(2,1)S(1)}, bf16[8,96,128]{2,1,0:T(8,128)(2,1)S(1)}, u32[]{:S(2)}, u32[]{:S(2)}) collective-permute-start(bf16[8,96,128]{2,1,0:T(8,128)(2,1)S(1)} %get-tuple-element.120), channel_id=1, source_target_pairs={{0,2},{1,3},{2,0},{3,1},{4,6},{5,7},{6,4},{7,5},{8,10},{9,11},{10,... | collective-permute-start | bytes 589832 | tf_op jit(solution)/shard_map/ppermute | solution.py:215
  194.5 13.3 %collective-permute-start.37 = (bf16[8,96,128]{2,1,0:T(8,128)(2,1)S(1)}, bf16[8,96,128]{2,1,0:T(8,128)(2,1)S(1)}, u32[]{:S(2)}, u32[]{:S(2)}) collective-permute-start(bf16[8,96,128]{2,1,0:T(8,128)(2,1)S(1)} %get-tuple-element.121), channel_id=1, source_target_pairs={{0,3},{1,2},{2,1},{3,0},{4,7},{5,6},{6,5},{7,4},{8,11},{9,10},{10,... | collective-permute-start | bytes 589832 | tf_op jit(solution)/shard_map/ppermute | solution.py:215
  205.0 31.3 %copy-start.2 = (bf16[16,96,1024]{2,1,0:T(8,128)(2,1)}, bf16[16,96,1024]{2,1,0:T(8,128)(2,1)S(1)}, u32[]{:S(2)}) copy-start(bf16[16,96,1024]{2,1,0:T(8,128)(2,1)S(1)} %get-tuple-element.129.refs_0_) | copy-start | bytes 9437188
  205.0 5.7 %collective-permute-start.28 = (bf16[8,96,128]{2,1,0:T(8,128)(2,1)S(1)}, bf16[8,96,128]{2,1,0:T(8,128)(2,1)S(1)}, u32[]{:S(2)}, u32[]{:S(2)}) collective-permute-start(bf16[8,96,128]{2,1,0:T(8,128)(2,1)S(1)} %get-tuple-element.110), channel_id=1, source_target_pairs={{0,1},{1,0},{2,3},{3,2},{4,5},{5,4},{6,7},{7,6},{8,9},{9,8},{10,11... | collective-permute-start | bytes 589832 | tf_op jit(solution)/shard_map/ppermute | solution.py:215
  205.4 6.9 %collective-permute-start.29 = (bf16[8,96,128]{2,1,0:T(8,128)(2,1)S(1)}, bf16[8,96,128]{2,1,0:T(8,128)(2,1)S(1)}, u32[]{:S(2)}, u32[]{:S(2)}) collective-permute-start(bf16[8,96,128]{2,1,0:T(8,128)(2,1)S(1)} %get-tuple-element.111), channel_id=1, source_target_pairs={{0,2},{1,3},{2,0},{3,1},{4,6},{5,7},{6,4},{7,5},{8,10},{9,11},{10,... | collective-permute-start | bytes 589832 | tf_op jit(solution)/shard_map/ppermute | solution.py:215
  205.4 11.7 %collective-permute-start.30 = (bf16[8,96,128]{2,1,0:T(8,128)(2,1)S(1)}, bf16[8,96,128]{2,1,0:T(8,128)(2,1)S(1)}, u32[]{:S(2)}, u32[]{:S(2)}) collective-permute-start(bf16[8,96,128]{2,1,0:T(8,128)(2,1)S(1)} %get-tuple-element.112), channel_id=1, source_target_pairs={{0,3},{1,2},{2,1},{3,0},{4,7},{5,6},{6,5},{7,4},{8,11},{9,10},{10,... | collective-permute-start | bytes 589832 | tf_op jit(solution)/shard_map/ppermute | solution.py:215
  209.6 9.5 %collective-permute-start.39 = (bf16[16,16,256]{2,1,0:T(8,128)(2,1)S(1)}, bf16[16,16,256]{2,1,0:T(8,128)(2,1)S(1)}, u32[]{:S(2)}, u32[]{:S(2)}) collective-permute-start(bf16[16,16,256]{2,1,0:T(8,128)(2,1)S(1)} %get-tuple-element.124), channel_id=1, source_target_pairs={{0,4},{1,5},{2,6},{3,7},{4,0},{5,1},{6,2},{7,3},{8,12},{9,13},{10,... | collective-permute-start | bytes 393224 | tf_op jit(solution)/shard_map/ppermute | solution.py:215
  219.0 8.3 %collective-permute-start.38 = (bf16[16,16,256]{2,1,0:T(8,128)(2,1)S(1)}, bf16[16,16,256]{2,1,0:T(8,128)(2,1)S(1)}, u32[]{:S(2)}, u32[]{:S(2)}) collective-permute-start(bf16[16,16,256]{2,1,0:T(8,128)(2,1)S(1)} %get-tuple-element.123), channel_id=1, source_target_pairs={{0,4},{1,5},{2,6},{3,7},{4,0},{5,1},{6,2},{7,3},{8,12},{9,13},{10,... | collective-permute-start | bytes 393224 | tf_op jit(solution)/shard_map/ppermute | solution.py:215
  236.3 5.5 %collective-permute-start.44 = (bf16[16,16,256]{2,1,0:T(8,128)(2,1)S(1)}, bf16[16,16,256]{2,1,0:T(8,128)(2,1)S(1)}, u32[]{:S(2)}, u32[]{:S(2)}) collective-permute-start(bf16[16,16,256]{2,1,0:T(8,128)(2,1)S(1)} %mix.11.mine_ref), channel_id=1, source_target_pairs={{0,4},{1,5},{2,6},{3,7},{4,0},{5,1},{6,2},{7,3},{8,12},{9,13},{10,... | collective-permute-start | bytes 393224 | tf_op jit(solution)/shard_map/ppermute | solution.py:215
  243.5 9.2 %copy-start.7 = (bf16[4,32]{1,0:T(4,128)(2,1)S(1)}, bf16[4,32]{1,0:T(4,128)(2,1)}, u32[]{:S(2)}) copy-start(bf16[4,32]{1,0:T(4,128)(2,1)} %param.16) | copy-start | bytes 772
  243.6 9.2 %copy-start.9 = (f32[4]{0:T(128)S(1)}, f32[4]{0:T(128)}, u32[]{:S(2)}) copy-start(f32[4]{0:T(128)} %param.18) | copy-start | bytes 52
  243.6 17.9 %collective-permute-start.45 = (bf16[8,96,128]{2,1,0:T(8,128)(2,1)S(1)}, bf16[8,96,128]{2,1,0:T(8,128)(2,1)S(1)}, u32[]{:S(2)}, u32[]{:S(2)}) collective-permute-start(bf16[8,96,128]{2,1,0:T(8,128)(2,1)S(1)} %get-tuple-element.133), channel_id=1, source_target_pairs={{0,1},{1,0},{2,3},{3,2},{4,5},{5,4},{6,7},{7,6},{8,9},{9,8},{10,11... | collective-permute-start | bytes 589832 | tf_op jit(solution)/shard_map/ppermute | solution.py:215
  252.6 5.6 %collective-permute-start.40 = (bf16[16,16,256]{2,1,0:T(8,128)(2,1)S(1)}, bf16[16,16,256]{2,1,0:T(8,128)(2,1)S(1)}, u32[]{:S(2)}, u32[]{:S(2)}) collective-permute-start(bf16[16,16,256]{2,1,0:T(8,128)(2,1)S(1)} %mix.10.mine_ref), channel_id=1, source_target_pairs={{0,4},{1,5},{2,6},{3,7},{4,0},{5,1},{6,2},{7,3},{8,12},{9,13},{10,... | collective-permute-start | bytes 393224 | tf_op jit(solution)/shard_map/ppermute | solution.py:215
  253.3 22.2 %collective-permute-start.46 = (bf16[8,96,128]{2,1,0:T(8,128)(2,1)S(1)}, bf16[8,96,128]{2,1,0:T(8,128)(2,1)S(1)}, u32[]{:S(2)}, u32[]{:S(2)}) collective-permute-start(bf16[8,96,128]{2,1,0:T(8,128)(2,1)S(1)} %get-tuple-element.134), channel_id=1, source_target_pairs={{0,2},{1,3},{2,0},{3,1},{4,6},{5,7},{6,4},{7,5},{8,10},{9,11},{10,... | collective-permute-start | bytes 589832 | tf_op jit(solution)/shard_map/ppermute | solution.py:215
  255.2 20.4 %collective-permute-start.47 = (bf16[8,96,128]{2,1,0:T(8,128)(2,1)S(1)}, bf16[8,96,128]{2,1,0:T(8,128)(2,1)S(1)}, u32[]{:S(2)}, u32[]{:S(2)}) collective-permute-start(bf16[8,96,128]{2,1,0:T(8,128)(2,1)S(1)} %get-tuple-element.135), channel_id=1, source_target_pairs={{0,3},{1,2},{2,1},{3,0},{4,7},{5,6},{6,5},{7,4},{8,11},{9,10},{10,... | collective-permute-start | bytes 589832 | tf_op jit(solution)/shard_map/ppermute | solution.py:215
  259.9 25.4 %collective-permute-start.41 = (bf16[8,96,128]{2,1,0:T(8,128)(2,1)S(1)}, bf16[8,96,128]{2,1,0:T(8,128)(2,1)S(1)}, u32[]{:S(2)}, u32[]{:S(2)}) collective-permute-start(bf16[8,96,128]{2,1,0:T(8,128)(2,1)S(1)} %get-tuple-element.126), channel_id=1, source_target_pairs={{0,1},{1,0},{2,3},{3,2},{4,5},{5,4},{6,7},{7,6},{8,9},{9,8},{10,11... | collective-permute-start | bytes 589832 | tf_op jit(solution)/shard_map/ppermute | solution.py:215
  261.4 23.9 %collective-permute-start.42 = (bf16[8,96,128]{2,1,0:T(8,128)(2,1)S(1)}, bf16[8,96,128]{2,1,0:T(8,128)(2,1)S(1)}, u32[]{:S(2)}, u32[]{:S(2)}) collective-permute-start(bf16[8,96,128]{2,1,0:T(8,128)(2,1)S(1)} %get-tuple-element.127), channel_id=1, source_target_pairs={{0,2},{1,3},{2,0},{3,1},{4,6},{5,7},{6,4},{7,5},{8,10},{9,11},{10,... | collective-permute-start | bytes 589832 | tf_op jit(solution)/shard_map/ppermute | solution.py:215
  261.4 23.9 %collective-permute-start.43 = (bf16[8,96,128]{2,1,0:T(8,128)(2,1)S(1)}, bf16[8,96,128]{2,1,0:T(8,128)(2,1)S(1)}, u32[]{:S(2)}, u32[]{:S(2)}) collective-permute-start(bf16[8,96,128]{2,1,0:T(8,128)(2,1)S(1)} %get-tuple-element.128), channel_id=1, source_target_pairs={{0,3},{1,2},{2,1},{3,0},{4,7},{5,6},{6,5},{7,4},{8,11},{9,10},{10,... | collective-permute-start | bytes 589832 | tf_op jit(solution)/shard_map/ppermute | solution.py:215
  262.7 1.9 copy-start.3
  295.1 25.6 %copy-start.4 = (f32[4,96,1024]{2,1,0:T(8,128)}, f32[4,96,1024]{2,1,0:T(8,128)S(1)}, u32[]{:S(2)}) copy-start(f32[4,96,1024]{2,1,0:T(8,128)S(1)} %get-tuple-element.137) | copy-start | bytes 4718596
  295.1 25.4 %copy-start.6 = (f32[96]{0:T(128)S(1)}, f32[96]{0:T(128)}, u32[]{:S(2)}) copy-start(f32[96]{0:T(128)} %param.17) | copy-start | bytes 1156
  295.8 17.7 %collective-permute-start.48 = (f32[96,1024]{1,0:T(8,128)S(1)}, f32[96,1024]{1,0:T(8,128)S(1)}, u32[]{:S(2)}, u32[]{:S(2)}) collective-permute-start(f32[96,1024]{1,0:T(8,128)S(1)} %multiply_bitcast_fusion), channel_id=1, source_target_pairs={{0,8},{8,16},{16,24},{1,9},{9,17},{17,25},{2,10},{10,18},{18,26},{... | collective-permute-start | bytes 1179656 | tf_op jit(solution)/shard_map/ppermute | solution.py:376
  313.6 6.5 %collective-permute-start.49 = (f32[96,1024]{1,0:T(8,128)S(1)}, f32[96,1024]{1,0:T(8,128)S(1)}, u32[]{:S(2)}, u32[]{:S(2)}) collective-permute-start(f32[96,1024]{1,0:T(8,128)S(1)} %add.55), channel_id=1, source_target_pairs={{0,16},{8,24},{1,17},{9,25},{2,18},{10,26},{3,19},{11,27},{4,20},{... | collective-permute-start | bytes 1179656 | tf_op jit(solution)/shard_map/ppermute | solution.py:376
  320.7 15.2 %collective-permute-start.50 = (f32[2,1,1024]{2,1,0:T(1,128)S(1)}, f32[2,1,1024]{2,1,0:T(1,128)S(1)}, u32[]{:S(2)}, u32[]{:S(2)}) collective-permute-start(f32[2,1,1024]{2,1,0:T(1,128)S(1)} %get-tuple-element.148), channel_id=1, source_target_pairs={{1,0},{2,1},{3,2},{4,3},{5,4},{6,5},{7,6},{0,7},{9,8},{10,9},{11,1... | collective-permute-start | bytes 24584 | tf_op jit(solution)/shard_map/ppermute | solution.py:389
  323.8 12.1 %collective-permute-start.51 = (f32[2,1,1024]{2,1,0:T(1,128)S(1)}, f32[2,1,1024]{2,1,0:T(1,128)S(1)}, u32[]{:S(2)}, u32[]{:S(2)}) collective-permute-start(f32[2,1,1024]{2,1,0:T(1,128)S(1)} %get-tuple-element.149), channel_id=1, source_target_pairs={{0,1},{1,2},{2,3},{3,4},{4,5},{5,6},{6,7},{7,0},{8,9},{9,10},{10,1... | collective-permute-start | bytes 24584 | tf_op jit(solution)/shard_map/ppermute | solution.py:388
  337.3 13.0 %collective-permute-start.52 = (f32[96,1024]{1,0:T(8,128)S(1)}, f32[96,1024]{1,0:T(8,128)S(1)}, u32[]{:S(2)}, u32[]{:S(2)}) collective-permute-start(f32[96,1024]{1,0:T(8,128)S(1)} %get-tuple-element.147), channel_id=1, source_target_pairs={{0,8},{8,16},{16,24},{1,9},{9,17},{17,25},{2,10},{10,18},{18,26},{... | collective-permute-start | bytes 1179656 | tf_op jit(solution)/shard_map/ppermute | solution.py:376

commit v2 on v1

v2 whole, which is shorter than its diff:
```python
import functools
import math

import jax
import jax.numpy as jnp
import numpy as np
from jax import lax
from jax.experimental import pallas as pl
from jax.experimental.pallas import tpu as pltpu
from jax.sharding import PartitionSpec as P

ITERS = 3
CHUNKS = 2
BF = jnp.bfloat16
F32 = jnp.float32
LANES = 128


def cost(flops, bytes_accessed, transcendentals=0):
    return pl.CostEstimate(
        flops=int(flops), bytes_accessed=int(bytes_accessed), transcendentals=int(transcendentals)
    )


def turned(rows, cols, length):
    phase = (rows[:, None] * cols[None, :]) % length
    return phase.astype(np.float32) * np.float32(2.0 * math.pi / length)


def x_tables(cells, modes, slices, total):
    angle = turned(np.arange(modes, dtype=np.int64), np.arange(cells, dtype=np.int64), cells)
    pair = np.stack([np.cos(angle), -np.sin(angle)], 0).astype(np.float32)
    factor = (np.where(np.arange(modes) == 0, 1.0, 2.0).astype(np.float32) / np.float32(total))
    inverse = pair * factor[None, :, None]
    own = modes // slices

    def by_slice(table):
        table = table.reshape(2, slices, own, cells).transpose(1, 0, 2, 3)
        return table.reshape(slices, 2 * own, cells).astype(BF)

    return by_slice(pair), by_slice(inverse)


def y_table(rows, modes, slices):
    index = np.arange(modes, dtype=np.int64)
    signed = np.where(index < modes // 2, index, index + (rows - modes))
    angle = turned(np.arange(rows, dtype=np.int64), signed, rows)
    both = np.concatenate([np.cos(angle), np.sin(angle)], 1).astype(np.float32)
    return both.reshape(slices, rows // slices, 2 * modes).astype(BF)


def dot(a, b, dims):
    return lax.dot_general(a, b, (dims, ((), ())), preferred_element_type=F32)


def store_near(state, table, near_refs, pack, rows, first=0):
    width = LANES // pack
    near = dot(state, table, ((1,), (0,)))
    for g in range(state.shape[0] // (pack * rows)):
        for d, ref in enumerate(near_refs):
            parts = []
            for j in range(pack):
                at = (g * pack + j) * rows
                parts.append(near[at : at + rows, d * width : (d + 1) * width])
            ref[first + g] = jnp.concatenate(parts, 1).astype(BF)


def near_kernel(pack, state_ref, table_ref, *near_refs):
    count, rows, cells = state_ref.shape
    state = state_ref[...].reshape(count * rows, cells)
    store_near(state, table_ref[...], near_refs, pack, rows)


def forward_y_kernel(pack, own, peers, *refs):
    near_refs, table_ref, keep_ref, send_ref = refs[:peers], refs[peers], refs[-2], refs[-1]
    modes = table_ref.shape[1] // 2
    for g in range(near_refs[0].shape[0]):
        near = jnp.concatenate([ref[g] for ref in near_refs], 0)
        both = dot(near, table_ref[...], ((0,), (0,)))
        for j in range(pack):
            for h, out_ref in ((0, keep_ref), (1, send_ref)):
                at = (j * 2 + h) * 2 * own
                real = both[at : at + own]
                imag = both[at + own : at + 2 * own]
                c = g * pack + j
                out_ref[c, :, :modes] = (real[:, :modes] + imag[:, modes:]).astype(out_ref.dtype)
                out_ref[c, :, modes:] = (imag[:, :modes] - real[:, modes:]).astype(out_ref.dtype)


def mix_kernel(chunks, *refs):
    keep_refs, got_refs = refs[:chunks], refs[chunks : 2 * chunks]
    weight_ref = refs[2 * chunks]
    out_refs = refs[2 * chunks + 1 : 3 * chunks + 1]
    spectrum, mixed = refs[3 * chunks + 1 :]
    own, channels, modes = weight_ref.shape[1], weight_ref.shape[2], weight_ref.shape[4]
    size = channels // chunks
    for n in range(chunks):
        value = keep_refs[n][...] + got_refs[n][...].astype(F32)
        spectrum[:, n * size : (n + 1) * size] = jnp.swapaxes(value, 0, 1)

    def step(k, carry):
        row = spectrum[k]
        real = [jnp.zeros((channels, modes), F32)] * 2
        imag = [jnp.zeros((channels, modes), F32)] * 2
        for i in range(channels):
            s0, s1 = row[i : i + 1, :modes], row[i : i + 1, modes:]
            w0 = weight_ref[0, k, i].astype(F32)
            w1 = weight_ref[1, k, i].astype(F32)
            real[i % 2] = real[i % 2] + (s0 * w0 - s1 * w1)
            imag[i % 2] = imag[i % 2] + (s0 * w1 + s1 * w0)
        mixed[k, :, :modes] = real[0] + real[1]
        mixed[k, :, modes:] = imag[0] + imag[1]
        return carry

    lax.fori_loop(0, own, step, 0)
    for n in range(chunks):
        value = jnp.swapaxes(mixed[:, n * size : (n + 1) * size], 0, 1)
        out_refs[n][...] = value.astype(BF)


def inverse_y_kernel(pack, own, peers, mine_ref, theirs_ref, table_ref, *back_refs):
    modes = table_ref.shape[1] // 2
    rows = table_ref.shape[0] // peers
    for g in range(back_refs[0].shape[0]):
        parts = []
        for j in range(pack):
            for ref in (mine_ref, theirs_ref):
                value = ref[g * pack + j].astype(F32)
                real, imag = value[:, :modes], value[:, modes:]
                parts.append(jnp.concatenate([real, -imag], 1))
                parts.append(jnp.concatenate([imag, real], 1))
        turned_modes = jnp.concatenate(parts, 0).astype(BF)
        back = dot(table_ref[...], turned_modes, ((1,), (1,)))
        for d in range(peers):
            back_refs[d][g] = back[d * rows : (d + 1) * rows].astype(BF)


def spread_of(pack, back_refs, table_ref):
    width = LANES // pack
    blocks = []
    for g in range(back_refs[0].shape[0]):
        values = [ref[g].astype(F32) for ref in back_refs]
        for j in range(pack):
            lanes = [v[:, j * width : (j + 1) * width] for v in values]
            blocks.append(jnp.concatenate(lanes, 1).astype(BF))
    return dot(jnp.concatenate(blocks, 0), table_ref[...], ((1,), (0,)))


def update_kernel(pack, peers, *refs):
    back_refs, (point_ref, inverse_ref, forward_ref) = refs[:peers], refs[peers : peers + 3]
    state_ref, near_refs = refs[peers + 3], refs[peers + 4 :]
    count, rows, cells = state_ref.shape
    point = point_ref[...].reshape(count * rows, cells)
    updated = jax.nn.gelu(spread_of(pack, back_refs, inverse_ref) + point, approximate=True)
    state = updated.astype(BF)
    state_ref[...] = state.reshape(count, rows, cells)
    store_near(state, forward_ref[...], near_refs, pack, rows)


def last_kernel(pack, peers, first, *refs):
    back_refs = refs[:peers]
    point_ref, inverse_ref, decoder_ref = refs[peers : peers + 3]
    earlier = refs[peers + 3 : -2]
    updated_ref, fields_ref = refs[-2:]
    count, rows, cells = updated_ref.shape
    group = pl.program_id(0)
    point = point_ref[...].reshape(count * rows, cells)
    updated = jax.nn.gelu(spread_of(pack, back_refs, inverse_ref) + point, approximate=True)
    updated_ref[...] = updated.reshape(count, rows, cells)

    @pl.when(group == 0)
    def _():
        fields_ref[...] = earlier[1][...] if earlier else jnp.zeros_like(fields_ref)

    def slab(t, carry):
        at = pl.ds(pl.multiple_of(t * 8, 8), 8)
        values = [updated_ref[c, at, :] for c in range(count)]
        for f in range(fields_ref.shape[0]):
            total = fields_ref[f, at, :]
            for c in range(count):
                total = total + decoder_ref[f, first + group * count + c] * values[c]
            fields_ref[f, at, :] = total
        return carry

    lax.fori_loop(0, rows // 8, slab, 0)


def pointwise_kernel(chunks, block, *refs):
    state_refs, (forcing_ref, weight_ref, bias_ref, out_ref) = refs[:chunks], refs[chunks:]
    channels, rows, cells = out_ref.shape
    count = channels * block
    for t in range(rows // block):
        at = slice(t * block, (t + 1) * block)
        state = jnp.concatenate([ref[:, at] for ref in state_refs], 0).reshape(count, cells)
        source = forcing_ref[:, at].reshape(count, cells).astype(F32) + bias_ref[...]
        out = dot(weight_ref[...], state, ((1,), (0,))) + source
        out_ref[:, at] = out.reshape(channels, block, cells)


def residual_kernel(
    fields_ref, geo_ref, below_ref, before_ref, after_ref, turning_ref, out_ref
):
    rows, cells = geo_ref.shape
    east, north, upward = fields_ref[0], fields_ref[1], fields_ref[2]
    geopotential = geo_ref[...]
    row = lax.broadcasted_iota(jnp.int32, (rows, cells), 0)

    def along_x(field):
        return (pltpu.roll(field, cells - 1, 1) - pltpu.roll(field, 1, 1)) * 0.5

    def along_y(field, which):
        later = jnp.where(row == rows - 1, after_ref[which], pltpu.roll(field, rows - 1, 0))
        earlier = jnp.where(row == 0, before_ref[which], pltpu.roll(field, 1, 0))
        return (later - earlier) * 0.5

    turning = turning_ref[...]
    out_ref[0] = along_x(east) + along_y(north, 0) + upward - below_ref[...]
    out_ref[1] = turning * north - along_x(geopotential)
    out_ref[2] = turning * east + along_y(geopotential, 1)


def on_device(forcing, spectral_weight, point_weight, point_bias, decoder, coriolis, layer_depth):
    level_count, channels, rows, cells = forcing.shape
    assert level_count == 1
    forcing = forcing[0]
    slices = lax.axis_size("gy")
    peers = slices // 2
    own = spectral_weight.shape[1]
    modes = own * slices
    ymodes = spectral_weight.shape[4]
    total_rows = rows * slices
    pack = LANES // (4 * own)
    groups = channels // pack
    part = groups // CHUNKS
    size = channels // CHUNKS
    wide = peers * 4 * own
    me = lax.axis_index("gy")

    forward_x, inverse_x = x_tables(cells, modes, slices, cells * total_rows)
    order = jnp.stack([me ^ d ^ (h * peers) for d in range(peers) for h in range(2)])
    near_table = jnp.take(jnp.asarray(forward_x), order, axis=0).reshape(wide, cells).T
    spread_table = jnp.take(jnp.asarray(inverse_x), order, axis=0).reshape(wide, cells)
    row_table = jnp.take(jnp.asarray(y_table(total_rows, ymodes, slices)), order[::2], axis=0)
    row_table = row_table.reshape(peers * rows, 2 * ymodes)

    block = next(b for b in (16, 8, rows) if rows % b == 0)
    blocks = next(b for b in (2, 1) if rows % (b * block) == 0)
    which = lax.broadcasted_iota(jnp.int32, (channels * block, channels), 0) // block
    pick = (which == lax.broadcasted_iota(jnp.int32, which.shape, 1)).astype(BF)
    square = jnp.dot(jnp.dot(pick, point_weight.T), pick.T)
    at = jnp.arange(channels * block, dtype=jnp.int32) % block
    square = jnp.where(at[:, None] == at[None, :], square, 0).astype(BF)
    bias = jnp.repeat(point_bias, block)[:, None]
    many = next(b for b in (4, 2, 1) if part % b == 0)

    def swap(value, distance):
        return lax.ppermute(value, "gy", [(g, g ^ distance) for g in range(slices)])

    def whole(shape):
        return pl.BlockSpec(shape, lambda i: (0,) * len(shape))

    cells_spec = pl.BlockSpec((many * pack, rows, cells), lambda i: (i, 0, 0))
    lane_spec = pl.BlockSpec((many, rows, LANES), lambda i: (i, 0, 0))
    lane_shape = jax.ShapeDtypeStruct((part, rows, LANES), BF)
    mode_spec = pl.BlockSpec((many * pack, own, 2 * ymodes), lambda i: (i, 0, 0))
    vmem = pl.BlockSpec(memory_space=pltpu.VMEM)

    def params(mib, *grid):
        return pltpu.CompilerParams(dimension_semantics=grid, vmem_limit_bytes=mib << 20)

    tile = size * rows * cells

    def offset_spec(n):
        return pl.BlockSpec((many * pack, rows, cells), lambda i: (i + n * (part // many), 0, 0))

    def near_of(n):
        return pl.pallas_call(
            functools.partial(near_kernel, pack),
            grid=(part // many,),
            in_specs=[offset_spec(n), whole((cells, wide))],
            out_specs=[lane_spec] * peers,
            out_shape=[lane_shape] * peers,
            compiler_params=params(6, "arbitrary"),
            cost_estimate=cost(2 * tile * wide, tile * 2),
            name="near",
        )(forcing, near_table)

    def exchange(parts):
        return [parts[0]] + [swap(parts[d], d) for d in range(1, peers)]

    def forward_y(parts):
        return pl.pallas_call(
            functools.partial(forward_y_kernel, pack, own, peers),
            grid=(part // many,),
            in_specs=[lane_spec] * peers + [whole(row_table.shape)],
            out_specs=[mode_spec] * 2,
            out_shape=[
                jax.ShapeDtypeStruct((size, own, 2 * ymodes), F32),
                jax.ShapeDtypeStruct((size, own, 2 * ymodes), BF),
            ],
            compiler_params=params(8, "arbitrary"),
            cost_estimate=cost(4 * part * LANES * peers * rows * ymodes, 2 * size * rows * wide),
            name="forward_y",
        )(*parts, row_table)

    def mix(kept, got):
        return pl.pallas_call(
            functools.partial(mix_kernel, CHUNKS),
            in_specs=[vmem] * (2 * CHUNKS + 1),
            out_specs=[vmem] * CHUNKS,
            out_shape=[jax.ShapeDtypeStruct((size, own, 2 * ymodes), BF)] * CHUNKS,
            scratch_shapes=[pltpu.VMEM((own, channels, 2 * ymodes), F32)] * 2,
            compiler_params=params(8),
            cost_estimate=cost(
                8 * own * channels**2 * ymodes, 4 * own * channels**2 * ymodes
            ),
            name="mix",
        )(*kept, *got, spectral_weight)

    def inverse_y(mine, theirs):
        return pl.pallas_call(
            functools.partial(inverse_y_kernel, pack, own, peers),
            grid=(part // many,),
            in_specs=[mode_spec] * 2 + [whole(row_table.shape)],
            out_specs=[lane_spec] * peers,
            out_shape=[lane_shape] * peers,
            compiler_params=params(8, "arbitrary"),
            cost_estimate=cost(4 * part * LANES * peers * rows * ymodes, 2 * size * rows * wide),
            name="inverse_y",
        )(mine, theirs, row_table)

    def pointwise(states):
        if len(states) == 1:
            specs = [pl.BlockSpec((channels, blocks * block, cells), lambda i: (0, i, 0))]
        else:
            specs = [pl.BlockSpec((size, blocks * block, cells), lambda i: (0, i, 0))] * CHUNKS
        return pl.pallas_call(
            functools.partial(pointwise_kernel, len(states), block),
            grid=(rows // (blocks * block),),
            in_specs=specs
            + [
                pl.BlockSpec((channels, blocks * block, cells), lambda i: (0, i, 0)),
                whole(square.shape),
                whole(bias.shape),
            ],
            out_specs=pl.BlockSpec((channels, blocks * block, cells), lambda i: (0, i, 0)),
            out_shape=jax.ShapeDtypeStruct((channels, rows, cells), F32),
            compiler_params=params(19, "arbitrary"),
            cost_estimate=cost(
                2 * channels * block * channels * rows * cells, 8 * channels * rows * cells
            ),
            name="pointwise",
        )(*states, forcing, square, bias)

    def update(backs, point, n):
        out = pl.pallas_call(
            functools.partial(update_kernel, pack, peers),
            grid=(part // many,),
            in_specs=[lane_spec] * peers
            + [offset_spec(n), whole(spread_table.shape), whole(near_table.shape)],
            out_specs=[cells_spec] + [lane_spec] * peers,
            out_shape=[jax.ShapeDtypeStruct((size, rows, cells), BF)] + [lane_shape] * peers,
            compiler_params=params(16, "arbitrary"),
            cost_estimate=cost(4 * tile * wide, 6 * tile, tile),
            name="update",
        )(*backs, point, spread_table, near_table)
        return out[0], out[1:]

    decoder_full = decoder.astype(F32)

    def last(backs, point, n, earlier):
        fields_shape = (decoder.shape[0], rows, cells)
        more = [pl.BlockSpec(memory_space=pl.ANY), whole(fields_shape)] if earlier else []
        return pl.pallas_call(
            functools.partial(last_kernel, pack, peers, n * size),
            grid=(part // many,),
            in_specs=[lane_spec] * peers
            + [
                offset_spec(n),
                whole(spread_table.shape),
                pl.BlockSpec(memory_space=pltpu.SMEM),
            ]
            + more,
            out_specs=[offset_spec(n), whole(fields_shape)],
            out_shape=[
                jax.ShapeDtypeStruct((channels, rows, cells), F32),
                jax.ShapeDtypeStruct(fields_shape, F32),
            ],
            input_output_aliases={peers + 3: 0} if earlier else {},
            compiler_params=params(20, "arbitrary"),
            cost_estimate=cost(2 * tile * wide, 8 * tile, tile),
            name="last",
        )(*backs, point, spread_table, decoder_full, *earlier)

    every = range(CHUNKS)
    nears = [near_of(n) for n in every]
    states = [forcing]
    for iteration in range(ITERS):
        arrived = [exchange(parts) for parts in nears]
        point = pointwise(states)
        halves = [forward_y(parts) for parts in arrived]
        kept = [half[0] for half in halves]
        got = [swap(half[1], peers) for half in halves]
        mixed = mix(kept, got)
        theirs = [swap(value, peers) for value in mixed]
        backs = [exchange(inverse_y(mixed[n], theirs[n])) for n in every]
        if iteration < ITERS - 1:
            done = [update(backs[n], point, n) for n in every]
            states = [pair[0] for pair in done]
            nears = [pair[1] for pair in done]
    done = []
    for n in every:
        done = last(backs[n], point, n, done)
    updated, fields = done
    north, upward, heat = fields[1], fields[2], fields[3]

    levels = lax.axis_size("lev")
    level = lax.axis_index("lev")

    def from_below(value, step):
        return lax.ppermute(value, "lev", [(s, s + step) for s in range(levels - step)])

    below = from_below(upward, 1)
    layer = lax.dynamic_index_in_dim(layer_depth, level, 0, keepdims=False) * heat
    if levels % 2 == 0 and rows % 16 == 0:
        half = rows // 2
        place = level % 2
        partner = [(s, s ^ 1) for s in range(levels)]
        other = lax.ppermute(layer, "lev", partner)
        both = lax.dynamic_slice_in_dim(layer + other, place * half, half, 0)
        lower = from_below(both, 2)
        step = 2
        while step < levels - 2:
            lower = lower + from_below(lower, step)
            step *= 2
        rest = lax.ppermute(lower, "lev", partner)
        lower = jnp.where(
            place == 0, jnp.concatenate([lower, rest], 0), jnp.concatenate([rest, lower], 0)
        )
        geopotential = layer + jnp.where(place == 0, 0.0, other) + lower
    else:
        geopotential = layer
        step = 1
        while step < levels:
            geopotential = geopotential + from_below(geopotential, step)
            step *= 2

    up = [(i, (i + 1) % slices) for i in range(slices)]
    down = [(j, i) for i, j in up]
    before = lax.ppermute(jnp.stack([north[-1:], geopotential[-1:]], 0), "gy", up)
    after = lax.ppermute(jnp.stack([north[:1], geopotential[:1]], 0), "gy", down)
    residual = pl.pallas_call(
        residual_kernel,
        in_specs=[vmem] * 6,
        out_specs=vmem,
        out_shape=jax.ShapeDtypeStruct((3, rows, cells), F32),
        compiler_params=params(8),
        cost_estimate=cost(20 * rows * cells, 36 * rows * cells),
        name="residual",
    )(fields, geopotential, below, before, after, coriolis[:, None])
    return updated[None], residual[:, None]


def solution(mesh):
    return jax.shard_map(
        on_device,
        mesh=mesh,
        in_specs=(
            P("lev", None, "gy", None),
            P(None, "gy", None, None, None),
            P(),
            P(),
            P(),
            P("gy"),
            P(),
        ),
        out_specs=(P("lev", None, "gy", None), P(None, "lev", "gy", None)),
        check_vma=False,
    )
```

time: 355 us -> 250 us (0.70)
  Pallas kernels: 176 us -> 69.1 us
  waiting for transfers between devices: 65 us -> 82.2 us
  other arithmetic: 19.9 us -> 2.9 us
  local copies, waits for them, and re-layouts: 20.4 us -> 24.2 us
    pallas_call x17 -> x15, Pallas kernels: 152 us -> 59.6 us  [the longest x3 16.4 us: pointwise(): pl.pallas_call(functools.partial(pointwise_kernel, len(states), block), g...]
    ppermute x48, waiting for transfers between devices: 50.6 us -> 72.8 us  [swap(): return lax.ppermute(value, 'gy', [(g, g ^ distance) for g in range(slices)])]
    ppermute x3 -> x2, starting transfers between devices: 22.7 us -> 5.76 us  [from_below(): lax.ppermute(value, 'lev', [(s, s + step) for s in range(levels - step)])]
    ppermute x2 -> x4, starting transfers between devices: 3.07 us -> 17 us  [the longest x1 12.3 us: on_device(): other = lax.ppermute(layer, 'lev', partner)]
    ppermute x3 -> x2, waiting for transfers between devices: 14.4 us -> 1.93 us  [from_below(): lax.ppermute(value, 'lev', [(s, s + step) for s in range(levels - step)])]
    broadcast_in_dim x1 -> x0, other arithmetic: 12.1 us -> none  [on_device(): updated[None]]
    unnamed x20 -> x36, local copies, waits for them, and re-layouts: 5.16 us -> 17.2 us
    pallas_call x6, Pallas kernels: 13.1 us -> 4.92 us  [forward_y(): pl.pallas_call(functools.partial(forward_y_kernel, pack, own, peers), gri...]
  transfers between devices with their start and end apart: 53 -> 54, of which waited for: 14 -> 25; matrix products, arithmetic and copies ran while one was open for 8% -> 2% of each run, Pallas kernels for 37% -> 18%
where the time goes in v2:
time: 250 us; the launch traced here: 247 us
  waiting for transfers between devices  82.2 us (33%)
  Pallas kernels  69.1 us (28%)
  starting transfers between devices  67.1 us (27%)
  local copies, waits for them, and re-layouts  24.2 us (10%)
  other arithmetic  2.9 us (1%)
    ppermute x48, waiting for transfers between devices, swap(): return lax.ppermute(value, 'gy', [(g, g ^ distance) for g in range(slices)])  72.8 us
    ppermute x48, starting transfers between devices, swap(): return lax.ppermute(value, 'gy', [(g, g ^ distance) for g in range(slices)])  44.3 us
    unnamed x36, local copies, waits for them, and re-layouts  17.2 us
    pallas_call x3, Pallas kernels, pointwise(): pl.pallas_call(functools.partial(pointwise_kernel, len(states), block), g...  16.4 us
    pallas_call x2, Pallas kernels, last(): pl.pallas_call(functools.partial(last_kernel, pack, peers, n * size), gri...  14.5 us
    pallas_call x4, Pallas kernels, update(): pl.pallas_call(functools.partial(update_kernel, pack, peers), grid=(part...  12.8 us
    ppermute x1, starting transfers between devices, on_device(): other = lax.ppermute(layer, 'lev', partner)  12.3 us
    pallas_call x3, Pallas kernels, mix(): pl.pallas_call(functools.partial(mix_kernel, CHUNKS), in_specs=[vmem] * (...  11.1 us
  transfers between devices with their start and end apart: 54, of which 25 were waited for; matrix products, arithmetic and copies ran while one was open for 2% of the time, Pallas kernels for 18%

profile of v2, /device:TPU:1, one launch (start us, length us, event | category | flops | bytes accessed | tf_op | source)
XLA Modules:
  0.0 247.5 jit_solution(15283551894119521600)
XLA Ops:
  0.8 1.6 gather_fusion.1
  2.4 1.6 gather_fusion.2
  4.4 2.8 %copy-done.2 = bf16[1,32,96,1024]{3,2,1,0:T(8,128)(2,1)S(1)} copy-done((bf16[1,32,96,1024]{3,2,1,0:T(8,128)(2,1)S(1)}, bf16[1,32,96,1024]{3,2,1,0:T(8,128)(2,1)}, u32[]{:S(2)}) %copy-start.2) | copy-done | bytes 6291480
  7.2 2.0 near.3
  9.2 2.1 collective-permute-start.3
  11.2 1.3 collective-permute-start.4
  12.5 1.3 near.2
  13.9 1.4 collective-permute-start
  15.3 1.3 collective-permute-start.1
  16.9 2.2 gather_fusion
  21.2 1.3 forward_y.7
  22.6 2.2 collective-permute-start.7
  25.4 6.4 %collective-permute-done.2.refs_3_ = bf16[8,96,128]{2,1,0:T(8,128)(2,1)S(1)} collective-permute-done((bf16[8,96,128]{2,1,0:T(8,128)(2,1)S(1)}, bf16[8,96,128]{2,1,0:T(8,128)(2,1)S(1)}, u32[]{:S(2)}, u32[]{:S(2)}) %collective-permute-start.2) | collective-permute-done | bytes 196640 | tf_op jit(solution)/shard_map/ppermute | solution.py:257
  34.0 6.6 %collective-permute-done.6.refs_2_ = bf16[16,16,256]{2,1,0:T(8,128)(2,1)S(1)} collective-permute-done((bf16[16,16,256]{2,1,0:T(8,128)(2,1)S(1)}, bf16[16,16,256]{2,1,0:T(8,128)(2,1)S(1)}, u32[]{:S(2)}, u32[]{:S(2)}) %collective-permute-start.6) | collective-permute-done | bytes 131104 | tf_op jit(solution)/shard_map/ppermute | solution.py:257
  40.6 3.4 %copy-done.5 = bf16[2,16,32,32,128]{4,3,2,1,0:T(8,128)(2,1)S(1)} copy-done((bf16[2,16,32,32,128]{4,3,2,1,0:T(8,128)(2,1)S(1)}, bf16[2,16,32,32,128]{4,3,2,1,0:T(8,128)(2,1)}, u32[]{:S(2)}) %copy-start.5) | copy-done | bytes 8388632
  44.0 3.7 %mix.3 = (bf16[16,16,256]{2,1,0:T(8,128)(2,1)S(1)}, bf16[16,16,256]{2,1,0:T(8,128)(2,1)S(1)}) custom-call(f32[16,16,256]{2,1,0:T(8,128)S(1)} %get-tuple-element.81.refs_0_, f32[16,16,256]{2,1,0:T(8,128)S(1)} %get-tuple-element.86.refs_1_, bf16[16,16,256]{2,1,0:T(8,128)(2,1)S(1)} %collective-permute-done.6.refs_2_, ...), custom_call_target="tpu_custom_call" | custom-call | flops 16777216 | bytes 8388608 | tf_op jit(solution)/shard_map/mix/pallas_call | solution.py:307
  48.6 2.4 collective-permute-start.8
  51.0 5.0 %collective-permute-done.15.theirs_ref = bf16[16,16,256]{2,1,0:T(8,128)(2,1)S(1)} collective-permute-done((bf16[16,16,256]{2,1,0:T(8,128)(2,1)S(1)}, bf16[16,16,256]{2,1,0:T(8,128)(2,1)S(1)}, u32[]{:S(2)}, u32[]{:S(2)}) %collective-permute-start.15) | collective-permute-done | bytes 131104 | tf_op jit(solution)/shard_map/ppermute | solution.py:257
  56.7 4.5 %collective-permute-start.16 = (bf16[8,96,128]{2,1,0:T(8,128)(2,1)S(1)}, bf16[8,96,128]{2,1,0:T(8,128)(2,1)S(1)}, u32[]{:S(2)}, u32[]{:S(2)}) collective-permute-start(bf16[8,96,128]{2,1,0:T(8,128)(2,1)S(1)} %get-tuple-element.101), channel_id=1, source_target_pairs={{0,1},{1,0},{2,3},{3,2},{4,5},{5,4},{6,7},{7,6},{8,9},{9,8},{10,11... | collective-permute-start | bytes 589832 | tf_op jit(solution)/shard_map/ppermute | solution.py:257
  62.4 2.8 %copy-done.3 = bf16[1,32,96,1024]{3,2,1,0:T(8,128)(2,1)S(1)} copy-done((bf16[1,32,96,1024]{3,2,1,0:T(8,128)(2,1)S(1)}, bf16[1,32,96,1024]{3,2,1,0:T(8,128)(2,1)}, u32[]{:S(2)}) %copy-start.3) | copy-done | bytes 6291480
  65.2 5.5 %pointwise.3.refs_4_ = f32[32,96,1024]{2,1,0:T(8,128)S(1)} custom-call(bf16[32,96,1024]{2,1,0:T(8,128)(2,1)S(1)} %bitcast.31, bf16[32,96,1024]{2,1,0:T(8,128)(2,1)S(1)} %bitcast.32, bf16[512,512]{1,0:T(8,128)(2,1)S(1)} %convolution_select_fusion.refs_2_.refs_3_, f32[512,1]{1,0:T(8,128)S(1)} %broadcast_in_dim_reshape.4.refs_3_.refs_4_), custom_call_target="tpu_custom_call" | custom-call | flops 3221225472 | bytes 25165824 | tf_op jit(solution)/shard_map/pointwise/pallas_call | solution.py:337
  71.8 2.4 collective-permute-start.11
  74.2 3.2 %update.5 = (bf16[16,96,1024]{2,1,0:T(8,128)(2,1)S(1)}, bf16[8,96,128]{2,1,0:T(8,128)(2,1)S(1)}, bf16[8,96,128]{2,1,0:T(8,128)(2,1)S(1)}, bf16[8,96,128]{2,1,0:T(8,128)(2,1)S(1)}, bf16[8,96,128]{2,1,0:T(8,128)(2,1)S(1)}) custom-call(bf16[8,96,128]{2,1,0:T(8,128)(2,1)S(1)} %get-tuple-element.100.refs_0_, ...), custom_call_target="tpu_custom_call" | custom-call | flops 1610612736 | bytes 9437184 | tf_op jit(solution)/shard_map/update/pallas_call | solution.py:356
  77.4 1.5 collective-permute-start.19
  81.5 3.2 %update.4 = (bf16[16,96,1024]{2,1,0:T(8,128)(2,1)S(1)}, bf16[8,96,128]{2,1,0:T(8,128)(2,1)S(1)}, bf16[8,96,128]{2,1,0:T(8,128)(2,1)S(1)}, bf16[8,96,128]{2,1,0:T(8,128)(2,1)S(1)}, bf16[8,96,128]{2,1,0:T(8,128)(2,1)S(1)}) custom-call(bf16[8,96,128]{2,1,0:T(8,128)(2,1)S(1)} %get-tuple-element.90.refs_0_, ...), custom_call_target="tpu_custom_call" | custom-call | flops 1610612736 | bytes 9437184 | tf_op jit(solution)/shard_map/update/pallas_call | solution.py:356
  85.5 4.4 %collective-permute-done.19.refs_1_ = bf16[8,96,128]{2,1,0:T(8,128)(2,1)S(1)} collective-permute-done((bf16[8,96,128]{2,1,0:T(8,128)(2,1)S(1)}, bf16[8,96,128]{2,1,0:T(8,128)(2,1)S(1)}, u32[]{:S(2)}, u32[]{:S(2)}) %collective-permute-start.19) | collective-permute-done | bytes 196640 | tf_op jit(solution)/shard_map/ppermute | solution.py:257
  90.7 2.5 %collective-permute-start.23 = (bf16[16,16,256]{2,1,0:T(8,128)(2,1)S(1)}, bf16[16,16,256]{2,1,0:T(8,128)(2,1)S(1)}, u32[]{:S(2)}, u32[]{:S(2)}) collective-permute-start(bf16[16,16,256]{2,1,0:T(8,128)(2,1)S(1)} %get-tuple-element.110), channel_id=1, source_target_pairs={{0,4},{1,5},{2,6},{3,7},{4,0},{5,1},{6,2},{7,3},{8,12},{9,13},{10,... | collective-permute-start | bytes 393224 | tf_op jit(solution)/shard_map/ppermute | solution.py:257
  93.2 4.6 %collective-permute-done.12.refs_1_ = bf16[8,96,128]{2,1,0:T(8,128)(2,1)S(1)} collective-permute-done((bf16[8,96,128]{2,1,0:T(8,128)(2,1)S(1)}, bf16[8,96,128]{2,1,0:T(8,128)(2,1)S(1)}, u32[]{:S(2)}, u32[]{:S(2)}) %collective-permute-start.12) | collective-permute-done | bytes 196640 | tf_op jit(solution)/shard_map/ppermute | solution.py:257
  100.5 7.8 %collective-permute-done.22.refs_2_ = bf16[16,16,256]{2,1,0:T(8,128)(2,1)S(1)} collective-permute-done((bf16[16,16,256]{2,1,0:T(8,128)(2,1)S(1)}, bf16[16,16,256]{2,1,0:T(8,128)(2,1)S(1)}, u32[]{:S(2)}, u32[]{:S(2)}) %collective-permute-start.22) | collective-permute-done | bytes 131104 | tf_op jit(solution)/shard_map/ppermute | solution.py:257
  108.3 3.7 %mix.4 = (bf16[16,16,256]{2,1,0:T(8,128)(2,1)S(1)}, bf16[16,16,256]{2,1,0:T(8,128)(2,1)S(1)}) custom-call(f32[16,16,256]{2,1,0:T(8,128)S(1)} %get-tuple-element.98.refs_0_, f32[16,16,256]{2,1,0:T(8,128)S(1)} %get-tuple-element.108.refs_1_, bf16[16,16,256]{2,1,0:T(8,128)(2,1)S(1)} %collective-permute-done.22.refs_2_, ...), custom_call_target="tpu_custom_call" | custom-call | flops 16777216 | bytes 8388608 | tf_op jit(solution)/shard_map/mix/pallas_call | solution.py:307
  112.1 5.7 %collective-permute-done.31.theirs_ref = bf16[16,16,256]{2,1,0:T(8,128)(2,1)S(1)} collective-permute-done((bf16[16,16,256]{2,1,0:T(8,128)(2,1)S(1)}, bf16[16,16,256]{2,1,0:T(8,128)(2,1)S(1)}, u32[]{:S(2)}, u32[]{:S(2)}) %collective-permute-start.31) | collective-permute-done | bytes 131104 | tf_op jit(solution)/shard_map/ppermute | solution.py:257
  118.6 1.6 collective-permute-start.33
  121.4 3.4 %collective-permute-done.24.theirs_ref = bf16[16,16,256]{2,1,0:T(8,128)(2,1)S(1)} collective-permute-done((bf16[16,16,256]{2,1,0:T(8,128)(2,1)S(1)}, bf16[16,16,256]{2,1,0:T(8,128)(2,1)S(1)}, u32[]{:S(2)}, u32[]{:S(2)}) %collective-permute-start.24) | collective-permute-done | bytes 131104 | tf_op jit(solution)/shard_map/ppermute | solution.py:257
  126.1 2.2 collective-permute-start.27
  128.3 5.5 %pointwise.4.refs_4_ = f32[32,96,1024]{2,1,0:T(8,128)S(1)} custom-call(bf16[16,96,1024]{2,1,0:T(8,128)(2,1)S(1)} %get-tuple-element.116.refs_0_, bf16[16,96,1024]{2,1,0:T(8,128)(2,1)S(1)} %get-tuple-element.117.refs_1_, bf16[32,96,1024]{2,1,0:T(8,128)(2,1)S(1)} %bitcast.35, bf16[512,512]{1,0:T(8,128)(2,1)S(1)} %convolution_select_fusion.refs_2_.refs_3_, ...), custom_call_target="tpu_custom_call" | custom-call | flops 3221225472 | bytes 25165824 | tf_op jit(solution)/shard_map/pointwise/pallas_call | solution.py:337
  133.8 3.2 %update.7 = (bf16[16,96,1024]{2,1,0:T(8,128)(2,1)S(1)}, bf16[8,96,128]{2,1,0:T(8,128)(2,1)S(1)}, bf16[8,96,128]{2,1,0:T(8,128)(2,1)S(1)}, bf16[8,96,128]{2,1,0:T(8,128)(2,1)S(1)}, bf16[8,96,128]{2,1,0:T(8,128)(2,1)S(1)}) custom-call(bf16[8,96,128]{2,1,0:T(8,128)(2,1)S(1)} %get-tuple-element.124.refs_0_, ...), custom_call_target="tpu_custom_call" | custom-call | flops 1610612736 | bytes 9437184 | tf_op jit(solution)/shard_map/update/pallas_call | solution.py:356
  137.0 1.6 copy-done.6
  139.1 2.2 collective-permute-start.37
  141.3 3.2 %update.6 = (bf16[16,96,1024]{2,1,0:T(8,128)(2,1)S(1)}, bf16[8,96,128]{2,1,0:T(8,128)(2,1)S(1)}, bf16[8,96,128]{2,1,0:T(8,128)(2,1)S(1)}, bf16[8,96,128]{2,1,0:T(8,128)(2,1)S(1)}, bf16[8,96,128]{2,1,0:T(8,128)(2,1)S(1)}) custom-call(bf16[8,96,128]{2,1,0:T(8,128)(2,1)S(1)} %get-tuple-element.112.refs_0_, ...), custom_call_target="tpu_custom_call" | custom-call | flops 1610612736 | bytes 9437184 | tf_op jit(solution)/shard_map/update/pallas_call | solution.py:356
  145.3 2.0 collective-permute-start.30
  148.5 1.6 collective-permute-done.28.refs_1_
  150.2 5.1 %collective-permute-done.30.refs_3_ = bf16[8,96,128]{2,1,0:T(8,128)(2,1)S(1)} collective-permute-done((bf16[8,96,128]{2,1,0:T(8,128)(2,1)S(1)}, bf16[8,96,128]{2,1,0:T(8,128)(2,1)S(1)}, u32[]{:S(2)}, u32[]{:S(2)}) %collective-permute-start.30) | collective-permute-done | bytes 196640 | tf_op jit(solution)/shard_map/ppermute | solution.py:257
  156.1 6.1 %collective-permute-done.38.refs_2_ = bf16[16,16,256]{2,1,0:T(8,128)(2,1)S(1)} collective-permute-done((bf16[16,16,256]{2,1,0:T(8,128)(2,1)S(1)}, bf16[16,16,256]{2,1,0:T(8,128)(2,1)S(1)}, u32[]{:S(2)}, u32[]{:S(2)}) %collective-permute-start.38) | collective-permute-done | bytes 131104 | tf_op jit(solution)/shard_map/ppermute | solution.py:257
  162.2 3.7 %mix.5 = (bf16[16,16,256]{2,1,0:T(8,128)(2,1)S(1)}, bf16[16,16,256]{2,1,0:T(8,128)(2,1)S(1)}) custom-call(f32[16,16,256]{2,1,0:T(8,128)S(1)} %get-tuple-element.122.refs_0_, f32[16,16,256]{2,1,0:T(8,128)S(1)} %get-tuple-element.132.refs_1_, bf16[16,16,256]{2,1,0:T(8,128)(2,1)S(1)} %collective-permute-done.38.refs_2_, ...), custom_call_target="tpu_custom_call" | custom-call | flops 16777216 | bytes 8388608 | tf_op jit(solution)/shard_map/mix/pallas_call | solution.py:307
  166.0 8.6 %collective-permute-done.44.theirs_ref = bf16[16,16,256]{2,1,0:T(8,128)(2,1)S(1)} collective-permute-done((bf16[16,16,256]{2,1,0:T(8,128)(2,1)S(1)}, bf16[16,16,256]{2,1,0:T(8,128)(2,1)S(1)}, u32[]{:S(2)}, u32[]{:S(2)}) %collective-permute-start.44) | collective-permute-done | bytes 131104 | tf_op jit(solution)/shard_map/ppermute | solution.py:257
  176.1 2.7 %collective-permute-start.46 = (bf16[8,96,128]{2,1,0:T(8,128)(2,1)S(1)}, bf16[8,96,128]{2,1,0:T(8,128)(2,1)S(1)}, u32[]{:S(2)}, u32[]{:S(2)}) collective-permute-start(bf16[8,96,128]{2,1,0:T(8,128)(2,1)S(1)} %get-tuple-element.145), channel_id=1, source_target_pairs={{0,2},{1,3},{2,0},{3,1},{4,6},{5,7},{6,4},{7,5},{8,10},{9,11},{10,... | collective-permute-start | bytes 589832 | tf_op jit(solution)/shard_map/ppermute | solution.py:257
  179.0 2.9 %collective-permute-done.40.theirs_ref = bf16[16,16,256]{2,1,0:T(8,128)(2,1)S(1)} collective-permute-done((bf16[16,16,256]{2,1,0:T(8,128)(2,1)S(1)}, bf16[16,16,256]{2,1,0:T(8,128)(2,1)S(1)}, u32[]{:S(2)}, u32[]{:S(2)}) %collective-permute-start.40) | collective-permute-done | bytes 131104 | tf_op jit(solution)/shard_map/ppermute | solution.py:257
  183.9 1.5 collective-permute-start.43
  185.3 2.8 %copy-done.4 = bf16[1,32,96,1024]{3,2,1,0:T(8,128)(2,1)S(1)} copy-done((bf16[1,32,96,1024]{3,2,1,0:T(8,128)(2,1)S(1)}, bf16[1,32,96,1024]{3,2,1,0:T(8,128)(2,1)}, u32[]{:S(2)}) %copy-start.4) | copy-done | bytes 6291480
  188.1 1.9 copy-done.7
  190.0 1.9 copy-done.9
  191.9 5.5 %pointwise.5.refs_4_ = f32[32,96,1024]{2,1,0:T(8,128)S(1)} custom-call(bf16[16,96,1024]{2,1,0:T(8,128)(2,1)S(1)} %copy-done.9, bf16[16,96,1024]{2,1,0:T(8,128)(2,1)S(1)} %copy-done.7, bf16[32,96,1024]{2,1,0:T(8,128)(2,1)S(1)} %bitcast.36, bf16[512,512]{1,0:T(8,128)(2,1)S(1)} %convolution_select_fusion.refs_2_.refs_3_, ...), custom_call_target="tpu_custom_call" | custom-call | flops 3221225472 | bytes 25165824 | tf_op jit(solution)/shard_map/pointwise/pallas_call | solution.py:337
  197.4 7.1 %last.2 = (f32[32,96,1024]{2,1,0:T(8,128)}, f32[4,96,1024]{2,1,0:T(8,128)S(1)}) custom-call(bf16[8,96,128]{2,1,0:T(8,128)(2,1)S(1)} %get-tuple-element.143.refs_0_, bf16[8,96,128]{2,1,0:T(8,128)(2,1)S(1)} %collective-permute-done.45.refs_1_, bf16[8,96,128]{2,1,0:T(8,128)(2,1)S(1)} %collective-permute-done.46.refs_2_, ...), custom_call_target="tpu_custom_call" | custom-call | flops 805306368 | bytes 12582912 | tf_op jit(solution)/shard_map/last/pallas_call | solution.py:374
  204.5 7.3 %last.3 = (f32[32,96,1024]{2,1,0:T(8,128)}, f32[4,96,1024]{2,1,0:T(8,128)S(1)}) custom-call(bf16[8,96,128]{2,1,0:T(8,128)(2,1)S(1)} %get-tuple-element.136.refs_0_, bf16[8,96,128]{2,1,0:T(8,128)(2,1)S(1)} %collective-permute-done.41.refs_1_, bf16[8,96,128]{2,1,0:T(8,128)(2,1)S(1)} %collective-permute-done.42.refs_2_, ...), custom_call_target="tpu_custom_call", output_to_operand_aliasing={{0}: (7, {})} | custom-call | flops 805306368 | bytes 12582912 | tf_op jit(solution)/shard_map/last/pallas_call | solution.py:374
  211.9 1.5 slice_bitcast_fusion
  213.4 12.3 %collective-permute-start.48 = (f32[96,1024]{1,0:T(8,128)S(1)}, f32[96,1024]{1,0:T(8,128)S(1)}, u32[]{:S(2)}, u32[]{:S(2)}) collective-permute-start(f32[96,1024]{1,0:T(8,128)S(1)} %get-tuple-element.158), channel_id=1, source_target_pairs={{0,8},{8,0},{16,24},{24,16},{1,9},{9,1},{17,25},{25,17},{2,10},{10... | collective-permute-start | bytes 1179656 | tf_op jit(solution)/shard_map/ppermute | solution.py:429
  225.7 1.3 collective-permute-done.48
  227.1 3.8 %collective-permute-start.49 = (f32[48,1024]{1,0:T(8,128)S(1)}, f32[48,1024]{1,0:T(8,128)S(1)}, u32[]{:S(2)}, u32[]{:S(2)}) collective-permute-start(f32[48,1024]{1,0:T(8,128)S(1)} %dynamic-slice_add_fusion), channel_id=1, source_target_pairs={{0,16},{8,24},{1,17},{9,25},{2,18},{10,26},{3,19},{11,27},{4,20},{... | collective-permute-start | bytes 589832 | tf_op jit(solution)/shard_map/ppermute | solution.py:421
  231.0 1.9 collective-permute-start.51
  232.9 1.9 collective-permute-done.49
  234.8 2.1 collective-permute-start.50
  238.1 2.6 %collective-permute-start.53 = (f32[2,1,1024]{2,1,0:T(1,128)S(1)}, f32[2,1,1024]{2,1,0:T(1,128)S(1)}, u32[]{:S(2)}, u32[]{:S(2)}) collective-permute-start(f32[2,1,1024]{2,1,0:T(1,128)S(1)} %pad_maximum_fusion.1), channel_id=1, source_target_pairs={{1,0},{2,1},{3,2},{4,3},{5,4},{6,5},{7,6},{0,7},{9,8},{10,9},{11,1... | collective-permute-start | bytes 24584 | tf_op jit(solution)/shard_map/ppermute | solution.py:451
  241.4 4.5 %collective-permute-done.52.before_ref = f32[2,1,1024]{2,1,0:T(1,128)S(1)} collective-permute-done((f32[2,1,1024]{2,1,0:T(1,128)S(1)}, f32[2,1,1024]{2,1,0:T(1,128)S(1)}, u32[]{:S(2)}, u32[]{:S(2)}) %collective-permute-start.52) | collective-permute-done | bytes 8224 | tf_op jit(solution)/shard_map/ppermute | solution.py:450
  245.9 1.6 residual.1
  (141 shorter events, 28.9 us)
Async XLA Ops:
  0.6 47.2 %copy-start = (bf16[32,32]{1,0:T(8,128)(2,1)S(1)}, bf16[32,32]{1,0:T(8,128)(2,1)}, u32[]{:S(2)}) copy-start(bf16[32,32]{1,0:T(8,128)(2,1)} %param.14) | copy-start | bytes 6148
  9.2 9.9 %collective-permute-start.3 = (bf16[8,96,128]{2,1,0:T(8,128)(2,1)S(1)}, bf16[8,96,128]{2,1,0:T(8,128)(2,1)S(1)}, u32[]{:S(2)}, u32[]{:S(2)}) collective-permute-start(bf16[8,96,128]{2,1,0:T(8,128)(2,1)S(1)} %get-tuple-element.83), channel_id=1, source_target_pairs={{0,1},{1,0},{2,3},{3,2},{4,5},{5,4},{6,7},{7,6},{8,9},{9,8},{10,11... | collective-permute-start | bytes 589832 | tf_op jit(solution)/shard_map/ppermute | solution.py:257
  11.2 8.9 %collective-permute-start.4 = (bf16[8,96,128]{2,1,0:T(8,128)(2,1)}, bf16[8,96,128]{2,1,0:T(8,128)(2,1)S(1)}, u32[]{:S(2)}, u32[]{:S(2)}) collective-permute-start(bf16[8,96,128]{2,1,0:T(8,128)(2,1)} %get-tuple-element.84), channel_id=1, source_target_pairs={{0,2},{1,3},{2,0},{3,1},{4,6},{5,7},{6,4},{7,5},{8,10},{9,11},{10,... | collective-permute-start | bytes 589832 | tf_op jit(solution)/shard_map/ppermute | solution.py:257
  12.5 21.2 %copy-start.12 = (f32[32]{0:T(128)S(1)}, f32[32]{0:T(128)}, u32[]{:S(2)}) copy-start(f32[32]{0:T(128)} %param.15) | copy-start | bytes 388
  12.5 8.7 %collective-permute-start.5 = (bf16[8,96,128]{2,1,0:T(8,128)(2,1)S(1)}, bf16[8,96,128]{2,1,0:T(8,128)(2,1)S(1)}, u32[]{:S(2)}, u32[]{:S(2)}) collective-permute-start(bf16[8,96,128]{2,1,0:T(8,128)(2,1)S(1)} %get-tuple-element.85), channel_id=1, source_target_pairs={{0,3},{1,2},{2,1},{3,0},{4,7},{5,6},{6,5},{7,4},{8,11},{9,10},{10,... | collective-permute-start | bytes 589832 | tf_op jit(solution)/shard_map/ppermute | solution.py:257
  13.9 10.9 %collective-permute-start = (bf16[8,96,128]{2,1,0:T(8,128)(2,1)S(1)}, bf16[8,96,128]{2,1,0:T(8,128)(2,1)S(1)}, u32[]{:S(2)}, u32[]{:S(2)}) collective-permute-start(bf16[8,96,128]{2,1,0:T(8,128)(2,1)S(1)} %get-tuple-element.78), channel_id=1, source_target_pairs={{0,1},{1,0},{2,3},{3,2},{4,5},{5,4},{6,7},{7,6},{8,9},{9,8},{10,11... | collective-permute-start | bytes 589832 | tf_op jit(solution)/shard_map/ppermute | solution.py:257
  15.3 10.1 %collective-permute-start.1 = (bf16[8,96,128]{2,1,0:T(8,128)(2,1)S(1)}, bf16[8,96,128]{2,1,0:T(8,128)(2,1)S(1)}, u32[]{:S(2)}, u32[]{:S(2)}) collective-permute-start(bf16[8,96,128]{2,1,0:T(8,128)(2,1)S(1)} %get-tuple-element.79), channel_id=1, source_target_pairs={{0,2},{1,3},{2,0},{3,1},{4,6},{5,7},{6,4},{7,5},{8,10},{9,11},{10,... | collective-permute-start | bytes 589832 | tf_op jit(solution)/shard_map/ppermute | solution.py:257
  19.1 12.8 %collective-permute-start.2 = (bf16[8,96,128]{2,1,0:T(8,128)(2,1)S(1)}, bf16[8,96,128]{2,1,0:T(8,128)(2,1)S(1)}, u32[]{:S(2)}, u32[]{:S(2)}) collective-permute-start(bf16[8,96,128]{2,1,0:T(8,128)(2,1)S(1)} %get-tuple-element.80), channel_id=1, source_target_pairs={{0,3},{1,2},{2,1},{3,0},{4,7},{5,6},{6,5},{7,4},{8,11},{9,10},{10,... | collective-permute-start | bytes 589832 | tf_op jit(solution)/shard_map/ppermute | solution.py:257
  22.6 11.4 %collective-permute-start.7 = (bf16[16,16,256]{2,1,0:T(8,128)(2,1)}, bf16[16,16,256]{2,1,0:T(8,128)(2,1)S(1)}, u32[]{:S(2)}, u32[]{:S(2)}) collective-permute-start(bf16[16,16,256]{2,1,0:T(8,128)(2,1)} %get-tuple-element.88), channel_id=1, source_target_pairs={{0,4},{1,5},{2,6},{3,7},{4,0},{5,1},{6,2},{7,3},{8,12},{9,13},{10,... | collective-permute-start | bytes 393224 | tf_op jit(solution)/shard_map/ppermute | solution.py:257
  32.6 8.1 %collective-permute-start.6 = (bf16[16,16,256]{2,1,0:T(8,128)(2,1)S(1)}, bf16[16,16,256]{2,1,0:T(8,128)(2,1)S(1)}, u32[]{:S(2)}, u32[]{:S(2)}) collective-permute-start(bf16[16,16,256]{2,1,0:T(8,128)(2,1)S(1)} %get-tuple-element.87), channel_id=1, source_target_pairs={{0,4},{1,5},{2,6},{3,7},{4,0},{5,1},{6,2},{7,3},{8,12},{9,13},{10,... | collective-permute-start | bytes 393224 | tf_op jit(solution)/shard_map/ppermute | solution.py:257
  47.7 8.2 %collective-permute-start.15 = (bf16[16,16,256]{2,1,0:T(8,128)(2,1)S(1)}, bf16[16,16,256]{2,1,0:T(8,128)(2,1)S(1)}, u32[]{:S(2)}, u32[]{:S(2)}) collective-permute-start(bf16[16,16,256]{2,1,0:T(8,128)(2,1)S(1)} %get-tuple-element.99.mine_ref), channel_id=1, source_target_pairs={{0,4},{1,5},{2,6},{3,7},{4,0},{5,1},{6,2},{7,3},{8,12},{9,13},{10,... | collective-permute-start | bytes 393224 | tf_op jit(solution)/shard_map/ppermute | solution.py:257
  48.6 22.1 %collective-permute-start.8 = (bf16[16,16,256]{2,1,0:T(8,128)(2,1)S(1)}, bf16[16,16,256]{2,1,0:T(8,128)(2,1)S(1)}, u32[]{:S(2)}, u32[]{:S(2)}) collective-permute-start(bf16[16,16,256]{2,1,0:T(8,128)(2,1)S(1)} %get-tuple-element.89.mine_ref), channel_id=1, source_target_pairs={{0,4},{1,5},{2,6},{3,7},{4,0},{5,1},{6,2},{7,3},{8,12},{9,13},{10,... | collective-permute-start | bytes 393224 | tf_op jit(solution)/shard_map/ppermute | solution.py:257
  56.7 17.4 %collective-permute-start.16 = (bf16[8,96,128]{2,1,0:T(8,128)(2,1)S(1)}, bf16[8,96,128]{2,1,0:T(8,128)(2,1)S(1)}, u32[]{:S(2)}, u32[]{:S(2)}) collective-permute-start(bf16[8,96,128]{2,1,0:T(8,128)(2,1)S(1)} %get-tuple-element.101), channel_id=1, source_target_pairs={{0,1},{1,0},{2,3},{3,2},{4,5},{5,4},{6,7},{7,6},{8,9},{9,8},{10,11... | collective-permute-start | bytes 589832 | tf_op jit(solution)/shard_map/ppermute | solution.py:257
  61.2 13.0 %collective-permute-start.17 = (bf16[8,96,128]{2,1,0:T(8,128)(2,1)S(1)}, bf16[8,96,128]{2,1,0:T(8,128)(2,1)S(1)}, u32[]{:S(2)}, u32[]{:S(2)}) collective-permute-start(bf16[8,96,128]{2,1,0:T(8,128)(2,1)S(1)} %get-tuple-element.102), channel_id=1, source_target_pairs={{0,2},{1,3},{2,0},{3,1},{4,6},{5,7},{6,4},{7,5},{8,10},{9,11},{10,... | collective-permute-start | bytes 589832 | tf_op jit(solution)/shard_map/ppermute | solution.py:257
  61.2 13.0 %collective-permute-start.18 = (bf16[8,96,128]{2,1,0:T(8,128)(2,1)S(1)}, bf16[8,96,128]{2,1,0:T(8,128)(2,1)S(1)}, u32[]{:S(2)}, u32[]{:S(2)}) collective-permute-start(bf16[8,96,128]{2,1,0:T(8,128)(2,1)S(1)} %get-tuple-element.103), channel_id=1, source_target_pairs={{0,3},{1,2},{2,1},{3,0},{4,7},{5,6},{6,5},{7,4},{8,11},{9,10},{10,... | collective-permute-start | bytes 589832 | tf_op jit(solution)/shard_map/ppermute | solution.py:257
  71.5 7.5 %collective-permute-start.10 = (bf16[8,96,128]{2,1,0:T(8,128)(2,1)S(1)}, bf16[8,96,128]{2,1,0:T(8,128)(2,1)S(1)}, u32[]{:S(2)}, u32[]{:S(2)}) collective-permute-start(bf16[8,96,128]{2,1,0:T(8,128)(2,1)S(1)} %get-tuple-element.92), channel_id=1, source_target_pairs={{0,2},{1,3},{2,0},{3,1},{4,6},{5,7},{6,4},{7,5},{8,10},{9,11},{10,... | collective-permute-start | bytes 589832 | tf_op jit(solution)/shard_map/ppermute | solution.py:257
  71.8 9.2 %collective-permute-start.11 = (bf16[8,96,128]{2,1,0:T(8,128)(2,1)S(1)}, bf16[8,96,128]{2,1,0:T(8,128)(2,1)S(1)}, u32[]{:S(2)}, u32[]{:S(2)}) collective-permute-start(bf16[8,96,128]{2,1,0:T(8,128)(2,1)S(1)} %get-tuple-element.93), channel_id=1, source_target_pairs={{0,3},{1,2},{2,1},{3,0},{4,7},{5,6},{6,5},{7,4},{8,11},{9,10},{10,... | collective-permute-start | bytes 589832 | tf_op jit(solution)/shard_map/ppermute | solution.py:257
  74.1 7.4 %collective-permute-start.9 = (bf16[8,96,128]{2,1,0:T(8,128)(2,1)S(1)}, bf16[8,96,128]{2,1,0:T(8,128)(2,1)S(1)}, u32[]{:S(2)}, u32[]{:S(2)}) collective-permute-start(bf16[8,96,128]{2,1,0:T(8,128)(2,1)S(1)} %get-tuple-element.91), channel_id=1, source_target_pairs={{0,1},{1,0},{2,3},{3,2},{4,5},{5,4},{6,7},{7,6},{8,9},{9,8},{10,11... | collective-permute-start | bytes 589832 | tf_op jit(solution)/shard_map/ppermute | solution.py:257
  77.4 12.5 %collective-permute-start.19 = (bf16[8,96,128]{2,1,0:T(8,128)(2,1)S(1)}, bf16[8,96,128]{2,1,0:T(8,128)(2,1)S(1)}, u32[]{:S(2)}, u32[]{:S(2)}) collective-permute-start(bf16[8,96,128]{2,1,0:T(8,128)(2,1)S(1)} %get-tuple-element.105), channel_id=1, source_target_pairs={{0,1},{1,0},{2,3},{3,2},{4,5},{5,4},{6,7},{7,6},{8,9},{9,8},{10,11... | collective-permute-start | bytes 589832 | tf_op jit(solution)/shard_map/ppermute | solution.py:257
  78.9 11.1 %collective-permute-start.20 = (bf16[8,96,128]{2,1,0:T(8,128)(2,1)S(1)}, bf16[8,96,128]{2,1,0:T(8,128)(2,1)S(1)}, u32[]{:S(2)}, u32[]{:S(2)}) collective-permute-start(bf16[8,96,128]{2,1,0:T(8,128)(2,1)S(1)} %get-tuple-element.106), channel_id=1, source_target_pairs={{0,2},{1,3},{2,0},{3,1},{4,6},{5,7},{6,4},{7,5},{8,10},{9,11},{10,... | collective-permute-start | bytes 589832 | tf_op jit(solution)/shard_map/ppermute | solution.py:257
  79.0 11.0 %collective-permute-start.21 = (bf16[8,96,128]{2,1,0:T(8,128)(2,1)S(1)}, bf16[8,96,128]{2,1,0:T(8,128)(2,1)S(1)}, u32[]{:S(2)}, u32[]{:S(2)}) collective-permute-start(bf16[8,96,128]{2,1,0:T(8,128)(2,1)S(1)} %get-tuple-element.107), channel_id=1, source_target_pairs={{0,3},{1,2},{2,1},{3,0},{4,7},{5,6},{6,5},{7,4},{8,11},{9,10},{10,... | collective-permute-start | bytes 589832 | tf_op jit(solution)/shard_map/ppermute | solution.py:257
  81.5 26.8 %slice-start.2 = ((s8[8388608]{0:T(1024)(128)(4,1)}), s8[4194304]{0:T(1024)(128)(4,1)S(1)}, s32[]{:S(2)}) async-start(s8[8388608]{0:T(1024)(128)(4,1)} %bitcast.37), calls=%async_computation.2 | async-start | bytes 8388608
  81.5 26.8 %slice-start.3 = ((s8[8388608]{0:T(1024)(128)(4,1)}), s8[4194304]{0:T(1024)(128)(4,1)S(1)}, s32[]{:S(2)}) async-start(s8[8388608]{0:T(1024)(128)(4,1)} %bitcast.37), calls=%async_computation.3 | async-start | bytes 8388608
  84.7 13.1 %collective-permute-start.12 = (bf16[8,96,128]{2,1,0:T(8,128)(2,1)S(1)}, bf16[8,96,128]{2,1,0:T(8,128)(2,1)S(1)}, u32[]{:S(2)}, u32[]{:S(2)}) collective-permute-start(bf16[8,96,128]{2,1,0:T(8,128)(2,1)S(1)} %get-tuple-element.95), channel_id=1, source_target_pairs={{0,1},{1,0},{2,3},{3,2},{4,5},{5,4},{6,7},{7,6},{8,9},{9,8},{10,11... | collective-permute-start | bytes 589832 | tf_op jit(solution)/shard_map/ppermute | solution.py:257
  84.8 13.0 %collective-permute-start.13 = (bf16[8,96,128]{2,1,0:T(8,128)(2,1)S(1)}, bf16[8,96,128]{2,1,0:T(8,128)(2,1)S(1)}, u32[]{:S(2)}, u32[]{:S(2)}) collective-permute-start(bf16[8,96,128]{2,1,0:T(8,128)(2,1)S(1)} %get-tuple-element.96), channel_id=1, source_target_pairs={{0,2},{1,3},{2,0},{3,1},{4,6},{5,7},{6,4},{7,5},{8,10},{9,11},{10,... | collective-permute-start | bytes 589832 | tf_op jit(solution)/shard_map/ppermute | solution.py:257
  89.9 8.7 %collective-permute-start.14 = (bf16[8,96,128]{2,1,0:T(8,128)(2,1)S(1)}, bf16[8,96,128]{2,1,0:T(8,128)(2,1)S(1)}, u32[]{:S(2)}, u32[]{:S(2)}) collective-permute-start(bf16[8,96,128]{2,1,0:T(8,128)(2,1)S(1)} %get-tuple-element.97), channel_id=1, source_target_pairs={{0,3},{1,2},{2,1},{3,0},{4,7},{5,6},{6,5},{7,4},{8,11},{9,10},{10,... | collective-permute-start | bytes 589832 | tf_op jit(solution)/shard_map/ppermute | solution.py:257
  90.7 9.8 %collective-permute-start.23 = (bf16[16,16,256]{2,1,0:T(8,128)(2,1)S(1)}, bf16[16,16,256]{2,1,0:T(8,128)(2,1)S(1)}, u32[]{:S(2)}, u32[]{:S(2)}) collective-permute-start(bf16[16,16,256]{2,1,0:T(8,128)(2,1)S(1)} %get-tuple-element.110), channel_id=1, source_target_pairs={{0,4},{1,5},{2,6},{3,7},{4,0},{5,1},{6,2},{7,3},{8,12},{9,13},{10,... | collective-permute-start | bytes 393224 | tf_op jit(solution)/shard_map/ppermute | solution.py:257
  98.6 29.7 %slice-start = ((s8[6291456]{0:T(1024)(128)(4,1)}), s8[4194304]{0:T(1024)(128)(4,1)S(1)}, s32[]{:S(2)}) async-start(s8[6291456]{0:T(1024)(128)(4,1)} %bitcast.33), calls=%async_computation | async-start | bytes 8388608
  99.3 8.9 %collective-permute-start.22 = (bf16[16,16,256]{2,1,0:T(8,128)(2,1)S(1)}, bf16[16,16,256]{2,1,0:T(8,128)(2,1)S(1)}, u32[]{:S(2)}, u32[]{:S(2)}) collective-permute-start(bf16[16,16,256]{2,1,0:T(8,128)(2,1)S(1)} %get-tuple-element.109), channel_id=1, source_target_pairs={{0,4},{1,5},{2,6},{3,7},{4,0},{5,1},{6,2},{7,3},{8,12},{9,13},{10,... | collective-permute-start | bytes 393224 | tf_op jit(solution)/shard_map/ppermute | solution.py:257
  108.3 20.0 %slice-start.1 = ((s8[6291456]{0:T(1024)(128)(4,1)}), s8[2097152]{0:T(1024)(128)(4,1)S(1)}, s32[]{:S(2)}) async-start(s8[6291456]{0:T(1024)(128)(4,1)} %bitcast.33), calls=%async_computation.1 | async-start | bytes 4194304
  112.0 5.7 %collective-permute-start.31 = (bf16[16,16,256]{2,1,0:T(8,128)(2,1)S(1)}, bf16[16,16,256]{2,1,0:T(8,128)(2,1)S(1)}, u32[]{:S(2)}, u32[]{:S(2)}) collective-permute-start(bf16[16,16,256]{2,1,0:T(8,128)(2,1)S(1)} %get-tuple-element.123.mine_ref), channel_id=1, source_target_pairs={{0,4},{1,5},{2,6},{3,7},{4,0},{5,1},{6,2},{7,3},{8,12},{9,13},{10,... | collective-permute-start | bytes 393224 | tf_op jit(solution)/shard_map/ppermute | solution.py:257
  118.5 7.6 %collective-permute-start.32 = (bf16[8,96,128]{2,1,0:T(8,128)(2,1)S(1)}, bf16[8,96,128]{2,1,0:T(8,128)(2,1)S(1)}, u32[]{:S(2)}, u32[]{:S(2)}) collective-permute-start(bf16[8,96,128]{2,1,0:T(8,128)(2,1)S(1)} %get-tuple-element.125), channel_id=1, source_target_pairs={{0,1},{1,0},{2,3},{3,2},{4,5},{5,4},{6,7},{7,6},{8,9},{9,8},{10,11... | collective-permute-start | bytes 589832 | tf_op jit(solution)/shard_map/ppermute | solution.py:257
  118.6 6.3 %collective-permute-start.24 = (bf16[16,16,256]{2,1,0:T(8,128)(2,1)S(1)}, bf16[16,16,256]{2,1,0:T(8,128)(2,1)S(1)}, u32[]{:S(2)}, u32[]{:S(2)}) collective-permute-start(bf16[16,16,256]{2,1,0:T(8,128)(2,1)S(1)} %get-tuple-element.111.mine_ref), channel_id=1, source_target_pairs={{0,4},{1,5},{2,6},{3,7},{4,0},{5,1},{6,2},{7,3},{8,12},{9,13},{10,... | collective-permute-start | bytes 393224 | tf_op jit(solution)/shard_map/ppermute | solution.py:257
  118.6 15.2 %collective-permute-start.33 = (bf16[8,96,128]{2,1,0:T(8,128)(2,1)S(1)}, bf16[8,96,128]{2,1,0:T(8,128)(2,1)S(1)}, u32[]{:S(2)}, u32[]{:S(2)}) collective-permute-start(bf16[8,96,128]{2,1,0:T(8,128)(2,1)S(1)} %get-tuple-element.126), channel_id=1, source_target_pairs={{0,2},{1,3},{2,0},{3,1},{4,6},{5,7},{6,4},{7,5},{8,10},{9,11},{10,... | collective-permute-start | bytes 589832 | tf_op jit(solution)/shard_map/ppermute | solution.py:257
  120.3 13.5 %collective-permute-start.34 = (bf16[8,96,128]{2,1,0:T(8,128)(2,1)S(1)}, bf16[8,96,128]{2,1,0:T(8,128)(2,1)S(1)}, u32[]{:S(2)}, u32[]{:S(2)}) collective-permute-start(bf16[8,96,128]{2,1,0:T(8,128)(2,1)S(1)} %get-tuple-element.127), channel_id=1, source_target_pairs={{0,3},{1,2},{2,1},{3,0},{4,7},{5,6},{6,5},{7,4},{8,11},{9,10},{10,... | collective-permute-start | bytes 589832 | tf_op jit(solution)/shard_map/ppermute | solution.py:257
  125.6 13.5 %collective-permute-start.25 = (bf16[8,96,128]{2,1,0:T(8,128)(2,1)S(1)}, bf16[8,96,128]{2,1,0:T(8,128)(2,1)S(1)}, u32[]{:S(2)}, u32[]{:S(2)}) collective-permute-start(bf16[8,96,128]{2,1,0:T(8,128)(2,1)S(1)} %get-tuple-element.113), channel_id=1, source_target_pairs={{0,1},{1,0},{2,3},{3,2},{4,5},{5,4},{6,7},{7,6},{8,9},{9,8},{10,11... | collective-permute-start | bytes 589832 | tf_op jit(solution)/shard_map/ppermute | solution.py:257
  126.1 15.3 %collective-permute-start.26 = (bf16[8,96,128]{2,1,0:T(8,128)(2,1)S(1)}, bf16[8,96,128]{2,1,0:T(8,128)(2,1)S(1)}, u32[]{:S(2)}, u32[]{:S(2)}) collective-permute-start(bf16[8,96,128]{2,1,0:T(8,128)(2,1)S(1)} %get-tuple-element.114), channel_id=1, source_target_pairs={{0,2},{1,3},{2,0},{3,1},{4,6},{5,7},{6,4},{7,5},{8,10},{9,11},{10,... | collective-permute-start | bytes 589832 | tf_op jit(solution)/shard_map/ppermute | solution.py:257
  126.1 15.3 %collective-permute-start.27 = (bf16[8,96,128]{2,1,0:T(8,128)(2,1)S(1)}, bf16[8,96,128]{2,1,0:T(8,128)(2,1)S(1)}, u32[]{:S(2)}, u32[]{:S(2)}) collective-permute-start(bf16[8,96,128]{2,1,0:T(8,128)(2,1)S(1)} %get-tuple-element.115), channel_id=1, source_target_pairs={{0,3},{1,2},{2,1},{3,0},{4,7},{5,6},{6,5},{7,4},{8,11},{9,10},{10,... | collective-permute-start | bytes 589832 | tf_op jit(solution)/shard_map/ppermute | solution.py:257
  138.7 6.6 %collective-permute-start.35 = (bf16[8,96,128]{2,1,0:T(8,128)(2,1)S(1)}, bf16[8,96,128]{2,1,0:T(8,128)(2,1)S(1)}, u32[]{:S(2)}, u32[]{:S(2)}) collective-permute-start(bf16[8,96,128]{2,1,0:T(8,128)(2,1)S(1)} %get-tuple-element.129), channel_id=1, source_target_pairs={{0,1},{1,0},{2,3},{3,2},{4,5},{5,4},{6,7},{7,6},{8,9},{9,8},{10,11... | collective-permute-start | bytes 589832 | tf_op jit(solution)/shard_map/ppermute | solution.py:257
  139.1 8.2 %collective-permute-start.36 = (bf16[8,96,128]{2,1,0:T(8,128)(2,1)S(1)}, bf16[8,96,128]{2,1,0:T(8,128)(2,1)S(1)}, u32[]{:S(2)}, u32[]{:S(2)}) collective-permute-start(bf16[8,96,128]{2,1,0:T(8,128)(2,1)S(1)} %get-tuple-element.130), channel_id=1, source_target_pairs={{0,2},{1,3},{2,0},{3,1},{4,6},{5,7},{6,4},{7,5},{8,10},{9,11},{10,... | collective-permute-start | bytes 589832 | tf_op jit(solution)/shard_map/ppermute | solution.py:257
  139.1 8.6 %collective-permute-start.37 = (bf16[8,96,128]{2,1,0:T(8,128)(2,1)S(1)}, bf16[8,96,128]{2,1,0:T(8,128)(2,1)S(1)}, u32[]{:S(2)}, u32[]{:S(2)}) collective-permute-start(bf16[8,96,128]{2,1,0:T(8,128)(2,1)S(1)} %get-tuple-element.131), channel_id=1, source_target_pairs={{0,3},{1,2},{2,1},{3,0},{4,7},{5,6},{6,5},{7,4},{8,11},{9,10},{10,... | collective-permute-start | bytes 589832 | tf_op jit(solution)/shard_map/ppermute | solution.py:257
  144.5 21.3 %copy-start.8 = (bf16[16,96,1024]{2,1,0:T(8,128)(2,1)}, bf16[16,96,1024]{2,1,0:T(8,128)(2,1)S(1)}, u32[]{:S(2)}) copy-start(bf16[16,96,1024]{2,1,0:T(8,128)(2,1)S(1)} %get-tuple-element.140.refs_0_) | copy-start | bytes 9437188
  144.5 5.6 %collective-permute-start.28 = (bf16[8,96,128]{2,1,0:T(8,128)(2,1)S(1)}, bf16[8,96,128]{2,1,0:T(8,128)(2,1)S(1)}, u32[]{:S(2)}, u32[]{:S(2)}) collective-permute-start(bf16[8,96,128]{2,1,0:T(8,128)(2,1)S(1)} %get-tuple-element.119), channel_id=1, source_target_pairs={{0,1},{1,0},{2,3},{3,2},{4,5},{5,4},{6,7},{7,6},{8,9},{9,8},{10,11... | collective-permute-start | bytes 589832 | tf_op jit(solution)/shard_map/ppermute | solution.py:257
  145.0 5.2 %collective-permute-start.29 = (bf16[8,96,128]{2,1,0:T(8,128)(2,1)S(1)}, bf16[8,96,128]{2,1,0:T(8,128)(2,1)S(1)}, u32[]{:S(2)}, u32[]{:S(2)}) collective-permute-start(bf16[8,96,128]{2,1,0:T(8,128)(2,1)S(1)} %get-tuple-element.120), channel_id=1, source_target_pairs={{0,2},{1,3},{2,0},{3,1},{4,6},{5,7},{6,4},{7,5},{8,10},{9,11},{10,... | collective-permute-start | bytes 589832 | tf_op jit(solution)/shard_map/ppermute | solution.py:257
  145.3 10.0 %collective-permute-start.30 = (bf16[8,96,128]{2,1,0:T(8,128)(2,1)S(1)}, bf16[8,96,128]{2,1,0:T(8,128)(2,1)S(1)}, u32[]{:S(2)}, u32[]{:S(2)}) collective-permute-start(bf16[8,96,128]{2,1,0:T(8,128)(2,1)S(1)} %get-tuple-element.121), channel_id=1, source_target_pairs={{0,3},{1,2},{2,1},{3,0},{4,7},{5,6},{6,5},{7,4},{8,11},{9,10},{10,... | collective-permute-start | bytes 589832 | tf_op jit(solution)/shard_map/ppermute | solution.py:257
  148.4 7.7 %collective-permute-start.39 = (bf16[16,16,256]{2,1,0:T(8,128)(2,1)S(1)}, bf16[16,16,256]{2,1,0:T(8,128)(2,1)S(1)}, u32[]{:S(2)}, u32[]{:S(2)}) collective-permute-start(bf16[16,16,256]{2,1,0:T(8,128)(2,1)S(1)} %get-tuple-element.134), channel_id=1, source_target_pairs={{0,4},{1,5},{2,6},{3,7},{4,0},{5,1},{6,2},{7,3},{8,12},{9,13},{10,... | collective-permute-start | bytes 393224 | tf_op jit(solution)/shard_map/ppermute | solution.py:257
  156.0 6.2 %collective-permute-start.38 = (bf16[16,16,256]{2,1,0:T(8,128)(2,1)S(1)}, bf16[16,16,256]{2,1,0:T(8,128)(2,1)S(1)}, u32[]{:S(2)}, u32[]{:S(2)}) collective-permute-start(bf16[16,16,256]{2,1,0:T(8,128)(2,1)S(1)} %get-tuple-element.133), channel_id=1, source_target_pairs={{0,4},{1,5},{2,6},{3,7},{4,0},{5,1},{6,2},{7,3},{8,12},{9,13},{10,... | collective-permute-start | bytes 393224 | tf_op jit(solution)/shard_map/ppermute | solution.py:257
  162.2 13.3 %copy-start.13 = (f32[4]{0:T(128)S(1)}, f32[4]{0:T(128)}, u32[]{:S(2)}) copy-start(f32[4]{0:T(128)} %param.18) | copy-start | bytes 52
  165.9 8.6 %collective-permute-start.44 = (bf16[16,16,256]{2,1,0:T(8,128)(2,1)S(1)}, bf16[16,16,256]{2,1,0:T(8,128)(2,1)S(1)}, u32[]{:S(2)}, u32[]{:S(2)}) collective-permute-start(bf16[16,16,256]{2,1,0:T(8,128)(2,1)S(1)} %get-tuple-element.142.mine_ref), channel_id=1, source_target_pairs={{0,4},{1,5},{2,6},{3,7},{4,0},{5,1},{6,2},{7,3},{8,12},{9,13},{10,... | collective-permute-start | bytes 393224 | tf_op jit(solution)/shard_map/ppermute | solution.py:257
  175.3 8.6 %collective-permute-start.45 = (bf16[8,96,128]{2,1,0:T(8,128)(2,1)S(1)}, bf16[8,96,128]{2,1,0:T(8,128)(2,1)S(1)}, u32[]{:S(2)}, u32[]{:S(2)}) collective-permute-start(bf16[8,96,128]{2,1,0:T(8,128)(2,1)S(1)} %get-tuple-element.144), channel_id=1, source_target_pairs={{0,1},{1,0},{2,3},{3,2},{4,5},{5,4},{6,7},{7,6},{8,9},{9,8},{10,11... | collective-permute-start | bytes 589832 | tf_op jit(solution)/shard_map/ppermute | solution.py:257
  175.4 6.5 %collective-permute-start.40 = (bf16[16,16,256]{2,1,0:T(8,128)(2,1)S(1)}, bf16[16,16,256]{2,1,0:T(8,128)(2,1)S(1)}, u32[]{:S(2)}, u32[]{:S(2)}) collective-permute-start(bf16[16,16,256]{2,1,0:T(8,128)(2,1)S(1)} %get-tuple-element.135.mine_ref), channel_id=1, source_target_pairs={{0,4},{1,5},{2,6},{3,7},{4,0},{5,1},{6,2},{7,3},{8,12},{9,13},{10,... | collective-permute-start | bytes 393224 | tf_op jit(solution)/shard_map/ppermute | solution.py:257
  176.1 21.2 %collective-permute-start.46 = (bf16[8,96,128]{2,1,0:T(8,128)(2,1)S(1)}, bf16[8,96,128]{2,1,0:T(8,128)(2,1)S(1)}, u32[]{:S(2)}, u32[]{:S(2)}) collective-permute-start(bf16[8,96,128]{2,1,0:T(8,128)(2,1)S(1)} %get-tuple-element.145), channel_id=1, source_target_pairs={{0,2},{1,3},{2,0},{3,1},{4,6},{5,7},{6,4},{7,5},{8,10},{9,11},{10,... | collective-permute-start | bytes 589832 | tf_op jit(solution)/shard_map/ppermute | solution.py:257
  178.8 18.6 %collective-permute-start.47 = (bf16[8,96,128]{2,1,0:T(8,128)(2,1)S(1)}, bf16[8,96,128]{2,1,0:T(8,128)(2,1)S(1)}, u32[]{:S(2)}, u32[]{:S(2)}) collective-permute-start(bf16[8,96,128]{2,1,0:T(8,128)(2,1)S(1)} %get-tuple-element.146), channel_id=1, source_target_pairs={{0,3},{1,2},{2,1},{3,0},{4,7},{5,6},{6,5},{7,4},{8,11},{9,10},{10,... | collective-permute-start | bytes 589832 | tf_op jit(solution)/shard_map/ppermute | solution.py:257
  182.6 21.9 %collective-permute-start.41 = (bf16[8,96,128]{2,1,0:T(8,128)(2,1)S(1)}, bf16[8,96,128]{2,1,0:T(8,128)(2,1)S(1)}, u32[]{:S(2)}, u32[]{:S(2)}) collective-permute-start(bf16[8,96,128]{2,1,0:T(8,128)(2,1)S(1)} %get-tuple-element.137), channel_id=1, source_target_pairs={{0,1},{1,0},{2,3},{3,2},{4,5},{5,4},{6,7},{7,6},{8,9},{9,8},{10,11... | collective-permute-start | bytes 589832 | tf_op jit(solution)/shard_map/ppermute | solution.py:257
  183.5 21.0 %collective-permute-start.42 = (bf16[8,96,128]{2,1,0:T(8,128)(2,1)S(1)}, bf16[8,96,128]{2,1,0:T(8,128)(2,1)S(1)}, u32[]{:S(2)}, u32[]{:S(2)}) collective-permute-start(bf16[8,96,128]{2,1,0:T(8,128)(2,1)S(1)} %get-tuple-element.138), channel_id=1, source_target_pairs={{0,2},{1,3},{2,0},{3,1},{4,6},{5,7},{6,4},{7,5},{8,10},{9,11},{10,... | collective-permute-start | bytes 589832 | tf_op jit(solution)/shard_map/ppermute | solution.py:257
  183.9 20.7 %collective-permute-start.43 = (bf16[8,96,128]{2,1,0:T(8,128)(2,1)S(1)}, bf16[8,96,128]{2,1,0:T(8,128)(2,1)S(1)}, u32[]{:S(2)}, u32[]{:S(2)}) collective-permute-start(bf16[8,96,128]{2,1,0:T(8,128)(2,1)S(1)} %get-tuple-element.139), channel_id=1, source_target_pairs={{0,3},{1,2},{2,1},{3,0},{4,7},{5,6},{6,5},{7,4},{8,11},{9,10},{10,... | collective-permute-start | bytes 589832 | tf_op jit(solution)/shard_map/ppermute | solution.py:257
  211.9 28.8 %copy-start.11 = (f32[96]{0:T(128)S(1)}, f32[96]{0:T(128)}, u32[]{:S(2)}) copy-start(f32[96]{0:T(128)} %param.17) | copy-start | bytes 1156
  211.9 35.6 %copy-start.1 = (bf16[32,32]{1,0:T(8,128)(2,1)S(1)}, bf16[32,32]{1,0:T(8,128)(2,1)}, u32[]{:S(2)}) copy-start(bf16[32,32]{1,0:T(8,128)(2,1)} %param.14) | copy-start | bytes 6148
  213.4 13.7 %collective-permute-start.48 = (f32[96,1024]{1,0:T(8,128)S(1)}, f32[96,1024]{1,0:T(8,128)S(1)}, u32[]{:S(2)}, u32[]{:S(2)}) collective-permute-start(f32[96,1024]{1,0:T(8,128)S(1)} %get-tuple-element.158), channel_id=1, source_target_pairs={{0,8},{8,0},{16,24},{24,16},{1,9},{9,1},{17,25},{25,17},{2,10},{10... | collective-permute-start | bytes 1179656 | tf_op jit(solution)/shard_map/ppermute | solution.py:429
  227.1 7.7 %collective-permute-start.49 = (f32[48,1024]{1,0:T(8,128)S(1)}, f32[48,1024]{1,0:T(8,128)S(1)}, u32[]{:S(2)}, u32[]{:S(2)}) collective-permute-start(f32[48,1024]{1,0:T(8,128)S(1)} %dynamic-slice_add_fusion), channel_id=1, source_target_pairs={{0,16},{8,24},{1,17},{9,25},{2,18},{10,26},{3,19},{11,27},{4,20},{... | collective-permute-start | bytes 589832 | tf_op jit(solution)/shard_map/ppermute | solution.py:421
  231.0 9.9 %collective-permute-start.51 = (f32[96,1024]{1,0:T(8,128)}, f32[96,1024]{1,0:T(8,128)S(1)}, u32[]{:S(2)}, u32[]{:S(2)}) collective-permute-start(f32[96,1024]{1,0:T(8,128)} %get-tuple-element.157), channel_id=1, source_target_pairs={{0,8},{8,16},{16,24},{1,9},{9,17},{17,25},{2,10},{10,18},{18,26},{... | collective-permute-start | bytes 1179656 | tf_op jit(solution)/shard_map/ppermute | solution.py:421
  234.8 3.1 %collective-permute-start.50 = (f32[48,1024]{1,0:T(8,128)S(1)}, f32[48,1024]{1,0:T(8,128)S(1)}, u32[]{:S(2)}, u32[]{:S(2)}) collective-permute-start(f32[48,1024]{1,0:T(8,128)S(1)} %collective-permute-done.49), channel_id=1, source_target_pairs={{0,8},{8,0},{16,24},{24,16},{1,9},{9,1},{17,25},{25,17},{2,10},{10... | collective-permute-start | bytes 589832 | tf_op jit(solution)/shard_map/ppermute | solution.py:436
  238.1 3.4 %collective-permute-start.53 = (f32[2,1,1024]{2,1,0:T(1,128)S(1)}, f32[2,1,1024]{2,1,0:T(1,128)S(1)}, u32[]{:S(2)}, u32[]{:S(2)}) collective-permute-start(f32[2,1,1024]{2,1,0:T(1,128)S(1)} %pad_maximum_fusion.1), channel_id=1, source_target_pairs={{1,0},{2,1},{3,2},{4,3},{5,4},{6,5},{7,6},{0,7},{9,8},{10,9},{11,1... | collective-permute-start | bytes 24584 | tf_op jit(solution)/shard_map/ppermute | solution.py:451
  240.6 5.3 %collective-permute-start.52 = (f32[2,1,1024]{2,1,0:T(1,128)S(1)}, f32[2,1,1024]{2,1,0:T(1,128)S(1)}, u32[]{:S(2)}, u32[]{:S(2)}) collective-permute-start(f32[2,1,1024]{2,1,0:T(1,128)S(1)} %pad_maximum_fusion), channel_id=1, source_target_pairs={{0,1},{1,2},{2,3},{3,4},{4,5},{5,6},{6,7},{7,0},{8,9},{9,10},{10,1... | collective-permute-start | bytes 24584 | tf_op jit(solution)/shard_map/ppermute | solution.py:450
  (8 other events, 30.4 us)

commit v3 on v2

--- a/solution.py
+++ b/solution.py
@@ -9,6 +9,7 @@
 from jax.experimental.pallas import tpu as pltpu
 from jax.sharding import PartitionSpec as P
 
+
 ITERS = 3
 CHUNKS = 2
 BF = jnp.bfloat16
@@ -38,7 +39,9 @@
         table = table.reshape(2, slices, own, cells).transpose(1, 0, 2, 3)
         return table.reshape(slices, 2 * own, cells).astype(BF)
 
-    return by_slice(pair), by_slice(inverse)
+    order = [d + h * (slices // 2) for d in range(slices // 2) for h in range(2)]
+    first, second = [by_slice(table)[order].reshape(-1, cells) for table in (pair, inverse)]
+    return np.ascontiguousarray(first.T), second
 
 
 def y_table(rows, modes, slices):
@@ -71,8 +74,53 @@
     store_near(state, table_ref[...], near_refs, pack, rows)
 
 
+def slice_order(own, peers, me, across, along):
+    wide = peers * 4 * own
+    block = 2 * own
+    mask = ((me % peers) * 2) | (me // peers)
+    place = lax.broadcasted_iota(jnp.int32, (wide, wide), across)
+    source = ((place // block) ^ mask) * block + place % block
+    return (lax.broadcasted_iota(jnp.int32, (wide, wide), along) == source).astype(BF)
+
+
+def forward_table_kernel(own, peers, me_ref, forward_ref, near_ref):
+    order = slice_order(own, peers, me_ref[0], 1, 0)
+    near_ref[...] = dot(forward_ref[...], order, ((1,), (0,))).astype(BF)
+
+
+def other_tables_kernel(own, peers, me_ref, inverse_ref, row_ref, spread_ref, rows_ref):
+    order = slice_order(own, peers, me_ref[0], 0, 1)
+    spread_ref[...] = dot(order, inverse_ref[...], ((1,), (0,))).astype(BF)
+    rows = row_ref.shape[1]
+    for d in range(peers):
+        rows_ref[d * rows : (d + 1) * rows] = row_ref[me_ref[0] ^ d]
+
+
+def small_kernel(block, weight_ref, bias_ref, decoder_ref, square_ref, column_ref, splat_ref):
+    channels = weight_ref.shape[0]
+    count = channels * block
+    row = lax.broadcasted_iota(jnp.int32, (count, channels), 0) // block
+    mine = row == lax.broadcasted_iota(jnp.int32, (count, channels), 1)
+    pick = mine.astype(BF)
+    left = dot(pick, weight_ref[...], ((1,), (1,))).astype(BF)
+    full = dot(left, pick, ((1,), (1,)))
+    down = lax.broadcasted_iota(jnp.int32, (count, count), 0) % block
+    across = lax.broadcasted_iota(jnp.int32, (count, count), 1) % block
+    square_ref[...] = jnp.where(down == across, full, 0.0).astype(BF)
+    column_ref[...] = jnp.sum(jnp.where(mine, bias_ref[...], 0.0), 1, keepdims=True)
+    fields = decoder_ref.shape[0]
+    lines = channels * fields
+    row = lax.broadcasted_iota(jnp.int32, (lines, channels), 0) // fields
+    pick = (row == lax.broadcasted_iota(jnp.int32, (lines, channels), 1)).astype(BF)
+    values = dot(pick, decoder_ref[...], ((1,), (1,)))
+    row = lax.broadcasted_iota(jnp.int32, (lines, fields), 0) % fields
+    own = row == lax.broadcasted_iota(jnp.int32, (lines, fields), 1)
+    value = jnp.sum(jnp.where(own, values, 0.0), 1, keepdims=True)
+    splat_ref[...] = jnp.broadcast_to(value, splat_ref.shape)
+
+
 def forward_y_kernel(pack, own, peers, *refs):
-    near_refs, table_ref, keep_ref, send_ref = refs[:peers], refs[peers], refs[-2], refs[-1]
+    near_refs, (table_ref, keep_ref, send_ref) = refs[:peers], refs[peers:]
     modes = table_ref.shape[1] // 2
     for g in range(near_refs[0].shape[0]):
         near = jnp.concatenate([ref[g] for ref in near_refs], 0)
@@ -87,40 +135,42 @@
                 out_ref[c, :, modes:] = (imag[:, :modes] - real[:, modes:]).astype(out_ref.dtype)
 
 
-def mix_kernel(chunks, *refs):
-    keep_refs, got_refs = refs[:chunks], refs[chunks : 2 * chunks]
-    weight_ref = refs[2 * chunks]
-    out_refs = refs[2 * chunks + 1 : 3 * chunks + 1]
-    spectrum, mixed = refs[3 * chunks + 1 :]
+def mix_kernel(n, chunks, *refs):
+    keep_ref, got_ref, weight_ref = refs[:3]
+    earlier = refs[3:4] if n > 0 else ()
+    out_refs = refs[3 + len(earlier) : -1]
+    spectrum = refs[-1]
     own, channels, modes = weight_ref.shape[1], weight_ref.shape[2], weight_ref.shape[4]
     size = channels // chunks
-    for n in range(chunks):
-        value = keep_refs[n][...] + got_refs[n][...].astype(F32)
-        spectrum[:, n * size : (n + 1) * size] = jnp.swapaxes(value, 0, 1)
+    value = keep_ref[...] + got_ref[...].astype(F32)
+    spectrum[...] = jnp.swapaxes(value, 0, 1)
+    total = out_refs[0] if n < chunks - 1 else earlier[0]
 
     def step(k, carry):
         row = spectrum[k]
-        real = [jnp.zeros((channels, modes), F32)] * 2
-        imag = [jnp.zeros((channels, modes), F32)] * 2
-        for i in range(channels):
+        zero = jnp.zeros((channels, modes), F32)
+        real, imag = [zero, zero], [zero, zero]
+        if earlier:
+            real[0], imag[0] = earlier[0][k, :, :modes], earlier[0][k, :, modes:]
+        for i in range(size):
             s0, s1 = row[i : i + 1, :modes], row[i : i + 1, modes:]
-            w0 = weight_ref[0, k, i].astype(F32)
-            w1 = weight_ref[1, k, i].astype(F32)
+            w0 = weight_ref[0, k, n * size + i].astype(F32)
+            w1 = weight_ref[1, k, n * size + i].astype(F32)
             real[i % 2] = real[i % 2] + (s0 * w0 - s1 * w1)
             imag[i % 2] = imag[i % 2] + (s0 * w1 + s1 * w0)
-        mixed[k, :, :modes] = real[0] + real[1]
-        mixed[k, :, modes:] = imag[0] + imag[1]
+        total[k, :, :modes] = real[0] + real[1]
+        total[k, :, modes:] = imag[0] + imag[1]
         return carry
 
     lax.fori_loop(0, own, step, 0)
-    for n in range(chunks):
-        value = jnp.swapaxes(mixed[:, n * size : (n + 1) * size], 0, 1)
-        out_refs[n][...] = value.astype(BF)
-
-
-def inverse_y_kernel(pack, own, peers, mine_ref, theirs_ref, table_ref, *back_refs):
-    modes = table_ref.shape[1] // 2
-    rows = table_ref.shape[0] // peers
+    if n == chunks - 1:
+        for c in range(chunks):
+            part = jnp.swapaxes(total[:, c * size : (c + 1) * size], 0, 1)
+            out_refs[c][...] = part.astype(BF)
+
+
+def inverse_y_kernel(pack, peers, mine_ref, theirs_ref, table_ref, *back_refs):
+    rows, modes = table_ref.shape[0] // peers, table_ref.shape[1] // 2
     for g in range(back_refs[0].shape[0]):
         parts = []
         for j in range(pack):
@@ -157,11 +207,12 @@
     store_near(state, forward_ref[...], near_refs, pack, rows)
 
 
-def last_kernel(pack, peers, first, *refs):
+def last_kernel(pack, peers, first, kinds, *refs):
     back_refs = refs[:peers]
-    point_ref, inverse_ref, decoder_ref = refs[peers : peers + 3]
-    earlier = refs[peers + 3 : -2]
-    updated_ref, fields_ref = refs[-2:]
+    me_ref, depth_ref, point_ref, inverse_ref, decoder_ref = refs[peers : peers + 5]
+    updated_ref, *field_refs = refs[-kinds - 3 : -2]
+    earlier = refs[peers + 5 : -kinds - 3]
+    low_ref, high_ref = refs[-2:]
     count, rows, cells = updated_ref.shape
     group = pl.program_id(0)
     point = point_ref[...].reshape(count * rows, cells)
@@ -170,19 +221,47 @@
 
     @pl.when(group == 0)
     def _():
-        fields_ref[...] = earlier[1][...] if earlier else jnp.zeros_like(fields_ref)
+        for f in range(kinds):
+            field_refs[f][...] = (
+                earlier[1 + f][...] if earlier else jnp.zeros((rows, cells), F32)
+            )
+
+    lanes = next(b for b in (LANES, cells) if cells % b == 0)
+    depth = depth_ref[me_ref[1]]
+    weights = []
+    for f in range(kinds):
+        lines = [
+            decoder_ref[pl.ds((first + group * count + c) * kinds + f, 1), :]
+            for c in range(count)
+        ]
+        lines = [line * depth for line in lines] if f == kinds - 1 else lines
+        weights.append([jnp.broadcast_to(line, (8, lanes)) for line in lines])
 
     def slab(t, carry):
         at = pl.ds(pl.multiple_of(t * 8, 8), 8)
-        values = [updated_ref[c, at, :] for c in range(count)]
-        for f in range(fields_ref.shape[0]):
-            total = fields_ref[f, at, :]
-            for c in range(count):
-                total = total + decoder_ref[f, first + group * count + c] * values[c]
-            fields_ref[f, at, :] = total
+        for start in range(0, cells, lanes):
+            to = slice(start, start + lanes)
+            values = [updated_ref[c, at, to] for c in range(count)]
+            for f in range(kinds):
+                terms = [weights[f][c] * values[c] for c in range(count)]
+                while len(terms) > 1:
+                    terms = [sum(terms[i + 1 : i + 2], terms[i]) for i in range(0, len(terms), 2)]
+                field_refs[f][at, to] += terms[0]
         return carry
 
     lax.fori_loop(0, rows // 8, slab, 0)
+
+    @pl.when(group == pl.num_programs(0) - 1)
+    def _():
+        for i, f in enumerate((1, kinds - 1)):
+            low_ref[i : i + 1] = field_refs[f][:1]
+            high_ref[i : i + 1] = field_refs[f][rows - 1 :]
+
+
+def pair_kernel(me_ref, layer_ref, other_ref, both_ref):
+    half = both_ref.shape[0]
+    at = pl.ds(pl.multiple_of((me_ref[1] & 1) * half, 8), half)
+    both_ref[...] = layer_ref[at, :] + other_ref[at, :]
 
 
 def pointwise_kernel(chunks, block, *refs):
@@ -197,26 +276,41 @@
         out_ref[:, at] = out.reshape(channels, block, cells)
 
 
-def residual_kernel(
-    fields_ref, geo_ref, below_ref, before_ref, after_ref, turning_ref, out_ref
-):
-    rows, cells = geo_ref.shape
-    east, north, upward = fields_ref[0], fields_ref[1], fields_ref[2]
-    geopotential = geo_ref[...]
+def residual_kernel(paired, shifts, *refs):
+    east_ref, north_ref, upward_ref, layer_ref, below_ref, before_ref, after_ref = refs[:7]
+    shift_refs, rest, out_ref = refs[7 : 7 + shifts], refs[7 + shifts : -1], refs[-1]
+    rows, cells = layer_ref.shape
+    geopotential = layer_ref[...]
+    turning_ref, lower_refs = rest[0], rest[1:]
+    if paired:
+        me_ref, other_ref, mine_ref, partner_ref = lower_refs
+        odd = (me_ref[1] & 1) == 1
+        mine, theirs = mine_ref[...], partner_ref[...]
+        lower = jnp.concatenate(
+            [jnp.where(odd, theirs, mine), jnp.where(odd, mine, theirs)], 0
+        )
+        geopotential = geopotential + jnp.where(odd, other_ref[...], 0.0) + lower
+    else:
+        for ref in lower_refs:
+            geopotential = geopotential + ref[...]
+    rims = [before_ref[1:2], after_ref[1:2]]
+    for ref in shift_refs:
+        rims = [rims[0] + ref[:1], rims[1] + ref[1:2]]
     row = lax.broadcasted_iota(jnp.int32, (rows, cells), 0)
 
     def along_x(field):
         return (pltpu.roll(field, cells - 1, 1) - pltpu.roll(field, 1, 1)) * 0.5
 
-    def along_y(field, which):
-        later = jnp.where(row == rows - 1, after_ref[which], pltpu.roll(field, rows - 1, 0))
-        earlier = jnp.where(row == 0, before_ref[which], pltpu.roll(field, 1, 0))
+    def along_y(field, first, last):
+        later = jnp.where(row == rows - 1, last, pltpu.roll(field, rows - 1, 0))
+        earlier = jnp.where(row == 0, first, pltpu.roll(field, 1, 0))
         return (later - earlier) * 0.5
 
-    turning = turning_ref[...]
-    out_ref[0] = along_x(east) + along_y(north, 0) + upward - below_ref[...]
+    east, north, turning = east_ref[...], north_ref[...], turning_ref[...]
+    north_y = along_y(north, before_ref[:1], after_ref[:1])
+    out_ref[0] = along_x(east) + north_y + upward_ref[...] - below_ref[...]
     out_ref[1] = turning * north - along_x(geopotential)
-    out_ref[2] = turning * east + along_y(geopotential, 1)
+    out_ref[2] = turning * east + along_y(geopotential, rims[0], rims[1])
 
 
 def on_device(forcing, spectral_weight, point_weight, point_bias, decoder, coriolis, layer_depth):
@@ -234,40 +328,67 @@
     part = groups // CHUNKS
     size = channels // CHUNKS
     wide = peers * 4 * own
-    me = lax.axis_index("gy")
+    me = jnp.stack([lax.axis_index("gy"), lax.axis_index("lev")]).astype(jnp.int32)
 
     forward_x, inverse_x = x_tables(cells, modes, slices, cells * total_rows)
-    order = jnp.stack([me ^ d ^ (h * peers) for d in range(peers) for h in range(2)])
-    near_table = jnp.take(jnp.asarray(forward_x), order, axis=0).reshape(wide, cells).T
-    spread_table = jnp.take(jnp.asarray(inverse_x), order, axis=0).reshape(wide, cells)
-    row_table = jnp.take(jnp.asarray(y_table(total_rows, ymodes, slices)), order[::2], axis=0)
-    row_table = row_table.reshape(peers * rows, 2 * ymodes)
+    smem = pl.BlockSpec(memory_space=pltpu.SMEM)
+    vmem = pl.BlockSpec(memory_space=pltpu.VMEM)
+
+    def whole(shape):
+        return pl.BlockSpec(shape, lambda i: (0,) * len(shape))
+
+    def params(mib, *grid):
+        return pltpu.CompilerParams(dimension_semantics=grid, vmem_limit_bytes=mib << 20)
+
 
     block = next(b for b in (16, 8, rows) if rows % b == 0)
-    blocks = next(b for b in (2, 1) if rows % (b * block) == 0)
-    which = lax.broadcasted_iota(jnp.int32, (channels * block, channels), 0) // block
-    pick = (which == lax.broadcasted_iota(jnp.int32, which.shape, 1)).astype(BF)
-    square = jnp.dot(jnp.dot(pick, point_weight.T), pick.T)
-    at = jnp.arange(channels * block, dtype=jnp.int32) % block
-    square = jnp.where(at[:, None] == at[None, :], square, 0).astype(BF)
-    bias = jnp.repeat(point_bias, block)[:, None]
+    blocks = 1
     many = next(b for b in (4, 2, 1) if part % b == 0)
+
+    near_table = pl.pallas_call(
+        functools.partial(forward_table_kernel, own, peers),
+        grid=(1,),
+        in_specs=[smem, whole((cells, wide))],
+        out_specs=whole((cells, wide)),
+        out_shape=jax.ShapeDtypeStruct((cells, wide), BF),
+        compiler_params=params(6, "arbitrary"),
+        cost_estimate=cost(2 * cells * wide * wide, 4 * cells * wide),
+        name="forward_table",
+    )(me, jnp.asarray(forward_x))
+    spread_table, row_table = pl.pallas_call(
+        functools.partial(other_tables_kernel, own, peers),
+        grid=(1,),
+        in_specs=[smem, whole((wide, cells)), whole((slices, rows, 2 * ymodes))],
+        out_specs=[whole((wide, cells)), whole((peers * rows, 2 * ymodes))],
+        out_shape=[
+            jax.ShapeDtypeStruct((wide, cells), BF),
+            jax.ShapeDtypeStruct((peers * rows, 2 * ymodes), BF),
+        ],
+        compiler_params=params(8, "arbitrary"),
+        cost_estimate=cost(2 * cells * wide * wide, 4 * cells * wide),
+        name="other_tables",
+    )(me, jnp.asarray(inverse_x), jnp.asarray(y_table(total_rows, ymodes, slices)))
+    square, bias, decoder_splat = pl.pallas_call(
+        functools.partial(small_kernel, block),
+        in_specs=[vmem] * 3,
+        out_specs=[vmem] * 3,
+        out_shape=[
+            jax.ShapeDtypeStruct((channels * block, channels * block), BF),
+            jax.ShapeDtypeStruct((channels * block, 1), F32),
+            jax.ShapeDtypeStruct((channels * decoder.shape[0], LANES), F32),
+        ],
+        compiler_params=params(8),
+        cost_estimate=cost(2 * channels * (channels * block) ** 2, 1 << 20),
+        name="small",
+    )(point_weight, point_bias[None, :], decoder)
 
     def swap(value, distance):
         return lax.ppermute(value, "gy", [(g, g ^ distance) for g in range(slices)])
-
-    def whole(shape):
-        return pl.BlockSpec(shape, lambda i: (0,) * len(shape))
 
     cells_spec = pl.BlockSpec((many * pack, rows, cells), lambda i: (i, 0, 0))
     lane_spec = pl.BlockSpec((many, rows, LANES), lambda i: (i, 0, 0))
     lane_shape = jax.ShapeDtypeStruct((part, rows, LANES), BF)
     mode_spec = pl.BlockSpec((many * pack, own, 2 * ymodes), lambda i: (i, 0, 0))
-    vmem = pl.BlockSpec(memory_space=pltpu.VMEM)
-
-    def params(mib, *grid):
-        return pltpu.CompilerParams(dimension_semantics=grid, vmem_limit_bytes=mib << 20)
-
     tile = size * rows * cells
 
     def offset_spec(n):
@@ -283,7 +404,7 @@
             compiler_params=params(6, "arbitrary"),
             cost_estimate=cost(2 * tile * wide, tile * 2),
             name="near",
-        )(forcing, near_table)
+        )(pltpu.with_memory_space_constraint(forcing, pltpu.HBM), near_table)
 
     def exchange(parts):
         return [parts[0]] + [swap(parts[d], d) for d in range(1, peers)]
@@ -303,23 +424,26 @@
             name="forward_y",
         )(*parts, row_table)
 
-    def mix(kept, got):
+    def mix(kept, got, n, earlier):
+        total = jax.ShapeDtypeStruct((own, channels, 2 * ymodes), F32)
+        ends = [jax.ShapeDtypeStruct((size, own, 2 * ymodes), BF)] * CHUNKS
+        final = n == CHUNKS - 1
         return pl.pallas_call(
-            functools.partial(mix_kernel, CHUNKS),
-            in_specs=[vmem] * (2 * CHUNKS + 1),
-            out_specs=[vmem] * CHUNKS,
-            out_shape=[jax.ShapeDtypeStruct((size, own, 2 * ymodes), BF)] * CHUNKS,
-            scratch_shapes=[pltpu.VMEM((own, channels, 2 * ymodes), F32)] * 2,
+            functools.partial(mix_kernel, n, CHUNKS),
+            in_specs=[vmem] * (3 + len(earlier)),
+            out_specs=[vmem] * len(ends) if final else [vmem],
+            out_shape=ends if final else [total],
+            scratch_shapes=[pltpu.VMEM((own, size, 2 * ymodes), F32)],
             compiler_params=params(8),
             cost_estimate=cost(
-                8 * own * channels**2 * ymodes, 4 * own * channels**2 * ymodes
+                8 * own * channels * size * ymodes, 4 * own * channels * size * ymodes
             ),
             name="mix",
-        )(*kept, *got, spectral_weight)
+        )(kept, got, spectral_weight, *earlier)
 
     def inverse_y(mine, theirs):
         return pl.pallas_call(
-            functools.partial(inverse_y_kernel, pack, own, peers),
+            functools.partial(inverse_y_kernel, pack, peers),
             grid=(part // many,),
             in_specs=[mode_spec] * 2 + [whole(row_table.shape)],
             out_specs=[lane_spec] * peers,
@@ -345,7 +469,7 @@
             ],
             out_specs=pl.BlockSpec((channels, blocks * block, cells), lambda i: (0, i, 0)),
             out_shape=jax.ShapeDtypeStruct((channels, rows, cells), F32),
-            compiler_params=params(19, "arbitrary"),
+            compiler_params=params(11, "arbitrary"),
             cost_estimate=cost(
                 2 * channels * block * channels * rows * cells, 8 * channels * rows * cells
             ),
@@ -366,31 +490,38 @@
         )(*backs, point, spread_table, near_table)
         return out[0], out[1:]
 
-    decoder_full = decoder.astype(F32)
+    few = next(b for b in (2, 1) if part % b == 0)
+    few_lanes = pl.BlockSpec((few, rows, LANES), lambda i: (i, 0, 0))
+
+    def few_spec(n):
+        return pl.BlockSpec(
+            (few * pack, rows, cells), lambda i: (i + n * (part // few), 0, 0)
+        )
 
     def last(backs, point, n, earlier):
-        fields_shape = (decoder.shape[0], rows, cells)
-        more = [pl.BlockSpec(memory_space=pl.ANY), whole(fields_shape)] if earlier else []
+        kinds = decoder.shape[0]
+        more = [whole((rows, cells))] * kinds
         return pl.pallas_call(
-            functools.partial(last_kernel, pack, peers, n * size),
-            grid=(part // many,),
-            in_specs=[lane_spec] * peers
+            functools.partial(last_kernel, pack, peers, n * size, kinds),
+            grid=(part // few,),
+            in_specs=[few_lanes] * peers
             + [
-                offset_spec(n),
+                smem,
+                smem,
+                few_spec(n),
                 whole(spread_table.shape),
-                pl.BlockSpec(memory_space=pltpu.SMEM),
+                whole(decoder_splat.shape),
             ]
-            + more,
-            out_specs=[offset_spec(n), whole(fields_shape)],
-            out_shape=[
-                jax.ShapeDtypeStruct((channels, rows, cells), F32),
-                jax.ShapeDtypeStruct(fields_shape, F32),
-            ],
-            input_output_aliases={peers + 3: 0} if earlier else {},
-            compiler_params=params(20, "arbitrary"),
+            + ([pl.BlockSpec(memory_space=pl.ANY)] + more if earlier else []),
+            out_specs=[few_spec(n)] + more + [whole((2, cells))] * 2,
+            out_shape=[jax.ShapeDtypeStruct((channels, rows, cells), F32)]
+            + [jax.ShapeDtypeStruct((rows, cells), F32)] * kinds
+            + [jax.ShapeDtypeStruct((2, cells), F32)] * 2,
+            input_output_aliases={peers + 5: 0} if earlier else {},
+            compiler_params=params(18, "arbitrary"),
             cost_estimate=cost(2 * tile * wide, 8 * tile, tile),
             name="last",
-        )(*backs, point, spread_table, decoder_full, *earlier)
+        )(*backs, me, layer_depth, point, spread_table, decoder_splat, *earlier[: kinds + 1])
 
     every = range(CHUNKS)
     nears = [near_of(n) for n in every]
@@ -401,8 +532,12 @@
         halves = [forward_y(parts) for parts in arrived]
         kept = [half[0] for half in halves]
         got = [swap(half[1], peers) for half in halves]
-        mixed = mix(kept, got)
-        theirs = [swap(value, peers) for value in mixed]
+        mixed = []
+        for n in every:
+            mixed = mix(kept[n], got[n], n, mixed)
+        theirs = []
+        for n in every:
+            theirs.append(swap(mixed[n], peers))
         backs = [exchange(inverse_y(mixed[n], theirs[n])) for n in every]
         if iteration < ITERS - 1:
             done = [update(backs[n], point, n) for n in every]
@@ -411,53 +546,53 @@
     done = []
     for n in every:
         done = last(backs[n], point, n, done)
-    updated, fields = done
-    north, upward, heat = fields[1], fields[2], fields[3]
+    updated, east, north, upward, layer, low, high = done
 
     levels = lax.axis_size("lev")
-    level = lax.axis_index("lev")
 
     def from_below(value, step):
         return lax.ppermute(value, "lev", [(s, s + step) for s in range(levels - step)])
 
-    below = from_below(upward, 1)
-    layer = lax.dynamic_index_in_dim(layer_depth, level, 0, keepdims=False) * heat
-    if levels % 2 == 0 and rows % 16 == 0:
-        half = rows // 2
-        place = level % 2
+    up = [(i, (i + 1) % slices) for i in range(slices)]
+    down = [(j, i) for i, j in up]
+    pairs = levels % 2 == 0 and rows % 16 == 0
+    if pairs:
         partner = [(s, s ^ 1) for s in range(levels)]
         other = lax.ppermute(layer, "lev", partner)
-        both = lax.dynamic_slice_in_dim(layer + other, place * half, half, 0)
+    below = from_below(upward, 1)
+    before = lax.ppermute(high, "gy", up)
+    after = lax.ppermute(low, "gy", down)
+    if pairs:
+        both = pl.pallas_call(
+            pair_kernel,
+            in_specs=[smem, vmem, vmem],
+            out_specs=vmem,
+            out_shape=jax.ShapeDtypeStruct((rows // 2, cells), F32),
+            compiler_params=params(2),
+            cost_estimate=cost(rows * cells, 8 * rows * cells),
+            name="pair",
+        )(me, layer, other)
         lower = from_below(both, 2)
         step = 2
         while step < levels - 2:
             lower = lower + from_below(lower, step)
             step *= 2
-        rest = lax.ppermute(lower, "lev", partner)
-        lower = jnp.where(
-            place == 0, jnp.concatenate([lower, rest], 0), jnp.concatenate([rest, lower], 0)
-        )
-        geopotential = layer + jnp.where(place == 0, 0.0, other) + lower
+        lowers = [me, other, lower, lax.ppermute(lower, "lev", partner)]
     else:
-        geopotential = layer
-        step = 1
-        while step < levels:
-            geopotential = geopotential + from_below(geopotential, step)
-            step *= 2
-
-    up = [(i, (i + 1) % slices) for i in range(slices)]
-    down = [(j, i) for i, j in up]
-    before = lax.ppermute(jnp.stack([north[-1:], geopotential[-1:]], 0), "gy", up)
-    after = lax.ppermute(jnp.stack([north[:1], geopotential[:1]], 0), "gy", down)
+        lowers = [from_below(layer, step) for step in range(1, levels)]
+    rims = jnp.concatenate([before[1:], after[1:]], 0)
+    shifts = [from_below(rims, step) for step in range(1, levels)]
     residual = pl.pallas_call(
-        residual_kernel,
-        in_specs=[vmem] * 6,
+        functools.partial(residual_kernel, pairs, len(shifts)),
+        in_specs=[vmem] * (8 + len(shifts))
+        + ([smem] if pairs else [vmem])
+        + [vmem] * (len(lowers) - 1),
         out_specs=vmem,
         out_shape=jax.ShapeDtypeStruct((3, rows, cells), F32),
-        compiler_params=params(8),
+        compiler_params=params(10),
         cost_estimate=cost(20 * rows * cells, 36 * rows * cells),
         name="residual",
-    )(fields, geopotential, below, before, after, coriolis[:, None])
+    )(east, north, upward, layer, below, before, after, *shifts, coriolis[:, None], *lowers)
     return updated[None], residual[:, None]
 
 

time: 250 us -> 232 us (0.928)
  local copies, waits for them, and re-layouts: 24.2 us -> 1.27 us
  Pallas kernels: 69.1 us -> 75.3 us
  other arithmetic: 2.9 us -> 0.09 us
  waiting for transfers between devices: 82.2 us -> 84.9 us
    unnamed x36 -> x24, local copies, waits for them, and re-layouts: 17.2 us -> 1.16 us
    gather x3 -> x0, local copies, waits for them, and re-layouts: 5.48 us -> none  [the longest x1 2.23 us: on_device(): jnp.take(jnp.asarray(y_table(total_rows, ymodes, slices)), order[::2], ax...]
    ppermute x3, waiting for transfers between devices: 6.13 us -> 1.04 us  [the longest x1 1.03 us: on_device(): before = lax.ppermute(high, 'gy', up)]
    ppermute x2 -> x5, waiting for transfers between devices: 1.93 us -> 6.87 us  [from_below(): lax.ppermute(value, 'lev', [(s, s + step) for s in range(levels - step)])]
    ppermute x2 -> x5, starting transfers between devices: 5.76 us -> 10.7 us  [from_below(): lax.ppermute(value, 'lev', [(s, s + step) for s in range(levels - step)])]
    ppermute x48, waiting for transfers between devices: 72.8 us -> 77 us  [swap(): return lax.ppermute(value, 'gy', [(g, g ^ distance) for g in range(slices)])]
    pallas_call x12 -> x19, Pallas kernels: 31.7 us -> 34.6 us  [the longest x2 13.7 us: last(): pl.pallas_call(functools.partial(last_kernel, pack, peers, n * size, kind...]
    ppermute x48, starting transfers between devices: 44.3 us -> 41.6 us  [swap(): return lax.ppermute(value, 'gy', [(g, g ^ distance) for g in range(slices)])]
  transfers between devices with their start and end apart: 54 -> 57, of which waited for: 25 -> 21; matrix products, arithmetic and copies ran while one was open for 2% -> 0% of each run, Pallas kernels for 18% -> 24%
where the time goes in v3:
time: 232 us; the launch traced here: 229 us
  waiting for transfers between devices  84.9 us (37%)
  Pallas kernels  75.3 us (32%)
  starting transfers between devices  66.5 us (29%)
    ppermute x48, waiting for transfers between devices, swap(): return lax.ppermute(value, 'gy', [(g, g ^ distance) for g in range(slices)])  77 us
    ppermute x48, starting transfers between devices, swap(): return lax.ppermute(value, 'gy', [(g, g ^ distance) for g in range(slices)])  41.6 us
    pallas_call x3, Pallas kernels, pointwise(): pl.pallas_call(functools.partial(pointwise_kernel, len(states), block), g...  18 us
    pallas_call x2, Pallas kernels, last(): pl.pallas_call(functools.partial(last_kernel, pack, peers, n * size, kind...  13.7 us
    pallas_call x4, Pallas kernels, update(): pl.pallas_call(functools.partial(update_kernel, pack, peers), grid=(part...  12.7 us
    pallas_call x6, Pallas kernels, mix(): pl.pallas_call(functools.partial(mix_kernel, n, CHUNKS), in_specs=[vmem]...  11.3 us
    ppermute x5, starting transfers between devices, from_below(): lax.ppermute(value, 'lev', [(s, s + step) for s in range(levels - step)])  10.7 us
    ppermute x1, starting transfers between devices, on_device(): other = lax.ppermute(layer, 'lev', partner)  10.1 us
  transfers between devices with their start and end apart: 57, of which 21 were waited for; matrix products, arithmetic and copies ran while one was open for 0% of the time, Pallas kernels for 24%

profile of v3, /device:TPU:1, one launch (start us, length us, event | category | flops | bytes accessed | tf_op | source)
XLA Modules:
  0.0 229.4 jit_solution(18223742646760297326)
XLA Ops:
  0.7 1.1 copy-done.1
  2.7 2.9 %near.3 = (bf16[8,96,128]{2,1,0:T(8,128)(2,1)S(1)}, bf16[8,96,128]{2,1,0:T(8,128)(2,1)S(1)}, bf16[8,96,128]{2,1,0:T(8,128)(2,1)S(1)}, bf16[8,96,128]{2,1,0:T(8,128)(2,1)S(1)}) custom-call(bf16[32,96,1024]{2,1,0:T(8,128)(2,1)} %bitcast.11, bf16[1024,256]{1,0:T(8,128)(2,1)S(1)} %forward_table.1.table_ref.refs_6_), custom_call_target="tpu_custom_call" | custom-call | flops 805306368 | bytes 3145728 | tf_op jit(solution)/shard_map/near/pallas_call | solution.py:398
  5.6 2.1 collective-permute-start.4
  7.7 1.3 collective-permute-start.5
  9.0 2.9 %near.2 = (bf16[8,96,128]{2,1,0:T(8,128)(2,1)S(1)}, bf16[8,96,128]{2,1,0:T(8,128)(2,1)S(1)}, bf16[8,96,128]{2,1,0:T(8,128)(2,1)S(1)}, bf16[8,96,128]{2,1,0:T(8,128)(2,1)S(1)}) custom-call(bf16[32,96,1024]{2,1,0:T(8,128)(2,1)} %bitcast.12, bf16[1024,256]{1,0:T(8,128)(2,1)S(1)} %forward_table.1.table_ref.refs_6_), custom_call_target="tpu_custom_call" | custom-call | flops 805306368 | bytes 3145728 | tf_op jit(solution)/shard_map/near/pallas_call | solution.py:398
  11.9 1.4 collective-permute-start
  13.3 1.2 collective-permute-start.1
  15.5 2.1 collective-permute-done.6.refs_3_
  18.3 2.2 collective-permute-start.7
  20.5 1.5 collective-permute-done.refs_1_
  22.0 6.8 %collective-permute-done.2.refs_3_ = bf16[8,96,128]{2,1,0:T(8,128)(2,1)S(1)} collective-permute-done((bf16[8,96,128]{2,1,0:T(8,128)(2,1)S(1)}, bf16[8,96,128]{2,1,0:T(8,128)(2,1)S(1)}, u32[]{:S(2)}, u32[]{:S(2)}) %collective-permute-start.2) | collective-permute-done | bytes 196640 | tf_op jit(solution)/shard_map/ppermute | solution.py:386
  29.5 1.2 collective-permute-start.3
  30.8 1.8 mix.6.refs_3_
  32.7 5.6 %collective-permute-done.3.refs_1_ = bf16[16,16,256]{2,1,0:T(8,128)(2,1)S(1)} collective-permute-done((bf16[16,16,256]{2,1,0:T(8,128)(2,1)S(1)}, bf16[16,16,256]{2,1,0:T(8,128)(2,1)S(1)}, u32[]{:S(2)}, u32[]{:S(2)}) %collective-permute-start.3) | collective-permute-done | bytes 131104 | tf_op jit(solution)/shard_map/ppermute | solution.py:386
  38.2 1.9 mix.7
  40.8 2.4 %collective-permute-start.8 = (bf16[16,16,256]{2,1,0:T(8,128)(2,1)S(1)}, bf16[16,16,256]{2,1,0:T(8,128)(2,1)S(1)}, u32[]{:S(2)}, u32[]{:S(2)}) collective-permute-start(bf16[16,16,256]{2,1,0:T(8,128)(2,1)S(1)} %get-tuple-element.102.mine_ref), channel_id=1, source_target_pairs={{0,4},{1,5},{2,6},{3,7},{4,0},{5,1},{6,2},{7,3},{8,12},{9,13},{10,... | collective-permute-start | bytes 393224 | tf_op jit(solution)/shard_map/ppermute | solution.py:386
  43.2 8.0 %collective-permute-done.16.theirs_ref = bf16[16,16,256]{2,1,0:T(8,128)(2,1)S(1)} collective-permute-done((bf16[16,16,256]{2,1,0:T(8,128)(2,1)S(1)}, bf16[16,16,256]{2,1,0:T(8,128)(2,1)S(1)}, u32[]{:S(2)}, u32[]{:S(2)}) %collective-permute-start.16) | collective-permute-done | bytes 131104 | tf_op jit(solution)/shard_map/ppermute | solution.py:386
  51.9 1.4 collective-permute-start.17
  53.4 1.3 collective-permute-start.19
  54.7 6.0 %pointwise.3.refs_4_ = f32[32,96,1024]{2,1,0:T(8,128)S(1)} custom-call(bf16[32,96,1024]{2,1,0:T(8,128)(2,1)S(1)} %bitcast.15, bf16[32,96,1024]{2,1,0:T(8,128)(2,1)S(1)} %bitcast.16, bf16[512,512]{1,0:T(8,128)(2,1)S(1)} %get-tuple-element.107.refs_2_.refs_3_, f32[512,1]{1,0:T(8,128)S(1)} %get-tuple-element.108.refs_3_.refs_4_), custom_call_target="tpu_custom_call" | custom-call | flops 3221225472 | bytes 25165824 | tf_op jit(solution)/shard_map/pointwise/pallas_call | solution.py:461
  61.7 2.3 %collective-permute-start.11 = (bf16[8,96,128]{2,1,0:T(8,128)(2,1)S(1)}, bf16[8,96,128]{2,1,0:T(8,128)(2,1)S(1)}, u32[]{:S(2)}, u32[]{:S(2)}) collective-permute-start(bf16[8,96,128]{2,1,0:T(8,128)(2,1)S(1)} %get-tuple-element.106), channel_id=1, source_target_pairs={{0,3},{1,2},{2,1},{3,0},{4,7},{5,6},{6,5},{7,4},{8,11},{9,10},{10,... | collective-permute-start | bytes 589832 | tf_op jit(solution)/shard_map/ppermute | solution.py:386
  64.2 3.2 %update.5 = (bf16[16,96,1024]{2,1,0:T(8,128)(2,1)S(1)}, bf16[8,96,128]{2,1,0:T(8,128)(2,1)S(1)}, bf16[8,96,128]{2,1,0:T(8,128)(2,1)S(1)}, bf16[8,96,128]{2,1,0:T(8,128)(2,1)S(1)}, bf16[8,96,128]{2,1,0:T(8,128)(2,1)S(1)}) custom-call(bf16[8,96,128]{2,1,0:T(8,128)(2,1)S(1)} %get-tuple-element.117.refs_0_, ...), custom_call_target="tpu_custom_call" | custom-call | flops 1610612736 | bytes 9437184 | tf_op jit(solution)/shard_map/update/pallas_call | solution.py:480
  67.4 1.4 collective-permute-start.20
  68.9 1.2 collective-permute-start.22
  70.1 1.8 collective-permute-done.11.refs_3_
  71.9 3.2 %update.4 = (bf16[16,96,1024]{2,1,0:T(8,128)(2,1)S(1)}, bf16[8,96,128]{2,1,0:T(8,128)(2,1)S(1)}, bf16[8,96,128]{2,1,0:T(8,128)(2,1)S(1)}, bf16[8,96,128]{2,1,0:T(8,128)(2,1)S(1)}, bf16[8,96,128]{2,1,0:T(8,128)(2,1)S(1)}) custom-call(bf16[8,96,128]{2,1,0:T(8,128)(2,1)S(1)} %get-tuple-element.103.refs_0_, ...), custom_call_target="tpu_custom_call" | custom-call | flops 1610612736 | bytes 9437184 | tf_op jit(solution)/shard_map/update/pallas_call | solution.py:480
  75.7 3.8 %collective-permute-done.20.refs_1_ = bf16[8,96,128]{2,1,0:T(8,128)(2,1)S(1)} collective-permute-done((bf16[8,96,128]{2,1,0:T(8,128)(2,1)S(1)}, bf16[8,96,128]{2,1,0:T(8,128)(2,1)S(1)}, u32[]{:S(2)}, u32[]{:S(2)}) %collective-permute-start.20) | collective-permute-done | bytes 196640 | tf_op jit(solution)/shard_map/ppermute | solution.py:386
  81.0 1.3 collective-permute-start.23
  82.3 5.4 %collective-permute-done.12.refs_1_ = bf16[8,96,128]{2,1,0:T(8,128)(2,1)S(1)} collective-permute-done((bf16[8,96,128]{2,1,0:T(8,128)(2,1)S(1)}, bf16[8,96,128]{2,1,0:T(8,128)(2,1)S(1)}, u32[]{:S(2)}, u32[]{:S(2)}) %collective-permute-start.12) | collective-permute-done | bytes 196640 | tf_op jit(solution)/shard_map/ppermute | solution.py:386
  89.4 1.8 mix.8.refs_3_
  91.3 6.0 %collective-permute-done.15.refs_1_ = bf16[16,16,256]{2,1,0:T(8,128)(2,1)S(1)} collective-permute-done((bf16[16,16,256]{2,1,0:T(8,128)(2,1)S(1)}, bf16[16,16,256]{2,1,0:T(8,128)(2,1)S(1)}, u32[]{:S(2)}, u32[]{:S(2)}) %collective-permute-start.15) | collective-permute-done | bytes 131104 | tf_op jit(solution)/shard_map/ppermute | solution.py:386
  97.3 1.9 mix.9
  99.3 5.9 %collective-permute-done.32.theirs_ref = bf16[16,16,256]{2,1,0:T(8,128)(2,1)S(1)} collective-permute-done((bf16[16,16,256]{2,1,0:T(8,128)(2,1)S(1)}, bf16[16,16,256]{2,1,0:T(8,128)(2,1)S(1)}, u32[]{:S(2)}, u32[]{:S(2)}) %collective-permute-start.32) | collective-permute-done | bytes 131104 | tf_op jit(solution)/shard_map/ppermute | solution.py:386
  106.0 2.8 %collective-permute-start.33 = (bf16[8,96,128]{2,1,0:T(8,128)(2,1)S(1)}, bf16[8,96,128]{2,1,0:T(8,128)(2,1)S(1)}, u32[]{:S(2)}, u32[]{:S(2)}) collective-permute-start(bf16[8,96,128]{2,1,0:T(8,128)(2,1)S(1)} %get-tuple-element.142), channel_id=1, source_target_pairs={{0,1},{1,0},{2,3},{3,2},{4,5},{5,4},{6,7},{7,6},{8,9},{9,8},{10,11... | collective-permute-start | bytes 589832 | tf_op jit(solution)/shard_map/ppermute | solution.py:386
  110.2 3.5 %collective-permute-done.24.theirs_ref = bf16[16,16,256]{2,1,0:T(8,128)(2,1)S(1)} collective-permute-done((bf16[16,16,256]{2,1,0:T(8,128)(2,1)S(1)}, bf16[16,16,256]{2,1,0:T(8,128)(2,1)S(1)}, u32[]{:S(2)}, u32[]{:S(2)}) %collective-permute-start.24) | collective-permute-done | bytes 131104 | tf_op jit(solution)/shard_map/ppermute | solution.py:386
  114.6 2.5 %collective-permute-start.27 = (bf16[8,96,128]{2,1,0:T(8,128)(2,1)S(1)}, bf16[8,96,128]{2,1,0:T(8,128)(2,1)S(1)}, u32[]{:S(2)}, u32[]{:S(2)}) collective-permute-start(bf16[8,96,128]{2,1,0:T(8,128)(2,1)S(1)} %get-tuple-element.131), channel_id=1, source_target_pairs={{0,3},{1,2},{2,1},{3,0},{4,7},{5,6},{6,5},{7,4},{8,11},{9,10},{10,... | collective-permute-start | bytes 589832 | tf_op jit(solution)/shard_map/ppermute | solution.py:386
  117.2 6.0 %pointwise.4.refs_4_ = f32[32,96,1024]{2,1,0:T(8,128)S(1)} custom-call(bf16[16,96,1024]{2,1,0:T(8,128)(2,1)S(1)} %get-tuple-element.132.refs_0_, bf16[16,96,1024]{2,1,0:T(8,128)(2,1)S(1)} %get-tuple-element.133.refs_1_, bf16[32,96,1024]{2,1,0:T(8,128)(2,1)S(1)} %bitcast.17, bf16[512,512]{1,0:T(8,128)(2,1)S(1)} %get-tuple-element.107.refs_2_.refs_3_, ...), custom_call_target="tpu_custom_call" | custom-call | flops 3221225472 | bytes 25165824 | tf_op jit(solution)/shard_map/pointwise/pallas_call | solution.py:461
  123.2 3.2 %update.7 = (bf16[16,96,1024]{2,1,0:T(8,128)(2,1)S(1)}, bf16[8,96,128]{2,1,0:T(8,128)(2,1)S(1)}, bf16[8,96,128]{2,1,0:T(8,128)(2,1)S(1)}, bf16[8,96,128]{2,1,0:T(8,128)(2,1)S(1)}, bf16[8,96,128]{2,1,0:T(8,128)(2,1)S(1)}) custom-call(bf16[8,96,128]{2,1,0:T(8,128)(2,1)S(1)} %get-tuple-element.141.refs_0_, ...), custom_call_target="tpu_custom_call" | custom-call | flops 1610612736 | bytes 9437184 | tf_op jit(solution)/shard_map/update/pallas_call | solution.py:480
  126.7 2.4 %collective-permute-start.38 = (bf16[8,96,128]{2,1,0:T(8,128)(2,1)S(1)}, bf16[8,96,128]{2,1,0:T(8,128)(2,1)S(1)}, u32[]{:S(2)}, u32[]{:S(2)}) collective-permute-start(bf16[8,96,128]{2,1,0:T(8,128)(2,1)S(1)} %get-tuple-element.148), channel_id=1, source_target_pairs={{0,3},{1,2},{2,1},{3,0},{4,7},{5,6},{6,5},{7,4},{8,11},{9,10},{10,... | collective-permute-start | bytes 589832 | tf_op jit(solution)/shard_map/ppermute | solution.py:386
  129.1 3.2 %update.6 = (bf16[16,96,1024]{2,1,0:T(8,128)(2,1)S(1)}, bf16[8,96,128]{2,1,0:T(8,128)(2,1)S(1)}, bf16[8,96,128]{2,1,0:T(8,128)(2,1)S(1)}, bf16[8,96,128]{2,1,0:T(8,128)(2,1)S(1)}, bf16[8,96,128]{2,1,0:T(8,128)(2,1)S(1)}) custom-call(bf16[8,96,128]{2,1,0:T(8,128)(2,1)S(1)} %get-tuple-element.128.refs_0_, ...), custom_call_target="tpu_custom_call" | custom-call | flops 1610612736 | bytes 9437184 | tf_op jit(solution)/shard_map/update/pallas_call | solution.py:480
  133.1 1.9 collective-permute-start.30
  136.8 2.7 %collective-permute-done.28.refs_1_ = bf16[8,96,128]{2,1,0:T(8,128)(2,1)S(1)} collective-permute-done((bf16[8,96,128]{2,1,0:T(8,128)(2,1)S(1)}, bf16[8,96,128]{2,1,0:T(8,128)(2,1)S(1)}, u32[]{:S(2)}, u32[]{:S(2)}) %collective-permute-start.28) | collective-permute-done | bytes 196640 | tf_op jit(solution)/shard_map/ppermute | solution.py:386
  139.5 1.6 collective-permute-done.29.refs_2_
  141.1 4.4 %collective-permute-done.30.refs_3_ = bf16[8,96,128]{2,1,0:T(8,128)(2,1)S(1)} collective-permute-done((bf16[8,96,128]{2,1,0:T(8,128)(2,1)S(1)}, bf16[8,96,128]{2,1,0:T(8,128)(2,1)S(1)}, u32[]{:S(2)}, u32[]{:S(2)}) %collective-permute-start.30) | collective-permute-done | bytes 196640 | tf_op jit(solution)/shard_map/ppermute | solution.py:386
  146.3 1.8 mix.10.refs_3_
  148.2 6.2 %collective-permute-done.31.refs_1_ = bf16[16,16,256]{2,1,0:T(8,128)(2,1)S(1)} collective-permute-done((bf16[16,16,256]{2,1,0:T(8,128)(2,1)S(1)}, bf16[16,16,256]{2,1,0:T(8,128)(2,1)S(1)}, u32[]{:S(2)}, u32[]{:S(2)}) %collective-permute-start.31) | collective-permute-done | bytes 131104 | tf_op jit(solution)/shard_map/ppermute | solution.py:386
  154.4 1.9 mix.11
  156.4 5.6 %collective-permute-done.44.theirs_ref = bf16[16,16,256]{2,1,0:T(8,128)(2,1)S(1)} collective-permute-done((bf16[16,16,256]{2,1,0:T(8,128)(2,1)S(1)}, bf16[16,16,256]{2,1,0:T(8,128)(2,1)S(1)}, u32[]{:S(2)}, u32[]{:S(2)}) %collective-permute-start.44) | collective-permute-done | bytes 131104 | tf_op jit(solution)/shard_map/ppermute | solution.py:386
  163.0 1.9 collective-permute-start.46
  164.9 1.1 collective-permute-start.47
  166.0 4.3 %collective-permute-done.40.theirs_ref = bf16[16,16,256]{2,1,0:T(8,128)(2,1)S(1)} collective-permute-done((bf16[16,16,256]{2,1,0:T(8,128)(2,1)S(1)}, bf16[16,16,256]{2,1,0:T(8,128)(2,1)S(1)}, u32[]{:S(2)}, u32[]{:S(2)}) %collective-permute-start.40) | collective-permute-done | bytes 131104 | tf_op jit(solution)/shard_map/ppermute | solution.py:386
  171.8 1.9 collective-permute-start.43
  173.8 6.0 %pointwise.5.refs_6_ = f32[32,96,1024]{2,1,0:T(8,128)S(1)} custom-call(bf16[16,96,1024]{2,1,0:T(8,128)(2,1)S(1)} %get-tuple-element.156.refs_0_, bf16[16,96,1024]{2,1,0:T(8,128)(2,1)S(1)} %get-tuple-element.157.refs_1_, bf16[32,96,1024]{2,1,0:T(8,128)(2,1)S(1)} %bitcast.18, bf16[512,512]{1,0:T(8,128)(2,1)S(1)} %get-tuple-element.107.refs_2_.refs_3_, ...), custom_call_target="tpu_custom_call" | custom-call | flops 3221225472 | bytes 25165824 | tf_op jit(solution)/shard_map/pointwise/pallas_call | solution.py:461
  179.8 6.8 %last.2 = (f32[32,96,1024]{2,1,0:T(8,128)}, f32[96,1024]{1,0:T(8,128)S(1)}, f32[96,1024]{1,0:T(8,128)S(1)}, f32[96,1024]{1,0:T(8,128)S(1)}, f32[96,1024]{1,0:T(8...) custom-call(bf16[8,96,128]{2,1,0:T(8,128)(2,1)S(1)} %get-tuple-element.160.refs_0_, ...), custom_call_target="tpu_custom_call" | custom-call | flops 805306368 | bytes 12582912 | tf_op jit(solution)/shard_map/last/pallas_call | solution.py:504
  186.7 6.8 %last.3 = (f32[32,96,1024]{2,1,0:T(8,128)}, f32[96,1024]{1,0:T(8,128)S(1)}, f32[96,1024]{1,0:T(8,128)S(1)}, f32[96,1024]{1,0:T(8,128)S(1)}, f32[96,1024]{1,0:T(8...) custom-call(bf16[8,96,128]{2,1,0:T(8,128)(2,1)S(1)} %get-tuple-element.152.refs_0_, ...), custom_call_target="tpu_custom_call", output_to_operand_aliasing={{0}: (9, {})} | custom-call | flops 805306368 | bytes 12582912 | tf_op jit(solution)/shard_map/last/pallas_call | solution.py:504
  193.5 10.1 %collective-permute-start.54 = (f32[96,1024]{1,0:T(8,128)S(1)}, f32[96,1024]{1,0:T(8,128)S(1)}, u32[]{:S(2)}, u32[]{:S(2)}) collective-permute-start(f32[96,1024]{1,0:T(8,128)S(1)} %get-tuple-element.173.layer_ref.refs_3_), channel_id=1, source_target_pairs={{0,8},{8,0},{16,24},{24,16},{1,9},{9,1},{17,25},{25,17},{2,10},{10... | collective-permute-start | bytes 1179656 | tf_op jit(solution)/shard_map/ppermute | solution.py:561
  203.6 1.9 collective-permute-start.48
  206.1 1.5 collective-permute-start.55
  207.6 6.9 %collective-permute-done.55.refs_13_ = f32[48,1024]{1,0:T(8,128)S(1)} collective-permute-done((f32[48,1024]{1,0:T(8,128)S(1)}, f32[48,1024]{1,0:T(8,128)S(1)}, u32[]{:S(2)}, u32[]{:S(2)}) %collective-permute-start.55) | collective-permute-done | bytes 196640 | tf_op jit(solution)/shard_map/ppermute | solution.py:554
  214.4 1.1 collective-permute-start.49
  215.6 3.0 %collective-permute-start.50 = (f32[2,1024]{1,0:T(2,128)S(1)}, f32[2,1024]{1,0:T(2,128)S(1)}, u32[]{:S(2)}, u32[]{:S(2)}) collective-permute-start(f32[2,1024]{1,0:T(2,128)S(1)} %get-tuple-element.175), channel_id=1, source_target_pairs={{1,0},{2,1},{3,2},{4,3},{5,4},{6,5},{7,6},{0,7},{9,8},{10,9},{11,1... | collective-permute-start | bytes 24584 | tf_op jit(solution)/shard_map/ppermute | solution.py:564
  219.7 5.4 %collective-permute-start.51 = (f32[2,1024]{1,0:T(2,128)S(1)}, f32[2,1024]{1,0:T(2,128)S(1)}, u32[]{:S(2)}, u32[]{:S(2)}) collective-permute-start(f32[2,1024]{1,0:T(2,128)S(1)} %pad_maximum_fusion), channel_id=1, source_target_pairs={{0,8},{8,16},{16,24},{1,9},{9,17},{17,25},{2,10},{10,18},{18,26},{... | collective-permute-start | bytes 24584 | tf_op jit(solution)/shard_map/ppermute | solution.py:554
  225.0 1.3 collective-permute-start.52
  227.2 2.2 residual.1
  (115 shorter events, 21.7 us)
Async XLA Ops:
  0.6 14.0 %copy-start = (bf16[256,1024]{1,0:T(8,128)(2,1)S(1)}, bf16[256,1024]{1,0:T(8,128)(2,1)}, u32[]{:S(2)}) copy-start(bf16[256,1024]{1,0:T(8,128)(2,1)} %constant.15.clone.inverse_ref) | copy-start | bytes 1572868
  1.8 12.8 %copy-start.2 = (bf16[8,96,256]{2,1,0:T(8,128)(2,1)S(1)}, bf16[8,96,256]{2,1,0:T(8,128)(2,1)}, u32[]{:S(2)}) copy-start(bf16[8,96,256]{2,1,0:T(8,128)(2,1)} %constant.16.clone.row_ref) | copy-start | bytes 1179652
  2.7 28.1 %slice-start = ((s8[8388608]{0:T(1024)(128)(4,1)}), s8[4194304]{0:T(1024)(128)(4,1)S(1)}, s32[]{:S(2)}) async-start(s8[8388608]{0:T(1024)(128)(4,1)} %bitcast.9), calls=%async_computation | async-start | bytes 8388608
  5.6 8.9 %collective-permute-start.4 = (bf16[8,96,128]{2,1,0:T(8,128)(2,1)S(1)}, bf16[8,96,128]{2,1,0:T(8,128)(2,1)S(1)}, u32[]{:S(2)}, u32[]{:S(2)}) collective-permute-start(bf16[8,96,128]{2,1,0:T(8,128)(2,1)S(1)} %get-tuple-element.97), channel_id=1, source_target_pairs={{0,1},{1,0},{2,3},{3,2},{4,5},{5,4},{6,7},{7,6},{8,9},{9,8},{10,11... | collective-permute-start | bytes 589832 | tf_op jit(solution)/shard_map/ppermute | solution.py:386
  7.7 7.8 %collective-permute-start.5 = (bf16[8,96,128]{2,1,0:T(8,128)(2,1)S(1)}, bf16[8,96,128]{2,1,0:T(8,128)(2,1)S(1)}, u32[]{:S(2)}, u32[]{:S(2)}) collective-permute-start(bf16[8,96,128]{2,1,0:T(8,128)(2,1)S(1)} %get-tuple-element.98), channel_id=1, source_target_pairs={{0,2},{1,3},{2,0},{3,1},{4,6},{5,7},{6,4},{7,5},{8,10},{9,11},{10,... | collective-permute-start | bytes 589832 | tf_op jit(solution)/shard_map/ppermute | solution.py:386
  9.0 21.8 %slice-start.1 = ((s8[8388608]{0:T(1024)(128)(4,1)}), s8[4194304]{0:T(1024)(128)(4,1)S(1)}, s32[]{:S(2)}) async-start(s8[8388608]{0:T(1024)(128)(4,1)} %bitcast.9), calls=%async_computation.1 | async-start | bytes 8388608
  9.0 8.5 %collective-permute-start.6 = (bf16[8,96,128]{2,1,0:T(8,128)(2,1)S(1)}, bf16[8,96,128]{2,1,0:T(8,128)(2,1)S(1)}, u32[]{:S(2)}, u32[]{:S(2)}) collective-permute-start(bf16[8,96,128]{2,1,0:T(8,128)(2,1)S(1)} %get-tuple-element.99), channel_id=1, source_target_pairs={{0,3},{1,2},{2,1},{3,0},{4,7},{5,6},{6,5},{7,4},{8,11},{9,10},{10,... | collective-permute-start | bytes 589832 | tf_op jit(solution)/shard_map/ppermute | solution.py:386
  11.9 10.1 %collective-permute-start = (bf16[8,96,128]{2,1,0:T(8,128)(2,1)S(1)}, bf16[8,96,128]{2,1,0:T(8,128)(2,1)S(1)}, u32[]{:S(2)}, u32[]{:S(2)}) collective-permute-start(bf16[8,96,128]{2,1,0:T(8,128)(2,1)S(1)} %get-tuple-element.90), channel_id=1, source_target_pairs={{0,1},{1,0},{2,3},{3,2},{4,5},{5,4},{6,7},{7,6},{8,9},{9,8},{10,11... | collective-permute-start | bytes 589832 | tf_op jit(solution)/shard_map/ppermute | solution.py:386
  13.3 8.7 %collective-permute-start.1 = (bf16[8,96,128]{2,1,0:T(8,128)(2,1)S(1)}, bf16[8,96,128]{2,1,0:T(8,128)(2,1)S(1)}, u32[]{:S(2)}, u32[]{:S(2)}) collective-permute-start(bf16[8,96,128]{2,1,0:T(8,128)(2,1)S(1)} %get-tuple-element.91), channel_id=1, source_target_pairs={{0,2},{1,3},{2,0},{3,1},{4,6},{5,7},{6,4},{7,5},{8,10},{9,11},{10,... | collective-permute-start | bytes 589832 | tf_op jit(solution)/shard_map/ppermute | solution.py:386
  14.5 14.3 %collective-permute-start.2 = (bf16[8,96,128]{2,1,0:T(8,128)(2,1)S(1)}, bf16[8,96,128]{2,1,0:T(8,128)(2,1)S(1)}, u32[]{:S(2)}, u32[]{:S(2)}) collective-permute-start(bf16[8,96,128]{2,1,0:T(8,128)(2,1)S(1)} %get-tuple-element.92), channel_id=1, source_target_pairs={{0,3},{1,2},{2,1},{3,0},{4,7},{5,6},{6,5},{7,4},{8,11},{9,10},{10,... | collective-permute-start | bytes 589832 | tf_op jit(solution)/shard_map/ppermute | solution.py:386
  18.3 12.5 %collective-permute-start.7 = (bf16[16,16,256]{2,1,0:T(8,128)(2,1)S(1)}, bf16[16,16,256]{2,1,0:T(8,128)(2,1)S(1)}, u32[]{:S(2)}, u32[]{:S(2)}) collective-permute-start(bf16[16,16,256]{2,1,0:T(8,128)(2,1)S(1)} %get-tuple-element.101), channel_id=1, source_target_pairs={{0,4},{1,5},{2,6},{3,7},{4,0},{5,1},{6,2},{7,3},{8,12},{9,13},{10,... | collective-permute-start | bytes 393224 | tf_op jit(solution)/shard_map/ppermute | solution.py:386
  29.5 8.7 %collective-permute-start.3 = (bf16[16,16,256]{2,1,0:T(8,128)(2,1)S(1)}, bf16[16,16,256]{2,1,0:T(8,128)(2,1)S(1)}, u32[]{:S(2)}, u32[]{:S(2)}) collective-permute-start(bf16[16,16,256]{2,1,0:T(8,128)(2,1)S(1)} %get-tuple-element.95), channel_id=1, source_target_pairs={{0,4},{1,5},{2,6},{3,7},{4,0},{5,1},{6,2},{7,3},{8,12},{9,13},{10,... | collective-permute-start | bytes 393224 | tf_op jit(solution)/shard_map/ppermute | solution.py:386
  30.8 23.8 %slice-start.2 = ((s8[6291456]{0:T(1024)(128)(4,1)}), s8[4194304]{0:T(1024)(128)(4,1)S(1)}, s32[]{:S(2)}) async-start(s8[6291456]{0:T(1024)(128)(4,1)} %bitcast.13), calls=%async_computation.2 | async-start | bytes 8388608
  38.2 16.4 %slice-start.3 = ((s8[6291456]{0:T(1024)(128)(4,1)}), s8[2097152]{0:T(1024)(128)(4,1)S(1)}, s32[]{:S(2)}) async-start(s8[6291456]{0:T(1024)(128)(4,1)} %bitcast.13), calls=%async_computation.3 | async-start | bytes 4194304
  40.2 11.0 %collective-permute-start.16 = (bf16[16,16,256]{2,1,0:T(8,128)(2,1)S(1)}, bf16[16,16,256]{2,1,0:T(8,128)(2,1)S(1)}, u32[]{:S(2)}, u32[]{:S(2)}) collective-permute-start(bf16[16,16,256]{2,1,0:T(8,128)(2,1)S(1)} %get-tuple-element.116.mine_ref), channel_id=1, source_target_pairs={{0,4},{1,5},{2,6},{3,7},{4,0},{5,1},{6,2},{7,3},{8,12},{9,13},{10,... | collective-permute-start | bytes 393224 | tf_op jit(solution)/shard_map/ppermute | solution.py:386
  40.8 19.9 %collective-permute-start.8 = (bf16[16,16,256]{2,1,0:T(8,128)(2,1)S(1)}, bf16[16,16,256]{2,1,0:T(8,128)(2,1)S(1)}, u32[]{:S(2)}, u32[]{:S(2)}) collective-permute-start(bf16[16,16,256]{2,1,0:T(8,128)(2,1)S(1)} %get-tuple-element.102.mine_ref), channel_id=1, source_target_pairs={{0,4},{1,5},{2,6},{3,7},{4,0},{5,1},{6,2},{7,3},{8,12},{9,13},{10,... | collective-permute-start | bytes 393224 | tf_op jit(solution)/shard_map/ppermute | solution.py:386
  51.9 12.1 %collective-permute-start.17 = (bf16[8,96,128]{2,1,0:T(8,128)(2,1)S(1)}, bf16[8,96,128]{2,1,0:T(8,128)(2,1)S(1)}, u32[]{:S(2)}, u32[]{:S(2)}) collective-permute-start(bf16[8,96,128]{2,1,0:T(8,128)(2,1)S(1)} %get-tuple-element.118), channel_id=1, source_target_pairs={{0,1},{1,0},{2,3},{3,2},{4,5},{5,4},{6,7},{7,6},{8,9},{9,8},{10,11... | collective-permute-start | bytes 589832 | tf_op jit(solution)/shard_map/ppermute | solution.py:386
  53.4 10.8 %collective-permute-start.18 = (bf16[8,96,128]{2,1,0:T(8,128)(2,1)S(1)}, bf16[8,96,128]{2,1,0:T(8,128)(2,1)S(1)}, u32[]{:S(2)}, u32[]{:S(2)}) collective-permute-start(bf16[8,96,128]{2,1,0:T(8,128)(2,1)S(1)} %get-tuple-element.119), channel_id=1, source_target_pairs={{0,2},{1,3},{2,0},{3,1},{4,6},{5,7},{6,4},{7,5},{8,10},{9,11},{10,... | collective-permute-start | bytes 589832 | tf_op jit(solution)/shard_map/ppermute | solution.py:386
  53.4 10.8 %collective-permute-start.19 = (bf16[8,96,128]{2,1,0:T(8,128)(2,1)S(1)}, bf16[8,96,128]{2,1,0:T(8,128)(2,1)S(1)}, u32[]{:S(2)}, u32[]{:S(2)}) collective-permute-start(bf16[8,96,128]{2,1,0:T(8,128)(2,1)S(1)} %get-tuple-element.120), channel_id=1, source_target_pairs={{0,3},{1,2},{2,1},{3,0},{4,7},{5,6},{6,5},{7,4},{8,11},{9,10},{10,... | collective-permute-start | bytes 589832 | tf_op jit(solution)/shard_map/ppermute | solution.py:386
  61.5 7.4 %collective-permute-start.10 = (bf16[8,96,128]{2,1,0:T(8,128)(2,1)S(1)}, bf16[8,96,128]{2,1,0:T(8,128)(2,1)S(1)}, u32[]{:S(2)}, u32[]{:S(2)}) collective-permute-start(bf16[8,96,128]{2,1,0:T(8,128)(2,1)S(1)} %get-tuple-element.105), channel_id=1, source_target_pairs={{0,2},{1,3},{2,0},{3,1},{4,6},{5,7},{6,4},{7,5},{8,10},{9,11},{10,... | collective-permute-start | bytes 589832 | tf_op jit(solution)/shard_map/ppermute | solution.py:386
  61.7 10.1 %collective-permute-start.11 = (bf16[8,96,128]{2,1,0:T(8,128)(2,1)S(1)}, bf16[8,96,128]{2,1,0:T(8,128)(2,1)S(1)}, u32[]{:S(2)}, u32[]{:S(2)}) collective-permute-start(bf16[8,96,128]{2,1,0:T(8,128)(2,1)S(1)} %get-tuple-element.106), channel_id=1, source_target_pairs={{0,3},{1,2},{2,1},{3,0},{4,7},{5,6},{6,5},{7,4},{8,11},{9,10},{10,... | collective-permute-start | bytes 589832 | tf_op jit(solution)/shard_map/ppermute | solution.py:386
  64.1 7.8 %collective-permute-start.9 = (bf16[8,96,128]{2,1,0:T(8,128)(2,1)S(1)}, bf16[8,96,128]{2,1,0:T(8,128)(2,1)S(1)}, u32[]{:S(2)}, u32[]{:S(2)}) collective-permute-start(bf16[8,96,128]{2,1,0:T(8,128)(2,1)S(1)} %get-tuple-element.104), channel_id=1, source_target_pairs={{0,1},{1,0},{2,3},{3,2},{4,5},{5,4},{6,7},{7,6},{8,9},{9,8},{10,11... | collective-permute-start | bytes 589832 | tf_op jit(solution)/shard_map/ppermute | solution.py:386
  67.4 12.1 %collective-permute-start.20 = (bf16[8,96,128]{2,1,0:T(8,128)(2,1)S(1)}, bf16[8,96,128]{2,1,0:T(8,128)(2,1)S(1)}, u32[]{:S(2)}, u32[]{:S(2)}) collective-permute-start(bf16[8,96,128]{2,1,0:T(8,128)(2,1)S(1)} %get-tuple-element.122), channel_id=1, source_target_pairs={{0,1},{1,0},{2,3},{3,2},{4,5},{5,4},{6,7},{7,6},{8,9},{9,8},{10,11... | collective-permute-start | bytes 589832 | tf_op jit(solution)/shard_map/ppermute | solution.py:386
  68.8 10.7 %collective-permute-start.21 = (bf16[8,96,128]{2,1,0:T(8,128)(2,1)S(1)}, bf16[8,96,128]{2,1,0:T(8,128)(2,1)S(1)}, u32[]{:S(2)}, u32[]{:S(2)}) collective-permute-start(bf16[8,96,128]{2,1,0:T(8,128)(2,1)S(1)} %get-tuple-element.123), channel_id=1, source_target_pairs={{0,2},{1,3},{2,0},{3,1},{4,6},{5,7},{6,4},{7,5},{8,10},{9,11},{10,... | collective-permute-start | bytes 589832 | tf_op jit(solution)/shard_map/ppermute | solution.py:386
  68.9 11.4 %collective-permute-start.22 = (bf16[8,96,128]{2,1,0:T(8,128)(2,1)S(1)}, bf16[8,96,128]{2,1,0:T(8,128)(2,1)S(1)}, u32[]{:S(2)}, u32[]{:S(2)}) collective-permute-start(bf16[8,96,128]{2,1,0:T(8,128)(2,1)S(1)} %get-tuple-element.124), channel_id=1, source_target_pairs={{0,3},{1,2},{2,1},{3,0},{4,7},{5,6},{6,5},{7,4},{8,11},{9,10},{10,... | collective-permute-start | bytes 589832 | tf_op jit(solution)/shard_map/ppermute | solution.py:386
  75.0 12.7 %collective-permute-start.12 = (bf16[8,96,128]{2,1,0:T(8,128)(2,1)S(1)}, bf16[8,96,128]{2,1,0:T(8,128)(2,1)S(1)}, u32[]{:S(2)}, u32[]{:S(2)}) collective-permute-start(bf16[8,96,128]{2,1,0:T(8,128)(2,1)S(1)} %get-tuple-element.111), channel_id=1, source_target_pairs={{0,1},{1,0},{2,3},{3,2},{4,5},{5,4},{6,7},{7,6},{8,9},{9,8},{10,11... | collective-permute-start | bytes 589832 | tf_op jit(solution)/shard_map/ppermute | solution.py:386
  75.4 12.3 %collective-permute-start.13 = (bf16[8,96,128]{2,1,0:T(8,128)(2,1)S(1)}, bf16[8,96,128]{2,1,0:T(8,128)(2,1)S(1)}, u32[]{:S(2)}, u32[]{:S(2)}) collective-permute-start(bf16[8,96,128]{2,1,0:T(8,128)(2,1)S(1)} %get-tuple-element.112), channel_id=1, source_target_pairs={{0,2},{1,3},{2,0},{3,1},{4,6},{5,7},{6,4},{7,5},{8,10},{9,11},{10,... | collective-permute-start | bytes 589832 | tf_op jit(solution)/shard_map/ppermute | solution.py:386
  79.5 9.2 %collective-permute-start.14 = (bf16[8,96,128]{2,1,0:T(8,128)(2,1)S(1)}, bf16[8,96,128]{2,1,0:T(8,128)(2,1)S(1)}, u32[]{:S(2)}, u32[]{:S(2)}) collective-permute-start(bf16[8,96,128]{2,1,0:T(8,128)(2,1)S(1)} %get-tuple-element.113), channel_id=1, source_target_pairs={{0,3},{1,2},{2,1},{3,0},{4,7},{5,6},{6,5},{7,4},{8,11},{9,10},{10,... | collective-permute-start | bytes 589832 | tf_op jit(solution)/shard_map/ppermute | solution.py:386
  81.0 8.4 %collective-permute-start.23 = (bf16[16,16,256]{2,1,0:T(8,128)(2,1)S(1)}, bf16[16,16,256]{2,1,0:T(8,128)(2,1)S(1)}, u32[]{:S(2)}, u32[]{:S(2)}) collective-permute-start(bf16[16,16,256]{2,1,0:T(8,128)(2,1)S(1)} %get-tuple-element.126), channel_id=1, source_target_pairs={{0,4},{1,5},{2,6},{3,7},{4,0},{5,1},{6,2},{7,3},{8,12},{9,13},{10,... | collective-permute-start | bytes 393224 | tf_op jit(solution)/shard_map/ppermute | solution.py:386
  89.3 8.0 %collective-permute-start.15 = (bf16[16,16,256]{2,1,0:T(8,128)(2,1)S(1)}, bf16[16,16,256]{2,1,0:T(8,128)(2,1)S(1)}, u32[]{:S(2)}, u32[]{:S(2)}) collective-permute-start(bf16[16,16,256]{2,1,0:T(8,128)(2,1)S(1)} %get-tuple-element.115), channel_id=1, source_target_pairs={{0,4},{1,5},{2,6},{3,7},{4,0},{5,1},{6,2},{7,3},{8,12},{9,13},{10,... | collective-permute-start | bytes 393224 | tf_op jit(solution)/shard_map/ppermute | solution.py:386
  99.2 6.0 %collective-permute-start.32 = (bf16[16,16,256]{2,1,0:T(8,128)(2,1)S(1)}, bf16[16,16,256]{2,1,0:T(8,128)(2,1)S(1)}, u32[]{:S(2)}, u32[]{:S(2)}) collective-permute-start(bf16[16,16,256]{2,1,0:T(8,128)(2,1)S(1)} %get-tuple-element.140.mine_ref), channel_id=1, source_target_pairs={{0,4},{1,5},{2,6},{3,7},{4,0},{5,1},{6,2},{7,3},{8,12},{9,13},{10,... | collective-permute-start | bytes 393224 | tf_op jit(solution)/shard_map/ppermute | solution.py:386
  106.0 8.6 %collective-permute-start.33 = (bf16[8,96,128]{2,1,0:T(8,128)(2,1)S(1)}, bf16[8,96,128]{2,1,0:T(8,128)(2,1)S(1)}, u32[]{:S(2)}, u32[]{:S(2)}) collective-permute-start(bf16[8,96,128]{2,1,0:T(8,128)(2,1)S(1)} %get-tuple-element.142), channel_id=1, source_target_pairs={{0,1},{1,0},{2,3},{3,2},{4,5},{5,4},{6,7},{7,6},{8,9},{9,8},{10,11... | collective-permute-start | bytes 589832 | tf_op jit(solution)/shard_map/ppermute | solution.py:386
  108.9 4.8 %collective-permute-start.24 = (bf16[16,16,256]{2,1,0:T(8,128)(2,1)S(1)}, bf16[16,16,256]{2,1,0:T(8,128)(2,1)S(1)}, u32[]{:S(2)}, u32[]{:S(2)}) collective-permute-start(bf16[16,16,256]{2,1,0:T(8,128)(2,1)S(1)} %get-tuple-element.127.mine_ref), channel_id=1, source_target_pairs={{0,4},{1,5},{2,6},{3,7},{4,0},{5,1},{6,2},{7,3},{8,12},{9,13},{10,... | collective-permute-start | bytes 393224 | tf_op jit(solution)/shard_map/ppermute | solution.py:386
  108.9 14.3 %collective-permute-start.34 = (bf16[8,96,128]{2,1,0:T(8,128)(2,1)S(1)}, bf16[8,96,128]{2,1,0:T(8,128)(2,1)S(1)}, u32[]{:S(2)}, u32[]{:S(2)}) collective-permute-start(bf16[8,96,128]{2,1,0:T(8,128)(2,1)S(1)} %get-tuple-element.143), channel_id=1, source_target_pairs={{0,2},{1,3},{2,0},{3,1},{4,6},{5,7},{6,4},{7,5},{8,10},{9,11},{10,... | collective-permute-start | bytes 589832 | tf_op jit(solution)/shard_map/ppermute | solution.py:386
  109.4 13.8 %collective-permute-start.35 = (bf16[8,96,128]{2,1,0:T(8,128)(2,1)S(1)}, bf16[8,96,128]{2,1,0:T(8,128)(2,1)S(1)}, u32[]{:S(2)}, u32[]{:S(2)}) collective-permute-start(bf16[8,96,128]{2,1,0:T(8,128)(2,1)S(1)} %get-tuple-element.144), channel_id=1, source_target_pairs={{0,3},{1,2},{2,1},{3,0},{4,7},{5,6},{6,5},{7,4},{8,11},{9,10},{10,... | collective-permute-start | bytes 589832 | tf_op jit(solution)/shard_map/ppermute | solution.py:386
  114.5 12.3 %collective-permute-start.25 = (bf16[8,96,128]{2,1,0:T(8,128)(2,1)S(1)}, bf16[8,96,128]{2,1,0:T(8,128)(2,1)S(1)}, u32[]{:S(2)}, u32[]{:S(2)}) collective-permute-start(bf16[8,96,128]{2,1,0:T(8,128)(2,1)S(1)} %get-tuple-element.129), channel_id=1, source_target_pairs={{0,1},{1,0},{2,3},{3,2},{4,5},{5,4},{6,7},{7,6},{8,9},{9,8},{10,11... | collective-permute-start | bytes 589832 | tf_op jit(solution)/shard_map/ppermute | solution.py:386
  114.6 14.5 %collective-permute-start.26 = (bf16[8,96,128]{2,1,0:T(8,128)(2,1)S(1)}, bf16[8,96,128]{2,1,0:T(8,128)(2,1)S(1)}, u32[]{:S(2)}, u32[]{:S(2)}) collective-permute-start(bf16[8,96,128]{2,1,0:T(8,128)(2,1)S(1)} %get-tuple-element.130), channel_id=1, source_target_pairs={{0,2},{1,3},{2,0},{3,1},{4,6},{5,7},{6,4},{7,5},{8,10},{9,11},{10,... | collective-permute-start | bytes 589832 | tf_op jit(solution)/shard_map/ppermute | solution.py:386
  114.6 14.5 %collective-permute-start.27 = (bf16[8,96,128]{2,1,0:T(8,128)(2,1)S(1)}, bf16[8,96,128]{2,1,0:T(8,128)(2,1)S(1)}, u32[]{:S(2)}, u32[]{:S(2)}) collective-permute-start(bf16[8,96,128]{2,1,0:T(8,128)(2,1)S(1)} %get-tuple-element.131), channel_id=1, source_target_pairs={{0,3},{1,2},{2,1},{3,0},{4,7},{5,6},{6,5},{7,4},{8,11},{9,10},{10,... | collective-permute-start | bytes 589832 | tf_op jit(solution)/shard_map/ppermute | solution.py:386
  126.4 6.7 %collective-permute-start.36 = (bf16[8,96,128]{2,1,0:T(8,128)(2,1)S(1)}, bf16[8,96,128]{2,1,0:T(8,128)(2,1)S(1)}, u32[]{:S(2)}, u32[]{:S(2)}) collective-permute-start(bf16[8,96,128]{2,1,0:T(8,128)(2,1)S(1)} %get-tuple-element.146), channel_id=1, source_target_pairs={{0,1},{1,0},{2,3},{3,2},{4,5},{5,4},{6,7},{7,6},{8,9},{9,8},{10,11... | collective-permute-start | bytes 589832 | tf_op jit(solution)/shard_map/ppermute | solution.py:386
  126.5 8.5 %collective-permute-start.37 = (bf16[8,96,128]{2,1,0:T(8,128)(2,1)S(1)}, bf16[8,96,128]{2,1,0:T(8,128)(2,1)S(1)}, u32[]{:S(2)}, u32[]{:S(2)}) collective-permute-start(bf16[8,96,128]{2,1,0:T(8,128)(2,1)S(1)} %get-tuple-element.147), channel_id=1, source_target_pairs={{0,2},{1,3},{2,0},{3,1},{4,6},{5,7},{6,4},{7,5},{8,10},{9,11},{10,... | collective-permute-start | bytes 589832 | tf_op jit(solution)/shard_map/ppermute | solution.py:386
  126.7 8.3 %collective-permute-start.38 = (bf16[8,96,128]{2,1,0:T(8,128)(2,1)S(1)}, bf16[8,96,128]{2,1,0:T(8,128)(2,1)S(1)}, u32[]{:S(2)}, u32[]{:S(2)}) collective-permute-start(bf16[8,96,128]{2,1,0:T(8,128)(2,1)S(1)} %get-tuple-element.148), channel_id=1, source_target_pairs={{0,3},{1,2},{2,1},{3,0},{4,7},{5,6},{6,5},{7,4},{8,11},{9,10},{10,... | collective-permute-start | bytes 589832 | tf_op jit(solution)/shard_map/ppermute | solution.py:386
  132.3 7.2 %collective-permute-start.28 = (bf16[8,96,128]{2,1,0:T(8,128)(2,1)S(1)}, bf16[8,96,128]{2,1,0:T(8,128)(2,1)S(1)}, u32[]{:S(2)}, u32[]{:S(2)}) collective-permute-start(bf16[8,96,128]{2,1,0:T(8,128)(2,1)S(1)} %get-tuple-element.135), channel_id=1, source_target_pairs={{0,1},{1,0},{2,3},{3,2},{4,5},{5,4},{6,7},{7,6},{8,9},{9,8},{10,11... | collective-permute-start | bytes 589832 | tf_op jit(solution)/shard_map/ppermute | solution.py:386
  133.1 8.0 %collective-permute-start.29 = (bf16[8,96,128]{2,1,0:T(8,128)(2,1)S(1)}, bf16[8,96,128]{2,1,0:T(8,128)(2,1)S(1)}, u32[]{:S(2)}, u32[]{:S(2)}) collective-permute-start(bf16[8,96,128]{2,1,0:T(8,128)(2,1)S(1)} %get-tuple-element.136), channel_id=1, source_target_pairs={{0,2},{1,3},{2,0},{3,1},{4,6},{5,7},{6,4},{7,5},{8,10},{9,11},{10,... | collective-permute-start | bytes 589832 | tf_op jit(solution)/shard_map/ppermute | solution.py:386
  133.1 12.5 %collective-permute-start.30 = (bf16[8,96,128]{2,1,0:T(8,128)(2,1)S(1)}, bf16[8,96,128]{2,1,0:T(8,128)(2,1)S(1)}, u32[]{:S(2)}, u32[]{:S(2)}) collective-permute-start(bf16[8,96,128]{2,1,0:T(8,128)(2,1)S(1)} %get-tuple-element.137), channel_id=1, source_target_pairs={{0,3},{1,2},{2,1},{3,0},{4,7},{5,6},{6,5},{7,4},{8,11},{9,10},{10,... | collective-permute-start | bytes 589832 | tf_op jit(solution)/shard_map/ppermute | solution.py:386
  135.8 10.6 %collective-permute-start.39 = (bf16[16,16,256]{2,1,0:T(8,128)(2,1)S(1)}, bf16[16,16,256]{2,1,0:T(8,128)(2,1)S(1)}, u32[]{:S(2)}, u32[]{:S(2)}) collective-permute-start(bf16[16,16,256]{2,1,0:T(8,128)(2,1)S(1)} %get-tuple-element.150), channel_id=1, source_target_pairs={{0,4},{1,5},{2,6},{3,7},{4,0},{5,1},{6,2},{7,3},{8,12},{9,13},{10,... | collective-permute-start | bytes 393224 | tf_op jit(solution)/shard_map/ppermute | solution.py:386
  146.3 8.2 %collective-permute-start.31 = (bf16[16,16,256]{2,1,0:T(8,128)(2,1)S(1)}, bf16[16,16,256]{2,1,0:T(8,128)(2,1)S(1)}, u32[]{:S(2)}, u32[]{:S(2)}) collective-permute-start(bf16[16,16,256]{2,1,0:T(8,128)(2,1)S(1)} %get-tuple-element.139), channel_id=1, source_target_pairs={{0,4},{1,5},{2,6},{3,7},{4,0},{5,1},{6,2},{7,3},{8,12},{9,13},{10,... | collective-permute-start | bytes 393224 | tf_op jit(solution)/shard_map/ppermute | solution.py:386
  156.4 5.7 %collective-permute-start.44 = (bf16[16,16,256]{2,1,0:T(8,128)(2,1)S(1)}, bf16[16,16,256]{2,1,0:T(8,128)(2,1)S(1)}, u32[]{:S(2)}, u32[]{:S(2)}) collective-permute-start(bf16[16,16,256]{2,1,0:T(8,128)(2,1)S(1)} %get-tuple-element.159.mine_ref), channel_id=1, source_target_pairs={{0,4},{1,5},{2,6},{3,7},{4,0},{5,1},{6,2},{7,3},{8,12},{9,13},{10,... | collective-permute-start | bytes 393224 | tf_op jit(solution)/shard_map/ppermute | solution.py:386
  162.9 9.0 %collective-permute-start.45 = (bf16[8,96,128]{2,1,0:T(8,128)(2,1)S(1)}, bf16[8,96,128]{2,1,0:T(8,128)(2,1)S(1)}, u32[]{:S(2)}, u32[]{:S(2)}) collective-permute-start(bf16[8,96,128]{2,1,0:T(8,128)(2,1)S(1)} %get-tuple-element.161), channel_id=1, source_target_pairs={{0,1},{1,0},{2,3},{3,2},{4,5},{5,4},{6,7},{7,6},{8,9},{9,8},{10,11... | collective-permute-start | bytes 589832 | tf_op jit(solution)/shard_map/ppermute | solution.py:386
  162.9 7.3 %collective-permute-start.40 = (bf16[16,16,256]{2,1,0:T(8,128)(2,1)S(1)}, bf16[16,16,256]{2,1,0:T(8,128)(2,1)S(1)}, u32[]{:S(2)}, u32[]{:S(2)}) collective-permute-start(bf16[16,16,256]{2,1,0:T(8,128)(2,1)S(1)} %get-tuple-element.151.mine_ref), channel_id=1, source_target_pairs={{0,4},{1,5},{2,6},{3,7},{4,0},{5,1},{6,2},{7,3},{8,12},{9,13},{10,... | collective-permute-start | bytes 393224 | tf_op jit(solution)/shard_map/ppermute | solution.py:386
  163.0 16.8 %collective-permute-start.46 = (bf16[8,96,128]{2,1,0:T(8,128)(2,1)S(1)}, bf16[8,96,128]{2,1,0:T(8,128)(2,1)S(1)}, u32[]{:S(2)}, u32[]{:S(2)}) collective-permute-start(bf16[8,96,128]{2,1,0:T(8,128)(2,1)S(1)} %get-tuple-element.162), channel_id=1, source_target_pairs={{0,2},{1,3},{2,0},{3,1},{4,6},{5,7},{6,4},{7,5},{8,10},{9,11},{10,... | collective-permute-start | bytes 589832 | tf_op jit(solution)/shard_map/ppermute | solution.py:386
  164.9 14.9 %collective-permute-start.47 = (bf16[8,96,128]{2,1,0:T(8,128)(2,1)S(1)}, bf16[8,96,128]{2,1,0:T(8,128)(2,1)S(1)}, u32[]{:S(2)}, u32[]{:S(2)}) collective-permute-start(bf16[8,96,128]{2,1,0:T(8,128)(2,1)S(1)} %get-tuple-element.163), channel_id=1, source_target_pairs={{0,3},{1,2},{2,1},{3,0},{4,7},{5,6},{6,5},{7,4},{8,11},{9,10},{10,... | collective-permute-start | bytes 589832 | tf_op jit(solution)/shard_map/ppermute | solution.py:386
  171.1 15.6 %collective-permute-start.41 = (bf16[8,96,128]{2,1,0:T(8,128)(2,1)S(1)}, bf16[8,96,128]{2,1,0:T(8,128)(2,1)S(1)}, u32[]{:S(2)}, u32[]{:S(2)}) collective-permute-start(bf16[8,96,128]{2,1,0:T(8,128)(2,1)S(1)} %get-tuple-element.153), channel_id=1, source_target_pairs={{0,1},{1,0},{2,3},{3,2},{4,5},{5,4},{6,7},{7,6},{8,9},{9,8},{10,11... | collective-permute-start | bytes 589832 | tf_op jit(solution)/shard_map/ppermute | solution.py:386
  171.8 14.8 %collective-permute-start.42 = (bf16[8,96,128]{2,1,0:T(8,128)(2,1)S(1)}, bf16[8,96,128]{2,1,0:T(8,128)(2,1)S(1)}, u32[]{:S(2)}, u32[]{:S(2)}) collective-permute-start(bf16[8,96,128]{2,1,0:T(8,128)(2,1)S(1)} %get-tuple-element.154), channel_id=1, source_target_pairs={{0,2},{1,3},{2,0},{3,1},{4,6},{5,7},{6,4},{7,5},{8,10},{9,11},{10,... | collective-permute-start | bytes 589832 | tf_op jit(solution)/shard_map/ppermute | solution.py:386
  171.8 14.8 %collective-permute-start.43 = (bf16[8,96,128]{2,1,0:T(8,128)(2,1)S(1)}, bf16[8,96,128]{2,1,0:T(8,128)(2,1)S(1)}, u32[]{:S(2)}, u32[]{:S(2)}) collective-permute-start(bf16[8,96,128]{2,1,0:T(8,128)(2,1)S(1)} %get-tuple-element.155), channel_id=1, source_target_pairs={{0,3},{1,2},{2,1},{3,0},{4,7},{5,6},{6,5},{7,4},{8,11},{9,10},{10,... | collective-permute-start | bytes 589832 | tf_op jit(solution)/shard_map/ppermute | solution.py:386
  186.7 40.3 %copy-start.7 = (f32[96]{0:T(128)S(1)}, f32[96]{0:T(128)}, u32[]{:S(2)}) copy-start(f32[96]{0:T(128)} %param.15) | copy-start | bytes 1156
  193.5 12.0 %collective-permute-start.54 = (f32[96,1024]{1,0:T(8,128)S(1)}, f32[96,1024]{1,0:T(8,128)S(1)}, u32[]{:S(2)}, u32[]{:S(2)}) collective-permute-start(f32[96,1024]{1,0:T(8,128)S(1)} %get-tuple-element.173.layer_ref.refs_3_), channel_id=1, source_target_pairs={{0,8},{8,0},{16,24},{24,16},{1,9},{9,1},{17,25},{25,17},{2,10},{10... | collective-permute-start | bytes 1179656 | tf_op jit(solution)/shard_map/ppermute | solution.py:561
  203.6 23.6 %collective-permute-start.48 = (f32[96,1024]{1,0:T(8,128)S(1)}, f32[96,1024]{1,0:T(8,128)S(1)}, u32[]{:S(2)}, u32[]{:S(2)}) collective-permute-start(f32[96,1024]{1,0:T(8,128)S(1)} %get-tuple-element.172.refs_2_), channel_id=1, source_target_pairs={{0,8},{8,16},{16,24},{1,9},{9,17},{17,25},{2,10},{10,18},{18,26},{... | collective-permute-start | bytes 1179656 | tf_op jit(solution)/shard_map/ppermute | solution.py:554
  206.1 8.3 %collective-permute-start.55 = (f32[48,1024]{1,0:T(8,128)S(1)}, f32[48,1024]{1,0:T(8,128)S(1)}, u32[]{:S(2)}, u32[]{:S(2)}) collective-permute-start(f32[48,1024]{1,0:T(8,128)S(1)} %pair.1), channel_id=1, source_target_pairs={{0,16},{8,24},{1,17},{9,25},{2,18},{10,26},{3,19},{11,27},{4,20},{... | collective-permute-start | bytes 589832 | tf_op jit(solution)/shard_map/ppermute | solution.py:554
  214.4 12.7 %collective-permute-start.56 = (f32[48,1024]{1,0:T(8,128)S(1)}, f32[48,1024]{1,0:T(8,128)S(1)}, u32[]{:S(2)}, u32[]{:S(2)}) collective-permute-start(f32[48,1024]{1,0:T(8,128)S(1)} %collective-permute-done.55.refs_13_), channel_id=1, source_target_pairs={{0,8},{8,0},{16,24},{24,16},{1,9},{9,1},{17,25},{25,17},{2,10},{10... | collective-permute-start | bytes 589832 | tf_op jit(solution)/shard_map/ppermute | solution.py:580
  214.4 5.2 %collective-permute-start.49 = (f32[2,1024]{1,0:T(2,128)S(1)}, f32[2,1024]{1,0:T(2,128)S(1)}, u32[]{:S(2)}, u32[]{:S(2)}) collective-permute-start(f32[2,1024]{1,0:T(2,128)S(1)} %get-tuple-element.174), channel_id=1, source_target_pairs={{0,1},{1,2},{2,3},{3,4},{4,5},{5,6},{6,7},{7,0},{8,9},{9,10},{10,1... | collective-permute-start | bytes 24584 | tf_op jit(solution)/shard_map/ppermute | solution.py:563
  215.6 4.1 %collective-permute-start.50 = (f32[2,1024]{1,0:T(2,128)S(1)}, f32[2,1024]{1,0:T(2,128)S(1)}, u32[]{:S(2)}, u32[]{:S(2)}) collective-permute-start(f32[2,1024]{1,0:T(2,128)S(1)} %get-tuple-element.175), channel_id=1, source_target_pairs={{1,0},{2,1},{3,2},{4,3},{5,4},{6,5},{7,6},{0,7},{9,8},{10,9},{11,1... | collective-permute-start | bytes 24584 | tf_op jit(solution)/shard_map/ppermute | solution.py:564
  219.7 7.4 %collective-permute-start.51 = (f32[2,1024]{1,0:T(2,128)S(1)}, f32[2,1024]{1,0:T(2,128)S(1)}, u32[]{:S(2)}, u32[]{:S(2)}) collective-permute-start(f32[2,1024]{1,0:T(2,128)S(1)} %pad_maximum_fusion), channel_id=1, source_target_pairs={{0,8},{8,16},{16,24},{1,9},{9,17},{17,25},{2,10},{10,18},{18,26},{... | collective-permute-start | bytes 24584 | tf_op jit(solution)/shard_map/ppermute | solution.py:554
  225.0 2.1 collective-permute-start.52
  226.3 0.8 collective-permute-start.53
  (5 other events, 35.6 us)

commit v4 on v3

--- a/solution.py
+++ b/solution.py
@@ -185,6 +185,12 @@
             back_refs[d][g] = back[d * rows : (d + 1) * rows].astype(BF)
 
 
+def gelu(x):
+    scale = math.sqrt(2.0 / math.pi)
+    half = 0.5 * x
+    return half + half * jnp.tanh(x * (scale + (scale * 0.044715) * (x * x)))
+
+
 def spread_of(pack, back_refs, table_ref):
     width = LANES // pack
     blocks = []
@@ -201,7 +207,7 @@
     state_ref, near_refs = refs[peers + 3], refs[peers + 4 :]
     count, rows, cells = state_ref.shape
     point = point_ref[...].reshape(count * rows, cells)
-    updated = jax.nn.gelu(spread_of(pack, back_refs, inverse_ref) + point, approximate=True)
+    updated = gelu(spread_of(pack, back_refs, inverse_ref) + point)
     state = updated.astype(BF)
     state_ref[...] = state.reshape(count, rows, cells)
     store_near(state, forward_ref[...], near_refs, pack, rows)
@@ -216,7 +222,7 @@
     count, rows, cells = updated_ref.shape
     group = pl.program_id(0)
     point = point_ref[...].reshape(count * rows, cells)
-    updated = jax.nn.gelu(spread_of(pack, back_refs, inverse_ref) + point, approximate=True)
+    updated = gelu(spread_of(pack, back_refs, inverse_ref) + point)
     updated_ref[...] = updated.reshape(count, rows, cells)
 
     @pl.when(group == 0)
@@ -258,10 +264,12 @@
             high_ref[i : i + 1] = field_refs[f][rows - 1 :]
 
 
-def pair_kernel(me_ref, layer_ref, other_ref, both_ref):
-    half = both_ref.shape[0]
+def pair_kernel(me_ref, layer_ref, other_ref, rims_ref, other_rims_ref, both_ref):
+    half = layer_ref.shape[0] // 2
     at = pl.ds(pl.multiple_of((me_ref[1] & 1) * half, 8), half)
-    both_ref[...] = layer_ref[at, :] + other_ref[at, :]
+    both_ref[:half] = layer_ref[at, :] + other_ref[at, :]
+    both_ref[half : half + 2] = rims_ref[...] + other_rims_ref[...]
+    both_ref[half + 2 :] = jnp.zeros((both_ref.shape[0] - half - 2, both_ref.shape[1]), F32)
 
 
 def pointwise_kernel(chunks, block, *refs):
@@ -276,26 +284,29 @@
         out_ref[:, at] = out.reshape(channels, block, cells)
 
 
-def residual_kernel(paired, shifts, *refs):
+def residual_kernel(paired, *refs):
     east_ref, north_ref, upward_ref, layer_ref, below_ref, before_ref, after_ref = refs[:7]
-    shift_refs, rest, out_ref = refs[7 : 7 + shifts], refs[7 + shifts : -1], refs[-1]
+    turning_ref, rims_ref, rest, out_ref = refs[7], refs[8], refs[9:-1], refs[-1]
     rows, cells = layer_ref.shape
     geopotential = layer_ref[...]
-    turning_ref, lower_refs = rest[0], rest[1:]
+    rims = rims_ref[...]
     if paired:
-        me_ref, other_ref, mine_ref, partner_ref = lower_refs
+        me_ref, other_ref, other_rims_ref, mine_ref, partner_ref = rest
         odd = (me_ref[1] & 1) == 1
-        mine, theirs = mine_ref[...], partner_ref[...]
+        half = rows // 2
+        mine, theirs = mine_ref[:half], partner_ref[:half]
         lower = jnp.concatenate(
             [jnp.where(odd, theirs, mine), jnp.where(odd, mine, theirs)], 0
         )
         geopotential = geopotential + jnp.where(odd, other_ref[...], 0.0) + lower
+        rims = rims + jnp.where(odd, other_rims_ref[...], 0.0) + mine_ref[half : half + 2]
     else:
-        for ref in lower_refs:
+        count = len(rest) // 2
+        for ref in rest[:count]:
             geopotential = geopotential + ref[...]
-    rims = [before_ref[1:2], after_ref[1:2]]
-    for ref in shift_refs:
-        rims = [rims[0] + ref[:1], rims[1] + ref[1:2]]
+        for ref in rest[count:]:
+            rims = rims + ref[...]
+    rims = [rims[:1], rims[1:]]
     row = lax.broadcasted_iota(jnp.int32, (rows, cells), 0)
 
     def along_x(field):
@@ -388,7 +399,8 @@
     cells_spec = pl.BlockSpec((many * pack, rows, cells), lambda i: (i, 0, 0))
     lane_spec = pl.BlockSpec((many, rows, LANES), lambda i: (i, 0, 0))
     lane_shape = jax.ShapeDtypeStruct((part, rows, LANES), BF)
-    mode_spec = pl.BlockSpec((many * pack, own, 2 * ymodes), lambda i: (i, 0, 0))
+    mode_spec = whole((size, own, 2 * ymodes))
+    part_spec = whole((part, rows, LANES))
     tile = size * rows * cells
 
     def offset_spec(n):
@@ -412,8 +424,8 @@
     def forward_y(parts):
         return pl.pallas_call(
             functools.partial(forward_y_kernel, pack, own, peers),
-            grid=(part // many,),
-            in_specs=[lane_spec] * peers + [whole(row_table.shape)],
+            grid=(1,),
+            in_specs=[part_spec] * peers + [whole(row_table.shape)],
             out_specs=[mode_spec] * 2,
             out_shape=[
                 jax.ShapeDtypeStruct((size, own, 2 * ymodes), F32),
@@ -444,9 +456,9 @@
     def inverse_y(mine, theirs):
         return pl.pallas_call(
             functools.partial(inverse_y_kernel, pack, peers),
-            grid=(part // many,),
+            grid=(1,),
             in_specs=[mode_spec] * 2 + [whole(row_table.shape)],
-            out_specs=[lane_spec] * peers,
+            out_specs=[part_spec] * peers,
             out_shape=[lane_shape] * peers,
             compiler_params=params(8, "arbitrary"),
             cost_estimate=cost(4 * part * LANES * peers * rows * ymodes, 2 * size * rows * wide),
@@ -562,29 +574,29 @@
     below = from_below(upward, 1)
     before = lax.ppermute(high, "gy", up)
     after = lax.ppermute(low, "gy", down)
+    rims = jnp.concatenate([before[1:], after[1:]], 0)
     if pairs:
+        other_rims = lax.ppermute(rims, "lev", partner)
         both = pl.pallas_call(
             pair_kernel,
-            in_specs=[smem, vmem, vmem],
+            in_specs=[smem] + [vmem] * 4,
             out_specs=vmem,
-            out_shape=jax.ShapeDtypeStruct((rows // 2, cells), F32),
+            out_shape=jax.ShapeDtypeStruct((rows // 2 + 8, cells), F32),
             compiler_params=params(2),
             cost_estimate=cost(rows * cells, 8 * rows * cells),
             name="pair",
-        )(me, layer, other)
+        )(me, layer, other, rims, other_rims)
         lower = from_below(both, 2)
         step = 2
         while step < levels - 2:
             lower = lower + from_below(lower, step)
             step *= 2
-        lowers = [me, other, lower, lax.ppermute(lower, "lev", partner)]
+        lowers = [me, other, other_rims, lower, lax.ppermute(lower, "lev", partner)]
     else:
-        lowers = [from_below(layer, step) for step in range(1, levels)]
-    rims = jnp.concatenate([before[1:], after[1:]], 0)
-    shifts = [from_below(rims, step) for step in range(1, levels)]
+        lowers = [from_below(v, step) for v in (layer, rims) for step in range(1, levels)]
     residual = pl.pallas_call(
-        functools.partial(residual_kernel, pairs, len(shifts)),
-        in_specs=[vmem] * (8 + len(shifts))
+        functools.partial(residual_kernel, pairs),
+        in_specs=[vmem] * 9
         + ([smem] if pairs else [vmem])
         + [vmem] * (len(lowers) - 1),
         out_specs=vmem,
@@ -592,7 +604,18 @@
         compiler_params=params(10),
         cost_estimate=cost(20 * rows * cells, 36 * rows * cells),
         name="residual",
-    )(east, north, upward, layer, below, before, after, *shifts, coriolis[:, None], *lowers)
+    )(
+        east,
+        north,
+        upward,
+        layer,
+        below,
+        before,
+        after,
+        coriolis[:, None],
+        rims,
+        *lowers,
+    )
     return updated[None], residual[:, None]
 
 

time: 232 us -> 226 us (0.974)
  Pallas kernels: 75.3 us -> 72.2 us
    ppermute x5 -> x2, starting transfers between devices: 10.7 us -> 5.53 us  [from_below(): lax.ppermute(value, 'lev', [(s, s + step) for s in range(levels - step)])]
    ppermute x1 -> x2, starting transfers between devices: 0.01 us -> 3.22 us  [the longest x1 2 us: on_device(): lowers = [me, other, other_rims, lower, lax.ppermute(lower, 'lev', partner)]]
    ppermute x48, starting transfers between devices: 41.6 us -> 44.6 us  [swap(): return lax.ppermute(value, 'gy', [(g, g ^ distance) for g in range(slices)])]
    ppermute x5 -> x2, waiting for transfers between devices: 6.87 us -> 5.57 us  [from_below(): lax.ppermute(value, 'lev', [(s, s + step) for s in range(levels - step)])]
  transfers between devices with their start and end apart: 57 -> 55, of which waited for: 21 -> 23; matrix products, arithmetic and copies ran while one was open for 0% -> 0% of each run, Pallas kernels for 24% -> 23%
where the time goes in v4:
time: 226 us; the launch traced here: 225 us
  waiting for transfers between devices  82.6 us (37%)
  Pallas kernels  72.2 us (32%)
  starting transfers between devices  68 us (30%)
    ppermute x48, waiting for transfers between devices, swap(): return lax.ppermute(value, 'gy', [(g, g ^ distance) for g in range(slices)])  75.2 us
    ppermute x48, starting transfers between devices, swap(): return lax.ppermute(value, 'gy', [(g, g ^ distance) for g in range(slices)])  44.6 us
    pallas_call x3, Pallas kernels, pointwise(): pl.pallas_call(functools.partial(pointwise_kernel, len(states), block), g...  18 us
    pallas_call x2, Pallas kernels, last(): pl.pallas_call(functools.partial(last_kernel, pack, peers, n * size, kind...  13.6 us
    pallas_call x4, Pallas kernels, update(): pl.pallas_call(functools.partial(update_kernel, pack, peers), grid=(part...  12.1 us
    pallas_call x6, Pallas kernels, mix(): pl.pallas_call(functools.partial(mix_kernel, n, CHUNKS), in_specs=[vmem]...  11.5 us
    ppermute x1, starting transfers between devices, on_device(): other = lax.ppermute(layer, 'lev', partner)  10.4 us
    pallas_call x2, Pallas kernels, near_of(): pl.pallas_call(functools.partial(near_kernel, pack), grid=(part // many,)...  5.78 us
  transfers between devices with their start and end apart: 55, of which 23 were waited for; matrix products, arithmetic and copies ran while one was open for 0% of the time, Pallas kernels for 23%

profile of v4, /device:TPU:1, one launch (start us, length us, event | category | flops | bytes accessed | tf_op | source)
XLA Modules:
  0.0 225.3 jit_solution(13684794438625421731)
XLA Ops:
  2.7 2.9 %near.3 = (bf16[8,96,128]{2,1,0:T(8,128)(2,1)S(1)}, bf16[8,96,128]{2,1,0:T(8,128)(2,1)S(1)}, bf16[8,96,128]{2,1,0:T(8,128)(2,1)S(1)}, bf16[8,96,128]{2,1,0:T(8,128)(2,1)S(1)}) custom-call(bf16[32,96,1024]{2,1,0:T(8,128)(2,1)} %bitcast.11, bf16[1024,256]{1,0:T(8,128)(2,1)S(1)} %forward_table.1.table_ref.refs_6_), custom_call_target="tpu_custom_call" | custom-call | flops 805306368 | bytes 3145728 | tf_op jit(solution)/shard_map/near/pallas_call | solution.py:410
  5.6 2.1 collective-permute-start.4
  7.7 1.3 collective-permute-start.5
  9.0 2.9 %near.2 = (bf16[8,96,128]{2,1,0:T(8,128)(2,1)S(1)}, bf16[8,96,128]{2,1,0:T(8,128)(2,1)S(1)}, bf16[8,96,128]{2,1,0:T(8,128)(2,1)S(1)}, bf16[8,96,128]{2,1,0:T(8,128)(2,1)S(1)}) custom-call(bf16[32,96,1024]{2,1,0:T(8,128)(2,1)} %bitcast.12, bf16[1024,256]{1,0:T(8,128)(2,1)S(1)} %forward_table.1.table_ref.refs_6_), custom_call_target="tpu_custom_call" | custom-call | flops 805306368 | bytes 3145728 | tf_op jit(solution)/shard_map/near/pallas_call | solution.py:410
  11.9 1.4 collective-permute-start
  15.5 2.1 collective-permute-done.6.refs_3_
  18.0 2.2 collective-permute-start.7
  20.3 1.7 collective-permute-done.refs_1_
  22.0 6.8 %collective-permute-done.2.refs_3_ = bf16[8,96,128]{2,1,0:T(8,128)(2,1)S(1)} collective-permute-done((bf16[8,96,128]{2,1,0:T(8,128)(2,1)S(1)}, bf16[8,96,128]{2,1,0:T(8,128)(2,1)S(1)}, u32[]{:S(2)}, u32[]{:S(2)}) %collective-permute-start.2) | collective-permute-done | bytes 196640 | tf_op jit(solution)/shard_map/ppermute | solution.py:397
  29.3 1.4 collective-permute-start.3
  30.7 1.8 mix.6.refs_3_
  32.6 5.4 %collective-permute-done.3.refs_1_ = bf16[16,16,256]{2,1,0:T(8,128)(2,1)S(1)} collective-permute-done((bf16[16,16,256]{2,1,0:T(8,128)(2,1)S(1)}, bf16[16,16,256]{2,1,0:T(8,128)(2,1)S(1)}, u32[]{:S(2)}, u32[]{:S(2)}) %collective-permute-start.3) | collective-permute-done | bytes 131104 | tf_op jit(solution)/shard_map/ppermute | solution.py:397
  38.0 1.9 mix.7
  40.6 2.4 %collective-permute-start.8 = (bf16[16,16,256]{2,1,0:T(8,128)(2,1)S(1)}, bf16[16,16,256]{2,1,0:T(8,128)(2,1)S(1)}, u32[]{:S(2)}, u32[]{:S(2)}) collective-permute-start(bf16[16,16,256]{2,1,0:T(8,128)(2,1)S(1)} %get-tuple-element.102.mine_ref), channel_id=1, source_target_pairs={{0,4},{1,5},{2,6},{3,7},{4,0},{5,1},{6,2},{7,3},{8,12},{9,13},{10,... | collective-permute-start | bytes 393224 | tf_op jit(solution)/shard_map/ppermute | solution.py:397
  42.9 8.4 %collective-permute-done.16.theirs_ref = bf16[16,16,256]{2,1,0:T(8,128)(2,1)S(1)} collective-permute-done((bf16[16,16,256]{2,1,0:T(8,128)(2,1)S(1)}, bf16[16,16,256]{2,1,0:T(8,128)(2,1)S(1)}, u32[]{:S(2)}, u32[]{:S(2)}) %collective-permute-start.16) | collective-permute-done | bytes 131104 | tf_op jit(solution)/shard_map/ppermute | solution.py:397
  52.9 1.7 collective-permute-start.19
  54.7 6.0 %pointwise.3.refs_4_ = f32[32,96,1024]{2,1,0:T(8,128)S(1)} custom-call(bf16[32,96,1024]{2,1,0:T(8,128)(2,1)S(1)} %bitcast.15, bf16[32,96,1024]{2,1,0:T(8,128)(2,1)S(1)} %bitcast.16, bf16[512,512]{1,0:T(8,128)(2,1)S(1)} %get-tuple-element.107.refs_2_.refs_3_, f32[512,1]{1,0:T(8,128)S(1)} %get-tuple-element.108.refs_3_.refs_4_), custom_call_target="tpu_custom_call" | custom-call | flops 3221225472 | bytes 25165824 | tf_op jit(solution)/shard_map/pointwise/pallas_call | solution.py:473
  61.3 2.1 collective-permute-start.11
  64.0 3.0 %update.5 = (bf16[16,96,1024]{2,1,0:T(8,128)(2,1)S(1)}, bf16[8,96,128]{2,1,0:T(8,128)(2,1)S(1)}, bf16[8,96,128]{2,1,0:T(8,128)(2,1)S(1)}, bf16[8,96,128]{2,1,0:T(8,128)(2,1)S(1)}, bf16[8,96,128]{2,1,0:T(8,128)(2,1)S(1)}) custom-call(bf16[8,96,128]{2,1,0:T(8,128)(2,1)S(1)} %get-tuple-element.117.refs_0_, ...), custom_call_target="tpu_custom_call" | custom-call | flops 1610612736 | bytes 9437184 | tf_op jit(solution)/shard_map/update/pallas_call | solution.py:492
  68.1 1.6 collective-permute-start.22
  69.7 1.5 collective-permute-done.11.refs_3_
  71.2 3.0 %update.4 = (bf16[16,96,1024]{2,1,0:T(8,128)(2,1)S(1)}, bf16[8,96,128]{2,1,0:T(8,128)(2,1)S(1)}, bf16[8,96,128]{2,1,0:T(8,128)(2,1)S(1)}, bf16[8,96,128]{2,1,0:T(8,128)(2,1)S(1)}, bf16[8,96,128]{2,1,0:T(8,128)(2,1)S(1)}) custom-call(bf16[8,96,128]{2,1,0:T(8,128)(2,1)S(1)} %get-tuple-element.103.refs_0_, ...), custom_call_target="tpu_custom_call" | custom-call | flops 1610612736 | bytes 9437184 | tf_op jit(solution)/shard_map/update/pallas_call | solution.py:492
  75.1 3.7 %collective-permute-done.20.refs_1_ = bf16[8,96,128]{2,1,0:T(8,128)(2,1)S(1)} collective-permute-done((bf16[8,96,128]{2,1,0:T(8,128)(2,1)S(1)}, bf16[8,96,128]{2,1,0:T(8,128)(2,1)S(1)}, u32[]{:S(2)}, u32[]{:S(2)}) %collective-permute-start.20) | collective-permute-done | bytes 196640 | tf_op jit(solution)/shard_map/ppermute | solution.py:397
  80.1 1.3 collective-permute-start.23
  81.4 5.3 %collective-permute-done.12.refs_1_ = bf16[8,96,128]{2,1,0:T(8,128)(2,1)S(1)} collective-permute-done((bf16[8,96,128]{2,1,0:T(8,128)(2,1)S(1)}, bf16[8,96,128]{2,1,0:T(8,128)(2,1)S(1)}, u32[]{:S(2)}, u32[]{:S(2)}) %collective-permute-start.12) | collective-permute-done | bytes 196640 | tf_op jit(solution)/shard_map/ppermute | solution.py:397
  86.7 1.6 collective-permute-done.14.refs_3_
  88.9 1.8 mix.8.refs_3_
  90.7 7.0 %collective-permute-done.15.refs_1_ = bf16[16,16,256]{2,1,0:T(8,128)(2,1)S(1)} collective-permute-done((bf16[16,16,256]{2,1,0:T(8,128)(2,1)S(1)}, bf16[16,16,256]{2,1,0:T(8,128)(2,1)S(1)}, u32[]{:S(2)}, u32[]{:S(2)}) %collective-permute-start.15) | collective-permute-done | bytes 131104 | tf_op jit(solution)/shard_map/ppermute | solution.py:397
  97.7 2.1 mix.9
  99.9 4.9 %collective-permute-done.32.theirs_ref = bf16[16,16,256]{2,1,0:T(8,128)(2,1)S(1)} collective-permute-done((bf16[16,16,256]{2,1,0:T(8,128)(2,1)S(1)}, bf16[16,16,256]{2,1,0:T(8,128)(2,1)S(1)}, u32[]{:S(2)}, u32[]{:S(2)}) %collective-permute-start.32) | collective-permute-done | bytes 131104 | tf_op jit(solution)/shard_map/ppermute | solution.py:397
  106.3 1.8 collective-permute-start.34
  109.0 2.7 %collective-permute-done.24.theirs_ref = bf16[16,16,256]{2,1,0:T(8,128)(2,1)S(1)} collective-permute-done((bf16[16,16,256]{2,1,0:T(8,128)(2,1)S(1)}, bf16[16,16,256]{2,1,0:T(8,128)(2,1)S(1)}, u32[]{:S(2)}, u32[]{:S(2)}) %collective-permute-start.24) | collective-permute-done | bytes 131104 | tf_op jit(solution)/shard_map/ppermute | solution.py:397
  112.2 1.3 collective-permute-start.25
  113.5 1.4 collective-permute-start.27
  115.0 6.0 %pointwise.4.refs_4_ = f32[32,96,1024]{2,1,0:T(8,128)S(1)} custom-call(bf16[16,96,1024]{2,1,0:T(8,128)(2,1)S(1)} %get-tuple-element.132.refs_0_, bf16[16,96,1024]{2,1,0:T(8,128)(2,1)S(1)} %get-tuple-element.133.refs_1_, bf16[32,96,1024]{2,1,0:T(8,128)(2,1)S(1)} %bitcast.17, bf16[512,512]{1,0:T(8,128)(2,1)S(1)} %get-tuple-element.107.refs_2_.refs_3_, ...), custom_call_target="tpu_custom_call" | custom-call | flops 3221225472 | bytes 25165824 | tf_op jit(solution)/shard_map/pointwise/pallas_call | solution.py:473
  121.0 3.0 %update.7 = (bf16[16,96,1024]{2,1,0:T(8,128)(2,1)S(1)}, bf16[8,96,128]{2,1,0:T(8,128)(2,1)S(1)}, bf16[8,96,128]{2,1,0:T(8,128)(2,1)S(1)}, bf16[8,96,128]{2,1,0:T(8,128)(2,1)S(1)}, bf16[8,96,128]{2,1,0:T(8,128)(2,1)S(1)}) custom-call(bf16[8,96,128]{2,1,0:T(8,128)(2,1)S(1)} %get-tuple-element.141.refs_0_, ...), custom_call_target="tpu_custom_call" | custom-call | flops 1610612736 | bytes 9437184 | tf_op jit(solution)/shard_map/update/pallas_call | solution.py:492
  124.0 1.3 collective-permute-start.36
  125.3 1.4 collective-permute-start.38
  126.8 3.0 %update.6 = (bf16[16,96,1024]{2,1,0:T(8,128)(2,1)S(1)}, bf16[8,96,128]{2,1,0:T(8,128)(2,1)S(1)}, bf16[8,96,128]{2,1,0:T(8,128)(2,1)S(1)}, bf16[8,96,128]{2,1,0:T(8,128)(2,1)S(1)}, bf16[8,96,128]{2,1,0:T(8,128)(2,1)S(1)}) custom-call(bf16[8,96,128]{2,1,0:T(8,128)(2,1)S(1)} %get-tuple-element.128.refs_0_, ...), custom_call_target="tpu_custom_call" | custom-call | flops 1610612736 | bytes 9437184 | tf_op jit(solution)/shard_map/update/pallas_call | solution.py:492
  129.8 1.3 collective-permute-start.28
  131.1 1.4 collective-permute-start.30
  132.5 1.4 collective-permute-done.38.refs_3_
  134.4 1.6 collective-permute-start.39
  136.0 2.9 %collective-permute-done.28.refs_1_ = bf16[8,96,128]{2,1,0:T(8,128)(2,1)S(1)} collective-permute-done((bf16[8,96,128]{2,1,0:T(8,128)(2,1)S(1)}, bf16[8,96,128]{2,1,0:T(8,128)(2,1)S(1)}, u32[]{:S(2)}, u32[]{:S(2)}) %collective-permute-start.28) | collective-permute-done | bytes 196640 | tf_op jit(solution)/shard_map/ppermute | solution.py:397
  138.9 3.3 %collective-permute-done.30.refs_3_ = bf16[8,96,128]{2,1,0:T(8,128)(2,1)S(1)} collective-permute-done((bf16[8,96,128]{2,1,0:T(8,128)(2,1)S(1)}, bf16[8,96,128]{2,1,0:T(8,128)(2,1)S(1)}, u32[]{:S(2)}, u32[]{:S(2)}) %collective-permute-start.30) | collective-permute-done | bytes 196640 | tf_op jit(solution)/shard_map/ppermute | solution.py:397
  143.0 1.8 mix.10.refs_3_
  144.9 3.7 %collective-permute-done.31.refs_1_ = bf16[16,16,256]{2,1,0:T(8,128)(2,1)S(1)} collective-permute-done((bf16[16,16,256]{2,1,0:T(8,128)(2,1)S(1)}, bf16[16,16,256]{2,1,0:T(8,128)(2,1)S(1)}, u32[]{:S(2)}, u32[]{:S(2)}) %collective-permute-start.31) | collective-permute-done | bytes 131104 | tf_op jit(solution)/shard_map/ppermute | solution.py:397
  148.5 1.9 mix.11
  151.4 7.7 %collective-permute-done.44.theirs_ref = bf16[16,16,256]{2,1,0:T(8,128)(2,1)S(1)} collective-permute-done((bf16[16,16,256]{2,1,0:T(8,128)(2,1)S(1)}, bf16[16,16,256]{2,1,0:T(8,128)(2,1)S(1)}, u32[]{:S(2)}, u32[]{:S(2)}) %collective-permute-start.44) | collective-permute-done | bytes 131104 | tf_op jit(solution)/shard_map/ppermute | solution.py:397
  160.3 2.2 collective-permute-start.46
  163.6 4.3 %collective-permute-done.40.theirs_ref = bf16[16,16,256]{2,1,0:T(8,128)(2,1)S(1)} collective-permute-done((bf16[16,16,256]{2,1,0:T(8,128)(2,1)S(1)}, bf16[16,16,256]{2,1,0:T(8,128)(2,1)S(1)}, u32[]{:S(2)}, u32[]{:S(2)}) %collective-permute-start.40) | collective-permute-done | bytes 131104 | tf_op jit(solution)/shard_map/ppermute | solution.py:397
  168.5 2.2 collective-permute-start.41
  170.7 1.3 collective-permute-start.43
  171.9 6.0 %pointwise.5.refs_6_ = f32[32,96,1024]{2,1,0:T(8,128)S(1)} custom-call(bf16[16,96,1024]{2,1,0:T(8,128)(2,1)S(1)} %get-tuple-element.156.refs_0_, bf16[16,96,1024]{2,1,0:T(8,128)(2,1)S(1)} %get-tuple-element.157.refs_1_, bf16[32,96,1024]{2,1,0:T(8,128)(2,1)S(1)} %bitcast.18, bf16[512,512]{1,0:T(8,128)(2,1)S(1)} %get-tuple-element.107.refs_2_.refs_3_, ...), custom_call_target="tpu_custom_call" | custom-call | flops 3221225472 | bytes 25165824 | tf_op jit(solution)/shard_map/pointwise/pallas_call | solution.py:473
  178.0 6.8 %last.2 = (f32[32,96,1024]{2,1,0:T(8,128)}, f32[96,1024]{1,0:T(8,128)S(1)}, f32[96,1024]{1,0:T(8,128)S(1)}, f32[96,1024]{1,0:T(8,128)S(1)}, f32[96,1024]{1,0:T(8...) custom-call(bf16[8,96,128]{2,1,0:T(8,128)(2,1)S(1)} %get-tuple-element.160.refs_0_, ...), custom_call_target="tpu_custom_call" | custom-call | flops 805306368 | bytes 12582912 | tf_op jit(solution)/shard_map/last/pallas_call | solution.py:516
  184.8 6.8 %last.3 = (f32[32,96,1024]{2,1,0:T(8,128)}, f32[96,1024]{1,0:T(8,128)S(1)}, f32[96,1024]{1,0:T(8,128)S(1)}, f32[96,1024]{1,0:T(8,128)S(1)}, f32[96,1024]{1,0:T(8...) custom-call(bf16[8,96,128]{2,1,0:T(8,128)(2,1)S(1)} %get-tuple-element.152.refs_0_, ...), custom_call_target="tpu_custom_call", output_to_operand_aliasing={{0}: (9, {})} | custom-call | flops 805306368 | bytes 12582912 | tf_op jit(solution)/shard_map/last/pallas_call | solution.py:516
  191.6 10.4 %collective-permute-start.51 = (f32[96,1024]{1,0:T(8,128)S(1)}, f32[96,1024]{1,0:T(8,128)S(1)}, u32[]{:S(2)}, u32[]{:S(2)}) collective-permute-start(f32[96,1024]{1,0:T(8,128)S(1)} %get-tuple-element.173.layer_ref.refs_3_), channel_id=1, source_target_pairs={{0,8},{8,0},{16,24},{24,16},{1,9},{9,1},{17,25},{25,17},{2,10},{10... | collective-permute-start | bytes 1179656 | tf_op jit(solution)/shard_map/ppermute | solution.py:573
  202.6 3.6 %collective-permute-start.50 = (f32[2,1024]{1,0:T(2,128)S(1)}, f32[2,1024]{1,0:T(2,128)S(1)}, u32[]{:S(2)}, u32[]{:S(2)}) collective-permute-start(f32[2,1024]{1,0:T(2,128)S(1)} %get-tuple-element.175), channel_id=1, source_target_pairs={{1,0},{2,1},{3,2},{4,3},{5,4},{6,5},{7,6},{0,7},{9,8},{10,9},{11,1... | collective-permute-start | bytes 24584 | tf_op jit(solution)/shard_map/ppermute | solution.py:576
  209.9 3.6 %collective-permute-start.53 = (f32[56,1024]{1,0:T(8,128)S(1)}, f32[56,1024]{1,0:T(8,128)S(1)}, u32[]{:S(2)}, u32[]{:S(2)}) collective-permute-start(f32[56,1024]{1,0:T(8,128)S(1)} %pair.1), channel_id=1, source_target_pairs={{0,16},{8,24},{1,17},{9,25},{2,18},{10,26},{3,19},{11,27},{4,20},{... | collective-permute-start | bytes 688136 | tf_op jit(solution)/shard_map/ppermute | solution.py:566
  213.5 1.9 collective-permute-start.48
  215.4 2.7 %collective-permute-done.53.refs_12_ = f32[56,1024]{1,0:T(8,128)S(1)} collective-permute-done((f32[56,1024]{1,0:T(8,128)S(1)}, f32[56,1024]{1,0:T(8,128)S(1)}, u32[]{:S(2)}, u32[]{:S(2)}) %collective-permute-start.53) | collective-permute-done | bytes 229408 | tf_op jit(solution)/shard_map/ppermute | solution.py:566
  218.1 2.0 collective-permute-start.54
  220.2 2.9 %collective-permute-done.48.refs_4_ = f32[96,1024]{1,0:T(8,128)S(1)} collective-permute-done((f32[96,1024]{1,0:T(8,128)S(1)}, f32[96,1024]{1,0:T(8,128)S(1)}, u32[]{:S(2)}, u32[]{:S(2)}) %collective-permute-start.48) | collective-permute-done | bytes 393248 | tf_op jit(solution)/shard_map/ppermute | solution.py:566
  223.1 2.2 residual.1
  (111 shorter events, 24.9 us)
Async XLA Ops:
  0.6 14.0 %copy-start = (bf16[256,1024]{1,0:T(8,128)(2,1)S(1)}, bf16[256,1024]{1,0:T(8,128)(2,1)}, u32[]{:S(2)}) copy-start(bf16[256,1024]{1,0:T(8,128)(2,1)} %constant.15.clone.inverse_ref) | copy-start | bytes 1572868
  1.8 12.8 %copy-start.2 = (bf16[8,96,256]{2,1,0:T(8,128)(2,1)S(1)}, bf16[8,96,256]{2,1,0:T(8,128)(2,1)}, u32[]{:S(2)}) copy-start(bf16[8,96,256]{2,1,0:T(8,128)(2,1)} %constant.16.clone.row_ref) | copy-start | bytes 1179652
  2.7 28.0 %slice-start = ((s8[8388608]{0:T(1024)(128)(4,1)}), s8[4194304]{0:T(1024)(128)(4,1)S(1)}, s32[]{:S(2)}) async-start(s8[8388608]{0:T(1024)(128)(4,1)} %bitcast.9), calls=%async_computation | async-start | bytes 8388608
  5.6 8.9 %collective-permute-start.4 = (bf16[8,96,128]{2,1,0:T(8,128)(2,1)S(1)}, bf16[8,96,128]{2,1,0:T(8,128)(2,1)S(1)}, u32[]{:S(2)}, u32[]{:S(2)}) collective-permute-start(bf16[8,96,128]{2,1,0:T(8,128)(2,1)S(1)} %get-tuple-element.97), channel_id=1, source_target_pairs={{0,1},{1,0},{2,3},{3,2},{4,5},{5,4},{6,7},{7,6},{8,9},{9,8},{10,11... | collective-permute-start | bytes 589832 | tf_op jit(solution)/shard_map/ppermute | solution.py:397
  7.7 7.8 %collective-permute-start.5 = (bf16[8,96,128]{2,1,0:T(8,128)(2,1)S(1)}, bf16[8,96,128]{2,1,0:T(8,128)(2,1)S(1)}, u32[]{:S(2)}, u32[]{:S(2)}) collective-permute-start(bf16[8,96,128]{2,1,0:T(8,128)(2,1)S(1)} %get-tuple-element.98), channel_id=1, source_target_pairs={{0,2},{1,3},{2,0},{3,1},{4,6},{5,7},{6,4},{7,5},{8,10},{9,11},{10,... | collective-permute-start | bytes 589832 | tf_op jit(solution)/shard_map/ppermute | solution.py:397
  9.0 21.7 %slice-start.1 = ((s8[8388608]{0:T(1024)(128)(4,1)}), s8[4194304]{0:T(1024)(128)(4,1)S(1)}, s32[]{:S(2)}) async-start(s8[8388608]{0:T(1024)(128)(4,1)} %bitcast.9), calls=%async_computation.1 | async-start | bytes 8388608
  9.0 8.5 %collective-permute-start.6 = (bf16[8,96,128]{2,1,0:T(8,128)(2,1)S(1)}, bf16[8,96,128]{2,1,0:T(8,128)(2,1)S(1)}, u32[]{:S(2)}, u32[]{:S(2)}) collective-permute-start(bf16[8,96,128]{2,1,0:T(8,128)(2,1)S(1)} %get-tuple-element.99), channel_id=1, source_target_pairs={{0,3},{1,2},{2,1},{3,0},{4,7},{5,6},{6,5},{7,4},{8,11},{9,10},{10,... | collective-permute-start | bytes 589832 | tf_op jit(solution)/shard_map/ppermute | solution.py:397
  11.9 10.1 %collective-permute-start = (bf16[8,96,128]{2,1,0:T(8,128)(2,1)S(1)}, bf16[8,96,128]{2,1,0:T(8,128)(2,1)S(1)}, u32[]{:S(2)}, u32[]{:S(2)}) collective-permute-start(bf16[8,96,128]{2,1,0:T(8,128)(2,1)S(1)} %get-tuple-element.90), channel_id=1, source_target_pairs={{0,1},{1,0},{2,3},{3,2},{4,5},{5,4},{6,7},{7,6},{8,9},{9,8},{10,11... | collective-permute-start | bytes 589832 | tf_op jit(solution)/shard_map/ppermute | solution.py:397
  13.3 8.7 %collective-permute-start.1 = (bf16[8,96,128]{2,1,0:T(8,128)(2,1)S(1)}, bf16[8,96,128]{2,1,0:T(8,128)(2,1)S(1)}, u32[]{:S(2)}, u32[]{:S(2)}) collective-permute-start(bf16[8,96,128]{2,1,0:T(8,128)(2,1)S(1)} %get-tuple-element.91), channel_id=1, source_target_pairs={{0,2},{1,3},{2,0},{3,1},{4,6},{5,7},{6,4},{7,5},{8,10},{9,11},{10,... | collective-permute-start | bytes 589832 | tf_op jit(solution)/shard_map/ppermute | solution.py:397
  14.5 14.3 %collective-permute-start.2 = (bf16[8,96,128]{2,1,0:T(8,128)(2,1)S(1)}, bf16[8,96,128]{2,1,0:T(8,128)(2,1)S(1)}, u32[]{:S(2)}, u32[]{:S(2)}) collective-permute-start(bf16[8,96,128]{2,1,0:T(8,128)(2,1)S(1)} %get-tuple-element.92), channel_id=1, source_target_pairs={{0,3},{1,2},{2,1},{3,0},{4,7},{5,6},{6,5},{7,4},{8,11},{9,10},{10,... | collective-permute-start | bytes 589832 | tf_op jit(solution)/shard_map/ppermute | solution.py:397
  18.0 12.6 %collective-permute-start.7 = (bf16[16,16,256]{2,1,0:T(8,128)(2,1)S(1)}, bf16[16,16,256]{2,1,0:T(8,128)(2,1)S(1)}, u32[]{:S(2)}, u32[]{:S(2)}) collective-permute-start(bf16[16,16,256]{2,1,0:T(8,128)(2,1)S(1)} %get-tuple-element.101), channel_id=1, source_target_pairs={{0,4},{1,5},{2,6},{3,7},{4,0},{5,1},{6,2},{7,3},{8,12},{9,13},{10,... | collective-permute-start | bytes 393224 | tf_op jit(solution)/shard_map/ppermute | solution.py:397
  29.3 8.7 %collective-permute-start.3 = (bf16[16,16,256]{2,1,0:T(8,128)(2,1)S(1)}, bf16[16,16,256]{2,1,0:T(8,128)(2,1)S(1)}, u32[]{:S(2)}, u32[]{:S(2)}) collective-permute-start(bf16[16,16,256]{2,1,0:T(8,128)(2,1)S(1)} %get-tuple-element.95), channel_id=1, source_target_pairs={{0,4},{1,5},{2,6},{3,7},{4,0},{5,1},{6,2},{7,3},{8,12},{9,13},{10,... | collective-permute-start | bytes 393224 | tf_op jit(solution)/shard_map/ppermute | solution.py:397
  30.7 9.4 %copy-start.4 = (bf16[32,32]{1,0:T(8,128)(2,1)S(1)}, bf16[32,32]{1,0:T(8,128)(2,1)}, u32[]{:S(2)}) copy-start(bf16[32,32]{1,0:T(8,128)(2,1)} %weight_ref.1) | copy-start | bytes 6148
  30.7 9.4 %copy-start.5 = (bf16[4,32]{1,0:T(4,128)(2,1)S(1)}, bf16[4,32]{1,0:T(4,128)(2,1)}, u32[]{:S(2)}) copy-start(bf16[4,32]{1,0:T(4,128)(2,1)} %decoder_ref.1) | copy-start | bytes 772
  30.7 23.9 %slice-start.2 = ((s8[6291456]{0:T(1024)(128)(4,1)}), s8[4194304]{0:T(1024)(128)(4,1)S(1)}, s32[]{:S(2)}) async-start(s8[6291456]{0:T(1024)(128)(4,1)} %bitcast.13), calls=%async_computation.2 | async-start | bytes 8388608
  38.0 16.7 %slice-start.3 = ((s8[6291456]{0:T(1024)(128)(4,1)}), s8[2097152]{0:T(1024)(128)(4,1)S(1)}, s32[]{:S(2)}) async-start(s8[6291456]{0:T(1024)(128)(4,1)} %bitcast.13), calls=%async_computation.3 | async-start | bytes 4194304
  39.9 11.4 %collective-permute-start.16 = (bf16[16,16,256]{2,1,0:T(8,128)(2,1)S(1)}, bf16[16,16,256]{2,1,0:T(8,128)(2,1)S(1)}, u32[]{:S(2)}, u32[]{:S(2)}) collective-permute-start(bf16[16,16,256]{2,1,0:T(8,128)(2,1)S(1)} %get-tuple-element.116.mine_ref), channel_id=1, source_target_pairs={{0,4},{1,5},{2,6},{3,7},{4,0},{5,1},{6,2},{7,3},{8,12},{9,13},{10,... | collective-permute-start | bytes 393224 | tf_op jit(solution)/shard_map/ppermute | solution.py:397
  40.6 20.1 %collective-permute-start.8 = (bf16[16,16,256]{2,1,0:T(8,128)(2,1)S(1)}, bf16[16,16,256]{2,1,0:T(8,128)(2,1)S(1)}, u32[]{:S(2)}, u32[]{:S(2)}) collective-permute-start(bf16[16,16,256]{2,1,0:T(8,128)(2,1)S(1)} %get-tuple-element.102.mine_ref), channel_id=1, source_target_pairs={{0,4},{1,5},{2,6},{3,7},{4,0},{5,1},{6,2},{7,3},{8,12},{9,13},{10,... | collective-permute-start | bytes 393224 | tf_op jit(solution)/shard_map/ppermute | solution.py:397
  51.9 11.5 %collective-permute-start.17 = (bf16[8,96,128]{2,1,0:T(8,128)(2,1)S(1)}, bf16[8,96,128]{2,1,0:T(8,128)(2,1)S(1)}, u32[]{:S(2)}, u32[]{:S(2)}) collective-permute-start(bf16[8,96,128]{2,1,0:T(8,128)(2,1)S(1)} %get-tuple-element.118), channel_id=1, source_target_pairs={{0,1},{1,0},{2,3},{3,2},{4,5},{5,4},{6,7},{7,6},{8,9},{9,8},{10,11... | collective-permute-start | bytes 589832 | tf_op jit(solution)/shard_map/ppermute | solution.py:397
  52.9 11.0 %collective-permute-start.18 = (bf16[8,96,128]{2,1,0:T(8,128)(2,1)S(1)}, bf16[8,96,128]{2,1,0:T(8,128)(2,1)S(1)}, u32[]{:S(2)}, u32[]{:S(2)}) collective-permute-start(bf16[8,96,128]{2,1,0:T(8,128)(2,1)S(1)} %get-tuple-element.119), channel_id=1, source_target_pairs={{0,2},{1,3},{2,0},{3,1},{4,6},{5,7},{6,4},{7,5},{8,10},{9,11},{10,... | collective-permute-start | bytes 589832 | tf_op jit(solution)/shard_map/ppermute | solution.py:397
  52.9 11.0 %collective-permute-start.19 = (bf16[8,96,128]{2,1,0:T(8,128)(2,1)S(1)}, bf16[8,96,128]{2,1,0:T(8,128)(2,1)S(1)}, u32[]{:S(2)}, u32[]{:S(2)}) collective-permute-start(bf16[8,96,128]{2,1,0:T(8,128)(2,1)S(1)} %get-tuple-element.120), channel_id=1, source_target_pairs={{0,3},{1,2},{2,1},{3,0},{4,7},{5,6},{6,5},{7,4},{8,11},{9,10},{10,... | collective-permute-start | bytes 589832 | tf_op jit(solution)/shard_map/ppermute | solution.py:397
  61.2 6.8 %collective-permute-start.10 = (bf16[8,96,128]{2,1,0:T(8,128)(2,1)S(1)}, bf16[8,96,128]{2,1,0:T(8,128)(2,1)S(1)}, u32[]{:S(2)}, u32[]{:S(2)}) collective-permute-start(bf16[8,96,128]{2,1,0:T(8,128)(2,1)S(1)} %get-tuple-element.105), channel_id=1, source_target_pairs={{0,2},{1,3},{2,0},{3,1},{4,6},{5,7},{6,4},{7,5},{8,10},{9,11},{10,... | collective-permute-start | bytes 589832 | tf_op jit(solution)/shard_map/ppermute | solution.py:397
  61.3 9.9 %collective-permute-start.11 = (bf16[8,96,128]{2,1,0:T(8,128)(2,1)S(1)}, bf16[8,96,128]{2,1,0:T(8,128)(2,1)S(1)}, u32[]{:S(2)}, u32[]{:S(2)}) collective-permute-start(bf16[8,96,128]{2,1,0:T(8,128)(2,1)S(1)} %get-tuple-element.106), channel_id=1, source_target_pairs={{0,3},{1,2},{2,1},{3,0},{4,7},{5,6},{6,5},{7,4},{8,11},{9,10},{10,... | collective-permute-start | bytes 589832 | tf_op jit(solution)/shard_map/ppermute | solution.py:397
  63.4 7.8 %collective-permute-start.9 = (bf16[8,96,128]{2,1,0:T(8,128)(2,1)S(1)}, bf16[8,96,128]{2,1,0:T(8,128)(2,1)S(1)}, u32[]{:S(2)}, u32[]{:S(2)}) collective-permute-start(bf16[8,96,128]{2,1,0:T(8,128)(2,1)S(1)} %get-tuple-element.104), channel_id=1, source_target_pairs={{0,1},{1,0},{2,3},{3,2},{4,5},{5,4},{6,7},{7,6},{8,9},{9,8},{10,11... | collective-permute-start | bytes 589832 | tf_op jit(solution)/shard_map/ppermute | solution.py:397
  67.0 11.8 %collective-permute-start.20 = (bf16[8,96,128]{2,1,0:T(8,128)(2,1)S(1)}, bf16[8,96,128]{2,1,0:T(8,128)(2,1)S(1)}, u32[]{:S(2)}, u32[]{:S(2)}) collective-permute-start(bf16[8,96,128]{2,1,0:T(8,128)(2,1)S(1)} %get-tuple-element.122), channel_id=1, source_target_pairs={{0,1},{1,0},{2,3},{3,2},{4,5},{5,4},{6,7},{7,6},{8,9},{9,8},{10,11... | collective-permute-start | bytes 589832 | tf_op jit(solution)/shard_map/ppermute | solution.py:397
  68.0 10.9 %collective-permute-start.21 = (bf16[8,96,128]{2,1,0:T(8,128)(2,1)S(1)}, bf16[8,96,128]{2,1,0:T(8,128)(2,1)S(1)}, u32[]{:S(2)}, u32[]{:S(2)}) collective-permute-start(bf16[8,96,128]{2,1,0:T(8,128)(2,1)S(1)} %get-tuple-element.123), channel_id=1, source_target_pairs={{0,2},{1,3},{2,0},{3,1},{4,6},{5,7},{6,4},{7,5},{8,10},{9,11},{10,... | collective-permute-start | bytes 589832 | tf_op jit(solution)/shard_map/ppermute | solution.py:397
  68.1 11.6 %collective-permute-start.22 = (bf16[8,96,128]{2,1,0:T(8,128)(2,1)S(1)}, bf16[8,96,128]{2,1,0:T(8,128)(2,1)S(1)}, u32[]{:S(2)}, u32[]{:S(2)}) collective-permute-start(bf16[8,96,128]{2,1,0:T(8,128)(2,1)S(1)} %get-tuple-element.124), channel_id=1, source_target_pairs={{0,3},{1,2},{2,1},{3,0},{4,7},{5,6},{6,5},{7,4},{8,11},{9,10},{10,... | collective-permute-start | bytes 589832 | tf_op jit(solution)/shard_map/ppermute | solution.py:397
  74.2 12.5 %collective-permute-start.12 = (bf16[8,96,128]{2,1,0:T(8,128)(2,1)S(1)}, bf16[8,96,128]{2,1,0:T(8,128)(2,1)S(1)}, u32[]{:S(2)}, u32[]{:S(2)}) collective-permute-start(bf16[8,96,128]{2,1,0:T(8,128)(2,1)S(1)} %get-tuple-element.111), channel_id=1, source_target_pairs={{0,1},{1,0},{2,3},{3,2},{4,5},{5,4},{6,7},{7,6},{8,9},{9,8},{10,11... | collective-permute-start | bytes 589832 | tf_op jit(solution)/shard_map/ppermute | solution.py:397
  74.8 11.9 %collective-permute-start.13 = (bf16[8,96,128]{2,1,0:T(8,128)(2,1)S(1)}, bf16[8,96,128]{2,1,0:T(8,128)(2,1)S(1)}, u32[]{:S(2)}, u32[]{:S(2)}) collective-permute-start(bf16[8,96,128]{2,1,0:T(8,128)(2,1)S(1)} %get-tuple-element.112), channel_id=1, source_target_pairs={{0,2},{1,3},{2,0},{3,1},{4,6},{5,7},{6,4},{7,5},{8,10},{9,11},{10,... | collective-permute-start | bytes 589832 | tf_op jit(solution)/shard_map/ppermute | solution.py:397
  78.8 9.5 %collective-permute-start.14 = (bf16[8,96,128]{2,1,0:T(8,128)(2,1)S(1)}, bf16[8,96,128]{2,1,0:T(8,128)(2,1)S(1)}, u32[]{:S(2)}, u32[]{:S(2)}) collective-permute-start(bf16[8,96,128]{2,1,0:T(8,128)(2,1)S(1)} %get-tuple-element.113), channel_id=1, source_target_pairs={{0,3},{1,2},{2,1},{3,0},{4,7},{5,6},{6,5},{7,4},{8,11},{9,10},{10,... | collective-permute-start | bytes 589832 | tf_op jit(solution)/shard_map/ppermute | solution.py:397
  80.1 8.7 %collective-permute-start.23 = (bf16[16,16,256]{2,1,0:T(8,128)(2,1)S(1)}, bf16[16,16,256]{2,1,0:T(8,128)(2,1)S(1)}, u32[]{:S(2)}, u32[]{:S(2)}) collective-permute-start(bf16[16,16,256]{2,1,0:T(8,128)(2,1)S(1)} %get-tuple-element.126), channel_id=1, source_target_pairs={{0,4},{1,5},{2,6},{3,7},{4,0},{5,1},{6,2},{7,3},{8,12},{9,13},{10,... | collective-permute-start | bytes 393224 | tf_op jit(solution)/shard_map/ppermute | solution.py:397
  88.8 8.9 %collective-permute-start.15 = (bf16[16,16,256]{2,1,0:T(8,128)(2,1)S(1)}, bf16[16,16,256]{2,1,0:T(8,128)(2,1)S(1)}, u32[]{:S(2)}, u32[]{:S(2)}) collective-permute-start(bf16[16,16,256]{2,1,0:T(8,128)(2,1)S(1)} %get-tuple-element.115), channel_id=1, source_target_pairs={{0,4},{1,5},{2,6},{3,7},{4,0},{5,1},{6,2},{7,3},{8,12},{9,13},{10,... | collective-permute-start | bytes 393224 | tf_op jit(solution)/shard_map/ppermute | solution.py:397
  99.8 5.0 %collective-permute-start.32 = (bf16[16,16,256]{2,1,0:T(8,128)(2,1)S(1)}, bf16[16,16,256]{2,1,0:T(8,128)(2,1)S(1)}, u32[]{:S(2)}, u32[]{:S(2)}) collective-permute-start(bf16[16,16,256]{2,1,0:T(8,128)(2,1)S(1)} %get-tuple-element.140.mine_ref), channel_id=1, source_target_pairs={{0,4},{1,5},{2,6},{3,7},{4,0},{5,1},{6,2},{7,3},{8,12},{9,13},{10,... | collective-permute-start | bytes 393224 | tf_op jit(solution)/shard_map/ppermute | solution.py:397
  105.3 8.2 %collective-permute-start.33 = (bf16[8,96,128]{2,1,0:T(8,128)(2,1)S(1)}, bf16[8,96,128]{2,1,0:T(8,128)(2,1)S(1)}, u32[]{:S(2)}, u32[]{:S(2)}) collective-permute-start(bf16[8,96,128]{2,1,0:T(8,128)(2,1)S(1)} %get-tuple-element.142), channel_id=1, source_target_pairs={{0,1},{1,0},{2,3},{3,2},{4,5},{5,4},{6,7},{7,6},{8,9},{9,8},{10,11... | collective-permute-start | bytes 589832 | tf_op jit(solution)/shard_map/ppermute | solution.py:397
  106.3 5.3 %collective-permute-start.24 = (bf16[16,16,256]{2,1,0:T(8,128)(2,1)S(1)}, bf16[16,16,256]{2,1,0:T(8,128)(2,1)S(1)}, u32[]{:S(2)}, u32[]{:S(2)}) collective-permute-start(bf16[16,16,256]{2,1,0:T(8,128)(2,1)S(1)} %get-tuple-element.127.mine_ref), channel_id=1, source_target_pairs={{0,4},{1,5},{2,6},{3,7},{4,0},{5,1},{6,2},{7,3},{8,12},{9,13},{10,... | collective-permute-start | bytes 393224 | tf_op jit(solution)/shard_map/ppermute | solution.py:397
  106.3 14.6 %collective-permute-start.34 = (bf16[8,96,128]{2,1,0:T(8,128)(2,1)S(1)}, bf16[8,96,128]{2,1,0:T(8,128)(2,1)S(1)}, u32[]{:S(2)}, u32[]{:S(2)}) collective-permute-start(bf16[8,96,128]{2,1,0:T(8,128)(2,1)S(1)} %get-tuple-element.143), channel_id=1, source_target_pairs={{0,2},{1,3},{2,0},{3,1},{4,6},{5,7},{6,4},{7,5},{8,10},{9,11},{10,... | collective-permute-start | bytes 589832 | tf_op jit(solution)/shard_map/ppermute | solution.py:397
  108.1 12.9 %collective-permute-start.35 = (bf16[8,96,128]{2,1,0:T(8,128)(2,1)S(1)}, bf16[8,96,128]{2,1,0:T(8,128)(2,1)S(1)}, u32[]{:S(2)}, u32[]{:S(2)}) collective-permute-start(bf16[8,96,128]{2,1,0:T(8,128)(2,1)S(1)} %get-tuple-element.144), channel_id=1, source_target_pairs={{0,3},{1,2},{2,1},{3,0},{4,7},{5,6},{6,5},{7,4},{8,11},{9,10},{10,... | collective-permute-start | bytes 589832 | tf_op jit(solution)/shard_map/ppermute | solution.py:397
  112.2 13.1 %collective-permute-start.25 = (bf16[8,96,128]{2,1,0:T(8,128)(2,1)S(1)}, bf16[8,96,128]{2,1,0:T(8,128)(2,1)S(1)}, u32[]{:S(2)}, u32[]{:S(2)}) collective-permute-start(bf16[8,96,128]{2,1,0:T(8,128)(2,1)S(1)} %get-tuple-element.129), channel_id=1, source_target_pairs={{0,1},{1,0},{2,3},{3,2},{4,5},{5,4},{6,7},{7,6},{8,9},{9,8},{10,11... | collective-permute-start | bytes 589832 | tf_op jit(solution)/shard_map/ppermute | solution.py:397
  113.5 13.3 %collective-permute-start.26 = (bf16[8,96,128]{2,1,0:T(8,128)(2,1)S(1)}, bf16[8,96,128]{2,1,0:T(8,128)(2,1)S(1)}, u32[]{:S(2)}, u32[]{:S(2)}) collective-permute-start(bf16[8,96,128]{2,1,0:T(8,128)(2,1)S(1)} %get-tuple-element.130), channel_id=1, source_target_pairs={{0,2},{1,3},{2,0},{3,1},{4,6},{5,7},{6,4},{7,5},{8,10},{9,11},{10,... | collective-permute-start | bytes 589832 | tf_op jit(solution)/shard_map/ppermute | solution.py:397
  113.5 13.2 %collective-permute-start.27 = (bf16[8,96,128]{2,1,0:T(8,128)(2,1)S(1)}, bf16[8,96,128]{2,1,0:T(8,128)(2,1)S(1)}, u32[]{:S(2)}, u32[]{:S(2)}) collective-permute-start(bf16[8,96,128]{2,1,0:T(8,128)(2,1)S(1)} %get-tuple-element.131), channel_id=1, source_target_pairs={{0,3},{1,2},{2,1},{3,0},{4,7},{5,6},{6,5},{7,4},{8,11},{9,10},{10,... | collective-permute-start | bytes 589832 | tf_op jit(solution)/shard_map/ppermute | solution.py:397
  124.0 7.0 %collective-permute-start.36 = (bf16[8,96,128]{2,1,0:T(8,128)(2,1)S(1)}, bf16[8,96,128]{2,1,0:T(8,128)(2,1)S(1)}, u32[]{:S(2)}, u32[]{:S(2)}) collective-permute-start(bf16[8,96,128]{2,1,0:T(8,128)(2,1)S(1)} %get-tuple-element.146), channel_id=1, source_target_pairs={{0,1},{1,0},{2,3},{3,2},{4,5},{5,4},{6,7},{7,6},{8,9},{9,8},{10,11... | collective-permute-start | bytes 589832 | tf_op jit(solution)/shard_map/ppermute | solution.py:397
  125.3 7.2 %collective-permute-start.37 = (bf16[8,96,128]{2,1,0:T(8,128)(2,1)S(1)}, bf16[8,96,128]{2,1,0:T(8,128)(2,1)S(1)}, u32[]{:S(2)}, u32[]{:S(2)}) collective-permute-start(bf16[8,96,128]{2,1,0:T(8,128)(2,1)S(1)} %get-tuple-element.147), channel_id=1, source_target_pairs={{0,2},{1,3},{2,0},{3,1},{4,6},{5,7},{6,4},{7,5},{8,10},{9,11},{10,... | collective-permute-start | bytes 589832 | tf_op jit(solution)/shard_map/ppermute | solution.py:397
  125.3 8.6 %collective-permute-start.38 = (bf16[8,96,128]{2,1,0:T(8,128)(2,1)S(1)}, bf16[8,96,128]{2,1,0:T(8,128)(2,1)S(1)}, u32[]{:S(2)}, u32[]{:S(2)}) collective-permute-start(bf16[8,96,128]{2,1,0:T(8,128)(2,1)S(1)} %get-tuple-element.148), channel_id=1, source_target_pairs={{0,3},{1,2},{2,1},{3,0},{4,7},{5,6},{6,5},{7,4},{8,11},{9,10},{10,... | collective-permute-start | bytes 589832 | tf_op jit(solution)/shard_map/ppermute | solution.py:397
  129.8 9.1 %collective-permute-start.28 = (bf16[8,96,128]{2,1,0:T(8,128)(2,1)S(1)}, bf16[8,96,128]{2,1,0:T(8,128)(2,1)S(1)}, u32[]{:S(2)}, u32[]{:S(2)}) collective-permute-start(bf16[8,96,128]{2,1,0:T(8,128)(2,1)S(1)} %get-tuple-element.135), channel_id=1, source_target_pairs={{0,1},{1,0},{2,3},{3,2},{4,5},{5,4},{6,7},{7,6},{8,9},{9,8},{10,11... | collective-permute-start | bytes 589832 | tf_op jit(solution)/shard_map/ppermute | solution.py:397
  131.1 7.8 %collective-permute-start.29 = (bf16[8,96,128]{2,1,0:T(8,128)(2,1)S(1)}, bf16[8,96,128]{2,1,0:T(8,128)(2,1)S(1)}, u32[]{:S(2)}, u32[]{:S(2)}) collective-permute-start(bf16[8,96,128]{2,1,0:T(8,128)(2,1)S(1)} %get-tuple-element.136), channel_id=1, source_target_pairs={{0,2},{1,3},{2,0},{3,1},{4,6},{5,7},{6,4},{7,5},{8,10},{9,11},{10,... | collective-permute-start | bytes 589832 | tf_op jit(solution)/shard_map/ppermute | solution.py:397
  131.1 11.2 %collective-permute-start.30 = (bf16[8,96,128]{2,1,0:T(8,128)(2,1)S(1)}, bf16[8,96,128]{2,1,0:T(8,128)(2,1)S(1)}, u32[]{:S(2)}, u32[]{:S(2)}) collective-permute-start(bf16[8,96,128]{2,1,0:T(8,128)(2,1)S(1)} %get-tuple-element.137), channel_id=1, source_target_pairs={{0,3},{1,2},{2,1},{3,0},{4,7},{5,6},{6,5},{7,4},{8,11},{9,10},{10,... | collective-permute-start | bytes 589832 | tf_op jit(solution)/shard_map/ppermute | solution.py:397
  134.4 8.6 %collective-permute-start.39 = (bf16[16,16,256]{2,1,0:T(8,128)(2,1)S(1)}, bf16[16,16,256]{2,1,0:T(8,128)(2,1)S(1)}, u32[]{:S(2)}, u32[]{:S(2)}) collective-permute-start(bf16[16,16,256]{2,1,0:T(8,128)(2,1)S(1)} %get-tuple-element.150), channel_id=1, source_target_pairs={{0,4},{1,5},{2,6},{3,7},{4,0},{5,1},{6,2},{7,3},{8,12},{9,13},{10,... | collective-permute-start | bytes 393224 | tf_op jit(solution)/shard_map/ppermute | solution.py:397
  142.7 5.8 %collective-permute-start.31 = (bf16[16,16,256]{2,1,0:T(8,128)(2,1)S(1)}, bf16[16,16,256]{2,1,0:T(8,128)(2,1)S(1)}, u32[]{:S(2)}, u32[]{:S(2)}) collective-permute-start(bf16[16,16,256]{2,1,0:T(8,128)(2,1)S(1)} %get-tuple-element.139), channel_id=1, source_target_pairs={{0,4},{1,5},{2,6},{3,7},{4,0},{5,1},{6,2},{7,3},{8,12},{9,13},{10,... | collective-permute-start | bytes 393224 | tf_op jit(solution)/shard_map/ppermute | solution.py:397
  150.5 8.7 %collective-permute-start.44 = (bf16[16,16,256]{2,1,0:T(8,128)(2,1)S(1)}, bf16[16,16,256]{2,1,0:T(8,128)(2,1)S(1)}, u32[]{:S(2)}, u32[]{:S(2)}) collective-permute-start(bf16[16,16,256]{2,1,0:T(8,128)(2,1)S(1)} %get-tuple-element.159.mine_ref), channel_id=1, source_target_pairs={{0,4},{1,5},{2,6},{3,7},{4,0},{5,1},{6,2},{7,3},{8,12},{9,13},{10,... | collective-permute-start | bytes 393224 | tf_op jit(solution)/shard_map/ppermute | solution.py:397
  159.8 10.9 %collective-permute-start.45 = (bf16[8,96,128]{2,1,0:T(8,128)(2,1)S(1)}, bf16[8,96,128]{2,1,0:T(8,128)(2,1)S(1)}, u32[]{:S(2)}, u32[]{:S(2)}) collective-permute-start(bf16[8,96,128]{2,1,0:T(8,128)(2,1)S(1)} %get-tuple-element.161), channel_id=1, source_target_pairs={{0,1},{1,0},{2,3},{3,2},{4,5},{5,4},{6,7},{7,6},{8,9},{9,8},{10,11... | collective-permute-start | bytes 589832 | tf_op jit(solution)/shard_map/ppermute | solution.py:397
  160.3 7.7 %collective-permute-start.40 = (bf16[16,16,256]{2,1,0:T(8,128)(2,1)S(1)}, bf16[16,16,256]{2,1,0:T(8,128)(2,1)S(1)}, u32[]{:S(2)}, u32[]{:S(2)}) collective-permute-start(bf16[16,16,256]{2,1,0:T(8,128)(2,1)S(1)} %get-tuple-element.151.mine_ref), channel_id=1, source_target_pairs={{0,4},{1,5},{2,6},{3,7},{4,0},{5,1},{6,2},{7,3},{8,12},{9,13},{10,... | collective-permute-start | bytes 393224 | tf_op jit(solution)/shard_map/ppermute | solution.py:397
  160.3 17.7 %collective-permute-start.46 = (bf16[8,96,128]{2,1,0:T(8,128)(2,1)S(1)}, bf16[8,96,128]{2,1,0:T(8,128)(2,1)S(1)}, u32[]{:S(2)}, u32[]{:S(2)}) collective-permute-start(bf16[8,96,128]{2,1,0:T(8,128)(2,1)S(1)} %get-tuple-element.162), channel_id=1, source_target_pairs={{0,2},{1,3},{2,0},{3,1},{4,6},{5,7},{6,4},{7,5},{8,10},{9,11},{10,... | collective-permute-start | bytes 589832 | tf_op jit(solution)/shard_map/ppermute | solution.py:397
  162.5 15.5 %collective-permute-start.47 = (bf16[8,96,128]{2,1,0:T(8,128)(2,1)S(1)}, bf16[8,96,128]{2,1,0:T(8,128)(2,1)S(1)}, u32[]{:S(2)}, u32[]{:S(2)}) collective-permute-start(bf16[8,96,128]{2,1,0:T(8,128)(2,1)S(1)} %get-tuple-element.163), channel_id=1, source_target_pairs={{0,3},{1,2},{2,1},{3,0},{4,7},{5,6},{6,5},{7,4},{8,11},{9,10},{10,... | collective-permute-start | bytes 589832 | tf_op jit(solution)/shard_map/ppermute | solution.py:397
  168.5 16.2 %collective-permute-start.41 = (bf16[8,96,128]{2,1,0:T(8,128)(2,1)S(1)}, bf16[8,96,128]{2,1,0:T(8,128)(2,1)S(1)}, u32[]{:S(2)}, u32[]{:S(2)}) collective-permute-start(bf16[8,96,128]{2,1,0:T(8,128)(2,1)S(1)} %get-tuple-element.153), channel_id=1, source_target_pairs={{0,1},{1,0},{2,3},{3,2},{4,5},{5,4},{6,7},{7,6},{8,9},{9,8},{10,11... | collective-permute-start | bytes 589832 | tf_op jit(solution)/shard_map/ppermute | solution.py:397
  170.7 14.1 %collective-permute-start.42 = (bf16[8,96,128]{2,1,0:T(8,128)(2,1)S(1)}, bf16[8,96,128]{2,1,0:T(8,128)(2,1)S(1)}, u32[]{:S(2)}, u32[]{:S(2)}) collective-permute-start(bf16[8,96,128]{2,1,0:T(8,128)(2,1)S(1)} %get-tuple-element.154), channel_id=1, source_target_pairs={{0,2},{1,3},{2,0},{3,1},{4,6},{5,7},{6,4},{7,5},{8,10},{9,11},{10,... | collective-permute-start | bytes 589832 | tf_op jit(solution)/shard_map/ppermute | solution.py:397
  170.7 14.1 %collective-permute-start.43 = (bf16[8,96,128]{2,1,0:T(8,128)(2,1)S(1)}, bf16[8,96,128]{2,1,0:T(8,128)(2,1)S(1)}, u32[]{:S(2)}, u32[]{:S(2)}) collective-permute-start(bf16[8,96,128]{2,1,0:T(8,128)(2,1)S(1)} %get-tuple-element.155), channel_id=1, source_target_pairs={{0,3},{1,2},{2,1},{3,0},{4,7},{5,6},{6,5},{7,4},{8,11},{9,10},{10,... | collective-permute-start | bytes 589832 | tf_op jit(solution)/shard_map/ppermute | solution.py:397
  184.8 35.3 %copy-start.7 = (f32[96]{0:T(128)S(1)}, f32[96]{0:T(128)}, u32[]{:S(2)}) copy-start(f32[96]{0:T(128)} %param.15) | copy-start | bytes 1156
  191.6 17.7 %collective-permute-start.51 = (f32[96,1024]{1,0:T(8,128)S(1)}, f32[96,1024]{1,0:T(8,128)S(1)}, u32[]{:S(2)}, u32[]{:S(2)}) collective-permute-start(f32[96,1024]{1,0:T(8,128)S(1)} %get-tuple-element.173.layer_ref.refs_3_), channel_id=1, source_target_pairs={{0,8},{8,0},{16,24},{24,16},{1,9},{9,1},{17,25},{25,17},{2,10},{10... | collective-permute-start | bytes 1179656 | tf_op jit(solution)/shard_map/ppermute | solution.py:573
  202.0 5.2 %collective-permute-start.49 = (f32[2,1024]{1,0:T(2,128)S(1)}, f32[2,1024]{1,0:T(2,128)S(1)}, u32[]{:S(2)}, u32[]{:S(2)}) collective-permute-start(f32[2,1024]{1,0:T(2,128)S(1)} %get-tuple-element.174), channel_id=1, source_target_pairs={{0,1},{1,2},{2,3},{3,4},{4,5},{5,6},{6,7},{7,0},{8,9},{9,10},{10,1... | collective-permute-start | bytes 24584 | tf_op jit(solution)/shard_map/ppermute | solution.py:575
  202.6 4.6 %collective-permute-start.50 = (f32[2,1024]{1,0:T(2,128)S(1)}, f32[2,1024]{1,0:T(2,128)S(1)}, u32[]{:S(2)}, u32[]{:S(2)}) collective-permute-start(f32[2,1024]{1,0:T(2,128)S(1)} %get-tuple-element.175), channel_id=1, source_target_pairs={{1,0},{2,1},{3,2},{4,3},{5,4},{6,5},{7,6},{0,7},{9,8},{10,9},{11,1... | collective-permute-start | bytes 24584 | tf_op jit(solution)/shard_map/ppermute | solution.py:576
  207.2 2.0 collective-permute-start.52
  209.9 8.2 %collective-permute-start.53 = (f32[56,1024]{1,0:T(8,128)S(1)}, f32[56,1024]{1,0:T(8,128)S(1)}, u32[]{:S(2)}, u32[]{:S(2)}) collective-permute-start(f32[56,1024]{1,0:T(8,128)S(1)} %pair.1), channel_id=1, source_target_pairs={{0,16},{8,24},{1,17},{9,25},{2,18},{10,26},{3,19},{11,27},{4,20},{... | collective-permute-start | bytes 688136 | tf_op jit(solution)/shard_map/ppermute | solution.py:566
  213.5 9.6 %collective-permute-start.48 = (f32[96,1024]{1,0:T(8,128)S(1)}, f32[96,1024]{1,0:T(8,128)S(1)}, u32[]{:S(2)}, u32[]{:S(2)}) collective-permute-start(f32[96,1024]{1,0:T(8,128)S(1)} %get-tuple-element.172.refs_2_), channel_id=1, source_target_pairs={{0,8},{8,16},{16,24},{1,9},{9,17},{17,25},{2,10},{10,18},{18,26},{... | collective-permute-start | bytes 1179656 | tf_op jit(solution)/shard_map/ppermute | solution.py:566
  218.1 5.0 %collective-permute-start.54 = (f32[56,1024]{1,0:T(8,128)S(1)}, f32[56,1024]{1,0:T(8,128)S(1)}, u32[]{:S(2)}, u32[]{:S(2)}) collective-permute-start(f32[56,1024]{1,0:T(8,128)S(1)} %collective-permute-done.53.refs_12_), channel_id=1, source_target_pairs={{0,8},{8,0},{16,24},{24,16},{1,9},{9,1},{17,25},{25,17},{2,10},{10... | collective-permute-start | bytes 688136 | tf_op jit(solution)/shard_map/ppermute | solution.py:594
  (3 other events, 16.5 us)

commit v5 on v4

--- a/solution.py
+++ b/solution.py
@@ -135,27 +135,28 @@
                 out_ref[c, :, modes:] = (imag[:, :modes] - real[:, modes:]).astype(out_ref.dtype)
 
 
-def mix_kernel(n, chunks, *refs):
+def mix_kernel(n, chunks, outputs, *refs):
     keep_ref, got_ref, weight_ref = refs[:3]
-    earlier = refs[3:4] if n > 0 else ()
-    out_refs = refs[3 + len(earlier) : -1]
-    spectrum = refs[-1]
+    earlier_ref = refs[3] if n > 0 else None
+    out_ref, spectrum, mixed = refs[-3:]
     own, channels, modes = weight_ref.shape[1], weight_ref.shape[2], weight_ref.shape[4]
     size = channels // chunks
     value = keep_ref[...] + got_ref[...].astype(F32)
     spectrum[...] = jnp.swapaxes(value, 0, 1)
-    total = out_refs[0] if n < chunks - 1 else earlier[0]
+    final = n == chunks - 1
+    total = mixed if final else out_ref
 
     def step(k, carry):
         row = spectrum[k]
-        zero = jnp.zeros((channels, modes), F32)
+        zero = jnp.zeros((outputs.stop - outputs.start, modes), F32)
         real, imag = [zero, zero], [zero, zero]
-        if earlier:
-            real[0], imag[0] = earlier[0][k, :, :modes], earlier[0][k, :, modes:]
+        if n > 0:
+            real[0] = earlier_ref[k, outputs, :modes]
+            imag[0] = earlier_ref[k, outputs, modes:]
         for i in range(size):
             s0, s1 = row[i : i + 1, :modes], row[i : i + 1, modes:]
-            w0 = weight_ref[0, k, n * size + i].astype(F32)
-            w1 = weight_ref[1, k, n * size + i].astype(F32)
+            w0 = weight_ref[0, k, n * size + i, outputs].astype(F32)
+            w1 = weight_ref[1, k, n * size + i, outputs].astype(F32)
             real[i % 2] = real[i % 2] + (s0 * w0 - s1 * w1)
             imag[i % 2] = imag[i % 2] + (s0 * w1 + s1 * w0)
         total[k, :, :modes] = real[0] + real[1]
@@ -163,10 +164,8 @@
         return carry
 
     lax.fori_loop(0, own, step, 0)
-    if n == chunks - 1:
-        for c in range(chunks):
-            part = jnp.swapaxes(total[:, c * size : (c + 1) * size], 0, 1)
-            out_refs[c][...] = part.astype(BF)
+    if final:
+        out_ref[...] = jnp.swapaxes(mixed[...], 0, 1).astype(BF)
 
 
 def inverse_y_kernel(pack, peers, mine_ref, theirs_ref, table_ref, *back_refs):
@@ -436,19 +435,23 @@
             name="forward_y",
         )(*parts, row_table)
 
-    def mix(kept, got, n, earlier):
-        total = jax.ShapeDtypeStruct((own, channels, 2 * ymodes), F32)
-        ends = [jax.ShapeDtypeStruct((size, own, 2 * ymodes), BF)] * CHUNKS
+    def mix(kept, got, n, earlier, outputs):
+        count = outputs.stop - outputs.start
         final = n == CHUNKS - 1
         return pl.pallas_call(
-            functools.partial(mix_kernel, n, CHUNKS),
+            functools.partial(mix_kernel, n, CHUNKS, outputs),
             in_specs=[vmem] * (3 + len(earlier)),
-            out_specs=[vmem] * len(ends) if final else [vmem],
-            out_shape=ends if final else [total],
-            scratch_shapes=[pltpu.VMEM((own, size, 2 * ymodes), F32)],
+            out_specs=vmem,
+            out_shape=jax.ShapeDtypeStruct((count, own, 2 * ymodes), BF)
+            if final
+            else jax.ShapeDtypeStruct((own, count, 2 * ymodes), F32),
+            scratch_shapes=[
+                pltpu.VMEM((own, size, 2 * ymodes), F32),
+                pltpu.VMEM((own, size, 2 * ymodes), F32),
+            ],
             compiler_params=params(8),
             cost_estimate=cost(
-                8 * own * channels * size * ymodes, 4 * own * channels * size * ymodes
+                8 * own * count * size * ymodes, 4 * own * count * size * ymodes
             ),
             name="mix",
         )(kept, got, spectral_weight, *earlier)
@@ -544,9 +547,13 @@
         halves = [forward_y(parts) for parts in arrived]
         kept = [half[0] for half in halves]
         got = [swap(half[1], peers) for half in halves]
-        mixed = []
-        for n in every:
-            mixed = mix(kept[n], got[n], n, mixed)
+        sums = []
+        for n in range(CHUNKS - 1):
+            sums = [mix(kept[n], got[n], n, sums, slice(0, channels))]
+        mixed = [
+            mix(kept[-1], got[-1], CHUNKS - 1, sums, slice(n * size, (n + 1) * size))
+            for n in every
+        ]
         theirs = []
         for n in every:
             theirs.append(swap(mixed[n], peers))

time: 226 us -> 223 us (0.987)
  starting transfers between devices: 68 us -> 61.1 us
  waiting for transfers between devices: 82.6 us -> 86.3 us
    ppermute x48, starting transfers between devices: 44.6 us -> 40.7 us  [swap(): return lax.ppermute(value, 'gy', [(g, g ^ distance) for g in range(slices)])]
    ppermute x48, waiting for transfers between devices: 75.2 us -> 78.3 us  [swap(): return lax.ppermute(value, 'gy', [(g, g ^ distance) for g in range(slices)])]
    ppermute x2, starting transfers between devices: 5.53 us -> 3.22 us  [from_below(): lax.ppermute(value, 'lev', [(s, s + step) for s in range(levels - step)])]
    pallas_call x6 -> x9, Pallas kernels: 11.5 us -> 11.9 us  [mix(): pl.pallas_call(functools.partial(mix_kernel, n, CHUNKS, outputs), in_spec...]
  transfers between devices with their start and end apart: 55 -> 55, of which waited for: 23 -> 24; matrix products, arithmetic and copies ran while one was open for 0% -> 0% of each run, Pallas kernels for 23% -> 25%
where the time goes in v5:
time: 223 us
  waiting for transfers between devices  86.3 us (39%)
  Pallas kernels  72.6 us (33%)
  starting transfers between devices  61.1 us (27%)
    ppermute x48, waiting for transfers between devices, swap(): return lax.ppermute(value, 'gy', [(g, g ^ distance) for g in range(slices)])  78.3 us
    ppermute x48, starting transfers between devices, swap(): return lax.ppermute(value, 'gy', [(g, g ^ distance) for g in range(slices)])  40.7 us
    pallas_call x3, Pallas kernels, pointwise(): pl.pallas_call(functools.partial(pointwise_kernel, len(states), block), g...  18 us
    pallas_call x2, Pallas kernels, last(): pl.pallas_call(functools.partial(last_kernel, pack, peers, n * size, kind...  13.6 us
    pallas_call x4, Pallas kernels, update(): pl.pallas_call(functools.partial(update_kernel, pack, peers), grid=(part...  12.1 us
    pallas_call x9, Pallas kernels, mix(): pl.pallas_call(functools.partial(mix_kernel, n, CHUNKS, outputs), in_spec...  11.9 us
    ppermute x1, starting transfers between devices, on_device(): other = lax.ppermute(layer, 'lev', partner)  10.3 us
    ppermute x2, waiting for transfers between devices, from_below(): lax.ppermute(value, 'lev', [(s, s + step) for s in range(levels - step)])  6.13 us
  transfers between devices with their start and end apart: 55, of which 24 were waited for; matrix products, arithmetic and copies ran while one was open for 0% of the time, Pallas kernels for 25%

profile of v5, /device:TPU:1, one launch (start us, length us, event | category | flops | bytes accessed | tf_op | source)
XLA Modules:
  0.0 222.6 jit_solution(8146468651595242719)
XLA Ops:
  2.7 2.9 %near.3 = (bf16[8,96,128]{2,1,0:T(8,128)(2,1)S(1)}, bf16[8,96,128]{2,1,0:T(8,128)(2,1)S(1)}, bf16[8,96,128]{2,1,0:T(8,128)(2,1)S(1)}, bf16[8,96,128]{2,1,0:T(8,128)(2,1)S(1)}) custom-call(bf16[32,96,1024]{2,1,0:T(8,128)(2,1)} %bitcast.11, bf16[1024,256]{1,0:T(8,128)(2,1)S(1)} %forward_table.1.table_ref.refs_6_), custom_call_target="tpu_custom_call" | custom-call | flops 805306368 | bytes 3145728 | tf_op jit(solution)/shard_map/near/pallas_call | solution.py:409
  5.6 2.1 collective-permute-start.4
  7.7 1.3 collective-permute-start.5
  9.0 2.9 %near.2 = (bf16[8,96,128]{2,1,0:T(8,128)(2,1)S(1)}, bf16[8,96,128]{2,1,0:T(8,128)(2,1)S(1)}, bf16[8,96,128]{2,1,0:T(8,128)(2,1)S(1)}, bf16[8,96,128]{2,1,0:T(8,128)(2,1)S(1)}) custom-call(bf16[32,96,1024]{2,1,0:T(8,128)(2,1)} %bitcast.12, bf16[1024,256]{1,0:T(8,128)(2,1)S(1)} %forward_table.1.table_ref.refs_6_), custom_call_target="tpu_custom_call" | custom-call | flops 805306368 | bytes 3145728 | tf_op jit(solution)/shard_map/near/pallas_call | solution.py:409
  11.9 1.4 collective-permute-start
  13.3 1.2 collective-permute-start.1
  15.5 2.1 collective-permute-done.6.refs_3_
  18.1 2.2 collective-permute-start.7
  20.3 1.7 collective-permute-done.refs_1_
  22.0 6.8 %collective-permute-done.2.refs_3_ = bf16[8,96,128]{2,1,0:T(8,128)(2,1)S(1)} collective-permute-done((bf16[8,96,128]{2,1,0:T(8,128)(2,1)S(1)}, bf16[8,96,128]{2,1,0:T(8,128)(2,1)S(1)}, u32[]{:S(2)}, u32[]{:S(2)}) %collective-permute-start.2) | collective-permute-done | bytes 196640 | tf_op jit(solution)/shard_map/ppermute | solution.py:396
  29.3 1.4 collective-permute-start.3
  30.7 1.8 mix.9.refs_3_
  32.6 5.4 %collective-permute-done.3.refs_1_ = bf16[16,16,256]{2,1,0:T(8,128)(2,1)S(1)} collective-permute-done((bf16[16,16,256]{2,1,0:T(8,128)(2,1)S(1)}, bf16[16,16,256]{2,1,0:T(8,128)(2,1)S(1)}, u32[]{:S(2)}, u32[]{:S(2)}) %collective-permute-start.3) | collective-permute-done | bytes 131104 | tf_op jit(solution)/shard_map/ppermute | solution.py:396
  40.7 2.4 %collective-permute-start.8 = (bf16[16,16,256]{2,1,0:T(8,128)(2,1)S(1)}, bf16[16,16,256]{2,1,0:T(8,128)(2,1)S(1)}, u32[]{:S(2)}, u32[]{:S(2)}) collective-permute-start(bf16[16,16,256]{2,1,0:T(8,128)(2,1)S(1)} %mix.10.mine_ref), channel_id=1, source_target_pairs={{0,4},{1,5},{2,6},{3,7},{4,0},{5,1},{6,2},{7,3},{8,12},{9,13},{10,... | collective-permute-start | bytes 393224 | tf_op jit(solution)/shard_map/ppermute | solution.py:396
  43.1 7.3 %collective-permute-done.16.theirs_ref = bf16[16,16,256]{2,1,0:T(8,128)(2,1)S(1)} collective-permute-done((bf16[16,16,256]{2,1,0:T(8,128)(2,1)S(1)}, bf16[16,16,256]{2,1,0:T(8,128)(2,1)S(1)}, u32[]{:S(2)}, u32[]{:S(2)}) %collective-permute-start.16) | collective-permute-done | bytes 131104 | tf_op jit(solution)/shard_map/ppermute | solution.py:396
  52.0 1.7 collective-permute-start.19
  53.8 6.0 %pointwise.3.refs_4_ = f32[32,96,1024]{2,1,0:T(8,128)S(1)} custom-call(bf16[32,96,1024]{2,1,0:T(8,128)(2,1)S(1)} %bitcast.15, bf16[32,96,1024]{2,1,0:T(8,128)(2,1)S(1)} %bitcast.16, bf16[512,512]{1,0:T(8,128)(2,1)S(1)} %get-tuple-element.100.refs_2_.refs_3_, f32[512,1]{1,0:T(8,128)S(1)} %get-tuple-element.101.refs_3_.refs_4_), custom_call_target="tpu_custom_call" | custom-call | flops 3221225472 | bytes 25165824 | tf_op jit(solution)/shard_map/pointwise/pallas_call | solution.py:476
  60.4 2.1 collective-permute-start.11
  63.1 3.0 %update.5 = (bf16[16,96,1024]{2,1,0:T(8,128)(2,1)S(1)}, bf16[8,96,128]{2,1,0:T(8,128)(2,1)S(1)}, bf16[8,96,128]{2,1,0:T(8,128)(2,1)S(1)}, bf16[8,96,128]{2,1,0:T(8,128)(2,1)S(1)}, bf16[8,96,128]{2,1,0:T(8,128)(2,1)S(1)}) custom-call(bf16[8,96,128]{2,1,0:T(8,128)(2,1)S(1)} %get-tuple-element.109.refs_0_, ...), custom_call_target="tpu_custom_call" | custom-call | flops 1610612736 | bytes 9437184 | tf_op jit(solution)/shard_map/update/pallas_call | solution.py:495
  67.2 1.6 collective-permute-start.22
  68.8 1.5 collective-permute-done.11.refs_3_
  70.3 3.0 %update.4 = (bf16[16,96,1024]{2,1,0:T(8,128)(2,1)S(1)}, bf16[8,96,128]{2,1,0:T(8,128)(2,1)S(1)}, bf16[8,96,128]{2,1,0:T(8,128)(2,1)S(1)}, bf16[8,96,128]{2,1,0:T(8,128)(2,1)S(1)}, bf16[8,96,128]{2,1,0:T(8,128)(2,1)S(1)}) custom-call(bf16[8,96,128]{2,1,0:T(8,128)(2,1)S(1)} %get-tuple-element.96.refs_0_, ...), custom_call_target="tpu_custom_call" | custom-call | flops 1610612736 | bytes 9437184 | tf_op jit(solution)/shard_map/update/pallas_call | solution.py:495
  74.2 3.7 %collective-permute-done.20.refs_1_ = bf16[8,96,128]{2,1,0:T(8,128)(2,1)S(1)} collective-permute-done((bf16[8,96,128]{2,1,0:T(8,128)(2,1)S(1)}, bf16[8,96,128]{2,1,0:T(8,128)(2,1)S(1)}, u32[]{:S(2)}, u32[]{:S(2)}) %collective-permute-start.20) | collective-permute-done | bytes 196640 | tf_op jit(solution)/shard_map/ppermute | solution.py:396
  79.2 1.3 collective-permute-start.23
  80.5 5.3 %collective-permute-done.12.refs_1_ = bf16[8,96,128]{2,1,0:T(8,128)(2,1)S(1)} collective-permute-done((bf16[8,96,128]{2,1,0:T(8,128)(2,1)S(1)}, bf16[8,96,128]{2,1,0:T(8,128)(2,1)S(1)}, u32[]{:S(2)}, u32[]{:S(2)}) %collective-permute-start.12) | collective-permute-done | bytes 196640 | tf_op jit(solution)/shard_map/ppermute | solution.py:396
  85.8 1.6 collective-permute-done.14.refs_3_
  88.0 1.8 mix.12.refs_3_
  89.8 7.0 %collective-permute-done.15.refs_1_ = bf16[16,16,256]{2,1,0:T(8,128)(2,1)S(1)} collective-permute-done((bf16[16,16,256]{2,1,0:T(8,128)(2,1)S(1)}, bf16[16,16,256]{2,1,0:T(8,128)(2,1)S(1)}, u32[]{:S(2)}, u32[]{:S(2)}) %collective-permute-start.15) | collective-permute-done | bytes 131104 | tf_op jit(solution)/shard_map/ppermute | solution.py:396
  97.9 4.9 %collective-permute-done.32.theirs_ref = bf16[16,16,256]{2,1,0:T(8,128)(2,1)S(1)} collective-permute-done((bf16[16,16,256]{2,1,0:T(8,128)(2,1)S(1)}, bf16[16,16,256]{2,1,0:T(8,128)(2,1)S(1)}, u32[]{:S(2)}, u32[]{:S(2)}) %collective-permute-start.32) | collective-permute-done | bytes 131104 | tf_op jit(solution)/shard_map/ppermute | solution.py:396
  104.3 1.2 mix.13.mine_ref
  105.6 1.7 collective-permute-start.34
  108.3 2.7 %collective-permute-done.24.theirs_ref = bf16[16,16,256]{2,1,0:T(8,128)(2,1)S(1)} collective-permute-done((bf16[16,16,256]{2,1,0:T(8,128)(2,1)S(1)}, bf16[16,16,256]{2,1,0:T(8,128)(2,1)S(1)}, u32[]{:S(2)}, u32[]{:S(2)}) %collective-permute-start.24) | collective-permute-done | bytes 131104 | tf_op jit(solution)/shard_map/ppermute | solution.py:396
  111.6 1.3 collective-permute-start.25
  112.8 1.5 collective-permute-start.27
  114.3 6.0 %pointwise.4.refs_4_ = f32[32,96,1024]{2,1,0:T(8,128)S(1)} custom-call(bf16[16,96,1024]{2,1,0:T(8,128)(2,1)S(1)} %get-tuple-element.123.refs_0_, bf16[16,96,1024]{2,1,0:T(8,128)(2,1)S(1)} %get-tuple-element.124.refs_1_, bf16[32,96,1024]{2,1,0:T(8,128)(2,1)S(1)} %bitcast.17, bf16[512,512]{1,0:T(8,128)(2,1)S(1)} %get-tuple-element.100.refs_2_.refs_3_, ...), custom_call_target="tpu_custom_call" | custom-call | flops 3221225472 | bytes 25165824 | tf_op jit(solution)/shard_map/pointwise/pallas_call | solution.py:476
  120.3 3.0 %update.7 = (bf16[16,96,1024]{2,1,0:T(8,128)(2,1)S(1)}, bf16[8,96,128]{2,1,0:T(8,128)(2,1)S(1)}, bf16[8,96,128]{2,1,0:T(8,128)(2,1)S(1)}, bf16[8,96,128]{2,1,0:T(8,128)(2,1)S(1)}, bf16[8,96,128]{2,1,0:T(8,128)(2,1)S(1)}) custom-call(bf16[8,96,128]{2,1,0:T(8,128)(2,1)S(1)} %get-tuple-element.131.refs_0_, ...), custom_call_target="tpu_custom_call" | custom-call | flops 1610612736 | bytes 9437184 | tf_op jit(solution)/shard_map/update/pallas_call | solution.py:495
  123.3 1.3 collective-permute-start.36
  124.6 1.5 collective-permute-start.38
  126.1 3.0 %update.6 = (bf16[16,96,1024]{2,1,0:T(8,128)(2,1)S(1)}, bf16[8,96,128]{2,1,0:T(8,128)(2,1)S(1)}, bf16[8,96,128]{2,1,0:T(8,128)(2,1)S(1)}, bf16[8,96,128]{2,1,0:T(8,128)(2,1)S(1)}, bf16[8,96,128]{2,1,0:T(8,128)(2,1)S(1)}) custom-call(bf16[8,96,128]{2,1,0:T(8,128)(2,1)S(1)} %get-tuple-element.119.refs_0_, ...), custom_call_target="tpu_custom_call" | custom-call | flops 1610612736 | bytes 9437184 | tf_op jit(solution)/shard_map/update/pallas_call | solution.py:495
  129.2 1.2 collective-permute-start.28
  130.4 1.5 collective-permute-start.30
  131.9 1.3 collective-permute-done.38.refs_3_
  133.9 4.3 %collective-permute-done.28.refs_1_ = bf16[8,96,128]{2,1,0:T(8,128)(2,1)S(1)} collective-permute-done((bf16[8,96,128]{2,1,0:T(8,128)(2,1)S(1)}, bf16[8,96,128]{2,1,0:T(8,128)(2,1)S(1)}, u32[]{:S(2)}, u32[]{:S(2)}) %collective-permute-start.28) | collective-permute-done | bytes 196640 | tf_op jit(solution)/shard_map/ppermute | solution.py:396
  138.2 3.3 %collective-permute-done.30.refs_3_ = bf16[8,96,128]{2,1,0:T(8,128)(2,1)S(1)} collective-permute-done((bf16[8,96,128]{2,1,0:T(8,128)(2,1)S(1)}, bf16[8,96,128]{2,1,0:T(8,128)(2,1)S(1)}, u32[]{:S(2)}, u32[]{:S(2)}) %collective-permute-start.30) | collective-permute-done | bytes 196640 | tf_op jit(solution)/shard_map/ppermute | solution.py:396
  142.1 1.8 mix.15.refs_3_
  144.0 4.4 %collective-permute-done.31.refs_1_ = bf16[16,16,256]{2,1,0:T(8,128)(2,1)S(1)} collective-permute-done((bf16[16,16,256]{2,1,0:T(8,128)(2,1)S(1)}, bf16[16,16,256]{2,1,0:T(8,128)(2,1)S(1)}, u32[]{:S(2)}, u32[]{:S(2)}) %collective-permute-start.31) | collective-permute-done | bytes 131104 | tf_op jit(solution)/shard_map/ppermute | solution.py:396
  149.6 8.7 %collective-permute-done.44.theirs_ref = bf16[16,16,256]{2,1,0:T(8,128)(2,1)S(1)} collective-permute-done((bf16[16,16,256]{2,1,0:T(8,128)(2,1)S(1)}, bf16[16,16,256]{2,1,0:T(8,128)(2,1)S(1)}, u32[]{:S(2)}, u32[]{:S(2)}) %collective-permute-start.44) | collective-permute-done | bytes 131104 | tf_op jit(solution)/shard_map/ppermute | solution.py:396
  160.1 1.6 collective-permute-start.46
  161.7 1.2 collective-permute-start.47
  162.9 5.4 %collective-permute-done.40.theirs_ref = bf16[16,16,256]{2,1,0:T(8,128)(2,1)S(1)} collective-permute-done((bf16[16,16,256]{2,1,0:T(8,128)(2,1)S(1)}, bf16[16,16,256]{2,1,0:T(8,128)(2,1)S(1)}, u32[]{:S(2)}, u32[]{:S(2)}) %collective-permute-start.40) | collective-permute-done | bytes 131104 | tf_op jit(solution)/shard_map/ppermute | solution.py:396
  169.2 2.4 %collective-permute-start.43 = (bf16[8,96,128]{2,1,0:T(8,128)(2,1)S(1)}, bf16[8,96,128]{2,1,0:T(8,128)(2,1)S(1)}, u32[]{:S(2)}, u32[]{:S(2)}) collective-permute-start(bf16[8,96,128]{2,1,0:T(8,128)(2,1)S(1)} %get-tuple-element.144), channel_id=1, source_target_pairs={{0,3},{1,2},{2,1},{3,0},{4,7},{5,6},{6,5},{7,4},{8,11},{9,10},{10,... | collective-permute-start | bytes 589832 | tf_op jit(solution)/shard_map/ppermute | solution.py:396
  171.6 6.0 %pointwise.5.refs_6_ = f32[32,96,1024]{2,1,0:T(8,128)S(1)} custom-call(bf16[16,96,1024]{2,1,0:T(8,128)(2,1)S(1)} %get-tuple-element.145.refs_0_, bf16[16,96,1024]{2,1,0:T(8,128)(2,1)S(1)} %get-tuple-element.146.refs_1_, bf16[32,96,1024]{2,1,0:T(8,128)(2,1)S(1)} %bitcast.18, bf16[512,512]{1,0:T(8,128)(2,1)S(1)} %get-tuple-element.100.refs_2_.refs_3_, ...), custom_call_target="tpu_custom_call" | custom-call | flops 3221225472 | bytes 25165824 | tf_op jit(solution)/shard_map/pointwise/pallas_call | solution.py:476
  177.6 6.8 %last.2 = (f32[32,96,1024]{2,1,0:T(8,128)}, f32[96,1024]{1,0:T(8,128)S(1)}, f32[96,1024]{1,0:T(8,128)S(1)}, f32[96,1024]{1,0:T(8,128)S(1)}, f32[96,1024]{1,0:T(8...) custom-call(bf16[8,96,128]{2,1,0:T(8,128)(2,1)S(1)} %get-tuple-element.148.refs_0_, ...), custom_call_target="tpu_custom_call" | custom-call | flops 805306368 | bytes 12582912 | tf_op jit(solution)/shard_map/last/pallas_call | solution.py:519
  184.4 6.8 %last.3 = (f32[32,96,1024]{2,1,0:T(8,128)}, f32[96,1024]{1,0:T(8,128)S(1)}, f32[96,1024]{1,0:T(8,128)S(1)}, f32[96,1024]{1,0:T(8,128)S(1)}, f32[96,1024]{1,0:T(8...) custom-call(bf16[8,96,128]{2,1,0:T(8,128)(2,1)S(1)} %get-tuple-element.141.refs_0_, ...), custom_call_target="tpu_custom_call", output_to_operand_aliasing={{0}: (9, {})} | custom-call | flops 805306368 | bytes 12582912 | tf_op jit(solution)/shard_map/last/pallas_call | solution.py:519
  191.2 10.3 %collective-permute-start.51 = (f32[96,1024]{1,0:T(8,128)S(1)}, f32[96,1024]{1,0:T(8,128)S(1)}, u32[]{:S(2)}, u32[]{:S(2)}) collective-permute-start(f32[96,1024]{1,0:T(8,128)S(1)} %get-tuple-element.161.layer_ref.refs_3_), channel_id=1, source_target_pairs={{0,8},{8,0},{16,24},{24,16},{1,9},{9,1},{17,25},{25,17},{2,10},{10... | collective-permute-start | bytes 1179656 | tf_op jit(solution)/shard_map/ppermute | solution.py:580
  201.6 1.5 collective-permute-start.49
  203.1 2.6 %collective-permute-start.50 = (f32[2,1024]{1,0:T(2,128)S(1)}, f32[2,1024]{1,0:T(2,128)S(1)}, u32[]{:S(2)}, u32[]{:S(2)}) collective-permute-start(f32[2,1024]{1,0:T(2,128)S(1)} %get-tuple-element.163), channel_id=1, source_target_pairs={{1,0},{2,1},{3,2},{4,3},{5,4},{6,5},{7,6},{0,7},{9,8},{10,9},{11,1... | collective-permute-start | bytes 24584 | tf_op jit(solution)/shard_map/ppermute | solution.py:583
  206.8 1.2 collective-permute-start.52
  209.4 1.3 collective-permute-start.53
  210.7 1.9 collective-permute-start.48
  212.7 2.9 %collective-permute-done.53.refs_12_ = f32[56,1024]{1,0:T(8,128)S(1)} collective-permute-done((f32[56,1024]{1,0:T(8,128)S(1)}, f32[56,1024]{1,0:T(8,128)S(1)}, u32[]{:S(2)}, u32[]{:S(2)}) %collective-permute-start.53) | collective-permute-done | bytes 229408 | tf_op jit(solution)/shard_map/ppermute | solution.py:573
  215.6 1.4 collective-permute-start.54
  217.2 3.2 %collective-permute-done.48.refs_4_ = f32[96,1024]{1,0:T(8,128)S(1)} collective-permute-done((f32[96,1024]{1,0:T(8,128)S(1)}, f32[96,1024]{1,0:T(8,128)S(1)}, u32[]{:S(2)}, u32[]{:S(2)}) %collective-permute-start.48) | collective-permute-done | bytes 393248 | tf_op jit(solution)/shard_map/ppermute | solution.py:573
  220.3 2.2 residual.1
  (114 shorter events, 25.4 us)
Async XLA Ops:
  0.6 14.0 %copy-start = (bf16[256,1024]{1,0:T(8,128)(2,1)S(1)}, bf16[256,1024]{1,0:T(8,128)(2,1)}, u32[]{:S(2)}) copy-start(bf16[256,1024]{1,0:T(8,128)(2,1)} %constant.15.clone.inverse_ref) | copy-start | bytes 1572868
  1.8 12.8 %copy-start.2 = (bf16[8,96,256]{2,1,0:T(8,128)(2,1)S(1)}, bf16[8,96,256]{2,1,0:T(8,128)(2,1)}, u32[]{:S(2)}) copy-start(bf16[8,96,256]{2,1,0:T(8,128)(2,1)} %constant.16.clone.row_ref) | copy-start | bytes 1179652
  2.7 28.0 %slice-start = ((s8[8388608]{0:T(1024)(128)(4,1)}), s8[4194304]{0:T(1024)(128)(4,1)S(1)}, s32[]{:S(2)}) async-start(s8[8388608]{0:T(1024)(128)(4,1)} %bitcast.9), calls=%async_computation | async-start | bytes 8388608
  5.6 8.9 %collective-permute-start.4 = (bf16[8,96,128]{2,1,0:T(8,128)(2,1)S(1)}, bf16[8,96,128]{2,1,0:T(8,128)(2,1)S(1)}, u32[]{:S(2)}, u32[]{:S(2)}) collective-permute-start(bf16[8,96,128]{2,1,0:T(8,128)(2,1)S(1)} %get-tuple-element.91), channel_id=1, source_target_pairs={{0,1},{1,0},{2,3},{3,2},{4,5},{5,4},{6,7},{7,6},{8,9},{9,8},{10,11... | collective-permute-start | bytes 589832 | tf_op jit(solution)/shard_map/ppermute | solution.py:396
  7.7 7.8 %collective-permute-start.5 = (bf16[8,96,128]{2,1,0:T(8,128)(2,1)S(1)}, bf16[8,96,128]{2,1,0:T(8,128)(2,1)S(1)}, u32[]{:S(2)}, u32[]{:S(2)}) collective-permute-start(bf16[8,96,128]{2,1,0:T(8,128)(2,1)S(1)} %get-tuple-element.92), channel_id=1, source_target_pairs={{0,2},{1,3},{2,0},{3,1},{4,6},{5,7},{6,4},{7,5},{8,10},{9,11},{10,... | collective-permute-start | bytes 589832 | tf_op jit(solution)/shard_map/ppermute | solution.py:396
  9.0 21.7 %slice-start.1 = ((s8[8388608]{0:T(1024)(128)(4,1)}), s8[4194304]{0:T(1024)(128)(4,1)S(1)}, s32[]{:S(2)}) async-start(s8[8388608]{0:T(1024)(128)(4,1)} %bitcast.9), calls=%async_computation.1 | async-start | bytes 8388608
  9.0 8.5 %collective-permute-start.6 = (bf16[8,96,128]{2,1,0:T(8,128)(2,1)S(1)}, bf16[8,96,128]{2,1,0:T(8,128)(2,1)S(1)}, u32[]{:S(2)}, u32[]{:S(2)}) collective-permute-start(bf16[8,96,128]{2,1,0:T(8,128)(2,1)S(1)} %get-tuple-element.93), channel_id=1, source_target_pairs={{0,3},{1,2},{2,1},{3,0},{4,7},{5,6},{6,5},{7,4},{8,11},{9,10},{10,... | collective-permute-start | bytes 589832 | tf_op jit(solution)/shard_map/ppermute | solution.py:396
  11.9 10.1 %collective-permute-start = (bf16[8,96,128]{2,1,0:T(8,128)(2,1)S(1)}, bf16[8,96,128]{2,1,0:T(8,128)(2,1)S(1)}, u32[]{:S(2)}, u32[]{:S(2)}) collective-permute-start(bf16[8,96,128]{2,1,0:T(8,128)(2,1)S(1)} %get-tuple-element.84), channel_id=1, source_target_pairs={{0,1},{1,0},{2,3},{3,2},{4,5},{5,4},{6,7},{7,6},{8,9},{9,8},{10,11... | collective-permute-start | bytes 589832 | tf_op jit(solution)/shard_map/ppermute | solution.py:396
  13.3 8.7 %collective-permute-start.1 = (bf16[8,96,128]{2,1,0:T(8,128)(2,1)S(1)}, bf16[8,96,128]{2,1,0:T(8,128)(2,1)S(1)}, u32[]{:S(2)}, u32[]{:S(2)}) collective-permute-start(bf16[8,96,128]{2,1,0:T(8,128)(2,1)S(1)} %get-tuple-element.85), channel_id=1, source_target_pairs={{0,2},{1,3},{2,0},{3,1},{4,6},{5,7},{6,4},{7,5},{8,10},{9,11},{10,... | collective-permute-start | bytes 589832 | tf_op jit(solution)/shard_map/ppermute | solution.py:396
  14.5 14.3 %collective-permute-start.2 = (bf16[8,96,128]{2,1,0:T(8,128)(2,1)S(1)}, bf16[8,96,128]{2,1,0:T(8,128)(2,1)S(1)}, u32[]{:S(2)}, u32[]{:S(2)}) collective-permute-start(bf16[8,96,128]{2,1,0:T(8,128)(2,1)S(1)} %get-tuple-element.86), channel_id=1, source_target_pairs={{0,3},{1,2},{2,1},{3,0},{4,7},{5,6},{6,5},{7,4},{8,11},{9,10},{10,... | collective-permute-start | bytes 589832 | tf_op jit(solution)/shard_map/ppermute | solution.py:396
  18.1 12.6 %collective-permute-start.7 = (bf16[16,16,256]{2,1,0:T(8,128)(2,1)S(1)}, bf16[16,16,256]{2,1,0:T(8,128)(2,1)S(1)}, u32[]{:S(2)}, u32[]{:S(2)}) collective-permute-start(bf16[16,16,256]{2,1,0:T(8,128)(2,1)S(1)} %get-tuple-element.95), channel_id=1, source_target_pairs={{0,4},{1,5},{2,6},{3,7},{4,0},{5,1},{6,2},{7,3},{8,12},{9,13},{10,... | collective-permute-start | bytes 393224 | tf_op jit(solution)/shard_map/ppermute | solution.py:396
  29.3 8.7 %collective-permute-start.3 = (bf16[16,16,256]{2,1,0:T(8,128)(2,1)S(1)}, bf16[16,16,256]{2,1,0:T(8,128)(2,1)S(1)}, u32[]{:S(2)}, u32[]{:S(2)}) collective-permute-start(bf16[16,16,256]{2,1,0:T(8,128)(2,1)S(1)} %get-tuple-element.89), channel_id=1, source_target_pairs={{0,4},{1,5},{2,6},{3,7},{4,0},{5,1},{6,2},{7,3},{8,12},{9,13},{10,... | collective-permute-start | bytes 393224 | tf_op jit(solution)/shard_map/ppermute | solution.py:396
  30.7 8.5 %copy-start.4 = (bf16[32,32]{1,0:T(8,128)(2,1)S(1)}, bf16[32,32]{1,0:T(8,128)(2,1)}, u32[]{:S(2)}) copy-start(bf16[32,32]{1,0:T(8,128)(2,1)} %weight_ref.1) | copy-start | bytes 6148
  30.7 8.5 %copy-start.5 = (bf16[4,32]{1,0:T(4,128)(2,1)S(1)}, bf16[4,32]{1,0:T(4,128)(2,1)}, u32[]{:S(2)}) copy-start(bf16[4,32]{1,0:T(4,128)(2,1)} %decoder_ref.1) | copy-start | bytes 772
  38.0 15.8 %slice-start.2 = ((s8[6291456]{0:T(1024)(128)(4,1)}), s8[4194304]{0:T(1024)(128)(4,1)S(1)}, s32[]{:S(2)}) async-start(s8[6291456]{0:T(1024)(128)(4,1)} %bitcast.13), calls=%async_computation.2 | async-start | bytes 8388608
  39.0 11.4 %collective-permute-start.16 = (bf16[16,16,256]{2,1,0:T(8,128)(2,1)S(1)}, bf16[16,16,256]{2,1,0:T(8,128)(2,1)S(1)}, u32[]{:S(2)}, u32[]{:S(2)}) collective-permute-start(bf16[16,16,256]{2,1,0:T(8,128)(2,1)S(1)} %mix.11.mine_ref), channel_id=1, source_target_pairs={{0,4},{1,5},{2,6},{3,7},{4,0},{5,1},{6,2},{7,3},{8,12},{9,13},{10,... | collective-permute-start | bytes 393224 | tf_op jit(solution)/shard_map/ppermute | solution.py:396
  39.7 14.1 %slice-start.3 = ((s8[6291456]{0:T(1024)(128)(4,1)}), s8[2097152]{0:T(1024)(128)(4,1)S(1)}, s32[]{:S(2)}) async-start(s8[6291456]{0:T(1024)(128)(4,1)} %bitcast.13), calls=%async_computation.3 | async-start | bytes 4194304
  40.7 19.0 %collective-permute-start.8 = (bf16[16,16,256]{2,1,0:T(8,128)(2,1)S(1)}, bf16[16,16,256]{2,1,0:T(8,128)(2,1)S(1)}, u32[]{:S(2)}, u32[]{:S(2)}) collective-permute-start(bf16[16,16,256]{2,1,0:T(8,128)(2,1)S(1)} %mix.10.mine_ref), channel_id=1, source_target_pairs={{0,4},{1,5},{2,6},{3,7},{4,0},{5,1},{6,2},{7,3},{8,12},{9,13},{10,... | collective-permute-start | bytes 393224 | tf_op jit(solution)/shard_map/ppermute | solution.py:396
  51.0 11.5 %collective-permute-start.17 = (bf16[8,96,128]{2,1,0:T(8,128)(2,1)S(1)}, bf16[8,96,128]{2,1,0:T(8,128)(2,1)S(1)}, u32[]{:S(2)}, u32[]{:S(2)}) collective-permute-start(bf16[8,96,128]{2,1,0:T(8,128)(2,1)S(1)} %get-tuple-element.110), channel_id=1, source_target_pairs={{0,1},{1,0},{2,3},{3,2},{4,5},{5,4},{6,7},{7,6},{8,9},{9,8},{10,11... | collective-permute-start | bytes 589832 | tf_op jit(solution)/shard_map/ppermute | solution.py:396
  52.0 11.0 %collective-permute-start.18 = (bf16[8,96,128]{2,1,0:T(8,128)(2,1)S(1)}, bf16[8,96,128]{2,1,0:T(8,128)(2,1)S(1)}, u32[]{:S(2)}, u32[]{:S(2)}) collective-permute-start(bf16[8,96,128]{2,1,0:T(8,128)(2,1)S(1)} %get-tuple-element.111), channel_id=1, source_target_pairs={{0,2},{1,3},{2,0},{3,1},{4,6},{5,7},{6,4},{7,5},{8,10},{9,11},{10,... | collective-permute-start | bytes 589832 | tf_op jit(solution)/shard_map/ppermute | solution.py:396
  52.0 11.0 %collective-permute-start.19 = (bf16[8,96,128]{2,1,0:T(8,128)(2,1)S(1)}, bf16[8,96,128]{2,1,0:T(8,128)(2,1)S(1)}, u32[]{:S(2)}, u32[]{:S(2)}) collective-permute-start(bf16[8,96,128]{2,1,0:T(8,128)(2,1)S(1)} %get-tuple-element.112), channel_id=1, source_target_pairs={{0,3},{1,2},{2,1},{3,0},{4,7},{5,6},{6,5},{7,4},{8,11},{9,10},{10,... | collective-permute-start | bytes 589832 | tf_op jit(solution)/shard_map/ppermute | solution.py:396
  60.3 6.8 %collective-permute-start.10 = (bf16[8,96,128]{2,1,0:T(8,128)(2,1)S(1)}, bf16[8,96,128]{2,1,0:T(8,128)(2,1)S(1)}, u32[]{:S(2)}, u32[]{:S(2)}) collective-permute-start(bf16[8,96,128]{2,1,0:T(8,128)(2,1)S(1)} %get-tuple-element.98), channel_id=1, source_target_pairs={{0,2},{1,3},{2,0},{3,1},{4,6},{5,7},{6,4},{7,5},{8,10},{9,11},{10,... | collective-permute-start | bytes 589832 | tf_op jit(solution)/shard_map/ppermute | solution.py:396
  60.4 9.9 %collective-permute-start.11 = (bf16[8,96,128]{2,1,0:T(8,128)(2,1)S(1)}, bf16[8,96,128]{2,1,0:T(8,128)(2,1)S(1)}, u32[]{:S(2)}, u32[]{:S(2)}) collective-permute-start(bf16[8,96,128]{2,1,0:T(8,128)(2,1)S(1)} %get-tuple-element.99), channel_id=1, source_target_pairs={{0,3},{1,2},{2,1},{3,0},{4,7},{5,6},{6,5},{7,4},{8,11},{9,10},{10,... | collective-permute-start | bytes 589832 | tf_op jit(solution)/shard_map/ppermute | solution.py:396
  62.5 7.8 %collective-permute-start.9 = (bf16[8,96,128]{2,1,0:T(8,128)(2,1)S(1)}, bf16[8,96,128]{2,1,0:T(8,128)(2,1)S(1)}, u32[]{:S(2)}, u32[]{:S(2)}) collective-permute-start(bf16[8,96,128]{2,1,0:T(8,128)(2,1)S(1)} %get-tuple-element.97), channel_id=1, source_target_pairs={{0,1},{1,0},{2,3},{3,2},{4,5},{5,4},{6,7},{7,6},{8,9},{9,8},{10,11... | collective-permute-start | bytes 589832 | tf_op jit(solution)/shard_map/ppermute | solution.py:396
  66.1 11.8 %collective-permute-start.20 = (bf16[8,96,128]{2,1,0:T(8,128)(2,1)S(1)}, bf16[8,96,128]{2,1,0:T(8,128)(2,1)S(1)}, u32[]{:S(2)}, u32[]{:S(2)}) collective-permute-start(bf16[8,96,128]{2,1,0:T(8,128)(2,1)S(1)} %get-tuple-element.114), channel_id=1, source_target_pairs={{0,1},{1,0},{2,3},{3,2},{4,5},{5,4},{6,7},{7,6},{8,9},{9,8},{10,11... | collective-permute-start | bytes 589832 | tf_op jit(solution)/shard_map/ppermute | solution.py:396
  67.1 10.9 %collective-permute-start.21 = (bf16[8,96,128]{2,1,0:T(8,128)(2,1)S(1)}, bf16[8,96,128]{2,1,0:T(8,128)(2,1)S(1)}, u32[]{:S(2)}, u32[]{:S(2)}) collective-permute-start(bf16[8,96,128]{2,1,0:T(8,128)(2,1)S(1)} %get-tuple-element.115), channel_id=1, source_target_pairs={{0,2},{1,3},{2,0},{3,1},{4,6},{5,7},{6,4},{7,5},{8,10},{9,11},{10,... | collective-permute-start | bytes 589832 | tf_op jit(solution)/shard_map/ppermute | solution.py:396
  67.2 11.5 %collective-permute-start.22 = (bf16[8,96,128]{2,1,0:T(8,128)(2,1)S(1)}, bf16[8,96,128]{2,1,0:T(8,128)(2,1)S(1)}, u32[]{:S(2)}, u32[]{:S(2)}) collective-permute-start(bf16[8,96,128]{2,1,0:T(8,128)(2,1)S(1)} %get-tuple-element.116), channel_id=1, source_target_pairs={{0,3},{1,2},{2,1},{3,0},{4,7},{5,6},{6,5},{7,4},{8,11},{9,10},{10,... | collective-permute-start | bytes 589832 | tf_op jit(solution)/shard_map/ppermute | solution.py:396
  73.3 12.5 %collective-permute-start.12 = (bf16[8,96,128]{2,1,0:T(8,128)(2,1)S(1)}, bf16[8,96,128]{2,1,0:T(8,128)(2,1)S(1)}, u32[]{:S(2)}, u32[]{:S(2)}) collective-permute-start(bf16[8,96,128]{2,1,0:T(8,128)(2,1)S(1)} %get-tuple-element.104), channel_id=1, source_target_pairs={{0,1},{1,0},{2,3},{3,2},{4,5},{5,4},{6,7},{7,6},{8,9},{9,8},{10,11... | collective-permute-start | bytes 589832 | tf_op jit(solution)/shard_map/ppermute | solution.py:396
  73.9 11.9 %collective-permute-start.13 = (bf16[8,96,128]{2,1,0:T(8,128)(2,1)S(1)}, bf16[8,96,128]{2,1,0:T(8,128)(2,1)S(1)}, u32[]{:S(2)}, u32[]{:S(2)}) collective-permute-start(bf16[8,96,128]{2,1,0:T(8,128)(2,1)S(1)} %get-tuple-element.105), channel_id=1, source_target_pairs={{0,2},{1,3},{2,0},{3,1},{4,6},{5,7},{6,4},{7,5},{8,10},{9,11},{10,... | collective-permute-start | bytes 589832 | tf_op jit(solution)/shard_map/ppermute | solution.py:396
  77.9 9.5 %collective-permute-start.14 = (bf16[8,96,128]{2,1,0:T(8,128)(2,1)S(1)}, bf16[8,96,128]{2,1,0:T(8,128)(2,1)S(1)}, u32[]{:S(2)}, u32[]{:S(2)}) collective-permute-start(bf16[8,96,128]{2,1,0:T(8,128)(2,1)S(1)} %get-tuple-element.106), channel_id=1, source_target_pairs={{0,3},{1,2},{2,1},{3,0},{4,7},{5,6},{6,5},{7,4},{8,11},{9,10},{10,... | collective-permute-start | bytes 589832 | tf_op jit(solution)/shard_map/ppermute | solution.py:396
  79.2 8.7 %collective-permute-start.23 = (bf16[16,16,256]{2,1,0:T(8,128)(2,1)S(1)}, bf16[16,16,256]{2,1,0:T(8,128)(2,1)S(1)}, u32[]{:S(2)}, u32[]{:S(2)}) collective-permute-start(bf16[16,16,256]{2,1,0:T(8,128)(2,1)S(1)} %get-tuple-element.118), channel_id=1, source_target_pairs={{0,4},{1,5},{2,6},{3,7},{4,0},{5,1},{6,2},{7,3},{8,12},{9,13},{10,... | collective-permute-start | bytes 393224 | tf_op jit(solution)/shard_map/ppermute | solution.py:396
  87.9 8.9 %collective-permute-start.15 = (bf16[16,16,256]{2,1,0:T(8,128)(2,1)S(1)}, bf16[16,16,256]{2,1,0:T(8,128)(2,1)S(1)}, u32[]{:S(2)}, u32[]{:S(2)}) collective-permute-start(bf16[16,16,256]{2,1,0:T(8,128)(2,1)S(1)} %get-tuple-element.108), channel_id=1, source_target_pairs={{0,4},{1,5},{2,6},{3,7},{4,0},{5,1},{6,2},{7,3},{8,12},{9,13},{10,... | collective-permute-start | bytes 393224 | tf_op jit(solution)/shard_map/ppermute | solution.py:396
  97.8 5.0 %collective-permute-start.32 = (bf16[16,16,256]{2,1,0:T(8,128)(2,1)S(1)}, bf16[16,16,256]{2,1,0:T(8,128)(2,1)S(1)}, u32[]{:S(2)}, u32[]{:S(2)}) collective-permute-start(bf16[16,16,256]{2,1,0:T(8,128)(2,1)S(1)} %mix.14.mine_ref), channel_id=1, source_target_pairs={{0,4},{1,5},{2,6},{3,7},{4,0},{5,1},{6,2},{7,3},{8,12},{9,13},{10,... | collective-permute-start | bytes 393224 | tf_op jit(solution)/shard_map/ppermute | solution.py:396
  103.4 9.4 %collective-permute-start.33 = (bf16[8,96,128]{2,1,0:T(8,128)(2,1)S(1)}, bf16[8,96,128]{2,1,0:T(8,128)(2,1)S(1)}, u32[]{:S(2)}, u32[]{:S(2)}) collective-permute-start(bf16[8,96,128]{2,1,0:T(8,128)(2,1)S(1)} %get-tuple-element.132), channel_id=1, source_target_pairs={{0,1},{1,0},{2,3},{3,2},{4,5},{5,4},{6,7},{7,6},{8,9},{9,8},{10,11... | collective-permute-start | bytes 589832 | tf_op jit(solution)/shard_map/ppermute | solution.py:396
  105.6 5.4 %collective-permute-start.24 = (bf16[16,16,256]{2,1,0:T(8,128)(2,1)S(1)}, bf16[16,16,256]{2,1,0:T(8,128)(2,1)S(1)}, u32[]{:S(2)}, u32[]{:S(2)}) collective-permute-start(bf16[16,16,256]{2,1,0:T(8,128)(2,1)S(1)} %mix.13.mine_ref), channel_id=1, source_target_pairs={{0,4},{1,5},{2,6},{3,7},{4,0},{5,1},{6,2},{7,3},{8,12},{9,13},{10,... | collective-permute-start | bytes 393224 | tf_op jit(solution)/shard_map/ppermute | solution.py:396
  105.6 14.6 %collective-permute-start.34 = (bf16[8,96,128]{2,1,0:T(8,128)(2,1)S(1)}, bf16[8,96,128]{2,1,0:T(8,128)(2,1)S(1)}, u32[]{:S(2)}, u32[]{:S(2)}) collective-permute-start(bf16[8,96,128]{2,1,0:T(8,128)(2,1)S(1)} %get-tuple-element.133), channel_id=1, source_target_pairs={{0,2},{1,3},{2,0},{3,1},{4,6},{5,7},{6,4},{7,5},{8,10},{9,11},{10,... | collective-permute-start | bytes 589832 | tf_op jit(solution)/shard_map/ppermute | solution.py:396
  107.4 12.9 %collective-permute-start.35 = (bf16[8,96,128]{2,1,0:T(8,128)(2,1)S(1)}, bf16[8,96,128]{2,1,0:T(8,128)(2,1)S(1)}, u32[]{:S(2)}, u32[]{:S(2)}) collective-permute-start(bf16[8,96,128]{2,1,0:T(8,128)(2,1)S(1)} %get-tuple-element.134), channel_id=1, source_target_pairs={{0,3},{1,2},{2,1},{3,0},{4,7},{5,6},{6,5},{7,4},{8,11},{9,10},{10,... | collective-permute-start | bytes 589832 | tf_op jit(solution)/shard_map/ppermute | solution.py:396
  111.6 13.1 %collective-permute-start.25 = (bf16[8,96,128]{2,1,0:T(8,128)(2,1)S(1)}, bf16[8,96,128]{2,1,0:T(8,128)(2,1)S(1)}, u32[]{:S(2)}, u32[]{:S(2)}) collective-permute-start(bf16[8,96,128]{2,1,0:T(8,128)(2,1)S(1)} %get-tuple-element.120), channel_id=1, source_target_pairs={{0,1},{1,0},{2,3},{3,2},{4,5},{5,4},{6,7},{7,6},{8,9},{9,8},{10,11... | collective-permute-start | bytes 589832 | tf_op jit(solution)/shard_map/ppermute | solution.py:396
  112.8 13.3 %collective-permute-start.26 = (bf16[8,96,128]{2,1,0:T(8,128)(2,1)S(1)}, bf16[8,96,128]{2,1,0:T(8,128)(2,1)S(1)}, u32[]{:S(2)}, u32[]{:S(2)}) collective-permute-start(bf16[8,96,128]{2,1,0:T(8,128)(2,1)S(1)} %get-tuple-element.121), channel_id=1, source_target_pairs={{0,2},{1,3},{2,0},{3,1},{4,6},{5,7},{6,4},{7,5},{8,10},{9,11},{10,... | collective-permute-start | bytes 589832 | tf_op jit(solution)/shard_map/ppermute | solution.py:396
  112.8 13.3 %collective-permute-start.27 = (bf16[8,96,128]{2,1,0:T(8,128)(2,1)S(1)}, bf16[8,96,128]{2,1,0:T(8,128)(2,1)S(1)}, u32[]{:S(2)}, u32[]{:S(2)}) collective-permute-start(bf16[8,96,128]{2,1,0:T(8,128)(2,1)S(1)} %get-tuple-element.122), channel_id=1, source_target_pairs={{0,3},{1,2},{2,1},{3,0},{4,7},{5,6},{6,5},{7,4},{8,11},{9,10},{10,... | collective-permute-start | bytes 589832 | tf_op jit(solution)/shard_map/ppermute | solution.py:396
  123.3 7.0 %collective-permute-start.36 = (bf16[8,96,128]{2,1,0:T(8,128)(2,1)S(1)}, bf16[8,96,128]{2,1,0:T(8,128)(2,1)S(1)}, u32[]{:S(2)}, u32[]{:S(2)}) collective-permute-start(bf16[8,96,128]{2,1,0:T(8,128)(2,1)S(1)} %get-tuple-element.136), channel_id=1, source_target_pairs={{0,1},{1,0},{2,3},{3,2},{4,5},{5,4},{6,7},{7,6},{8,9},{9,8},{10,11... | collective-permute-start | bytes 589832 | tf_op jit(solution)/shard_map/ppermute | solution.py:396
  124.6 7.3 %collective-permute-start.37 = (bf16[8,96,128]{2,1,0:T(8,128)(2,1)S(1)}, bf16[8,96,128]{2,1,0:T(8,128)(2,1)S(1)}, u32[]{:S(2)}, u32[]{:S(2)}) collective-permute-start(bf16[8,96,128]{2,1,0:T(8,128)(2,1)S(1)} %get-tuple-element.137), channel_id=1, source_target_pairs={{0,2},{1,3},{2,0},{3,1},{4,6},{5,7},{6,4},{7,5},{8,10},{9,11},{10,... | collective-permute-start | bytes 589832 | tf_op jit(solution)/shard_map/ppermute | solution.py:396
  124.6 8.6 %collective-permute-start.38 = (bf16[8,96,128]{2,1,0:T(8,128)(2,1)S(1)}, bf16[8,96,128]{2,1,0:T(8,128)(2,1)S(1)}, u32[]{:S(2)}, u32[]{:S(2)}) collective-permute-start(bf16[8,96,128]{2,1,0:T(8,128)(2,1)S(1)} %get-tuple-element.138), channel_id=1, source_target_pairs={{0,3},{1,2},{2,1},{3,0},{4,7},{5,6},{6,5},{7,4},{8,11},{9,10},{10,... | collective-permute-start | bytes 589832 | tf_op jit(solution)/shard_map/ppermute | solution.py:396
  129.2 9.1 %collective-permute-start.28 = (bf16[8,96,128]{2,1,0:T(8,128)(2,1)S(1)}, bf16[8,96,128]{2,1,0:T(8,128)(2,1)S(1)}, u32[]{:S(2)}, u32[]{:S(2)}) collective-permute-start(bf16[8,96,128]{2,1,0:T(8,128)(2,1)S(1)} %get-tuple-element.126), channel_id=1, source_target_pairs={{0,1},{1,0},{2,3},{3,2},{4,5},{5,4},{6,7},{7,6},{8,9},{9,8},{10,11... | collective-permute-start | bytes 589832 | tf_op jit(solution)/shard_map/ppermute | solution.py:396
  130.4 7.9 %collective-permute-start.29 = (bf16[8,96,128]{2,1,0:T(8,128)(2,1)S(1)}, bf16[8,96,128]{2,1,0:T(8,128)(2,1)S(1)}, u32[]{:S(2)}, u32[]{:S(2)}) collective-permute-start(bf16[8,96,128]{2,1,0:T(8,128)(2,1)S(1)} %get-tuple-element.127), channel_id=1, source_target_pairs={{0,2},{1,3},{2,0},{3,1},{4,6},{5,7},{6,4},{7,5},{8,10},{9,11},{10,... | collective-permute-start | bytes 589832 | tf_op jit(solution)/shard_map/ppermute | solution.py:396
  130.4 11.1 %collective-permute-start.30 = (bf16[8,96,128]{2,1,0:T(8,128)(2,1)S(1)}, bf16[8,96,128]{2,1,0:T(8,128)(2,1)S(1)}, u32[]{:S(2)}, u32[]{:S(2)}) collective-permute-start(bf16[8,96,128]{2,1,0:T(8,128)(2,1)S(1)} %get-tuple-element.128), channel_id=1, source_target_pairs={{0,3},{1,2},{2,1},{3,0},{4,7},{5,6},{6,5},{7,4},{8,11},{9,10},{10,... | collective-permute-start | bytes 589832 | tf_op jit(solution)/shard_map/ppermute | solution.py:396
  133.7 8.4 %collective-permute-start.39 = (bf16[16,16,256]{2,1,0:T(8,128)(2,1)S(1)}, bf16[16,16,256]{2,1,0:T(8,128)(2,1)S(1)}, u32[]{:S(2)}, u32[]{:S(2)}) collective-permute-start(bf16[16,16,256]{2,1,0:T(8,128)(2,1)S(1)} %get-tuple-element.140), channel_id=1, source_target_pairs={{0,4},{1,5},{2,6},{3,7},{4,0},{5,1},{6,2},{7,3},{8,12},{9,13},{10,... | collective-permute-start | bytes 393224 | tf_op jit(solution)/shard_map/ppermute | solution.py:396
  142.0 6.3 %collective-permute-start.31 = (bf16[16,16,256]{2,1,0:T(8,128)(2,1)S(1)}, bf16[16,16,256]{2,1,0:T(8,128)(2,1)S(1)}, u32[]{:S(2)}, u32[]{:S(2)}) collective-permute-start(bf16[16,16,256]{2,1,0:T(8,128)(2,1)S(1)} %get-tuple-element.130), channel_id=1, source_target_pairs={{0,4},{1,5},{2,6},{3,7},{4,0},{5,1},{6,2},{7,3},{8,12},{9,13},{10,... | collective-permute-start | bytes 393224 | tf_op jit(solution)/shard_map/ppermute | solution.py:396
  149.4 9.0 %collective-permute-start.44 = (bf16[16,16,256]{2,1,0:T(8,128)(2,1)S(1)}, bf16[16,16,256]{2,1,0:T(8,128)(2,1)S(1)}, u32[]{:S(2)}, u32[]{:S(2)}) collective-permute-start(bf16[16,16,256]{2,1,0:T(8,128)(2,1)S(1)} %mix.17.mine_ref), channel_id=1, source_target_pairs={{0,4},{1,5},{2,6},{3,7},{4,0},{5,1},{6,2},{7,3},{8,12},{9,13},{10,... | collective-permute-start | bytes 393224 | tf_op jit(solution)/shard_map/ppermute | solution.py:396
  158.9 10.2 %collective-permute-start.45 = (bf16[8,96,128]{2,1,0:T(8,128)(2,1)S(1)}, bf16[8,96,128]{2,1,0:T(8,128)(2,1)S(1)}, u32[]{:S(2)}, u32[]{:S(2)}) collective-permute-start(bf16[8,96,128]{2,1,0:T(8,128)(2,1)S(1)} %get-tuple-element.149), channel_id=1, source_target_pairs={{0,1},{1,0},{2,3},{3,2},{4,5},{5,4},{6,7},{7,6},{8,9},{9,8},{10,11... | collective-permute-start | bytes 589832 | tf_op jit(solution)/shard_map/ppermute | solution.py:396
  160.1 8.2 %collective-permute-start.40 = (bf16[16,16,256]{2,1,0:T(8,128)(2,1)S(1)}, bf16[16,16,256]{2,1,0:T(8,128)(2,1)S(1)}, u32[]{:S(2)}, u32[]{:S(2)}) collective-permute-start(bf16[16,16,256]{2,1,0:T(8,128)(2,1)S(1)} %mix.16.mine_ref), channel_id=1, source_target_pairs={{0,4},{1,5},{2,6},{3,7},{4,0},{5,1},{6,2},{7,3},{8,12},{9,13},{10,... | collective-permute-start | bytes 393224 | tf_op jit(solution)/shard_map/ppermute | solution.py:396
  160.1 17.5 %collective-permute-start.46 = (bf16[8,96,128]{2,1,0:T(8,128)(2,1)S(1)}, bf16[8,96,128]{2,1,0:T(8,128)(2,1)S(1)}, u32[]{:S(2)}, u32[]{:S(2)}) collective-permute-start(bf16[8,96,128]{2,1,0:T(8,128)(2,1)S(1)} %get-tuple-element.150), channel_id=1, source_target_pairs={{0,2},{1,3},{2,0},{3,1},{4,6},{5,7},{6,4},{7,5},{8,10},{9,11},{10,... | collective-permute-start | bytes 589832 | tf_op jit(solution)/shard_map/ppermute | solution.py:396
  161.7 15.9 %collective-permute-start.47 = (bf16[8,96,128]{2,1,0:T(8,128)(2,1)S(1)}, bf16[8,96,128]{2,1,0:T(8,128)(2,1)S(1)}, u32[]{:S(2)}, u32[]{:S(2)}) collective-permute-start(bf16[8,96,128]{2,1,0:T(8,128)(2,1)S(1)} %get-tuple-element.151), channel_id=1, source_target_pairs={{0,3},{1,2},{2,1},{3,0},{4,7},{5,6},{6,5},{7,4},{8,11},{9,10},{10,... | collective-permute-start | bytes 589832 | tf_op jit(solution)/shard_map/ppermute | solution.py:396
  168.9 15.5 %collective-permute-start.41 = (bf16[8,96,128]{2,1,0:T(8,128)(2,1)S(1)}, bf16[8,96,128]{2,1,0:T(8,128)(2,1)S(1)}, u32[]{:S(2)}, u32[]{:S(2)}) collective-permute-start(bf16[8,96,128]{2,1,0:T(8,128)(2,1)S(1)} %get-tuple-element.142), channel_id=1, source_target_pairs={{0,1},{1,0},{2,3},{3,2},{4,5},{5,4},{6,7},{7,6},{8,9},{9,8},{10,11... | collective-permute-start | bytes 589832 | tf_op jit(solution)/shard_map/ppermute | solution.py:396
  169.2 15.2 %collective-permute-start.42 = (bf16[8,96,128]{2,1,0:T(8,128)(2,1)S(1)}, bf16[8,96,128]{2,1,0:T(8,128)(2,1)S(1)}, u32[]{:S(2)}, u32[]{:S(2)}) collective-permute-start(bf16[8,96,128]{2,1,0:T(8,128)(2,1)S(1)} %get-tuple-element.143), channel_id=1, source_target_pairs={{0,2},{1,3},{2,0},{3,1},{4,6},{5,7},{6,4},{7,5},{8,10},{9,11},{10,... | collective-permute-start | bytes 589832 | tf_op jit(solution)/shard_map/ppermute | solution.py:396
  169.2 15.2 %collective-permute-start.43 = (bf16[8,96,128]{2,1,0:T(8,128)(2,1)S(1)}, bf16[8,96,128]{2,1,0:T(8,128)(2,1)S(1)}, u32[]{:S(2)}, u32[]{:S(2)}) collective-permute-start(bf16[8,96,128]{2,1,0:T(8,128)(2,1)S(1)} %get-tuple-element.144), channel_id=1, source_target_pairs={{0,3},{1,2},{2,1},{3,0},{4,7},{5,6},{6,5},{7,4},{8,11},{9,10},{10,... | collective-permute-start | bytes 589832 | tf_op jit(solution)/shard_map/ppermute | solution.py:396
  184.4 32.6 %copy-start.7 = (f32[96]{0:T(128)S(1)}, f32[96]{0:T(128)}, u32[]{:S(2)}) copy-start(f32[96]{0:T(128)} %param.15) | copy-start | bytes 1156
  191.2 17.6 %collective-permute-start.51 = (f32[96,1024]{1,0:T(8,128)S(1)}, f32[96,1024]{1,0:T(8,128)S(1)}, u32[]{:S(2)}, u32[]{:S(2)}) collective-permute-start(f32[96,1024]{1,0:T(8,128)S(1)} %get-tuple-element.161.layer_ref.refs_3_), channel_id=1, source_target_pairs={{0,8},{8,0},{16,24},{24,16},{1,9},{9,1},{17,25},{25,17},{2,10},{10... | collective-permute-start | bytes 1179656 | tf_op jit(solution)/shard_map/ppermute | solution.py:580
  201.6 5.2 %collective-permute-start.49 = (f32[2,1024]{1,0:T(2,128)S(1)}, f32[2,1024]{1,0:T(2,128)S(1)}, u32[]{:S(2)}, u32[]{:S(2)}) collective-permute-start(f32[2,1024]{1,0:T(2,128)S(1)} %get-tuple-element.162), channel_id=1, source_target_pairs={{0,1},{1,2},{2,3},{3,4},{4,5},{5,6},{6,7},{7,0},{8,9},{9,10},{10,1... | collective-permute-start | bytes 24584 | tf_op jit(solution)/shard_map/ppermute | solution.py:582
  203.1 3.7 %collective-permute-start.50 = (f32[2,1024]{1,0:T(2,128)S(1)}, f32[2,1024]{1,0:T(2,128)S(1)}, u32[]{:S(2)}, u32[]{:S(2)}) collective-permute-start(f32[2,1024]{1,0:T(2,128)S(1)} %get-tuple-element.163), channel_id=1, source_target_pairs={{1,0},{2,1},{3,2},{4,3},{5,4},{6,5},{7,6},{0,7},{9,8},{10,9},{11,1... | collective-permute-start | bytes 24584 | tf_op jit(solution)/shard_map/ppermute | solution.py:583
  206.8 2.0 collective-permute-start.52
  209.4 6.2 %collective-permute-start.53 = (f32[56,1024]{1,0:T(8,128)S(1)}, f32[56,1024]{1,0:T(8,128)S(1)}, u32[]{:S(2)}, u32[]{:S(2)}) collective-permute-start(f32[56,1024]{1,0:T(8,128)S(1)} %pair.1), channel_id=1, source_target_pairs={{0,16},{8,24},{1,17},{9,25},{2,18},{10,26},{3,19},{11,27},{4,20},{... | collective-permute-start | bytes 688136 | tf_op jit(solution)/shard_map/ppermute | solution.py:573
  210.7 9.6 %collective-permute-start.48 = (f32[96,1024]{1,0:T(8,128)S(1)}, f32[96,1024]{1,0:T(8,128)S(1)}, u32[]{:S(2)}, u32[]{:S(2)}) collective-permute-start(f32[96,1024]{1,0:T(8,128)S(1)} %get-tuple-element.160.refs_2_), channel_id=1, source_target_pairs={{0,8},{8,16},{16,24},{1,9},{9,17},{17,25},{2,10},{10,18},{18,26},{... | collective-permute-start | bytes 1179656 | tf_op jit(solution)/shard_map/ppermute | solution.py:573
  215.6 4.7 %collective-permute-start.54 = (f32[56,1024]{1,0:T(8,128)S(1)}, f32[56,1024]{1,0:T(8,128)S(1)}, u32[]{:S(2)}, u32[]{:S(2)}) collective-permute-start(f32[56,1024]{1,0:T(8,128)S(1)} %collective-permute-done.53.refs_12_), channel_id=1, source_target_pairs={{0,8},{8,0},{16,24},{24,16},{1,9},{9,1},{17,25},{25,17},{2,10},{10... | collective-permute-start | bytes 688136 | tf_op jit(solution)/shard_map/ppermute | solution.py:601
  (3 other events, 15.6 us)

commit v6 on v5

--- a/solution.py
+++ b/solution.py
@@ -32,7 +32,7 @@
     angle = turned(np.arange(modes, dtype=np.int64), np.arange(cells, dtype=np.int64), cells)
     pair = np.stack([np.cos(angle), -np.sin(angle)], 0).astype(np.float32)
     factor = (np.where(np.arange(modes) == 0, 1.0, 2.0).astype(np.float32) / np.float32(total))
-    inverse = pair * factor[None, :, None]
+    inverse = pair * factor[None, :, None] * np.float32(0.5)
     own = modes // slices
 
     def by_slice(table):
@@ -106,8 +106,8 @@
     full = dot(left, pick, ((1,), (1,)))
     down = lax.broadcasted_iota(jnp.int32, (count, count), 0) % block
     across = lax.broadcasted_iota(jnp.int32, (count, count), 1) % block
-    square_ref[...] = jnp.where(down == across, full, 0.0).astype(BF)
-    column_ref[...] = jnp.sum(jnp.where(mine, bias_ref[...], 0.0), 1, keepdims=True)
+    square_ref[...] = jnp.where(down == across, 0.5 * full, 0.0).astype(BF)
+    column_ref[...] = 0.5 * jnp.sum(jnp.where(mine, bias_ref[...], 0.0), 1, keepdims=True)
     fields = decoder_ref.shape[0]
     lines = channels * fields
     row = lax.broadcasted_iota(jnp.int32, (lines, channels), 0) // fields
@@ -184,10 +184,9 @@
             back_refs[d][g] = back[d * rows : (d + 1) * rows].astype(BF)
 
 
-def gelu(x):
-    scale = math.sqrt(2.0 / math.pi)
-    half = 0.5 * x
-    return half + half * jnp.tanh(x * (scale + (scale * 0.044715) * (x * x)))
+def gelu(half):
+    scale = 2.0 * math.sqrt(2.0 / math.pi)
+    return half + half * jnp.tanh(half * (scale + (scale * 4.0 * 0.044715) * (half * half)))
 
 
 def spread_of(pack, back_refs, table_ref):
@@ -278,7 +277,7 @@
     for t in range(rows // block):
         at = slice(t * block, (t + 1) * block)
         state = jnp.concatenate([ref[:, at] for ref in state_refs], 0).reshape(count, cells)
-        source = forcing_ref[:, at].reshape(count, cells).astype(F32) + bias_ref[...]
+        source = 0.5 * forcing_ref[:, at].reshape(count, cells).astype(F32) + bias_ref[...]
         out = dot(weight_ref[...], state, ((1,), (0,))) + source
         out_ref[:, at] = out.reshape(channels, block, cells)
 

time: 223 us -> 224 us (level)
  starting transfers between devices: 61.1 us -> 63.6 us
  transfers between devices with their start and end apart: 55 -> 55, of which waited for: 24 -> 24; matrix products, arithmetic and copies ran while one was open for 0% -> 0% of each run, Pallas kernels for 25% -> 24%
where the time goes in v6:
time: 224 us
  waiting for transfers between devices  86.3 us (39%)
  Pallas kernels  71 us (32%)
  starting transfers between devices  63.6 us (28%)
    ppermute x48, waiting for transfers between devices, swap(): return lax.ppermute(value, 'gy', [(g, g ^ distance) for g in range(slices)])  78.9 us
    ppermute x48, starting transfers between devices, swap(): return lax.ppermute(value, 'gy', [(g, g ^ distance) for g in range(slices)])  41.4 us
    pallas_call x3, Pallas kernels, pointwise(): pl.pallas_call(functools.partial(pointwise_kernel, len(states), block), g...  18 us
    pallas_call x2, Pallas kernels, last(): pl.pallas_call(functools.partial(last_kernel, pack, peers, n * size, kind...  12.9 us
    pallas_call x9, Pallas kernels, mix(): pl.pallas_call(functools.partial(mix_kernel, n, CHUNKS, outputs), in_spec...  11.9 us
    pallas_call x4, Pallas kernels, update(): pl.pallas_call(functools.partial(update_kernel, pack, peers), grid=(part...  11.1 us
    ppermute x1, starting transfers between devices, on_device(): other = lax.ppermute(layer, 'lev', partner)  10.2 us
    pallas_call x2, Pallas kernels, near_of(): pl.pallas_call(functools.partial(near_kernel, pack), grid=(part // many,)...  5.78 us
  transfers between devices with their start and end apart: 55, of which 24 were waited for; matrix products, arithmetic and copies ran while one was open for 0% of the time, Pallas kernels for 24%

profile of v6, /device:TPU:1, one launch (start us, length us, event | category | flops | bytes accessed | tf_op | source)
XLA Modules:
  0.0 223.5 jit_solution(13807402193115877498)
XLA Ops:
  2.7 2.9 %near.3 = (bf16[8,96,128]{2,1,0:T(8,128)(2,1)S(1)}, bf16[8,96,128]{2,1,0:T(8,128)(2,1)S(1)}, bf16[8,96,128]{2,1,0:T(8,128)(2,1)S(1)}, bf16[8,96,128]{2,1,0:T(8,128)(2,1)S(1)}) custom-call(bf16[32,96,1024]{2,1,0:T(8,128)(2,1)} %bitcast.11, bf16[1024,256]{1,0:T(8,128)(2,1)S(1)} %forward_table.1.table_ref.refs_6_), custom_call_target="tpu_custom_call" | custom-call | flops 805306368 | bytes 3145728 | tf_op jit(solution)/shard_map/near/pallas_call | solution.py:408
  5.6 2.1 collective-permute-start.4
  7.7 1.3 collective-permute-start.5
  9.0 2.9 %near.2 = (bf16[8,96,128]{2,1,0:T(8,128)(2,1)S(1)}, bf16[8,96,128]{2,1,0:T(8,128)(2,1)S(1)}, bf16[8,96,128]{2,1,0:T(8,128)(2,1)S(1)}, bf16[8,96,128]{2,1,0:T(8,128)(2,1)S(1)}) custom-call(bf16[32,96,1024]{2,1,0:T(8,128)(2,1)} %bitcast.12, bf16[1024,256]{1,0:T(8,128)(2,1)S(1)} %forward_table.1.table_ref.refs_6_), custom_call_target="tpu_custom_call" | custom-call | flops 805306368 | bytes 3145728 | tf_op jit(solution)/shard_map/near/pallas_call | solution.py:408
  11.9 1.4 collective-permute-start
  13.3 1.2 collective-permute-start.1
  15.5 2.1 collective-permute-done.6.refs_3_
  18.1 2.2 collective-permute-start.7
  20.3 1.7 collective-permute-done.refs_1_
  22.0 6.8 %collective-permute-done.2.refs_3_ = bf16[8,96,128]{2,1,0:T(8,128)(2,1)S(1)} collective-permute-done((bf16[8,96,128]{2,1,0:T(8,128)(2,1)S(1)}, bf16[8,96,128]{2,1,0:T(8,128)(2,1)S(1)}, u32[]{:S(2)}, u32[]{:S(2)}) %collective-permute-start.2) | collective-permute-done | bytes 196640 | tf_op jit(solution)/shard_map/ppermute | solution.py:395
  29.3 1.4 collective-permute-start.3
  30.7 1.8 mix.9.refs_3_
  32.6 5.4 %collective-permute-done.3.refs_1_ = bf16[16,16,256]{2,1,0:T(8,128)(2,1)S(1)} collective-permute-done((bf16[16,16,256]{2,1,0:T(8,128)(2,1)S(1)}, bf16[16,16,256]{2,1,0:T(8,128)(2,1)S(1)}, u32[]{:S(2)}, u32[]{:S(2)}) %collective-permute-start.3) | collective-permute-done | bytes 131104 | tf_op jit(solution)/shard_map/ppermute | solution.py:395
  40.7 2.4 %collective-permute-start.8 = (bf16[16,16,256]{2,1,0:T(8,128)(2,1)S(1)}, bf16[16,16,256]{2,1,0:T(8,128)(2,1)S(1)}, u32[]{:S(2)}, u32[]{:S(2)}) collective-permute-start(bf16[16,16,256]{2,1,0:T(8,128)(2,1)S(1)} %mix.10.mine_ref), channel_id=1, source_target_pairs={{0,4},{1,5},{2,6},{3,7},{4,0},{5,1},{6,2},{7,3},{8,12},{9,13},{10,... | collective-permute-start | bytes 393224 | tf_op jit(solution)/shard_map/ppermute | solution.py:395
  43.1 7.3 %collective-permute-done.16.theirs_ref = bf16[16,16,256]{2,1,0:T(8,128)(2,1)S(1)} collective-permute-done((bf16[16,16,256]{2,1,0:T(8,128)(2,1)S(1)}, bf16[16,16,256]{2,1,0:T(8,128)(2,1)S(1)}, u32[]{:S(2)}, u32[]{:S(2)}) %collective-permute-start.16) | collective-permute-done | bytes 131104 | tf_op jit(solution)/shard_map/ppermute | solution.py:395
  52.0 1.7 collective-permute-start.19
  53.8 6.0 %pointwise.3.refs_4_ = f32[32,96,1024]{2,1,0:T(8,128)S(1)} custom-call(bf16[32,96,1024]{2,1,0:T(8,128)(2,1)S(1)} %bitcast.15, bf16[32,96,1024]{2,1,0:T(8,128)(2,1)S(1)} %bitcast.16, bf16[512,512]{1,0:T(8,128)(2,1)S(1)} %get-tuple-element.100.refs_2_.refs_3_, f32[512,1]{1,0:T(8,128)S(1)} %get-tuple-element.101.refs_3_.refs_4_), custom_call_target="tpu_custom_call" | custom-call | flops 3221225472 | bytes 25165824 | tf_op jit(solution)/shard_map/pointwise/pallas_call | solution.py:475
  60.4 2.1 collective-permute-start.11
  63.1 2.8 %update.5 = (bf16[16,96,1024]{2,1,0:T(8,128)(2,1)S(1)}, bf16[8,96,128]{2,1,0:T(8,128)(2,1)S(1)}, bf16[8,96,128]{2,1,0:T(8,128)(2,1)S(1)}, bf16[8,96,128]{2,1,0:T(8,128)(2,1)S(1)}, bf16[8,96,128]{2,1,0:T(8,128)(2,1)S(1)}) custom-call(bf16[8,96,128]{2,1,0:T(8,128)(2,1)S(1)} %get-tuple-element.109.refs_0_, ...), custom_call_target="tpu_custom_call" | custom-call | flops 1610612736 | bytes 9437184 | tf_op jit(solution)/shard_map/update/pallas_call | solution.py:494
  66.9 1.6 collective-permute-start.22
  68.6 1.7 collective-permute-done.11.refs_3_
  70.3 2.8 %update.4 = (bf16[16,96,1024]{2,1,0:T(8,128)(2,1)S(1)}, bf16[8,96,128]{2,1,0:T(8,128)(2,1)S(1)}, bf16[8,96,128]{2,1,0:T(8,128)(2,1)S(1)}, bf16[8,96,128]{2,1,0:T(8,128)(2,1)S(1)}, bf16[8,96,128]{2,1,0:T(8,128)(2,1)S(1)}) custom-call(bf16[8,96,128]{2,1,0:T(8,128)(2,1)S(1)} %get-tuple-element.96.refs_0_, ...), custom_call_target="tpu_custom_call" | custom-call | flops 1610612736 | bytes 9437184 | tf_op jit(solution)/shard_map/update/pallas_call | solution.py:494
  74.0 4.0 %collective-permute-done.20.refs_1_ = bf16[8,96,128]{2,1,0:T(8,128)(2,1)S(1)} collective-permute-done((bf16[8,96,128]{2,1,0:T(8,128)(2,1)S(1)}, bf16[8,96,128]{2,1,0:T(8,128)(2,1)S(1)}, u32[]{:S(2)}, u32[]{:S(2)}) %collective-permute-start.20) | collective-permute-done | bytes 196640 | tf_op jit(solution)/shard_map/ppermute | solution.py:395
  79.2 1.3 collective-permute-start.23
  80.5 5.1 %collective-permute-done.12.refs_1_ = bf16[8,96,128]{2,1,0:T(8,128)(2,1)S(1)} collective-permute-done((bf16[8,96,128]{2,1,0:T(8,128)(2,1)S(1)}, bf16[8,96,128]{2,1,0:T(8,128)(2,1)S(1)}, u32[]{:S(2)}, u32[]{:S(2)}) %collective-permute-start.12) | collective-permute-done | bytes 196640 | tf_op jit(solution)/shard_map/ppermute | solution.py:395
  85.7 1.9 collective-permute-done.14.refs_3_
  88.1 1.8 mix.12.refs_3_
  90.0 6.9 %collective-permute-done.15.refs_1_ = bf16[16,16,256]{2,1,0:T(8,128)(2,1)S(1)} collective-permute-done((bf16[16,16,256]{2,1,0:T(8,128)(2,1)S(1)}, bf16[16,16,256]{2,1,0:T(8,128)(2,1)S(1)}, u32[]{:S(2)}, u32[]{:S(2)}) %collective-permute-start.15) | collective-permute-done | bytes 131104 | tf_op jit(solution)/shard_map/ppermute | solution.py:395
  98.0 4.8 %collective-permute-done.32.theirs_ref = bf16[16,16,256]{2,1,0:T(8,128)(2,1)S(1)} collective-permute-done((bf16[16,16,256]{2,1,0:T(8,128)(2,1)S(1)}, bf16[16,16,256]{2,1,0:T(8,128)(2,1)S(1)}, u32[]{:S(2)}, u32[]{:S(2)}) %collective-permute-start.32) | collective-permute-done | bytes 131104 | tf_op jit(solution)/shard_map/ppermute | solution.py:395
  104.5 1.2 mix.13.mine_ref
  105.8 1.8 collective-permute-start.34
  108.4 2.7 %collective-permute-done.24.theirs_ref = bf16[16,16,256]{2,1,0:T(8,128)(2,1)S(1)} collective-permute-done((bf16[16,16,256]{2,1,0:T(8,128)(2,1)S(1)}, bf16[16,16,256]{2,1,0:T(8,128)(2,1)S(1)}, u32[]{:S(2)}, u32[]{:S(2)}) %collective-permute-start.24) | collective-permute-done | bytes 131104 | tf_op jit(solution)/shard_map/ppermute | solution.py:395
  111.7 1.2 collective-permute-start.25
  112.9 1.5 collective-permute-start.27
  114.4 6.0 %pointwise.4.refs_4_ = f32[32,96,1024]{2,1,0:T(8,128)S(1)} custom-call(bf16[16,96,1024]{2,1,0:T(8,128)(2,1)S(1)} %get-tuple-element.123.refs_0_, bf16[16,96,1024]{2,1,0:T(8,128)(2,1)S(1)} %get-tuple-element.124.refs_1_, bf16[32,96,1024]{2,1,0:T(8,128)(2,1)S(1)} %bitcast.17, bf16[512,512]{1,0:T(8,128)(2,1)S(1)} %get-tuple-element.100.refs_2_.refs_3_, ...), custom_call_target="tpu_custom_call" | custom-call | flops 3221225472 | bytes 25165824 | tf_op jit(solution)/shard_map/pointwise/pallas_call | solution.py:475
  120.5 2.8 %update.7 = (bf16[16,96,1024]{2,1,0:T(8,128)(2,1)S(1)}, bf16[8,96,128]{2,1,0:T(8,128)(2,1)S(1)}, bf16[8,96,128]{2,1,0:T(8,128)(2,1)S(1)}, bf16[8,96,128]{2,1,0:T(8,128)(2,1)S(1)}, bf16[8,96,128]{2,1,0:T(8,128)(2,1)S(1)}) custom-call(bf16[8,96,128]{2,1,0:T(8,128)(2,1)S(1)} %get-tuple-element.131.refs_0_, ...), custom_call_target="tpu_custom_call" | custom-call | flops 1610612736 | bytes 9437184 | tf_op jit(solution)/shard_map/update/pallas_call | solution.py:494
  123.3 1.2 collective-permute-start.36
  124.5 1.5 collective-permute-start.38
  126.0 2.8 %update.6 = (bf16[16,96,1024]{2,1,0:T(8,128)(2,1)S(1)}, bf16[8,96,128]{2,1,0:T(8,128)(2,1)S(1)}, bf16[8,96,128]{2,1,0:T(8,128)(2,1)S(1)}, bf16[8,96,128]{2,1,0:T(8,128)(2,1)S(1)}, bf16[8,96,128]{2,1,0:T(8,128)(2,1)S(1)}) custom-call(bf16[8,96,128]{2,1,0:T(8,128)(2,1)S(1)} %get-tuple-element.119.refs_0_, ...), custom_call_target="tpu_custom_call" | custom-call | flops 1610612736 | bytes 9437184 | tf_op jit(solution)/shard_map/update/pallas_call | solution.py:494
  128.8 1.2 collective-permute-start.28
  130.0 1.3 collective-permute-done.36.refs_1_
  131.5 1.7 collective-permute-done.38.refs_3_
  134.1 4.4 %collective-permute-done.28.refs_1_ = bf16[8,96,128]{2,1,0:T(8,128)(2,1)S(1)} collective-permute-done((bf16[8,96,128]{2,1,0:T(8,128)(2,1)S(1)}, bf16[8,96,128]{2,1,0:T(8,128)(2,1)S(1)}, u32[]{:S(2)}, u32[]{:S(2)}) %collective-permute-start.28) | collective-permute-done | bytes 196640 | tf_op jit(solution)/shard_map/ppermute | solution.py:395
  138.5 3.4 %collective-permute-done.30.refs_3_ = bf16[8,96,128]{2,1,0:T(8,128)(2,1)S(1)} collective-permute-done((bf16[8,96,128]{2,1,0:T(8,128)(2,1)S(1)}, bf16[8,96,128]{2,1,0:T(8,128)(2,1)S(1)}, u32[]{:S(2)}, u32[]{:S(2)}) %collective-permute-start.30) | collective-permute-done | bytes 196640 | tf_op jit(solution)/shard_map/ppermute | solution.py:395
  142.5 1.8 mix.15.refs_3_
  144.3 3.8 %collective-permute-done.31.refs_1_ = bf16[16,16,256]{2,1,0:T(8,128)(2,1)S(1)} collective-permute-done((bf16[16,16,256]{2,1,0:T(8,128)(2,1)S(1)}, bf16[16,16,256]{2,1,0:T(8,128)(2,1)S(1)}, u32[]{:S(2)}, u32[]{:S(2)}) %collective-permute-start.31) | collective-permute-done | bytes 131104 | tf_op jit(solution)/shard_map/ppermute | solution.py:395
  150.0 7.5 %collective-permute-done.44.theirs_ref = bf16[16,16,256]{2,1,0:T(8,128)(2,1)S(1)} collective-permute-done((bf16[16,16,256]{2,1,0:T(8,128)(2,1)S(1)}, bf16[16,16,256]{2,1,0:T(8,128)(2,1)S(1)}, u32[]{:S(2)}, u32[]{:S(2)}) %collective-permute-start.44) | collective-permute-done | bytes 131104 | tf_op jit(solution)/shard_map/ppermute | solution.py:395
  160.2 1.9 collective-permute-start.46
  162.1 1.2 collective-permute-start.47
  163.3 5.4 %collective-permute-done.40.theirs_ref = bf16[16,16,256]{2,1,0:T(8,128)(2,1)S(1)} collective-permute-done((bf16[16,16,256]{2,1,0:T(8,128)(2,1)S(1)}, bf16[16,16,256]{2,1,0:T(8,128)(2,1)S(1)}, u32[]{:S(2)}, u32[]{:S(2)}) %collective-permute-start.40) | collective-permute-done | bytes 131104 | tf_op jit(solution)/shard_map/ppermute | solution.py:395
  169.4 2.5 %collective-permute-start.43 = (bf16[8,96,128]{2,1,0:T(8,128)(2,1)S(1)}, bf16[8,96,128]{2,1,0:T(8,128)(2,1)S(1)}, u32[]{:S(2)}, u32[]{:S(2)}) collective-permute-start(bf16[8,96,128]{2,1,0:T(8,128)(2,1)S(1)} %get-tuple-element.144), channel_id=1, source_target_pairs={{0,3},{1,2},{2,1},{3,0},{4,7},{5,6},{6,5},{7,4},{8,11},{9,10},{10,... | collective-permute-start | bytes 589832 | tf_op jit(solution)/shard_map/ppermute | solution.py:395
  172.0 6.0 %pointwise.5.refs_6_ = f32[32,96,1024]{2,1,0:T(8,128)S(1)} custom-call(bf16[16,96,1024]{2,1,0:T(8,128)(2,1)S(1)} %get-tuple-element.145.refs_0_, bf16[16,96,1024]{2,1,0:T(8,128)(2,1)S(1)} %get-tuple-element.146.refs_1_, bf16[32,96,1024]{2,1,0:T(8,128)(2,1)S(1)} %bitcast.18, bf16[512,512]{1,0:T(8,128)(2,1)S(1)} %get-tuple-element.100.refs_2_.refs_3_, ...), custom_call_target="tpu_custom_call" | custom-call | flops 3221225472 | bytes 25165824 | tf_op jit(solution)/shard_map/pointwise/pallas_call | solution.py:475
  178.0 6.4 %last.2 = (f32[32,96,1024]{2,1,0:T(8,128)}, f32[96,1024]{1,0:T(8,128)S(1)}, f32[96,1024]{1,0:T(8,128)S(1)}, f32[96,1024]{1,0:T(8,128)S(1)}, f32[96,1024]{1,0:T(8...) custom-call(bf16[8,96,128]{2,1,0:T(8,128)(2,1)S(1)} %get-tuple-element.148.refs_0_, ...), custom_call_target="tpu_custom_call" | custom-call | flops 805306368 | bytes 12582912 | tf_op jit(solution)/shard_map/last/pallas_call | solution.py:518
  184.5 6.4 %last.3 = (f32[32,96,1024]{2,1,0:T(8,128)}, f32[96,1024]{1,0:T(8,128)S(1)}, f32[96,1024]{1,0:T(8,128)S(1)}, f32[96,1024]{1,0:T(8,128)S(1)}, f32[96,1024]{1,0:T(8...) custom-call(bf16[8,96,128]{2,1,0:T(8,128)(2,1)S(1)} %get-tuple-element.141.refs_0_, ...), custom_call_target="tpu_custom_call", output_to_operand_aliasing={{0}: (9, {})} | custom-call | flops 805306368 | bytes 12582912 | tf_op jit(solution)/shard_map/last/pallas_call | solution.py:518
  190.9 10.2 %collective-permute-start.51 = (f32[96,1024]{1,0:T(8,128)S(1)}, f32[96,1024]{1,0:T(8,128)S(1)}, u32[]{:S(2)}, u32[]{:S(2)}) collective-permute-start(f32[96,1024]{1,0:T(8,128)S(1)} %get-tuple-element.161.layer_ref.refs_3_), channel_id=1, source_target_pairs={{0,8},{8,0},{16,24},{24,16},{1,9},{9,1},{17,25},{25,17},{2,10},{10... | collective-permute-start | bytes 1179656 | tf_op jit(solution)/shard_map/ppermute | solution.py:579
  201.1 1.2 collective-permute-start.49
  202.3 3.0 %collective-permute-start.50 = (f32[2,1024]{1,0:T(2,128)S(1)}, f32[2,1024]{1,0:T(2,128)S(1)}, u32[]{:S(2)}, u32[]{:S(2)}) collective-permute-start(f32[2,1024]{1,0:T(2,128)S(1)} %get-tuple-element.163), channel_id=1, source_target_pairs={{1,0},{2,1},{3,2},{4,3},{5,4},{6,5},{7,6},{0,7},{9,8},{10,9},{11,1... | collective-permute-start | bytes 24584 | tf_op jit(solution)/shard_map/ppermute | solution.py:582
  206.3 1.2 collective-permute-start.52
  209.0 2.7 %collective-permute-start.53 = (f32[56,1024]{1,0:T(8,128)S(1)}, f32[56,1024]{1,0:T(8,128)S(1)}, u32[]{:S(2)}, u32[]{:S(2)}) collective-permute-start(f32[56,1024]{1,0:T(8,128)S(1)} %pair.1), channel_id=1, source_target_pairs={{0,16},{8,24},{1,17},{9,25},{2,18},{10,26},{3,19},{11,27},{4,20},{... | collective-permute-start | bytes 688136 | tf_op jit(solution)/shard_map/ppermute | solution.py:572
  211.7 1.9 collective-permute-start.48
  213.6 2.7 %collective-permute-done.53.refs_12_ = f32[56,1024]{1,0:T(8,128)S(1)} collective-permute-done((f32[56,1024]{1,0:T(8,128)S(1)}, f32[56,1024]{1,0:T(8,128)S(1)}, u32[]{:S(2)}, u32[]{:S(2)}) %collective-permute-start.53) | collective-permute-done | bytes 229408 | tf_op jit(solution)/shard_map/ppermute | solution.py:572
  216.3 2.0 collective-permute-start.54
  218.4 2.9 %collective-permute-done.48.refs_4_ = f32[96,1024]{1,0:T(8,128)S(1)} collective-permute-done((f32[96,1024]{1,0:T(8,128)S(1)}, f32[96,1024]{1,0:T(8,128)S(1)}, u32[]{:S(2)}, u32[]{:S(2)}) %collective-permute-start.48) | collective-permute-done | bytes 393248 | tf_op jit(solution)/shard_map/ppermute | solution.py:572
  221.3 2.2 residual.1
  (114 shorter events, 27.0 us)
Async XLA Ops:
  0.6 14.0 %copy-start = (bf16[256,1024]{1,0:T(8,128)(2,1)S(1)}, bf16[256,1024]{1,0:T(8,128)(2,1)}, u32[]{:S(2)}) copy-start(bf16[256,1024]{1,0:T(8,128)(2,1)} %constant.15.clone.inverse_ref) | copy-start | bytes 1572868
  1.8 12.8 %copy-start.2 = (bf16[8,96,256]{2,1,0:T(8,128)(2,1)S(1)}, bf16[8,96,256]{2,1,0:T(8,128)(2,1)}, u32[]{:S(2)}) copy-start(bf16[8,96,256]{2,1,0:T(8,128)(2,1)} %constant.16.clone.row_ref) | copy-start | bytes 1179652
  2.7 28.0 %slice-start = ((s8[8388608]{0:T(1024)(128)(4,1)}), s8[4194304]{0:T(1024)(128)(4,1)S(1)}, s32[]{:S(2)}) async-start(s8[8388608]{0:T(1024)(128)(4,1)} %bitcast.9), calls=%async_computation | async-start | bytes 8388608
  5.6 8.9 %collective-permute-start.4 = (bf16[8,96,128]{2,1,0:T(8,128)(2,1)S(1)}, bf16[8,96,128]{2,1,0:T(8,128)(2,1)S(1)}, u32[]{:S(2)}, u32[]{:S(2)}) collective-permute-start(bf16[8,96,128]{2,1,0:T(8,128)(2,1)S(1)} %get-tuple-element.91), channel_id=1, source_target_pairs={{0,1},{1,0},{2,3},{3,2},{4,5},{5,4},{6,7},{7,6},{8,9},{9,8},{10,11... | collective-permute-start | bytes 589832 | tf_op jit(solution)/shard_map/ppermute | solution.py:395
  7.7 7.8 %collective-permute-start.5 = (bf16[8,96,128]{2,1,0:T(8,128)(2,1)S(1)}, bf16[8,96,128]{2,1,0:T(8,128)(2,1)S(1)}, u32[]{:S(2)}, u32[]{:S(2)}) collective-permute-start(bf16[8,96,128]{2,1,0:T(8,128)(2,1)S(1)} %get-tuple-element.92), channel_id=1, source_target_pairs={{0,2},{1,3},{2,0},{3,1},{4,6},{5,7},{6,4},{7,5},{8,10},{9,11},{10,... | collective-permute-start | bytes 589832 | tf_op jit(solution)/shard_map/ppermute | solution.py:395
  9.0 21.7 %slice-start.1 = ((s8[8388608]{0:T(1024)(128)(4,1)}), s8[4194304]{0:T(1024)(128)(4,1)S(1)}, s32[]{:S(2)}) async-start(s8[8388608]{0:T(1024)(128)(4,1)} %bitcast.9), calls=%async_computation.1 | async-start | bytes 8388608
  9.0 8.5 %collective-permute-start.6 = (bf16[8,96,128]{2,1,0:T(8,128)(2,1)S(1)}, bf16[8,96,128]{2,1,0:T(8,128)(2,1)S(1)}, u32[]{:S(2)}, u32[]{:S(2)}) collective-permute-start(bf16[8,96,128]{2,1,0:T(8,128)(2,1)S(1)} %get-tuple-element.93), channel_id=1, source_target_pairs={{0,3},{1,2},{2,1},{3,0},{4,7},{5,6},{6,5},{7,4},{8,11},{9,10},{10,... | collective-permute-start | bytes 589832 | tf_op jit(solution)/shard_map/ppermute | solution.py:395
  11.9 10.1 %collective-permute-start = (bf16[8,96,128]{2,1,0:T(8,128)(2,1)S(1)}, bf16[8,96,128]{2,1,0:T(8,128)(2,1)S(1)}, u32[]{:S(2)}, u32[]{:S(2)}) collective-permute-start(bf16[8,96,128]{2,1,0:T(8,128)(2,1)S(1)} %get-tuple-element.84), channel_id=1, source_target_pairs={{0,1},{1,0},{2,3},{3,2},{4,5},{5,4},{6,7},{7,6},{8,9},{9,8},{10,11... | collective-permute-start | bytes 589832 | tf_op jit(solution)/shard_map/ppermute | solution.py:395
  13.3 8.7 %collective-permute-start.1 = (bf16[8,96,128]{2,1,0:T(8,128)(2,1)S(1)}, bf16[8,96,128]{2,1,0:T(8,128)(2,1)S(1)}, u32[]{:S(2)}, u32[]{:S(2)}) collective-permute-start(bf16[8,96,128]{2,1,0:T(8,128)(2,1)S(1)} %get-tuple-element.85), channel_id=1, source_target_pairs={{0,2},{1,3},{2,0},{3,1},{4,6},{5,7},{6,4},{7,5},{8,10},{9,11},{10,... | collective-permute-start | bytes 589832 | tf_op jit(solution)/shard_map/ppermute | solution.py:395
  14.5 14.3 %collective-permute-start.2 = (bf16[8,96,128]{2,1,0:T(8,128)(2,1)S(1)}, bf16[8,96,128]{2,1,0:T(8,128)(2,1)S(1)}, u32[]{:S(2)}, u32[]{:S(2)}) collective-permute-start(bf16[8,96,128]{2,1,0:T(8,128)(2,1)S(1)} %get-tuple-element.86), channel_id=1, source_target_pairs={{0,3},{1,2},{2,1},{3,0},{4,7},{5,6},{6,5},{7,4},{8,11},{9,10},{10,... | collective-permute-start | bytes 589832 | tf_op jit(solution)/shard_map/ppermute | solution.py:395
  18.1 12.6 %collective-permute-start.7 = (bf16[16,16,256]{2,1,0:T(8,128)(2,1)S(1)}, bf16[16,16,256]{2,1,0:T(8,128)(2,1)S(1)}, u32[]{:S(2)}, u32[]{:S(2)}) collective-permute-start(bf16[16,16,256]{2,1,0:T(8,128)(2,1)S(1)} %get-tuple-element.95), channel_id=1, source_target_pairs={{0,4},{1,5},{2,6},{3,7},{4,0},{5,1},{6,2},{7,3},{8,12},{9,13},{10,... | collective-permute-start | bytes 393224 | tf_op jit(solution)/shard_map/ppermute | solution.py:395
  29.3 8.7 %collective-permute-start.3 = (bf16[16,16,256]{2,1,0:T(8,128)(2,1)S(1)}, bf16[16,16,256]{2,1,0:T(8,128)(2,1)S(1)}, u32[]{:S(2)}, u32[]{:S(2)}) collective-permute-start(bf16[16,16,256]{2,1,0:T(8,128)(2,1)S(1)} %get-tuple-element.89), channel_id=1, source_target_pairs={{0,4},{1,5},{2,6},{3,7},{4,0},{5,1},{6,2},{7,3},{8,12},{9,13},{10,... | collective-permute-start | bytes 393224 | tf_op jit(solution)/shard_map/ppermute | solution.py:395
  30.7 8.5 %copy-start.4 = (bf16[32,32]{1,0:T(8,128)(2,1)S(1)}, bf16[32,32]{1,0:T(8,128)(2,1)}, u32[]{:S(2)}) copy-start(bf16[32,32]{1,0:T(8,128)(2,1)} %weight_ref.1) | copy-start | bytes 6148
  30.7 8.5 %copy-start.5 = (bf16[4,32]{1,0:T(4,128)(2,1)S(1)}, bf16[4,32]{1,0:T(4,128)(2,1)}, u32[]{:S(2)}) copy-start(bf16[4,32]{1,0:T(4,128)(2,1)} %decoder_ref.1) | copy-start | bytes 772
  38.0 15.8 %slice-start.2 = ((s8[6291456]{0:T(1024)(128)(4,1)}), s8[4194304]{0:T(1024)(128)(4,1)S(1)}, s32[]{:S(2)}) async-start(s8[6291456]{0:T(1024)(128)(4,1)} %bitcast.13), calls=%async_computation.2 | async-start | bytes 8388608
  39.0 11.4 %collective-permute-start.16 = (bf16[16,16,256]{2,1,0:T(8,128)(2,1)S(1)}, bf16[16,16,256]{2,1,0:T(8,128)(2,1)S(1)}, u32[]{:S(2)}, u32[]{:S(2)}) collective-permute-start(bf16[16,16,256]{2,1,0:T(8,128)(2,1)S(1)} %mix.11.mine_ref), channel_id=1, source_target_pairs={{0,4},{1,5},{2,6},{3,7},{4,0},{5,1},{6,2},{7,3},{8,12},{9,13},{10,... | collective-permute-start | bytes 393224 | tf_op jit(solution)/shard_map/ppermute | solution.py:395
  39.7 14.1 %slice-start.3 = ((s8[6291456]{0:T(1024)(128)(4,1)}), s8[2097152]{0:T(1024)(128)(4,1)S(1)}, s32[]{:S(2)}) async-start(s8[6291456]{0:T(1024)(128)(4,1)} %bitcast.13), calls=%async_computation.3 | async-start | bytes 4194304
  40.7 19.0 %collective-permute-start.8 = (bf16[16,16,256]{2,1,0:T(8,128)(2,1)S(1)}, bf16[16,16,256]{2,1,0:T(8,128)(2,1)S(1)}, u32[]{:S(2)}, u32[]{:S(2)}) collective-permute-start(bf16[16,16,256]{2,1,0:T(8,128)(2,1)S(1)} %mix.10.mine_ref), channel_id=1, source_target_pairs={{0,4},{1,5},{2,6},{3,7},{4,0},{5,1},{6,2},{7,3},{8,12},{9,13},{10,... | collective-permute-start | bytes 393224 | tf_op jit(solution)/shard_map/ppermute | solution.py:395
  51.0 11.5 %collective-permute-start.17 = (bf16[8,96,128]{2,1,0:T(8,128)(2,1)S(1)}, bf16[8,96,128]{2,1,0:T(8,128)(2,1)S(1)}, u32[]{:S(2)}, u32[]{:S(2)}) collective-permute-start(bf16[8,96,128]{2,1,0:T(8,128)(2,1)S(1)} %get-tuple-element.110), channel_id=1, source_target_pairs={{0,1},{1,0},{2,3},{3,2},{4,5},{5,4},{6,7},{7,6},{8,9},{9,8},{10,11... | collective-permute-start | bytes 589832 | tf_op jit(solution)/shard_map/ppermute | solution.py:395
  52.0 11.0 %collective-permute-start.18 = (bf16[8,96,128]{2,1,0:T(8,128)(2,1)S(1)}, bf16[8,96,128]{2,1,0:T(8,128)(2,1)S(1)}, u32[]{:S(2)}, u32[]{:S(2)}) collective-permute-start(bf16[8,96,128]{2,1,0:T(8,128)(2,1)S(1)} %get-tuple-element.111), channel_id=1, source_target_pairs={{0,2},{1,3},{2,0},{3,1},{4,6},{5,7},{6,4},{7,5},{8,10},{9,11},{10,... | collective-permute-start | bytes 589832 | tf_op jit(solution)/shard_map/ppermute | solution.py:395
  52.0 11.0 %collective-permute-start.19 = (bf16[8,96,128]{2,1,0:T(8,128)(2,1)S(1)}, bf16[8,96,128]{2,1,0:T(8,128)(2,1)S(1)}, u32[]{:S(2)}, u32[]{:S(2)}) collective-permute-start(bf16[8,96,128]{2,1,0:T(8,128)(2,1)S(1)} %get-tuple-element.112), channel_id=1, source_target_pairs={{0,3},{1,2},{2,1},{3,0},{4,7},{5,6},{6,5},{7,4},{8,11},{9,10},{10,... | collective-permute-start | bytes 589832 | tf_op jit(solution)/shard_map/ppermute | solution.py:395
  60.4 6.6 %collective-permute-start.10 = (bf16[8,96,128]{2,1,0:T(8,128)(2,1)S(1)}, bf16[8,96,128]{2,1,0:T(8,128)(2,1)S(1)}, u32[]{:S(2)}, u32[]{:S(2)}) collective-permute-start(bf16[8,96,128]{2,1,0:T(8,128)(2,1)S(1)} %get-tuple-element.98), channel_id=1, source_target_pairs={{0,2},{1,3},{2,0},{3,1},{4,6},{5,7},{6,4},{7,5},{8,10},{9,11},{10,... | collective-permute-start | bytes 589832 | tf_op jit(solution)/shard_map/ppermute | solution.py:395
  60.4 9.9 %collective-permute-start.11 = (bf16[8,96,128]{2,1,0:T(8,128)(2,1)S(1)}, bf16[8,96,128]{2,1,0:T(8,128)(2,1)S(1)}, u32[]{:S(2)}, u32[]{:S(2)}) collective-permute-start(bf16[8,96,128]{2,1,0:T(8,128)(2,1)S(1)} %get-tuple-element.99), channel_id=1, source_target_pairs={{0,3},{1,2},{2,1},{3,0},{4,7},{5,6},{6,5},{7,4},{8,11},{9,10},{10,... | collective-permute-start | bytes 589832 | tf_op jit(solution)/shard_map/ppermute | solution.py:395
  62.5 7.8 %collective-permute-start.9 = (bf16[8,96,128]{2,1,0:T(8,128)(2,1)S(1)}, bf16[8,96,128]{2,1,0:T(8,128)(2,1)S(1)}, u32[]{:S(2)}, u32[]{:S(2)}) collective-permute-start(bf16[8,96,128]{2,1,0:T(8,128)(2,1)S(1)} %get-tuple-element.97), channel_id=1, source_target_pairs={{0,1},{1,0},{2,3},{3,2},{4,5},{5,4},{6,7},{7,6},{8,9},{9,8},{10,11... | collective-permute-start | bytes 589832 | tf_op jit(solution)/shard_map/ppermute | solution.py:395
  65.9 12.1 %collective-permute-start.20 = (bf16[8,96,128]{2,1,0:T(8,128)(2,1)S(1)}, bf16[8,96,128]{2,1,0:T(8,128)(2,1)S(1)}, u32[]{:S(2)}, u32[]{:S(2)}) collective-permute-start(bf16[8,96,128]{2,1,0:T(8,128)(2,1)S(1)} %get-tuple-element.114), channel_id=1, source_target_pairs={{0,1},{1,0},{2,3},{3,2},{4,5},{5,4},{6,7},{7,6},{8,9},{9,8},{10,11... | collective-permute-start | bytes 589832 | tf_op jit(solution)/shard_map/ppermute | solution.py:395
  66.9 11.2 %collective-permute-start.21 = (bf16[8,96,128]{2,1,0:T(8,128)(2,1)S(1)}, bf16[8,96,128]{2,1,0:T(8,128)(2,1)S(1)}, u32[]{:S(2)}, u32[]{:S(2)}) collective-permute-start(bf16[8,96,128]{2,1,0:T(8,128)(2,1)S(1)} %get-tuple-element.115), channel_id=1, source_target_pairs={{0,2},{1,3},{2,0},{3,1},{4,6},{5,7},{6,4},{7,5},{8,10},{9,11},{10,... | collective-permute-start | bytes 589832 | tf_op jit(solution)/shard_map/ppermute | solution.py:395
  66.9 11.8 %collective-permute-start.22 = (bf16[8,96,128]{2,1,0:T(8,128)(2,1)S(1)}, bf16[8,96,128]{2,1,0:T(8,128)(2,1)S(1)}, u32[]{:S(2)}, u32[]{:S(2)}) collective-permute-start(bf16[8,96,128]{2,1,0:T(8,128)(2,1)S(1)} %get-tuple-element.116), channel_id=1, source_target_pairs={{0,3},{1,2},{2,1},{3,0},{4,7},{5,6},{6,5},{7,4},{8,11},{9,10},{10,... | collective-permute-start | bytes 589832 | tf_op jit(solution)/shard_map/ppermute | solution.py:395
  73.1 12.6 %collective-permute-start.12 = (bf16[8,96,128]{2,1,0:T(8,128)(2,1)S(1)}, bf16[8,96,128]{2,1,0:T(8,128)(2,1)S(1)}, u32[]{:S(2)}, u32[]{:S(2)}) collective-permute-start(bf16[8,96,128]{2,1,0:T(8,128)(2,1)S(1)} %get-tuple-element.104), channel_id=1, source_target_pairs={{0,1},{1,0},{2,3},{3,2},{4,5},{5,4},{6,7},{7,6},{8,9},{9,8},{10,11... | collective-permute-start | bytes 589832 | tf_op jit(solution)/shard_map/ppermute | solution.py:395
  73.7 12.0 %collective-permute-start.13 = (bf16[8,96,128]{2,1,0:T(8,128)(2,1)S(1)}, bf16[8,96,128]{2,1,0:T(8,128)(2,1)S(1)}, u32[]{:S(2)}, u32[]{:S(2)}) collective-permute-start(bf16[8,96,128]{2,1,0:T(8,128)(2,1)S(1)} %get-tuple-element.105), channel_id=1, source_target_pairs={{0,2},{1,3},{2,0},{3,1},{4,6},{5,7},{6,4},{7,5},{8,10},{9,11},{10,... | collective-permute-start | bytes 589832 | tf_op jit(solution)/shard_map/ppermute | solution.py:395
  77.9 9.6 %collective-permute-start.14 = (bf16[8,96,128]{2,1,0:T(8,128)(2,1)S(1)}, bf16[8,96,128]{2,1,0:T(8,128)(2,1)S(1)}, u32[]{:S(2)}, u32[]{:S(2)}) collective-permute-start(bf16[8,96,128]{2,1,0:T(8,128)(2,1)S(1)} %get-tuple-element.106), channel_id=1, source_target_pairs={{0,3},{1,2},{2,1},{3,0},{4,7},{5,6},{6,5},{7,4},{8,11},{9,10},{10,... | collective-permute-start | bytes 589832 | tf_op jit(solution)/shard_map/ppermute | solution.py:395
  79.2 8.9 %collective-permute-start.23 = (bf16[16,16,256]{2,1,0:T(8,128)(2,1)S(1)}, bf16[16,16,256]{2,1,0:T(8,128)(2,1)S(1)}, u32[]{:S(2)}, u32[]{:S(2)}) collective-permute-start(bf16[16,16,256]{2,1,0:T(8,128)(2,1)S(1)} %get-tuple-element.118), channel_id=1, source_target_pairs={{0,4},{1,5},{2,6},{3,7},{4,0},{5,1},{6,2},{7,3},{8,12},{9,13},{10,... | collective-permute-start | bytes 393224 | tf_op jit(solution)/shard_map/ppermute | solution.py:395
  88.1 8.8 %collective-permute-start.15 = (bf16[16,16,256]{2,1,0:T(8,128)(2,1)S(1)}, bf16[16,16,256]{2,1,0:T(8,128)(2,1)S(1)}, u32[]{:S(2)}, u32[]{:S(2)}) collective-permute-start(bf16[16,16,256]{2,1,0:T(8,128)(2,1)S(1)} %get-tuple-element.108), channel_id=1, source_target_pairs={{0,4},{1,5},{2,6},{3,7},{4,0},{5,1},{6,2},{7,3},{8,12},{9,13},{10,... | collective-permute-start | bytes 393224 | tf_op jit(solution)/shard_map/ppermute | solution.py:395
  97.9 4.9 %collective-permute-start.32 = (bf16[16,16,256]{2,1,0:T(8,128)(2,1)S(1)}, bf16[16,16,256]{2,1,0:T(8,128)(2,1)S(1)}, u32[]{:S(2)}, u32[]{:S(2)}) collective-permute-start(bf16[16,16,256]{2,1,0:T(8,128)(2,1)S(1)} %mix.14.mine_ref), channel_id=1, source_target_pairs={{0,4},{1,5},{2,6},{3,7},{4,0},{5,1},{6,2},{7,3},{8,12},{9,13},{10,... | collective-permute-start | bytes 393224 | tf_op jit(solution)/shard_map/ppermute | solution.py:395
  103.4 9.5 %collective-permute-start.33 = (bf16[8,96,128]{2,1,0:T(8,128)(2,1)S(1)}, bf16[8,96,128]{2,1,0:T(8,128)(2,1)S(1)}, u32[]{:S(2)}, u32[]{:S(2)}) collective-permute-start(bf16[8,96,128]{2,1,0:T(8,128)(2,1)S(1)} %get-tuple-element.132), channel_id=1, source_target_pairs={{0,1},{1,0},{2,3},{3,2},{4,5},{5,4},{6,7},{7,6},{8,9},{9,8},{10,11... | collective-permute-start | bytes 589832 | tf_op jit(solution)/shard_map/ppermute | solution.py:395
  105.7 5.5 %collective-permute-start.24 = (bf16[16,16,256]{2,1,0:T(8,128)(2,1)S(1)}, bf16[16,16,256]{2,1,0:T(8,128)(2,1)S(1)}, u32[]{:S(2)}, u32[]{:S(2)}) collective-permute-start(bf16[16,16,256]{2,1,0:T(8,128)(2,1)S(1)} %mix.13.mine_ref), channel_id=1, source_target_pairs={{0,4},{1,5},{2,6},{3,7},{4,0},{5,1},{6,2},{7,3},{8,12},{9,13},{10,... | collective-permute-start | bytes 393224 | tf_op jit(solution)/shard_map/ppermute | solution.py:395
  105.8 14.7 %collective-permute-start.34 = (bf16[8,96,128]{2,1,0:T(8,128)(2,1)S(1)}, bf16[8,96,128]{2,1,0:T(8,128)(2,1)S(1)}, u32[]{:S(2)}, u32[]{:S(2)}) collective-permute-start(bf16[8,96,128]{2,1,0:T(8,128)(2,1)S(1)} %get-tuple-element.133), channel_id=1, source_target_pairs={{0,2},{1,3},{2,0},{3,1},{4,6},{5,7},{6,4},{7,5},{8,10},{9,11},{10,... | collective-permute-start | bytes 589832 | tf_op jit(solution)/shard_map/ppermute | solution.py:395
  107.6 12.9 %collective-permute-start.35 = (bf16[8,96,128]{2,1,0:T(8,128)(2,1)S(1)}, bf16[8,96,128]{2,1,0:T(8,128)(2,1)S(1)}, u32[]{:S(2)}, u32[]{:S(2)}) collective-permute-start(bf16[8,96,128]{2,1,0:T(8,128)(2,1)S(1)} %get-tuple-element.134), channel_id=1, source_target_pairs={{0,3},{1,2},{2,1},{3,0},{4,7},{5,6},{6,5},{7,4},{8,11},{9,10},{10,... | collective-permute-start | bytes 589832 | tf_op jit(solution)/shard_map/ppermute | solution.py:395
  111.7 12.7 %collective-permute-start.25 = (bf16[8,96,128]{2,1,0:T(8,128)(2,1)S(1)}, bf16[8,96,128]{2,1,0:T(8,128)(2,1)S(1)}, u32[]{:S(2)}, u32[]{:S(2)}) collective-permute-start(bf16[8,96,128]{2,1,0:T(8,128)(2,1)S(1)} %get-tuple-element.120), channel_id=1, source_target_pairs={{0,1},{1,0},{2,3},{3,2},{4,5},{5,4},{6,7},{7,6},{8,9},{9,8},{10,11... | collective-permute-start | bytes 589832 | tf_op jit(solution)/shard_map/ppermute | solution.py:395
  112.9 13.1 %collective-permute-start.26 = (bf16[8,96,128]{2,1,0:T(8,128)(2,1)S(1)}, bf16[8,96,128]{2,1,0:T(8,128)(2,1)S(1)}, u32[]{:S(2)}, u32[]{:S(2)}) collective-permute-start(bf16[8,96,128]{2,1,0:T(8,128)(2,1)S(1)} %get-tuple-element.121), channel_id=1, source_target_pairs={{0,2},{1,3},{2,0},{3,1},{4,6},{5,7},{6,4},{7,5},{8,10},{9,11},{10,... | collective-permute-start | bytes 589832 | tf_op jit(solution)/shard_map/ppermute | solution.py:395
  112.9 13.1 %collective-permute-start.27 = (bf16[8,96,128]{2,1,0:T(8,128)(2,1)S(1)}, bf16[8,96,128]{2,1,0:T(8,128)(2,1)S(1)}, u32[]{:S(2)}, u32[]{:S(2)}) collective-permute-start(bf16[8,96,128]{2,1,0:T(8,128)(2,1)S(1)} %get-tuple-element.122), channel_id=1, source_target_pairs={{0,3},{1,2},{2,1},{3,0},{4,7},{5,6},{6,5},{7,4},{8,11},{9,10},{10,... | collective-permute-start | bytes 589832 | tf_op jit(solution)/shard_map/ppermute | solution.py:395
  123.3 8.0 %collective-permute-start.36 = (bf16[8,96,128]{2,1,0:T(8,128)(2,1)S(1)}, bf16[8,96,128]{2,1,0:T(8,128)(2,1)S(1)}, u32[]{:S(2)}, u32[]{:S(2)}) collective-permute-start(bf16[8,96,128]{2,1,0:T(8,128)(2,1)S(1)} %get-tuple-element.136), channel_id=1, source_target_pairs={{0,1},{1,0},{2,3},{3,2},{4,5},{5,4},{6,7},{7,6},{8,9},{9,8},{10,11... | collective-permute-start | bytes 589832 | tf_op jit(solution)/shard_map/ppermute | solution.py:395
  124.5 7.0 %collective-permute-start.37 = (bf16[8,96,128]{2,1,0:T(8,128)(2,1)S(1)}, bf16[8,96,128]{2,1,0:T(8,128)(2,1)S(1)}, u32[]{:S(2)}, u32[]{:S(2)}) collective-permute-start(bf16[8,96,128]{2,1,0:T(8,128)(2,1)S(1)} %get-tuple-element.137), channel_id=1, source_target_pairs={{0,2},{1,3},{2,0},{3,1},{4,6},{5,7},{6,4},{7,5},{8,10},{9,11},{10,... | collective-permute-start | bytes 589832 | tf_op jit(solution)/shard_map/ppermute | solution.py:395
  124.5 8.8 %collective-permute-start.38 = (bf16[8,96,128]{2,1,0:T(8,128)(2,1)S(1)}, bf16[8,96,128]{2,1,0:T(8,128)(2,1)S(1)}, u32[]{:S(2)}, u32[]{:S(2)}) collective-permute-start(bf16[8,96,128]{2,1,0:T(8,128)(2,1)S(1)} %get-tuple-element.138), channel_id=1, source_target_pairs={{0,3},{1,2},{2,1},{3,0},{4,7},{5,6},{6,5},{7,4},{8,11},{9,10},{10,... | collective-permute-start | bytes 589832 | tf_op jit(solution)/shard_map/ppermute | solution.py:395
  128.8 9.7 %collective-permute-start.28 = (bf16[8,96,128]{2,1,0:T(8,128)(2,1)S(1)}, bf16[8,96,128]{2,1,0:T(8,128)(2,1)S(1)}, u32[]{:S(2)}, u32[]{:S(2)}) collective-permute-start(bf16[8,96,128]{2,1,0:T(8,128)(2,1)S(1)} %get-tuple-element.126), channel_id=1, source_target_pairs={{0,1},{1,0},{2,3},{3,2},{4,5},{5,4},{6,7},{7,6},{8,9},{9,8},{10,11... | collective-permute-start | bytes 589832 | tf_op jit(solution)/shard_map/ppermute | solution.py:395
  130.0 8.5 %collective-permute-start.29 = (bf16[8,96,128]{2,1,0:T(8,128)(2,1)S(1)}, bf16[8,96,128]{2,1,0:T(8,128)(2,1)S(1)}, u32[]{:S(2)}, u32[]{:S(2)}) collective-permute-start(bf16[8,96,128]{2,1,0:T(8,128)(2,1)S(1)} %get-tuple-element.127), channel_id=1, source_target_pairs={{0,2},{1,3},{2,0},{3,1},{4,6},{5,7},{6,4},{7,5},{8,10},{9,11},{10,... | collective-permute-start | bytes 589832 | tf_op jit(solution)/shard_map/ppermute | solution.py:395
  131.3 10.6 %collective-permute-start.30 = (bf16[8,96,128]{2,1,0:T(8,128)(2,1)S(1)}, bf16[8,96,128]{2,1,0:T(8,128)(2,1)S(1)}, u32[]{:S(2)}, u32[]{:S(2)}) collective-permute-start(bf16[8,96,128]{2,1,0:T(8,128)(2,1)S(1)} %get-tuple-element.128), channel_id=1, source_target_pairs={{0,3},{1,2},{2,1},{3,0},{4,7},{5,6},{6,5},{7,4},{8,11},{9,10},{10,... | collective-permute-start | bytes 589832 | tf_op jit(solution)/shard_map/ppermute | solution.py:395
  133.7 8.7 %collective-permute-start.39 = (bf16[16,16,256]{2,1,0:T(8,128)(2,1)S(1)}, bf16[16,16,256]{2,1,0:T(8,128)(2,1)S(1)}, u32[]{:S(2)}, u32[]{:S(2)}) collective-permute-start(bf16[16,16,256]{2,1,0:T(8,128)(2,1)S(1)} %get-tuple-element.140), channel_id=1, source_target_pairs={{0,4},{1,5},{2,6},{3,7},{4,0},{5,1},{6,2},{7,3},{8,12},{9,13},{10,... | collective-permute-start | bytes 393224 | tf_op jit(solution)/shard_map/ppermute | solution.py:395
  142.4 5.8 %collective-permute-start.31 = (bf16[16,16,256]{2,1,0:T(8,128)(2,1)S(1)}, bf16[16,16,256]{2,1,0:T(8,128)(2,1)S(1)}, u32[]{:S(2)}, u32[]{:S(2)}) collective-permute-start(bf16[16,16,256]{2,1,0:T(8,128)(2,1)S(1)} %get-tuple-element.130), channel_id=1, source_target_pairs={{0,4},{1,5},{2,6},{3,7},{4,0},{5,1},{6,2},{7,3},{8,12},{9,13},{10,... | collective-permute-start | bytes 393224 | tf_op jit(solution)/shard_map/ppermute | solution.py:395
  149.2 8.3 %collective-permute-start.44 = (bf16[16,16,256]{2,1,0:T(8,128)(2,1)S(1)}, bf16[16,16,256]{2,1,0:T(8,128)(2,1)S(1)}, u32[]{:S(2)}, u32[]{:S(2)}) collective-permute-start(bf16[16,16,256]{2,1,0:T(8,128)(2,1)S(1)} %mix.17.mine_ref), channel_id=1, source_target_pairs={{0,4},{1,5},{2,6},{3,7},{4,0},{5,1},{6,2},{7,3},{8,12},{9,13},{10,... | collective-permute-start | bytes 393224 | tf_op jit(solution)/shard_map/ppermute | solution.py:395
  158.1 11.3 %collective-permute-start.45 = (bf16[8,96,128]{2,1,0:T(8,128)(2,1)S(1)}, bf16[8,96,128]{2,1,0:T(8,128)(2,1)S(1)}, u32[]{:S(2)}, u32[]{:S(2)}) collective-permute-start(bf16[8,96,128]{2,1,0:T(8,128)(2,1)S(1)} %get-tuple-element.149), channel_id=1, source_target_pairs={{0,1},{1,0},{2,3},{3,2},{4,5},{5,4},{6,7},{7,6},{8,9},{9,8},{10,11... | collective-permute-start | bytes 589832 | tf_op jit(solution)/shard_map/ppermute | solution.py:395
  160.1 8.5 %collective-permute-start.40 = (bf16[16,16,256]{2,1,0:T(8,128)(2,1)S(1)}, bf16[16,16,256]{2,1,0:T(8,128)(2,1)S(1)}, u32[]{:S(2)}, u32[]{:S(2)}) collective-permute-start(bf16[16,16,256]{2,1,0:T(8,128)(2,1)S(1)} %mix.16.mine_ref), channel_id=1, source_target_pairs={{0,4},{1,5},{2,6},{3,7},{4,0},{5,1},{6,2},{7,3},{8,12},{9,13},{10,... | collective-permute-start | bytes 393224 | tf_op jit(solution)/shard_map/ppermute | solution.py:395
  160.2 17.8 %collective-permute-start.46 = (bf16[8,96,128]{2,1,0:T(8,128)(2,1)S(1)}, bf16[8,96,128]{2,1,0:T(8,128)(2,1)S(1)}, u32[]{:S(2)}, u32[]{:S(2)}) collective-permute-start(bf16[8,96,128]{2,1,0:T(8,128)(2,1)S(1)} %get-tuple-element.150), channel_id=1, source_target_pairs={{0,2},{1,3},{2,0},{3,1},{4,6},{5,7},{6,4},{7,5},{8,10},{9,11},{10,... | collective-permute-start | bytes 589832 | tf_op jit(solution)/shard_map/ppermute | solution.py:395
  162.1 15.9 %collective-permute-start.47 = (bf16[8,96,128]{2,1,0:T(8,128)(2,1)S(1)}, bf16[8,96,128]{2,1,0:T(8,128)(2,1)S(1)}, u32[]{:S(2)}, u32[]{:S(2)}) collective-permute-start(bf16[8,96,128]{2,1,0:T(8,128)(2,1)S(1)} %get-tuple-element.151), channel_id=1, source_target_pairs={{0,3},{1,2},{2,1},{3,0},{4,7},{5,6},{6,5},{7,4},{8,11},{9,10},{10,... | collective-permute-start | bytes 589832 | tf_op jit(solution)/shard_map/ppermute | solution.py:395
  169.2 15.2 %collective-permute-start.41 = (bf16[8,96,128]{2,1,0:T(8,128)(2,1)S(1)}, bf16[8,96,128]{2,1,0:T(8,128)(2,1)S(1)}, u32[]{:S(2)}, u32[]{:S(2)}) collective-permute-start(bf16[8,96,128]{2,1,0:T(8,128)(2,1)S(1)} %get-tuple-element.142), channel_id=1, source_target_pairs={{0,1},{1,0},{2,3},{3,2},{4,5},{5,4},{6,7},{7,6},{8,9},{9,8},{10,11... | collective-permute-start | bytes 589832 | tf_op jit(solution)/shard_map/ppermute | solution.py:395
  169.3 15.1 %collective-permute-start.42 = (bf16[8,96,128]{2,1,0:T(8,128)(2,1)S(1)}, bf16[8,96,128]{2,1,0:T(8,128)(2,1)S(1)}, u32[]{:S(2)}, u32[]{:S(2)}) collective-permute-start(bf16[8,96,128]{2,1,0:T(8,128)(2,1)S(1)} %get-tuple-element.143), channel_id=1, source_target_pairs={{0,2},{1,3},{2,0},{3,1},{4,6},{5,7},{6,4},{7,5},{8,10},{9,11},{10,... | collective-permute-start | bytes 589832 | tf_op jit(solution)/shard_map/ppermute | solution.py:395
  169.4 15.0 %collective-permute-start.43 = (bf16[8,96,128]{2,1,0:T(8,128)(2,1)S(1)}, bf16[8,96,128]{2,1,0:T(8,128)(2,1)S(1)}, u32[]{:S(2)}, u32[]{:S(2)}) collective-permute-start(bf16[8,96,128]{2,1,0:T(8,128)(2,1)S(1)} %get-tuple-element.144), channel_id=1, source_target_pairs={{0,3},{1,2},{2,1},{3,0},{4,7},{5,6},{6,5},{7,4},{8,11},{9,10},{10,... | collective-permute-start | bytes 589832 | tf_op jit(solution)/shard_map/ppermute | solution.py:395
  184.5 33.8 %copy-start.7 = (f32[96]{0:T(128)S(1)}, f32[96]{0:T(128)}, u32[]{:S(2)}) copy-start(f32[96]{0:T(128)} %param.15) | copy-start | bytes 1156
  190.9 17.5 %collective-permute-start.51 = (f32[96,1024]{1,0:T(8,128)S(1)}, f32[96,1024]{1,0:T(8,128)S(1)}, u32[]{:S(2)}, u32[]{:S(2)}) collective-permute-start(f32[96,1024]{1,0:T(8,128)S(1)} %get-tuple-element.161.layer_ref.refs_3_), channel_id=1, source_target_pairs={{0,8},{8,0},{16,24},{24,16},{1,9},{9,1},{17,25},{25,17},{2,10},{10... | collective-permute-start | bytes 1179656 | tf_op jit(solution)/shard_map/ppermute | solution.py:579
  201.1 5.2 %collective-permute-start.49 = (f32[2,1024]{1,0:T(2,128)S(1)}, f32[2,1024]{1,0:T(2,128)S(1)}, u32[]{:S(2)}, u32[]{:S(2)}) collective-permute-start(f32[2,1024]{1,0:T(2,128)S(1)} %get-tuple-element.162), channel_id=1, source_target_pairs={{0,1},{1,2},{2,3},{3,4},{4,5},{5,6},{6,7},{7,0},{8,9},{9,10},{10,1... | collective-permute-start | bytes 24584 | tf_op jit(solution)/shard_map/ppermute | solution.py:581
  202.3 4.0 %collective-permute-start.50 = (f32[2,1024]{1,0:T(2,128)S(1)}, f32[2,1024]{1,0:T(2,128)S(1)}, u32[]{:S(2)}, u32[]{:S(2)}) collective-permute-start(f32[2,1024]{1,0:T(2,128)S(1)} %get-tuple-element.163), channel_id=1, source_target_pairs={{1,0},{2,1},{3,2},{4,3},{5,4},{6,5},{7,6},{0,7},{9,8},{10,9},{11,1... | collective-permute-start | bytes 24584 | tf_op jit(solution)/shard_map/ppermute | solution.py:582
  206.3 2.0 collective-permute-start.52
  209.0 7.3 %collective-permute-start.53 = (f32[56,1024]{1,0:T(8,128)S(1)}, f32[56,1024]{1,0:T(8,128)S(1)}, u32[]{:S(2)}, u32[]{:S(2)}) collective-permute-start(f32[56,1024]{1,0:T(8,128)S(1)} %pair.1), channel_id=1, source_target_pairs={{0,16},{8,24},{1,17},{9,25},{2,18},{10,26},{3,19},{11,27},{4,20},{... | collective-permute-start | bytes 688136 | tf_op jit(solution)/shard_map/ppermute | solution.py:572
  211.7 9.6 %collective-permute-start.48 = (f32[96,1024]{1,0:T(8,128)S(1)}, f32[96,1024]{1,0:T(8,128)S(1)}, u32[]{:S(2)}, u32[]{:S(2)}) collective-permute-start(f32[96,1024]{1,0:T(8,128)S(1)} %get-tuple-element.160.refs_2_), channel_id=1, source_target_pairs={{0,8},{8,16},{16,24},{1,9},{9,17},{17,25},{2,10},{10,18},{18,26},{... | collective-permute-start | bytes 1179656 | tf_op jit(solution)/shard_map/ppermute | solution.py:572
  216.3 5.0 %collective-permute-start.54 = (f32[56,1024]{1,0:T(8,128)S(1)}, f32[56,1024]{1,0:T(8,128)S(1)}, u32[]{:S(2)}, u32[]{:S(2)}) collective-permute-start(f32[56,1024]{1,0:T(8,128)S(1)} %collective-permute-done.53.refs_12_), channel_id=1, source_target_pairs={{0,8},{8,0},{16,24},{24,16},{1,9},{9,1},{17,25},{25,17},{2,10},{10... | collective-permute-start | bytes 688136 | tf_op jit(solution)/shard_map/ppermute | solution.py:600
  (3 other events, 15.6 us)
